TPU v7x, 128 devices: a whole 4x4x4 slice. The times are simulated.
128 devices in a mesh: row: 8 (over x, core), col: 16 (over z, y).
Axes of the slice: x: 4, y: 4, z: 4, core: 2. Of those that a mesh axis runs over, the one named last changes fastest.
Arguments:
- surface_head: float32 [512, 4096], P('row', 'col'), may hold values from -6 to 6
- conduct_x: float32 [512, 4096], P('row', 'col'), may hold values from 0.01 to 0.1
- conduct_y: float32 [512, 4096], P('row', 'col'), may hold values from 0.01 to 0.1
- porosity: float32 [512, 4096], P('row', 'col'), may hold values from 0.45 to 1
- rainfall: float32 [512, 4096], P('row', 'col'), may hold values from 0.005 to 0.1
- pipe_head: float32 [32, 32768], P(None, ('row', 'col')), may hold values from -6 to 6
- pipe_class: int32 [32768], P(('row', 'col')), may hold values from 0 to 3
- pipe_up: int32 [32768], P(('row', 'col')), may hold values from 0 to 4095
- pipe_down: int32 [32768], P(('row', 'col')), may hold values from 0 to 4095
- pipe_matrices: float32 [4, 32, 32], replicated
- link_cell: int32 [128, 128, 64], P(('row', 'col')), may hold values from -1 to 16383, as said below
- link_node: int32 [128, 128, 64], P(None, ('row', 'col')), may hold values from -1 to 8191, as said below
- link_coef: float32 [128, 128, 64], P(None, ('row', 'col')), may hold values from 0.05 to 0.4
Outputs:
- surface_out: float32 [512, 4096], P('row', 'col')
- pipe_out: float32 [32, 32768], P(None, ('row', 'col'))
Inputs may be any that keep to these rules, and one draw needn't show every extreme that they name: `link_cell`: for each source tile and pipe owner the live slots come first; each is a cell of the source tile counted row by row; the other slots are -1. In every draw some tile sends 64 live slots to some owner. `link_node`: -1 exactly where link_cell is -1 at the same source tile, owner and slot; else a node of the owner's pipes, numbered node * 256 + pipe.
All inputs are finite; a program needn't handle non-finite values.
Results may differ from a plain program's by a relative error of at most 0.00015.
Values sent between devices are 32-bit elements; how exact they have to be, the bound alone decides.
No kernel may reach another device: no remote copies, remote signals or barrier semaphores. Data moves between devices by JAX's collectives and lax.ppermute only.
A program may use at most 64 MiB of HBM per device.

v0:
```python
import jax
import jax.numpy as jnp
from jax import lax
from jax.sharding import PartitionSpec as P

CLASSES = 4
SWEEPS = 4
STEPS = 3


boundary_gain = 0.5


def passed_along(block, axis, distance):
    devices = range(lax.axis_size(axis))
    route = [(i - distance, i) for i in devices if i - distance in devices]
    return lax.ppermute(block, axis, route)


def with_halo(block, sides, width):
    for axis, dim in sides:
        count = lax.axis_size(axis)
        forward = [(i, i + 1) for i in range(count - 1)]
        backward = [(target, source) for source, target in forward]
        low = lax.ppermute(
            lax.slice_in_dim(block, block.shape[dim] - width, None, axis=dim), axis, forward
        )
        high = lax.ppermute(lax.slice_in_dim(block, 0, width, axis=dim), axis, backward)
        block = jnp.concatenate([low, block, high], axis=dim)
    return block


def sweep_once(
    center, north, south, west, east, north_gain, south_gain, west_gain, east_gain, inverse, source
):
    change = (
        north_gain * (north - center)
        + south_gain * (south - center)
        + west_gain * (west - center)
        + east_gain * (east - center)
    )
    return center + change * inverse + source


def body(
    surface_head,
    conduct_x,
    conduct_y,
    porosity,
    rainfall,
    pipe_head,
    pipe_class,
    pipe_up,
    pipe_down,
    pipe_matrices,
    link_cell,
    link_node,
    link_coef,
):
    tile_rows, tile_cols = surface_head.shape
    inverse = 1.0 / porosity
    from_above = passed_along(conduct_x[-1:, :], "row", 1)
    north_gain = jnp.concatenate([from_above, conduct_x[:-1, :]], axis=0)
    from_left = passed_along(conduct_y[:, -1:], "col", 1)
    west_gain = jnp.concatenate([from_left, conduct_y[:, :-1]], axis=1)
    cell_index = link_cell[0]
    cell_live = cell_index >= 0
    cell_safe = jnp.where(cell_live, cell_index, 0)
    node_index = link_node[:, 0, :]
    node_live = node_index >= 0
    node_safe = jnp.where(node_live, node_index, 0)
    link_gain = link_coef[:, 0, :]
    inverse_flat = inverse.reshape(-1)
    surface = surface_head
    pipe_state = pipe_head
    for coupling_step in range(STEPS):
        for sweep_index in range(SWEEPS):
            padded = with_halo(surface, (("row", 0), ("col", 1)), 1)
            surface = sweep_once(
                surface,
                padded[:-2, 1:-1],
                padded[2:, 1:-1],
                padded[1:-1, :-2],
                padded[1:-1, 2:],
                north_gain,
                conduct_x,
                west_gain,
                conduct_y,
                inverse,
                rainfall,
            )
        surface_flat = surface.reshape(-1)
        sent_heads = jnp.where(cell_live, surface_flat[cell_safe], 0.0)
        pipe_flat = pipe_state.reshape(-1)
        pipe_at_slots = jnp.where(node_live, pipe_flat[node_safe], 0.0)
        arrived = lax.all_to_all(
            sent_heads, ("row", "col"), split_axis=0, concat_axis=0, tiled=True
        )
        manhole_flow = jnp.where(node_live, link_gain * (arrived - pipe_at_slots), 0.0)
        inflow = jnp.zeros_like(pipe_flat).at[node_safe].add(manhole_flow).reshape(pipe_state.shape)
        returned = lax.all_to_all(
            manhole_flow, ("row", "col"), split_axis=0, concat_axis=0, tiled=True
        )
        surface = (
            surface_flat.at[cell_safe]
            .add(-(returned * inverse_flat[cell_safe]))
            .reshape(tile_rows, tile_cols)
        )
        first_heads, last_heads = (
            lax.all_gather(pipe_state[0], "col", axis=0, tiled=True),
            lax.all_gather(pipe_state[-1], "col", axis=0, tiled=True),
        )
        balance = pipe_state + inflow
        balance = balance.at[0].add(boundary_gain * last_heads[pipe_up])
        balance = balance.at[-1].add(boundary_gain * first_heads[pipe_down])
        updated = jnp.zeros_like(pipe_state)
        for class_index in range(CLASSES):
            product = jnp.dot(
                pipe_matrices[class_index],
                balance,
                precision=lax.Precision.HIGHEST,
                preferred_element_type=jnp.float32,
            )
            updated = jnp.where(pipe_class[None, :] == class_index, product, updated)
        pipe_state = updated
    return (surface, pipe_state)


def solution(mesh):
    placed = (
        P("row", "col"),
        P("row", "col"),
        P("row", "col"),
        P("row", "col"),
        P("row", "col"),
        P(None, ("row", "col")),
        P(("row", "col")),
        P(("row", "col")),
        P(("row", "col")),
        P(),
        P(("row", "col"), None, None),
        P(None, ("row", "col"), None),
        P(None, ("row", "col"), None),
    )
    return jax.shard_map(
        body,
        mesh=mesh,
        in_specs=placed,
        out_specs=(P("row", "col"), P(None, ("row", "col"))),
        check_vma=False,
    )
```

profile of v0, /device:TPU:1, one launch (start us, length us, event | category | flops | bytes accessed | tf_op | source)
XLA Modules:
  0.0 1038.9 jit_solution(1538303368657251957)
XLA Ops:
  1.4 3.3 collective-permute-start.2
  4.7 3.1 collective-permute-start.1
  8.5 2.5 collective-permute-start
  11.9 3.2 collective-permute-start.3
  20.0 4.0 collective-permute-start.4
  25.2 3.3 collective-permute-start.7
  28.6 3.0 collective-permute-start.6
  33.7 4.6 collective-permute-start.8
  38.3 23.2 %all-gather = f32[1,4096]{1,0:T(1,128)S(1)} all-gather(f32[1,256]{1,0:T(1,128)S(1)} %get-tuple-element.133), channel_id=2, replica_groups=mesh['row'=8,'col'=16] {'col'}, dimensions={1}, use_global_device_ids=true | all-gather | bytes 17408 | tf_op jit(solution)/shard_map/all_gather | solution.py:111
  63.3 7.5 collective-permute-start.11
  70.8 4.7 collective-permute-start.10
  77.7 4.0 collective-permute-start.12
  82.9 1.9 collective-permute-start.15
  84.8 5.3 collective-permute-start.14
  92.2 4.6 collective-permute-start.16
  96.8 19.4 %all-gather.1 = f32[1,4096]{1,0:T(1,128)S(1)} all-gather(f32[1,256]{1,0:T(1,128)S(1)} %get-tuple-element.132), channel_id=3, replica_groups=mesh['row'=8,'col'=16] {'col'}, dimensions={1}, use_global_device_ids=true | all-gather | bytes 17408 | tf_op jit(solution)/shard_map/all_gather | solution.py:110
  118.2 45.5 %gather_fusion = f32[8192]{0:T(1024)S(1)} fusion(f32[16384]{0:T(1024)S(1)} %bitcast.123, s32[8192]{0:T(1024)S(1)} %broadcast_clamp_fusion.1), kind=kCustom, calls=%fused_computation | custom fusion | bytes 98304 | tf_op jit(solution)/shard_map/gather | solution.py:93
  164.5 12.9 %all-to-all-start = ((f32[128,1,64]{2,1,0:T(1,128)}), f32[128,1,64]{2,1,0:T(1,128)S(1)}, u32[]{:S(2)}, u32[]{:S(2)}) async-start(f32[128,1,64]{2,1,0:T(1,128)} %bitcast.2), calls=%async_computation | async-start | bytes 131072 | tf_op jit(solution)/shard_map/all_to_all | solution.py:96
  177.5 45.5 %gather_fusion.1 = f32[8192]{0:T(1024)S(1)} fusion(f32[8192]{0:T(1024)S(1)} %bitcast.130, s32[8192]{0:T(1024)S(1)} %broadcast_clamp_fusion), kind=kCustom, calls=%fused_computation.1 | custom fusion | bytes 98304 | tf_op jit(solution)/shard_map/gather | solution.py:95
  224.1 45.5 %gather_fusion.2 = f32[8192]{0:T(1024)S(1)} fusion(f32[16384]{0:T(1024)S(1)} %bitcast.132, s32[8192]{0:T(1024)S(1)} %broadcast_clamp_fusion.1), kind=kCustom, calls=%fused_computation.2 | custom fusion | bytes 98304 | tf_op jit(solution)/shard_map/gather | solution.py:106
  270.3 9.8 all-to-all-start.1
  280.2 44.8 %scatter_custom_fusion.1 = f32[8192]{0:T(1024)S(1)} fusion(s32[8192]{0:T(1024)S(1)} %reshape.369, f32[8192]{0:T(1024)S(1)} %reshape.475, f32[]{:T(128)} %constant.152.clone.1), kind=kCustom, calls=%fused_computation.362 | custom fusion | flops 8192 | bytes 32772 | tf_op jit(solution)/shard_map/scatter-add | solution.py:100
  325.2 50.1 %scatter_fusion = f32[16384]{0:T(1024)S(1)} fusion(f32[16384]{0:T(1024)S(1)} %bitcast.124, s32[8192]{0:T(1024)S(1)} %reshape.465, f32[8192]{0:T(1024)S(1)} %reshape.467), kind=kCustom, calls=%fused_computation.13 | custom fusion | flops 8192 | bytes 131072 | tf_op jit(solution)/shard_map/scatter-add | solution.py:106
  375.4 2.9 collective-permute-start.19
  378.3 3.0 collective-permute-start.18
  383.4 9.9 collective-permute-start.20
  394.5 2.1 collective-permute-start.23
  396.6 4.8 collective-permute-start.22
  403.6 4.6 collective-permute-start.24
  409.3 1.9 collective-permute-start.27
  411.3 5.0 collective-permute-start.26
  418.4 4.6 collective-permute-start.28
  423.0 25.3 %all-gather.2 = f32[1,4096]{1,0:T(1,128)S(1)} all-gather(f32[1,256]{1,0:T(1,128)S(1)} %get-tuple-element.131), channel_id=4, replica_groups=mesh['row'=8,'col'=16] {'col'}, dimensions={1}, use_global_device_ids=true | all-gather | bytes 17408 | tf_op jit(solution)/shard_map/all_gather | solution.py:111
  450.1 5.2 collective-permute-start.31
  455.3 7.0 collective-permute-start.30
  464.4 4.0 collective-permute-start.32
  468.4 17.8 %all-gather.3 = f32[1,4096]{1,0:T(1,128)S(1)} all-gather(f32[1,256]{1,0:T(1,128)S(1)} %get-tuple-element.130), channel_id=5, replica_groups=mesh['row'=8,'col'=16] {'col'}, dimensions={1}, use_global_device_ids=true | all-gather | bytes 17408 | tf_op jit(solution)/shard_map/all_gather | solution.py:110
  488.1 45.5 %gather_fusion.3 = f32[8192]{0:T(1024)S(1)} fusion(f32[16384]{0:T(1024)S(1)} %bitcast.125, s32[8192]{0:T(1024)S(1)} %broadcast_clamp_fusion.1), kind=kCustom, calls=%fused_computation.3 | custom fusion | bytes 98304 | tf_op jit(solution)/shard_map/gather | solution.py:93
  534.4 12.9 %all-to-all-start.2 = ((f32[128,1,64]{2,1,0:T(1,128)}), f32[128,1,64]{2,1,0:T(1,128)S(1)}, u32[]{:S(2)}, u32[]{:S(2)}) async-start(f32[128,1,64]{2,1,0:T(1,128)} %bitcast.9), calls=%async_computation.2 | async-start | bytes 131072 | tf_op jit(solution)/shard_map/all_to_all | solution.py:96
  547.3 45.5 %gather_fusion.6 = f32[8192]{0:T(1024)S(1)} fusion(f32[8192]{0:T(1024)S(1)} %bitcast.131, s32[8192]{0:T(1024)S(1)} %broadcast_clamp_fusion), kind=kCustom, calls=%fused_computation.6 | custom fusion | bytes 98304 | tf_op jit(solution)/shard_map/gather | solution.py:95
  593.6 9.8 all-to-all-start.3
  603.5 44.8 %scatter_custom_fusion.3 = f32[8192]{0:T(1024)S(1)} fusion(s32[8192]{0:T(1024)S(1)} %reshape.369, f32[8192]{0:T(1024)S(1)} %reshape.491, f32[]{:T(128)} %constant.152.clone.1), kind=kCustom, calls=%fused_computation.360 | custom fusion | flops 8192 | bytes 32772 | tf_op jit(solution)/shard_map/scatter-add | solution.py:100
  648.5 50.1 %scatter_fusion.1 = f32[16384]{0:T(1024)S(1)} fusion(f32[16384]{0:T(1024)S(1)} %bitcast.126, s32[8192]{0:T(1024)S(1)} %reshape.465, f32[8192]{0:T(1024)S(1)} %reshape.483), kind=kCustom, calls=%fused_computation.15 | custom fusion | flops 8192 | bytes 131072 | tf_op jit(solution)/shard_map/scatter-add | solution.py:106
  698.7 2.9 collective-permute-start.35
  701.6 3.0 collective-permute-start.34
  706.7 9.9 collective-permute-start.36
  717.8 2.1 collective-permute-start.39
  719.9 4.8 collective-permute-start.38
  726.9 4.6 collective-permute-start.40
  732.6 1.9 collective-permute-start.43
  734.6 5.0 collective-permute-start.42
  741.7 4.6 collective-permute-start.44
  746.3 25.3 %all-gather.4 = f32[1,4096]{1,0:T(1,128)S(1)} all-gather(f32[1,256]{1,0:T(1,128)S(1)} %get-tuple-element.129), channel_id=6, replica_groups=mesh['row'=8,'col'=16] {'col'}, dimensions={1}, use_global_device_ids=true | all-gather | bytes 17408 | tf_op jit(solution)/shard_map/all_gather | solution.py:111
  773.4 5.2 collective-permute-start.47
  778.6 7.0 collective-permute-start.46
  787.7 4.0 collective-permute-start.48
  791.7 17.8 %all-gather.5 = f32[1,4096]{1,0:T(1,128)S(1)} all-gather(f32[1,256]{1,0:T(1,128)S(1)} %get-tuple-element.128), channel_id=7, replica_groups=mesh['row'=8,'col'=16] {'col'}, dimensions={1}, use_global_device_ids=true | all-gather | bytes 17408 | tf_op jit(solution)/shard_map/all_gather | solution.py:110
  811.4 45.5 %gather_fusion.7 = f32[8192]{0:T(1024)S(1)} fusion(f32[16384]{0:T(1024)S(1)} %bitcast.127, s32[8192]{0:T(1024)S(1)} %broadcast_clamp_fusion.1), kind=kCustom, calls=%fused_computation.7 | custom fusion | bytes 98304 | tf_op jit(solution)/shard_map/gather | solution.py:93
  857.6 12.9 %all-to-all-start.4 = ((f32[128,1,64]{2,1,0:T(1,128)}), f32[128,1,64]{2,1,0:T(1,128)S(1)}, u32[]{:S(2)}, u32[]{:S(2)}) async-start(f32[128,1,64]{2,1,0:T(1,128)} %bitcast.27), calls=%async_computation.4 | async-start | bytes 131072 | tf_op jit(solution)/shard_map/all_to_all | solution.py:96
  870.5 45.5 %gather_fusion.10 = f32[8192]{0:T(1024)S(1)} fusion(f32[8192]{0:T(1024)S(1)} %bitcast.129, s32[8192]{0:T(1024)S(1)} %broadcast_clamp_fusion), kind=kCustom, calls=%fused_computation.10 | custom fusion | bytes 98304 | tf_op jit(solution)/shard_map/gather | solution.py:95
  916.3 44.8 %scatter_custom_fusion.5 = f32[8192]{0:T(1024)S(1)} fusion(s32[8192]{0:T(1024)S(1)} %reshape.369, f32[8192]{0:T(1024)S(1)} %reshape.507, f32[]{:T(128)} %constant.152.clone.1), kind=kCustom, calls=%fused_computation.358 | custom fusion | flops 8192 | bytes 32772 | tf_op jit(solution)/shard_map/scatter-add | solution.py:100
  962.4 15.9 %all-to-all-start.5 = ((f32[128,1,64]{2,1,0:T(1,128)}), f32[128,1,64]{2,1,0:T(1,128)S(1)}, u32[]{:S(2)}, u32[]{:S(2)}) async-start(f32[128,1,64]{2,1,0:T(1,128)} %bitcast.35), calls=%async_computation.5 | async-start | bytes 131072 | tf_op jit(solution)/shard_map/all_to_all | solution.py:101
  979.1 8.9 all-to-all-done.5
  988.1 50.1 %scatter_fusion.2 = f32[16384]{0:T(1024)S(1)} fusion(f32[16384]{0:T(1024)S(1)} %bitcast.128, s32[8192]{0:T(1024)S(1)} %reshape.465, f32[8192]{0:T(1024)S(1)} %reshape.499), kind=kCustom, calls=%fused_computation.17 | custom fusion | flops 8192 | bytes 131072 | tf_op jit(solution)/shard_map/scatter-add | solution.py:106
  (243 shorter events, 56.5 us)
Async XLA Ops:
  1.4 17.1 %collective-permute-start.2 = (f32[1,256]{1,0:T(1,128)S(1)}, f32[1,256]{1,0:T(1,128)S(1)}, u32[]{:S(2)}, u32[]{:S(2)}) collective-permute-start(f32[1,256]{1,0:T(1,128)S(1)} %get-tuple-element.127), channel_id=1, source_target_pairs={{16,0},{32,16},{48,32},{64,48},{80,64},{96,80},{112,96},{17,1},{33... | collective-permute-start | bytes 3080 | tf_op jit(solution)/shard_map/ppermute | solution.py:28
  4.7 13.8 %collective-permute-start.1 = (f32[1,256]{1,0:T(1,128)S(1)}, f32[1,256]{1,0:T(1,128)S(1)}, u32[]{:S(2)}, u32[]{:S(2)}) collective-permute-start(f32[1,256]{1,0:T(1,128)S(1)} %get-tuple-element.126), channel_id=1, source_target_pairs={{0,16},{16,32},{32,48},{48,64},{64,80},{80,96},{96,112},{1,17},{17... | collective-permute-start | bytes 3080 | tf_op jit(solution)/shard_map/ppermute | solution.py:25
  8.5 6.6 copy-start.7
  8.5 15.5 %collective-permute-start = (f32[1,256]{1,0:T(1,128)S(1)}, f32[1,256]{1,0:T(1,128)S(1)}, u32[]{:S(2)}, u32[]{:S(2)}) collective-permute-start(f32[1,256]{1,0:T(1,128)S(1)} %slice.500), channel_id=1, source_target_pairs={{0,16},{16,32},{32,48},{48,64},{64,80},{80,96},{96,112},{1,17},{17... | collective-permute-start | bytes 3080 | tf_op jit(solution)/shard_map/ppermute | solution.py:17
  11.9 12.2 %collective-permute-start.3 = (f32[64,1]{1,0:T(8,128)S(1)}, f32[64,1]{1,0:T(8,128)S(1)}, u32[]{:S(2)}, u32[]{:S(2)}) collective-permute-start(f32[64,1]{1,0:T(8,128)S(1)} %slice.506), channel_id=1, source_target_pairs={{0,1},{1,2},{2,3},{3,4},{4,5},{5,6},{6,7},{7,8},{8,9},{9,10},{10,1... | collective-permute-start | bytes 776 | tf_op jit(solution)/shard_map/ppermute | solution.py:17
  17.0 1.5 copy-start.5
  18.4 6.6 copy-start.3
  18.5 6.6 copy-start
  18.5 6.6 copy-start.1
  18.6 5.4 copy-start.11
  18.6 5.5 collective-permute-start.5
  20.0 5.0 collective-permute-start.4
  25.2 6.4 collective-permute-start.7
  28.6 3.7 collective-permute-start.6
  32.4 30.8 %collective-permute-start.9 = (f32[66,1]{1,0:T(8,128)S(1)}, f32[66,1]{1,0:T(8,128)S(1)}, u32[]{:S(2)}, u32[]{:S(2)}) collective-permute-start(f32[66,1]{1,0:T(8,128)S(1)} %get-tuple-element.101), channel_id=1, source_target_pairs={{1,0},{2,1},{3,2},{4,3},{5,4},{6,5},{7,6},{8,7},{9,8},{10,9},{11,1... | collective-permute-start | bytes 800 | tf_op jit(solution)/shard_map/ppermute | solution.py:28
  33.7 29.5 %collective-permute-start.8 = (f32[66,1]{1,0:T(8,128)S(1)}, f32[66,1]{1,0:T(8,128)S(1)}, u32[]{:S(2)}, u32[]{:S(2)}) collective-permute-start(f32[66,1]{1,0:T(8,128)S(1)} %get-tuple-element.100), channel_id=1, source_target_pairs={{0,1},{1,2},{2,3},{3,4},{4,5},{5,6},{6,7},{7,8},{8,9},{9,10},{10,1... | collective-permute-start | bytes 800 | tf_op jit(solution)/shard_map/ppermute | solution.py:25
  63.3 12.2 %collective-permute-start.11 = (f32[1,256]{1,0:T(1,128)S(1)}, f32[1,256]{1,0:T(1,128)S(1)}, u32[]{:S(2)}, u32[]{:S(2)}) collective-permute-start(f32[1,256]{1,0:T(1,128)S(1)} %get-tuple-element.123), channel_id=1, source_target_pairs={{16,0},{32,16},{48,32},{64,48},{80,64},{96,80},{112,96},{17,1},{33... | collective-permute-start | bytes 3080 | tf_op jit(solution)/shard_map/ppermute | solution.py:28
  70.8 5.4 collective-permute-start.10
  76.3 5.4 copy-start.12
  76.3 5.4 collective-permute-start.13
  77.7 5.0 collective-permute-start.12
  82.9 7.3 collective-permute-start.15
  84.8 6.0 collective-permute-start.14
  90.9 27.1 %collective-permute-start.17 = (f32[66,1]{1,0:T(8,128)S(1)}, f32[66,1]{1,0:T(8,128)S(1)}, u32[]{:S(2)}, u32[]{:S(2)}) collective-permute-start(f32[66,1]{1,0:T(8,128)S(1)} %get-tuple-element.97), channel_id=1, source_target_pairs={{1,0},{2,1},{3,2},{4,3},{5,4},{6,5},{7,6},{8,7},{9,8},{10,9},{11,1... | collective-permute-start | bytes 800 | tf_op jit(solution)/shard_map/ppermute | solution.py:28
  92.2 25.8 %collective-permute-start.16 = (f32[66,1]{1,0:T(8,128)S(1)}, f32[66,1]{1,0:T(8,128)S(1)}, u32[]{:S(2)}, u32[]{:S(2)}) collective-permute-start(f32[66,1]{1,0:T(8,128)S(1)} %get-tuple-element.96), channel_id=1, source_target_pairs={{0,1},{1,2},{2,3},{3,4},{4,5},{5,6},{6,7},{7,8},{8,9},{9,10},{10,1... | collective-permute-start | bytes 800 | tf_op jit(solution)/shard_map/ppermute | solution.py:25
  164.5 105.2 %all-to-all-start = ((f32[128,1,64]{2,1,0:T(1,128)}), f32[128,1,64]{2,1,0:T(1,128)S(1)}, u32[]{:S(2)}, u32[]{:S(2)}) async-start(f32[128,1,64]{2,1,0:T(1,128)} %bitcast.2), calls=%async_computation | async-start | bytes 131072 | tf_op jit(solution)/shard_map/all_to_all | solution.py:96
  270.3 54.8 %all-to-all-start.1 = ((f32[128,1,64]{2,1,0:T(1,128)}), f32[128,1,64]{2,1,0:T(1,128)S(1)}, u32[]{:S(2)}, u32[]{:S(2)}) async-start(f32[128,1,64]{2,1,0:T(1,128)} %bitcast.5), calls=%async_computation.1 | async-start | bytes 131072 | tf_op jit(solution)/shard_map/all_to_all | solution.py:101
  325.2 56.1 %copy-start.4 = (f32[4,32,32]{2,1,0:T(8,128)S(1)}, f32[4,32,32]{2,1,0:T(8,128)}, u32[]{:S(2)}) copy-start(f32[4,32,32]{2,1,0:T(8,128)} %param.34) | copy-start | bytes 49156
  375.4 6.2 collective-permute-start.19
  378.3 3.7 collective-permute-start.18
  382.2 11.4 %collective-permute-start.21 = (f32[66,1]{1,0:T(8,128)S(1)}, f32[66,1]{1,0:T(8,128)S(1)}, u32[]{:S(2)}, u32[]{:S(2)}) collective-permute-start(f32[66,1]{1,0:T(8,128)S(1)} %get-tuple-element.95), channel_id=1, source_target_pairs={{1,0},{2,1},{3,2},{4,3},{5,4},{6,5},{7,6},{8,7},{9,8},{10,9},{11,1... | collective-permute-start | bytes 800 | tf_op jit(solution)/shard_map/ppermute | solution.py:28
  383.4 11.0 %collective-permute-start.20 = (f32[66,1]{1,0:T(8,128)S(1)}, f32[66,1]{1,0:T(8,128)S(1)}, u32[]{:S(2)}, u32[]{:S(2)}) collective-permute-start(f32[66,1]{1,0:T(8,128)S(1)} %get-tuple-element.94), channel_id=1, source_target_pairs={{0,1},{1,2},{2,3},{3,4},{4,5},{5,6},{6,7},{7,8},{8,9},{9,10},{10,1... | collective-permute-start | bytes 800 | tf_op jit(solution)/shard_map/ppermute | solution.py:25
  394.5 7.1 collective-permute-start.23
  396.6 5.5 collective-permute-start.22
  402.3 6.1 collective-permute-start.25
  403.6 5.6 collective-permute-start.24
  409.3 7.0 collective-permute-start.27
  411.3 5.7 collective-permute-start.26
  417.1 32.9 %collective-permute-start.29 = (f32[66,1]{1,0:T(8,128)S(1)}, f32[66,1]{1,0:T(8,128)S(1)}, u32[]{:S(2)}, u32[]{:S(2)}) collective-permute-start(f32[66,1]{1,0:T(8,128)S(1)} %get-tuple-element.91), channel_id=1, source_target_pairs={{1,0},{2,1},{3,2},{4,3},{5,4},{6,5},{7,6},{8,7},{9,8},{10,9},{11,1... | collective-permute-start | bytes 800 | tf_op jit(solution)/shard_map/ppermute | solution.py:28
  418.4 31.6 %collective-permute-start.28 = (f32[66,1]{1,0:T(8,128)S(1)}, f32[66,1]{1,0:T(8,128)S(1)}, u32[]{:S(2)}, u32[]{:S(2)}) collective-permute-start(f32[66,1]{1,0:T(8,128)S(1)} %get-tuple-element.90), channel_id=1, source_target_pairs={{0,1},{1,2},{2,3},{3,4},{4,5},{5,6},{6,7},{7,8},{8,9},{9,10},{10,1... | collective-permute-start | bytes 800 | tf_op jit(solution)/shard_map/ppermute | solution.py:25
  450.1 12.2 %collective-permute-start.31 = (f32[1,256]{1,0:T(1,128)S(1)}, f32[1,256]{1,0:T(1,128)S(1)}, u32[]{:S(2)}, u32[]{:S(2)}) collective-permute-start(f32[1,256]{1,0:T(1,128)S(1)} %get-tuple-element.113), channel_id=1, source_target_pairs={{16,0},{32,16},{48,32},{64,48},{80,64},{96,80},{112,96},{17,1},{33... | collective-permute-start | bytes 3080 | tf_op jit(solution)/shard_map/ppermute | solution.py:28
  455.3 7.7 collective-permute-start.30
  463.1 24.8 %collective-permute-start.33 = (f32[66,1]{1,0:T(8,128)S(1)}, f32[66,1]{1,0:T(8,128)S(1)}, u32[]{:S(2)}, u32[]{:S(2)}) collective-permute-start(f32[66,1]{1,0:T(8,128)S(1)} %get-tuple-element.89), channel_id=1, source_target_pairs={{1,0},{2,1},{3,2},{4,3},{5,4},{6,5},{7,6},{8,7},{9,8},{10,9},{11,1... | collective-permute-start | bytes 800 | tf_op jit(solution)/shard_map/ppermute | solution.py:28
  464.4 23.5 %collective-permute-start.32 = (f32[66,1]{1,0:T(8,128)S(1)}, f32[66,1]{1,0:T(8,128)S(1)}, u32[]{:S(2)}, u32[]{:S(2)}) collective-permute-start(f32[66,1]{1,0:T(8,128)S(1)} %get-tuple-element.88), channel_id=1, source_target_pairs={{0,1},{1,2},{2,3},{3,4},{4,5},{5,6},{6,7},{7,8},{8,9},{9,10},{10,1... | collective-permute-start | bytes 800 | tf_op jit(solution)/shard_map/ppermute | solution.py:25
  534.4 58.6 %all-to-all-start.2 = ((f32[128,1,64]{2,1,0:T(1,128)}), f32[128,1,64]{2,1,0:T(1,128)S(1)}, u32[]{:S(2)}, u32[]{:S(2)}) async-start(f32[128,1,64]{2,1,0:T(1,128)} %bitcast.9), calls=%async_computation.2 | async-start | bytes 131072 | tf_op jit(solution)/shard_map/all_to_all | solution.py:96
  593.6 54.8 %all-to-all-start.3 = ((f32[128,1,64]{2,1,0:T(1,128)}), f32[128,1,64]{2,1,0:T(1,128)S(1)}, u32[]{:S(2)}, u32[]{:S(2)}) async-start(f32[128,1,64]{2,1,0:T(1,128)} %bitcast.23), calls=%async_computation.3 | async-start | bytes 131072 | tf_op jit(solution)/shard_map/all_to_all | solution.py:101
  698.7 6.2 collective-permute-start.35
  701.6 3.7 collective-permute-start.34
  705.4 11.4 %collective-permute-start.37 = (f32[66,1]{1,0:T(8,128)S(1)}, f32[66,1]{1,0:T(8,128)S(1)}, u32[]{:S(2)}, u32[]{:S(2)}) collective-permute-start(f32[66,1]{1,0:T(8,128)S(1)} %get-tuple-element.87), channel_id=1, source_target_pairs={{1,0},{2,1},{3,2},{4,3},{5,4},{6,5},{7,6},{8,7},{9,8},{10,9},{11,1... | collective-permute-start | bytes 800 | tf_op jit(solution)/shard_map/ppermute | solution.py:28
  706.7 11.0 %collective-permute-start.36 = (f32[66,1]{1,0:T(8,128)S(1)}, f32[66,1]{1,0:T(8,128)S(1)}, u32[]{:S(2)}, u32[]{:S(2)}) collective-permute-start(f32[66,1]{1,0:T(8,128)S(1)} %get-tuple-element.86), channel_id=1, source_target_pairs={{0,1},{1,2},{2,3},{3,4},{4,5},{5,6},{6,7},{7,8},{8,9},{9,10},{10,1... | collective-permute-start | bytes 800 | tf_op jit(solution)/shard_map/ppermute | solution.py:25
  717.8 7.1 collective-permute-start.39
  719.9 5.5 collective-permute-start.38
  725.6 6.1 collective-permute-start.41
  726.9 5.6 collective-permute-start.40
  732.6 7.0 collective-permute-start.43
  734.6 5.7 collective-permute-start.42
  740.4 32.9 %collective-permute-start.45 = (f32[66,1]{1,0:T(8,128)S(1)}, f32[66,1]{1,0:T(8,128)S(1)}, u32[]{:S(2)}, u32[]{:S(2)}) collective-permute-start(f32[66,1]{1,0:T(8,128)S(1)} %get-tuple-element.83), channel_id=1, source_target_pairs={{1,0},{2,1},{3,2},{4,3},{5,4},{6,5},{7,6},{8,7},{9,8},{10,9},{11,1... | collective-permute-start | bytes 800 | tf_op jit(solution)/shard_map/ppermute | solution.py:28
  741.7 31.6 %collective-permute-start.44 = (f32[66,1]{1,0:T(8,128)S(1)}, f32[66,1]{1,0:T(8,128)S(1)}, u32[]{:S(2)}, u32[]{:S(2)}) collective-permute-start(f32[66,1]{1,0:T(8,128)S(1)} %get-tuple-element.82), channel_id=1, source_target_pairs={{0,1},{1,2},{2,3},{3,4},{4,5},{5,6},{6,7},{7,8},{8,9},{9,10},{10,1... | collective-permute-start | bytes 800 | tf_op jit(solution)/shard_map/ppermute | solution.py:25
  773.4 12.2 %collective-permute-start.47 = (f32[1,256]{1,0:T(1,128)S(1)}, f32[1,256]{1,0:T(1,128)S(1)}, u32[]{:S(2)}, u32[]{:S(2)}) collective-permute-start(f32[1,256]{1,0:T(1,128)S(1)} %get-tuple-element.105), channel_id=1, source_target_pairs={{16,0},{32,16},{48,32},{64,48},{80,64},{96,80},{112,96},{17,1},{33... | collective-permute-start | bytes 3080 | tf_op jit(solution)/shard_map/ppermute | solution.py:28
  778.6 7.7 collective-permute-start.46
  786.4 24.8 %collective-permute-start.49 = (f32[66,1]{1,0:T(8,128)S(1)}, f32[66,1]{1,0:T(8,128)S(1)}, u32[]{:S(2)}, u32[]{:S(2)}) collective-permute-start(f32[66,1]{1,0:T(8,128)S(1)} %get-tuple-element.81), channel_id=1, source_target_pairs={{1,0},{2,1},{3,2},{4,3},{5,4},{6,5},{7,6},{8,7},{9,8},{10,9},{11,1... | collective-permute-start | bytes 800 | tf_op jit(solution)/shard_map/ppermute | solution.py:28
  787.7 23.5 %collective-permute-start.48 = (f32[66,1]{1,0:T(8,128)S(1)}, f32[66,1]{1,0:T(8,128)S(1)}, u32[]{:S(2)}, u32[]{:S(2)}) collective-permute-start(f32[66,1]{1,0:T(8,128)S(1)} %get-tuple-element.80), channel_id=1, source_target_pairs={{0,1},{1,2},{2,3},{3,4},{4,5},{5,6},{6,7},{7,8},{8,9},{9,10},{10,1... | collective-permute-start | bytes 800 | tf_op jit(solution)/shard_map/ppermute | solution.py:25
  857.6 58.6 %all-to-all-start.4 = ((f32[128,1,64]{2,1,0:T(1,128)}), f32[128,1,64]{2,1,0:T(1,128)S(1)}, u32[]{:S(2)}, u32[]{:S(2)}) async-start(f32[128,1,64]{2,1,0:T(1,128)} %bitcast.27), calls=%async_computation.4 | async-start | bytes 131072 | tf_op jit(solution)/shard_map/all_to_all | solution.py:96
  962.4 25.6 %all-to-all-start.5 = ((f32[128,1,64]{2,1,0:T(1,128)}), f32[128,1,64]{2,1,0:T(1,128)S(1)}, u32[]{:S(2)}, u32[]{:S(2)}) async-start(f32[128,1,64]{2,1,0:T(1,128)} %bitcast.35), calls=%async_computation.5 | async-start | bytes 131072 | tf_op jit(solution)/shard_map/all_to_all | solution.py:101
  (5 other events, 3.8 us)
where the time goes:
time: 1040 us
  local copies, waits for them, and re-layouts  339 us (33%)
  other arithmetic  290 us (28%)
  starting transfers between devices  255 us (25%)
  blocking collectives  129 us (12%)
  waiting for transfers between devices  21.3 us (2%)
    scatter-add x3, other arithmetic, body(): surface = surface_flat.at[cell_safe].add(-(returned * inverse_flat[cell_s...  150 us
    gather x9, local copies, waits for them, and re-layouts, body(): pipe_at_slots = jnp.where(node_live, pipe_flat[node_safe], 0.0)  137 us
    gather x6, local copies, waits for them, and re-layouts, body(): sent_heads = jnp.where(cell_live, surface_flat[cell_safe], 0.0)  137 us
    scatter-add x3, other arithmetic, body(): jnp.zeros_like(pipe_flat).at[node_safe].add(manhole_flow)  134 us
    ppermute x24, starting transfers between devices, with_halo(): lax.ppermute(lax.slice_in_dim(block, block.shape[dim] - width, None, axis...  119 us
    all_gather x3, blocking collectives, body(): lax.all_gather(pipe_state[-1], 'col', axis=0, tiled=True)  73.7 us
    ppermute x24, starting transfers between devices, with_halo(): lax.ppermute(lax.slice_in_dim(block, 0, width, axis=dim), axis, backward)  55.9 us
    all_gather x3, blocking collectives, body(): lax.all_gather(pipe_state[0], 'col', axis=0, tiled=True)  54.9 us
  transfers between devices with their start and end apart: 56, of which 18 were waited for; matrix products, arithmetic and copies ran while one was open for 28% of the time, Pallas kernels for 0%

commit v1 on v0

v1 whole, which is shorter than its diff:
```python
import functools

import jax
import jax.numpy as jnp
from jax import lax
from jax.experimental import pallas as pl
from jax.experimental.pallas import tpu as pltpu
from jax.sharding import PartitionSpec as P

CLASSES = 4
SWEEPS = 4
STEPS = 3
F32 = jnp.float32
BF16 = jnp.bfloat16

boundary_gain = 0.5

HALO_ROWS = 4
HALO_COLS = 12
ZONE = 8


def iota(shape, dim):
    return lax.broadcasted_iota(jnp.int32, shape, dim)


def packed(x):
    return jnp.concatenate([x[:64], x[64:]], axis=1)


def low_halves(block):
    lane = iota((64, 128), 1)
    return jnp.where(lane < 64, block[:64], pltpu.roll(block[64:], 64, 1))


def high_halves(block):
    lane = iota((64, 128), 1)
    return jnp.where(lane < 64, pltpu.roll(block[:64], 64, 1), block[64:])


def paired(low, high):
    lane = iota((64, 128), 1)
    top = jnp.where(lane < 64, low, pltpu.roll(high, 64, 1))
    bottom = jnp.where(lane < 64, pltpu.roll(low, 64, 1), high)
    return jnp.concatenate([top, bottom], axis=0)


def beside(values):
    lane = iota((128, 128), 1)
    both = paired(values, values)
    return jnp.where(lane < 64, pltpu.roll(both, 1, 0), pltpu.roll(both, 127, 0))


def gathered(table_ref, rows, high, low):
    low = jnp.bitwise_and(low, 127)

    found = jnp.zeros(high.shape, F32)
    for row in range(rows):
        line = jnp.broadcast_to(table_ref[row : row + 1, :], high.shape)
        found = jnp.where(high == row, jnp.take_along_axis(line, low, axis=1), found)
    return found


def summed(high_ref, low_ref, value_ref, high_size, low_size):
    rows = high_ref.shape[0]

    def step(index, total):
        start = pl.multiple_of(index * 8, 8)
        high = high_ref[pl.ds(start, 8), :]
        low = low_ref[pl.ds(start, 8), :]
        value = value_ref[pl.ds(start, 8), :]
        coarse = value.astype(BF16).astype(F32)
        fine = value - coarse
        row_hot, coarse_hot, fine_hot = [], [], []
        for j in range(8):
            row_hot.append(
                jnp.where(iota((high_size, 128), 0) == high[j : j + 1], 1.0, 0.0).astype(BF16)
            )
            same = iota((low_size, 128), 0) == low[j : j + 1]
            coarse_hot.append(jnp.where(same, coarse[j : j + 1], 0.0).astype(BF16))
            fine_hot.append(jnp.where(same, fine[j : j + 1], 0.0).astype(BF16))
        row_hot = jnp.concatenate(row_hot, axis=1)
        value_hot = jnp.concatenate(
            [jnp.concatenate(coarse_hot, axis=1), jnp.concatenate(fine_hot, axis=1)], axis=0
        )
        return total + lax.dot_general(
            row_hot, value_hot, (((1,), (1,)), ((), ())), preferred_element_type=F32
        )

    total = lax.fori_loop(0, rows // 8, step, jnp.zeros((high_size, 2 * low_size), F32))
    return total


def cell_place(cell):
    high = jnp.where(
        cell >= 0, jnp.bitwise_and(cell >> 7, 1) * 64 + (cell >> 8), -1
    )
    return high, jnp.bitwise_and(cell, 127)


def node_place(node):
    high = jnp.where(
        node >= 0, jnp.bitwise_and(node >> 7, 1) * 32 + (node >> 8), -1
    )
    return high, jnp.bitwise_and(node, 127)


def pipe_table(state):
    return jnp.concatenate([state[:, :128], state[:, 128:]], axis=0)


def pack_rows_kernel(place_ref, surface, cond_x, cond_y, porosity, rainfall, pipes, out):
    row = place_ref[0]
    fields = [surface[...], cond_x[...], cond_y[...], 1.0 / porosity[...], rainfall[...]]
    ends = pipe_table(pipes[...])
    ends = [ends[0:1], ends[32:33], ends[31:32], ends[63:64]]
    for target in range(8):
        upward = target < row
        for index, field in enumerate(fields):
            strip = jnp.where(upward, field[:4], field[60:])
            out[target, pl.ds(index * 8, 4), :] = strip[:, :128]
            out[target, pl.ds(index * 8 + 4, 4), :] = strip[:, 128:]
        out[target, pl.ds(40, 8), :] = jnp.broadcast_to(ends[target % 4], (8, 128))


def neighbours(place_ref):
    row = place_ref[0]
    above, below = jnp.maximum(row - 1, 0), jnp.minimum(row + 1, 7)
    return above, below, row > 0, row < 7


def pack_cols_kernel(
    place_ref, got, surface, cond_x, cond_y, porosity, rainfall, link_cell, fields_out, out
):
    above, below, has_above, has_below = neighbours(place_ref)
    fields = [surface[...], cond_x[...], cond_y[...], 1.0 / porosity[...], rainfall[...]]
    lane = iota((72, 128), 1)
    message = jnp.zeros((72, 128), F32)
    for index, field in enumerate(fields):
        over = got[above, pl.ds(index * 8, 8), :]
        under = got[below, pl.ds(index * 8, 8), :]
        over = jnp.where(has_above, over, 0.0)
        under = jnp.where(has_below, under, 0.0)
        tall = [
            jnp.concatenate([field[:, half * 128 : half * 128 + 128],
                             under[half * 4 : half * 4 + 4], over[half * 4 : half * 4 + 4]], axis=0)
            for half in range(2)
        ]
        fields_out[index, :, 0:128] = tall[0]
        fields_out[index, :, 128:256] = tall[1]
        edges = jnp.where(
            lane < HALO_COLS, tall[0], jnp.where(lane >= 128 - HALO_COLS, tall[1], 0.0)
        )
        if index:
            edges = pltpu.roll(edges, index * 2 * HALO_COLS, 1)
        message = message + edges
    out[0:72, :] = message
    out[72:136, :] = packed(link_cell[...]).astype(F32)


def swept(state, gains):
    def once(_, w):
        return (
            gains[0] * w
            + gains[1] * pltpu.roll(w, 1, 0)
            + gains[2] * pltpu.roll(w, 71, 0)
            + gains[3] * pltpu.roll(w, 1, 1)
            + gains[4] * pltpu.roll(w, 383, 1)
            + gains[5]
        )

    for i in range(SWEEPS):
        state = once(i, state)
    return state


def build_message(out, heads, nodes, got, ends_at):
    out[:, 0:128] = paired(heads, nodes)
    out[:, 128:256] = beside(nodes)
    for source in range(8):
        out[pl.ds(source * 16, 16), 256:384] = jnp.broadcast_to(
            got[source, pl.ds(ends_at, 1), :], (16, 128)
        )


def zone_heads(edge, zone_place, edge_ref, zone_ref):
    lane = iota((64, 128), 1)
    edge_ref[...] = jnp.where(lane < ZONE, edge, pltpu.roll(edge, 2 * ZONE, 1))
    lane8 = iota((8, 128), 1)
    table = jnp.zeros((8, 128), F32)
    for s in range(8):
        line = edge_ref[pl.ds(s, 8, stride=8), :]
        if s:
            line = pltpu.roll(line, s * 16, 1)
        table = jnp.where((lane8 >> 4) == s, line, table)
    zone_ref[...] = table
    zone_row, zone_col = zone_place
    high = jnp.where(zone_row >= 0, zone_row >> 3, -1)
    low = jnp.bitwise_and(zone_row, 7) * 16 + zone_col
    return gathered(zone_ref, 8, high, low)


def sweep_and_gather(
    state, gains, cell_place_, node_place_, zone_place, table, surface_out, heads_out, zone_out,
    nodes_out, cell_table, edge_ref, zone_ref,
):
    state = swept(state, gains)
    surface_out[...] = state[:64]
    cell_table[0:64, :] = state[:64, 0:128]
    cell_table[64:128, :] = state[:64, 128:256]
    heads = gathered(cell_table, 128, *cell_place_)
    heads_out[...] = heads
    if zone_place is not None:
        zone_out[...] = zone_heads(state[:64, 256:384], zone_place, edge_ref, zone_ref)
    nodes = gathered(table, 64, *node_place_)
    nodes_out[...] = nodes
    return heads, nodes


def first_sweep_kernel(
    fields, from_west, from_east, got, link_cell, link_node, link_coef, pipes,
    gains_out, inverse_out, zone_row_out, zone_col_out, surface_out, heads_out, zone_out, nodes_out,
    table_out, out, cell_table, edge_ref, zone_ref,
):
    lane = iota((72, 128), 1)
    wide = []
    for index in range(5):
        west, east = from_west[0:72, :], from_east[0:72, :]
        if index:
            west = pltpu.roll(west, 128 - index * 2 * HALO_COLS, 1)
            east = pltpu.roll(east, 128 - index * 2 * HALO_COLS, 1)
        edge = jnp.where(
            lane < HALO_COLS, east, jnp.where(lane >= 128 - HALO_COLS, west, 0.0)
        )
        wide.append(jnp.concatenate([fields[index], edge], axis=1))
    state, cond_x, cond_y, inverse, rainfall = wide
    north = pltpu.roll(cond_x, 1, 0)
    west = pltpu.roll(cond_y, 1, 1)
    gains = [
        1.0 - (north + cond_x + west + cond_y) * inverse,
        north * inverse, cond_x * inverse, west * inverse, cond_y * inverse, rainfall,
    ]
    for index, gain in enumerate(gains):
        gains_out[index] = gain
    inverse_out[...] = inverse[:64]
    west_cell = from_west[72:136, :].astype(jnp.int32)
    east_cell = from_east[72:136, :].astype(jnp.int32)
    cells = paired(west_cell, east_cell)
    col = jnp.bitwise_and(cells, 255)
    is_west = iota((128, 128), 1) < 64
    inside = jnp.where(is_west, jnp.where(col >= 256 - ZONE, 1, 0), jnp.where(col < ZONE, 1, 0))
    zone_row = jnp.where((cells >= 0) & (inside == 1), cells >> 8, -1)
    zone_col = jnp.where(is_west, col - (256 - 2 * ZONE), col)
    zone_row_out[...] = zone_row
    zone_col_out[...] = zone_col
    table_out[...] = pipe_table(pipes[...])
    heads, nodes = sweep_and_gather(
        state, gains, cell_place(packed(link_cell[...])), node_place(packed(link_node[...])),
        (zone_row, zone_col), table_out, surface_out, heads_out, zone_out, nodes_out,
        cell_table, edge_ref, zone_ref,
    )
    build_message(out, heads, nodes, got, 40)
    coef = packed(link_coef[...])
    out[:, 384:512] = paired(coef, coef)
    out[:, 512:640] = beside(coef)


def sweep_kernel(
    place_ref, surface, got, gains_ref, link_cell, link_node, zone_row, zone_col, table,
    surface_out, heads_out, zone_out, nodes_out, out, cell_table, edge_ref, zone_ref,
):
    above, below, has_above, has_below = neighbours(place_ref)
    over = jnp.where(has_above, got[above, pl.ds(0, 16), :], 0.0)
    under = jnp.where(has_below, got[below, pl.ds(0, 16), :], 0.0)
    columns = []
    for block in range(3):
        columns.append(
            jnp.concatenate(
                [surface[:, block * 128 : block * 128 + 128],
                 under[block * 4 : block * 4 + 4], over[block * 4 : block * 4 + 4]], axis=0
            )
        )
    state = jnp.concatenate(columns, axis=1)
    gains = [gains_ref[index] for index in range(6)]
    heads, nodes = sweep_and_gather(
        state, gains, cell_place(packed(link_cell[...])), node_place(packed(link_node[...])),
        (zone_row[...], zone_col[...]), table, surface_out, heads_out, zone_out, nodes_out,
        cell_table, edge_ref, zone_ref,
    )
    build_message(out, heads, nodes, got, 12)


def update_kernel(
    first, last,
    place_ref, got, surface, inverse, heads, zone, nodes, link_cell, link_node, link_coef,
    zone_row, zone_col, table, meets, classes, matrices, *rest,
):
    rest = list(rest)
    if first:
        own_coef = low_halves(got[:, 384:512])
        zone_coef = got[:, 512:640]
    else:
        own_coef = rest.pop(0)[...]
        zone_coef = rest.pop(0)[...]
    if last:
        surface_out, pipes_out = rest[:2]
        rest = rest[2:]
    else:
        surface_out, table_out, out = rest[:3]
        rest = rest[3:]
        if first:
            rest[0][...] = own_coef
            rest[1][...] = zone_coef
            rest = rest[2:]
    high_ref, low_ref, value_ref, zone_value_ref = rest
    row = place_ref[0]
    block = got[:, 0:128]
    high, low = cell_place(packed(link_cell[...]))
    high_ref[...] = high
    low_ref[...] = low
    value_ref[...] = jnp.where(high >= 0, own_coef * (heads[...] - high_halves(block)), 0.0)
    lost = summed(high_ref, low_ref, value_ref, 128, 128)
    lost = lost[:, :128] + lost[:, 128:]
    left = surface[:, 0:128] - inverse[:, 0:128] * lost[:64]
    right = surface[:, 128:256] - inverse[:, 128:256] * lost[64:]
    surface_out[:, 0:128] = left
    surface_out[:, 128:256] = right
    if not last:
        zone_value_ref[...] = jnp.where(
            zone_row[...] >= 0, zone_coef * (zone[...] - got[:, 128:256]), 0.0
        )
        lost = summed(zone_row, zone_col, zone_value_ref, 64, 64)
        lost = lost[:, :64] + lost[:, 64:]
        lost = jnp.concatenate([lost, jnp.zeros((64, 64), F32)], axis=1)
        lane = iota((64, 128), 1)
        lost = jnp.where(
            lane < ZONE, lost,
            jnp.where(lane >= 128 - ZONE, pltpu.roll(lost, 128 - 2 * ZONE, 1), 0.0),
        )
        edge = surface[:, 256:384] - inverse[:, 256:384] * lost
        surface_out[:, 256:384] = edge
    high, low = node_place(packed(link_node[...]))
    high_ref[...] = high
    low_ref[...] = low
    value_ref[...] = jnp.where(
        high >= 0, packed(link_coef[...]) * (low_halves(block) - nodes[...]), 0.0
    )
    inflow = summed(high_ref, low_ref, value_ref, 64, 128)
    balance = table[...] + (inflow[:, :128] + inflow[:, 128:])
    meet = meets[...]
    meet_row = iota((8, 128), 0)
    meet_high = jnp.bitwise_and(meet >> 7, 1) * 16 + (meet >> 8)
    meet_high = jnp.where(meet_row < 2, meet_high + 32, meet_high)
    met = gathered(got.at[:, 256:384], 64, meet_high, meet) * boundary_gain
    node_row = iota((32, 128), 0)
    parts = []
    for half in range(2):
        part = balance[half * 32 : half * 32 + 32]
        part = part + jnp.where(
            node_row == 0, met[half : half + 1],
            jnp.where(node_row == 31, met[2 + half : 3 + half], 0.0),
        )
        products = jnp.dot(
            matrices[...], part, precision=lax.Precision.HIGHEST, preferred_element_type=F32
        )
        kind = classes[half : half + 1, :]
        updated = jnp.zeros((32, 128), F32)
        for index in range(CLASSES):
            updated = jnp.where(kind == index, products[index * 32 : index * 32 + 32], updated)
        parts.append(updated)
    if last:
        pipes_out[:, 0:128] = parts[0]
        pipes_out[:, 128:256] = parts[1]
        return
    table_out[0:32, :] = parts[0]
    table_out[32:64, :] = parts[1]
    ends = [parts[0][0:1], parts[1][0:1], parts[0][31:32], parts[1][31:32]]
    blocks = [left, right, edge]
    for target in range(8):
        upward = target < row
        for index, field in enumerate(blocks):
            out[target, pl.ds(index * 4, 4), :] = jnp.where(upward, field[:4], field[60:])
        out[target, pl.ds(12, 4), :] = jnp.broadcast_to(ends[target % 4], (4, 128))


def shape(*dims, dtype=F32):
    return jax.ShapeDtypeStruct(dims, dtype)


def call(kernel, inputs, outputs, scratch=(), scalars=1):
    smem = pl.BlockSpec(memory_space=pltpu.SMEM)
    vmem = pl.BlockSpec(memory_space=pltpu.VMEM)
    return pl.pallas_call(
        kernel,
        out_shape=outputs,
        in_specs=[smem] * scalars + [vmem] * (len(inputs) - scalars),
        out_specs=[vmem] * len(outputs),
        scratch_shapes=list(scratch),
        compiler_params=pltpu.CompilerParams(vmem_limit_bytes=32 << 20),
    )(*inputs)


def along(block, axis, distance):
    devices = range(lax.axis_size(axis))
    route = [(i, i + distance) for i in devices if i + distance in devices]
    return lax.ppermute(block, axis, route)


def body(
    surface_head, conduct_x, conduct_y, porosity, rainfall, pipe_head, pipe_class, pipe_up,
    pipe_down, pipe_matrices, link_cell, link_node, link_coef,
):
    place = lax.axis_index("row").astype(jnp.int32).reshape(1)
    link_cell = link_cell[0]
    link_node = link_node[:, 0, :]
    link_coef = link_coef[:, 0, :]
    meets = jnp.concatenate(
        [pipe_up.reshape(2, 128), pipe_down.reshape(2, 128), jnp.zeros((4, 128), jnp.int32)], axis=0
    )
    classes = pipe_class.reshape(2, 128)
    matrices = pipe_matrices.reshape(CLASSES * 32, 32)
    fields = (surface_head, conduct_x, conduct_y, porosity, rainfall)

    (sent,) = call(pack_rows_kernel, (place, *fields, pipe_head), [shape(8, 48, 128)])
    got = lax.all_to_all(sent, "row", split_axis=0, concat_axis=0, tiled=True)
    tall, sent = call(
        pack_cols_kernel, (place, got, *fields, link_cell), [shape(5, 72, 256), shape(136, 128)]
    )
    from_west = along(sent, "col", 1)
    from_east = along(sent, "col", -1)
    gather_scratch = [pltpu.VMEM((128, 128), F32), pltpu.VMEM((64, 128), F32), pltpu.VMEM((8, 128), F32)]
    sum_scratch = [
        pltpu.VMEM((64, 128), jnp.int32), pltpu.VMEM((64, 128), jnp.int32),
        pltpu.VMEM((64, 128), F32), pltpu.VMEM((128, 128), F32),
    ]
    swept_shapes = [shape(64, 384), shape(64, 128), shape(128, 128), shape(64, 128)]
    gains, inverse, zone_row, zone_col, surface, heads, zone, nodes, table, sent = call(
        first_sweep_kernel,
        (tall, from_west, from_east, got, link_cell, link_node, link_coef, pipe_head),
        [shape(6, 72, 384), shape(64, 384), shape(128, 128, dtype=jnp.int32),
         shape(128, 128, dtype=jnp.int32), *swept_shapes, shape(64, 128), shape(128, 640)],
        gather_scratch, scalars=0,
    )
    coefs = ()
    for step in range(STEPS):
        if step:
            surface, heads, zone, nodes, sent = call(
                sweep_kernel,
                (place, surface, got, gains, link_cell, link_node, zone_row, zone_col, table),
                [*swept_shapes, shape(128, 384)], gather_scratch,
            )
        got = lax.all_to_all(sent, ("row", "col"), split_axis=0, concat_axis=0, tiled=True)
        last = step == STEPS - 1
        outputs = [shape(64, 256), shape(32, 256)] if last else [
            shape(64, 384), shape(64, 128), shape(8, 16, 128)
        ]
        if not step:
            outputs += [shape(64, 128), shape(128, 128)]
        done = call(
            functools.partial(update_kernel, step == 0, last),
            (place, got, surface, inverse, heads, zone, nodes, link_cell, link_node, link_coef,
             zone_row, zone_col, table, meets, classes, matrices, *coefs),
            outputs, sum_scratch,
        )
        if last:
            return tuple(done)
        surface, table, sent = done[:3]
        if not step:
            coefs = tuple(done[3:])
        got = lax.all_to_all(sent, "row", split_axis=0, concat_axis=0, tiled=True)


def solution(mesh):
    placed = (
        P("row", "col"),
        P("row", "col"),
        P("row", "col"),
        P("row", "col"),
        P("row", "col"),
        P(None, ("row", "col")),
        P(("row", "col")),
        P(("row", "col")),
        P(("row", "col")),
        P(),
        P(("row", "col"), None, None),
        P(None, ("row", "col"), None),
        P(None, ("row", "col"), None),
    )
    return jax.shard_map(
        body,
        mesh=mesh,
        in_specs=placed,
        out_specs=(P("row", "col"), P(None, ("row", "col"))),
        check_vma=False,
    )
```

time: 1040 us -> 140 us (0.13)
  local copies, waits for them, and re-layouts: 339 us -> 8.35 us
  other arithmetic: 290 us -> 0.07 us
  starting transfers between devices: 255 us -> 22.4 us
  blocking collectives: 129 us -> 44.9 us
  Pallas kernels: 0 us -> 42.3 us
    gather x23 -> x0, local copies, waits for them, and re-layouts: 330 us -> none  [the longest x9 137 us: body(): pipe_at_slots = jnp.where(node_live, pipe_flat[node_safe], 0.0)]
    scatter-add x6 -> x0, other arithmetic: 285 us -> none  [the longest x3 150 us: body(): surface = surface_flat.at[cell_safe].add(-(returned * inverse_flat[cell_s...]
    ppermute x50 -> x2, starting transfers between devices: 181 us -> 4.5 us  [along(): return lax.ppermute(block, axis, route)]
    all_gather x6 -> x0, blocking collectives: 129 us -> none  [the longest x3 73.7 us: body(): lax.all_gather(pipe_state[-1], 'col', axis=0, tiled=True)]
    all_to_all x6 -> x2, starting transfers between devices: 74 us -> 17.9 us  [the longest x1 12 us: body(): lax.all_to_all(sent, ('row', 'col'), split_axis=0, concat_axis=0, tiled=T...]
    all_to_all x0 -> x4, blocking collectives: none -> 44.9 us  [the longest x2 29.5 us: body(): lax.all_to_all(sent, ('row', 'col'), split_axis=0, concat_axis=0, tiled=T...]
    pallas_call x0 -> x8, Pallas kernels: none -> 42.3 us  [call(): pl.pallas_call(kernel, out_shape=outputs, in_specs=[smem] * scalars + [vm...]
  transfers between devices with their start and end apart: 56 -> 4, of which waited for: 18 -> 3; matrix products, arithmetic and copies ran while one was open for 28% -> 0% of each run, Pallas kernels for 0% -> 0%
where the time goes in v1:
time: 140 us; the launch traced here: 139 us
  blocking collectives  44.9 us (32%)
  Pallas kernels  42.3 us (30%)
  starting transfers between devices  22.4 us (16%)
  waiting for transfers between devices  20.6 us (15%)
  local copies, waits for them, and re-layouts  8.35 us (6%)
    pallas_call x8, Pallas kernels, call(): pl.pallas_call(kernel, out_shape=outputs, in_specs=[smem] * scalars + [vm...  42.3 us
    all_to_all x2, blocking collectives, body(): lax.all_to_all(sent, ('row', 'col'), split_axis=0, concat_axis=0, tiled=T...  29.5 us
    all_to_all x2, blocking collectives, body(): got = lax.all_to_all(sent, 'row', split_axis=0, concat_axis=0, tiled=True)  15.4 us
    all_to_all x1, starting transfers between devices, body(): lax.all_to_all(sent, ('row', 'col'), split_axis=0, concat_axis=0, tiled=T...  12 us
    all_to_all x1, waiting for transfers between devices, body(): lax.all_to_all(sent, ('row', 'col'), split_axis=0, concat_axis=0, tiled=T...  11.3 us
    unnamed x44, local copies, waits for them, and re-layouts  6.8 us
    all_to_all x1, starting transfers between devices, body(): got = lax.all_to_all(sent, 'row', split_axis=0, concat_axis=0, tiled=True)  5.94 us
    all_to_all x1, waiting for transfers between devices, body(): got = lax.all_to_all(sent, 'row', split_axis=0, concat_axis=0, tiled=True)  5.79 us
  transfers between devices with their start and end apart: 4, of which 3 were waited for; matrix products, arithmetic and copies ran while one was open for 0% of the time, Pallas kernels for 0%

profile of v1, /device:TPU:1, one launch (start us, length us, event | category | flops | bytes accessed | tf_op | source)
XLA Modules:
  0.0 139.5 jit_solution(12020296218795620179)
XLA Ops:
  0.6 0.0 copy-start.1
  0.6 0.8 copy-done.1
  1.5 0.0 copy-start.3
  1.5 0.8 copy-done.3
  2.3 0.0 copy-start.5
  2.3 0.8 copy-done.5
  3.2 0.0 copy-start.7
  3.2 0.8 copy-done.7
  4.0 0.0 copy-start.9
  4.0 0.8 copy-done.9
  4.8 0.0 copy-start.11
  4.8 0.8 copy-done.11
  5.6 0.7 shard_map.140
  6.3 0.0 copy-start.14
  6.3 0.0 copy-start.4
  6.3 0.0 copy-start.6
  6.3 0.0 copy-start.8
  6.3 0.0 copy-start.10
  6.3 5.9 %all-to-all-start = ((f32[8,48,128]{2,1,0:T(8,128)}), f32[8,48,128]{2,1,0:T(8,128)S(1)}, u32[]{:S(2)}, u32[]{:S(2)}) async-start(f32[8,48,128]{2,1,0:T(8,128)} %shard_map.140), calls=%async_computation | async-start | bytes 393216 | tf_op jit(solution)/shard_map/all_to_all | solution.py:425
  12.3 0.0 copy-done.14
  12.3 0.0 copy-start.2
  12.3 0.1 copy.18
  12.4 5.8 %all-to-all-done.got = f32[8,48,128]{2,1,0:T(8,128)S(1)} async-done(((f32[8,48,128]{2,1,0:T(8,128)}), f32[8,48,128]{2,1,0:T(8,128)S(1)}, u32[]{:S(2)}, u32[]{:S(2)}) %all-to-all-start) | async-done | bytes 196640 | tf_op jit(solution)/shard_map/all_to_all | solution.py:425
  18.2 0.0 copy-done.4
  18.2 0.0 copy-done.6
  18.2 0.0 copy-done.8
  18.2 0.0 copy-done.10
  18.2 0.0 copy-done.2
  18.2 0.0 copy-start.15
  18.2 0.1 shard_map.141
  18.3 0.0 copy-start.16
  18.4 3.2 %collective-permute-start = (f32[136,128]{1,0:T(8,128)S(1)}, f32[136,128]{1,0:T(8,128)S(1)}, u32[]{:S(2)}, u32[]{:S(2)}) collective-permute-start(f32[136,128]{1,0:T(8,128)S(1)} %get-tuple-element.33), channel_id=1, source_target_pairs={{0,1},{1,2},{2,3},{3,4},{4,5},{5,6},{6,7},{7,8},{8,9},{9,10},{10,1... | collective-permute-start | bytes 208904 | tf_op jit(solution)/shard_map/ppermute | solution.py:406
  21.6 1.3 collective-permute-start.1
  22.9 0.0 copy-done.15
  22.9 0.1 copy.19
  23.0 0.0 copy-done.16
  23.0 0.0 copy-start.12
  23.0 0.1 copy.20
  23.1 0.0 collective-permute-done.from_west
  23.1 3.5 %collective-permute-done.1.from_east = f32[136,128]{1,0:T(8,128)S(1)} collective-permute-done((f32[136,128]{1,0:T(8,128)S(1)}, f32[136,128]{1,0:T(8,128)S(1)}, u32[]{:S(2)}, u32[]{:S(2)}) %collective-permute-start.1) | collective-permute-done | bytes 69664 | tf_op jit(solution)/shard_map/ppermute | solution.py:406
  26.6 0.0 copy-done.12
  26.6 5.7 %shard_map.142 = (f32[6,72,384]{2,1,0:T(8,128)S(1)}, f32[64,384]{1,0:T(8,128)S(1)}, s32[128,128]{1,0:T(8,128)S(1)}, s32[128,128]{1,0:T(8,128)S(1)}, f32[64,384]{...) custom-call(f32[5,72,256]{2,1,0:T(8,128)S(1)} %get-tuple-element.32., ...), custom_call_target="tpu_custom_call" | custom-call | tf_op jit(solution)/shard_map/pallas_call | solution.py:393
  32.4 1.1 copy.21
  33.4 0.0 copy-start.18
  33.4 12.0 %all-to-all-start.1 = ((f32[128,1,640]{2,1,0:T(1,128)}), f32[128,1,640]{2,1,0:T(1,128)S(1)}, u32[]{:S(2)}, u32[]{:S(2)}) async-start(f32[128,1,640]{2,1,0:T(1,128)} %copy.21), calls=%async_computation.1 | async-start | bytes 655360 | tf_op jit(solution)/shard_map/all_to_all | solution.py:452
  45.4 0.1 pad.2.clone
  45.5 0.0 copy-done.18
  45.5 0.7 copy-done.17
  46.2 0.1 add_add_fusion.meets
  46.3 11.3 %all-to-all-done.1 = f32[128,1,640]{2,1,0:T(1,128)S(1)} async-done(((f32[128,1,640]{2,1,0:T(1,128)}), f32[128,1,640]{2,1,0:T(1,128)S(1)}, u32[]{:S(2)}, u32[]{:S(2)}) %all-to-all-start.1) | async-done | bytes 327712 | tf_op jit(solution)/shard_map/all_to_all | solution.py:452
  57.6 0.0 copy-start.13
  57.6 0.8 copy-done
  58.4 0.0 copy-done.13
  58.4 9.2 %shard_map.143 = (f32[64,384]{1,0:T(8,128)S(1)}, f32[64,128]{1,0:T(8,128)S(1)}, f32[8,16,128]{2,1,0:T(8,128)S(1)}, f32[64,128]{1,0:T(8,128)S(1)}, f32[128,128]{1,0:T(8,128)S(1)}) custom-call(s32[1]{0:T(128)} %bitcast.place_ref, f32[128,640]{1,0:T(8,128)S(1)} %bitcast.37, f32[64,384]{1,0:T(8,128)S(1)} %get-tuple-element.35.surface, ...), custom_call_target="tpu_custom_call" | custom-call | tf_op jit(solution)/shard_map/pallas_call | solution.py:393
  67.6 7.7 %all_to_all.48.got = f32[8,16,128]{2,1,0:T(8,128)S(1)} all-to-all(f32[8,16,128]{2,1,0:T(8,128)S(1)} %get-tuple-element.44), channel_id=1, replica_groups=mesh['row'=8,'col'=16] {'row'}, dimensions={0} | all-to-all | bytes 131072 | tf_op jit(solution)/shard_map/all_to_all | solution.py:470
  75.3 5.5 %shard_map.144 = (f32[64,384]{1,0:T(8,128)S(1)}, f32[64,128]{1,0:T(8,128)S(1)}, f32[128,128]{1,0:T(8,128)S(1)}, f32[64,128]{1,0:T(8,128)S(1)}, f32[128,384]{1,0:T(8,128)S(1)}) custom-call(s32[1]{0:T(128)} %bitcast.place_ref, f32[64,384]{1,0:T(8,128)S(1)} %get-tuple-element.43.surface, f32[8,16,128]{2,1,0:T(8,128)S(1)} %all_to_all.48.got, ...), custom_call_target="tpu_custom_call" | custom-call | tf_op jit(solution)/shard_map/pallas_call | solution.py:393
  80.9 0.2 copy.22
  81.1 14.7 %all_to_all.49 = f32[128,1,384]{2,1,0:T(1,128)S(1)} all-to-all(f32[128,1,384]{2,1,0:T(1,128)S(1)} %copy.22), channel_id=1, replica_groups=mesh['row'=8,'col'=16] {'row','col'}, dimensions={0} | all-to-all | bytes 393216 | tf_op jit(solution)/shard_map/all_to_all | solution.py:452
  95.8 9.2 %shard_map.145 = (f32[64,384]{1,0:T(8,128)S(1)}, f32[64,128]{1,0:T(8,128)S(1)}, f32[8,16,128]{2,1,0:T(8,128)S(1)}) custom-call(s32[1]{0:T(128)} %bitcast.place_ref, f32[128,384]{1,0:T(8,128)S(1)} %bitcast.39, f32[64,384]{1,0:T(8,128)S(1)} %get-tuple-element.48.surface, f32[64,384]{1,0:T(8,128)S(1)} %get-tuple-element.36.inverse, ...), custom_call_target="tpu_custom_call" | custom-call | tf_op jit(solution)/shard_map/pallas_call | solution.py:393
  105.0 7.7 %all_to_all.50.got = f32[8,16,128]{2,1,0:T(8,128)S(1)} all-to-all(f32[8,16,128]{2,1,0:T(8,128)S(1)} %get-tuple-element.55), channel_id=1, replica_groups=mesh['row'=8,'col'=16] {'row'}, dimensions={0} | all-to-all | bytes 131072 | tf_op jit(solution)/shard_map/all_to_all | solution.py:470
  112.7 5.5 %shard_map.146 = (f32[64,384]{1,0:T(8,128)S(1)}, f32[64,128]{1,0:T(8,128)S(1)}, f32[128,128]{1,0:T(8,128)S(1)}, f32[64,128]{1,0:T(8,128)S(1)}, f32[128,384]{1,0:T(8,128)S(1)}) custom-call(s32[1]{0:T(128)} %bitcast.place_ref, f32[64,384]{1,0:T(8,128)S(1)} %get-tuple-element.54.surface, f32[8,16,128]{2,1,0:T(8,128)S(1)} %all_to_all.50.got, ...), custom_call_target="tpu_custom_call" | custom-call | tf_op jit(solution)/shard_map/pallas_call | solution.py:393
  118.2 0.2 copy.23
  118.5 14.8 %all_to_all.51 = f32[128,1,384]{2,1,0:T(1,128)S(1)} all-to-all(f32[128,1,384]{2,1,0:T(1,128)S(1)} %copy.23), channel_id=1, replica_groups=mesh['row'=8,'col'=16] {'row','col'}, dimensions={0} | all-to-all | bytes 393216 | tf_op jit(solution)/shard_map/all_to_all | solution.py:452
  133.2 6.2 %shard_map.147 = (f32[64,256]{1,0:T(8,128)}, f32[32,256]{1,0:T(8,128)}) custom-call(s32[1]{0:T(128)} %bitcast.place_ref, f32[128,384]{1,0:T(8,128)S(1)} %bitcast.38, f32[64,384]{1,0:T(8,128)S(1)} %get-tuple-element.58.surface, f32[64,384]{1,0:T(8,128)S(1)} %get-tuple-element.36.inverse, f32[64,128]{1,0:T(8,128)S(1)} %get-tuple-element.59.heads, ...), custom_call_target="tpu_custom_call" | custom-call | tf_op jit(solution)/shard_map/pallas_call | solution.py:393
  (6 shorter events, 0.1 us)
Async XLA Ops:
  0.6 0.8 copy-start.1
  1.5 0.8 copy-start.3
  2.3 0.8 copy-start.5
  3.2 0.8 copy-start.7
  4.0 0.8 copy-start.9
  4.8 0.8 copy-start.11
  6.3 6.0 %copy-start.14 = (s32[1,128,64]{1,2,0:T(8,128)S(1)}, s32[1,128,64]{1,2,0:T(8,128)}, u32[]{:S(2)}) copy-start(s32[1,128,64]{1,2,0:T(8,128)} %param.23) | copy-start | bytes 98308
  6.3 11.9 %copy-start.4 = (f32[64,256]{1,0:T(8,128)S(1)}, f32[64,256]{1,0:T(8,128)}, u32[]{:S(2)}) copy-start(f32[64,256]{1,0:T(8,128)} %cond_x.3) | copy-start | bytes 196612
  6.3 11.9 %copy-start.6 = (f32[64,256]{1,0:T(8,128)S(1)}, f32[64,256]{1,0:T(8,128)}, u32[]{:S(2)}) copy-start(f32[64,256]{1,0:T(8,128)} %cond_y.3) | copy-start | bytes 196612
  6.3 11.9 %copy-start.8 = (f32[64,256]{1,0:T(8,128)S(1)}, f32[64,256]{1,0:T(8,128)}, u32[]{:S(2)}) copy-start(f32[64,256]{1,0:T(8,128)} %porosity.3) | copy-start | bytes 196612
  6.3 11.9 %copy-start.10 = (f32[64,256]{1,0:T(8,128)S(1)}, f32[64,256]{1,0:T(8,128)}, u32[]{:S(2)}) copy-start(f32[64,256]{1,0:T(8,128)} %rainfall.3) | copy-start | bytes 196612
  6.3 11.8 %all-to-all-start = ((f32[8,48,128]{2,1,0:T(8,128)}), f32[8,48,128]{2,1,0:T(8,128)S(1)}, u32[]{:S(2)}, u32[]{:S(2)}) async-start(f32[8,48,128]{2,1,0:T(8,128)} %shard_map.140), calls=%async_computation | async-start | bytes 393216 | tf_op jit(solution)/shard_map/all_to_all | solution.py:425
  12.3 5.9 %copy-start.2 = (f32[64,256]{1,0:T(8,128)S(1)}, f32[64,256]{1,0:T(8,128)}, u32[]{:S(2)}) copy-start(f32[64,256]{1,0:T(8,128)} %surface.3) | copy-start | bytes 196612
  18.2 4.7 %copy-start.15 = (s32[128,1,64]{0,2,1:T(8,128)S(1)}, s32[128,1,64]{0,2,1:T(8,128)}, u32[]{:S(2)}) copy-start(s32[128,1,64]{0,2,1:T(8,128)} %param.24) | copy-start | bytes 98308
  18.3 4.6 %copy-start.16 = (f32[128,1,64]{0,2,1:T(8,128)S(1)}, f32[128,1,64]{0,2,1:T(8,128)}, u32[]{:S(2)}) copy-start(f32[128,1,64]{0,2,1:T(8,128)} %param.25) | copy-start | bytes 98308
  18.4 4.7 %collective-permute-start = (f32[136,128]{1,0:T(8,128)S(1)}, f32[136,128]{1,0:T(8,128)S(1)}, u32[]{:S(2)}, u32[]{:S(2)}) collective-permute-start(f32[136,128]{1,0:T(8,128)S(1)} %get-tuple-element.33), channel_id=1, source_target_pairs={{0,1},{1,2},{2,3},{3,4},{4,5},{5,6},{6,7},{7,8},{8,9},{9,10},{10,1... | collective-permute-start | bytes 208904 | tf_op jit(solution)/shard_map/ppermute | solution.py:406
  21.6 5.1 %collective-permute-start.1 = (f32[136,128]{1,0:T(8,128)S(1)}, f32[136,128]{1,0:T(8,128)S(1)}, u32[]{:S(2)}, u32[]{:S(2)}) collective-permute-start(f32[136,128]{1,0:T(8,128)S(1)} %get-tuple-element.33), channel_id=1, source_target_pairs={{1,0},{2,1},{3,2},{4,3},{5,4},{6,5},{7,6},{8,7},{9,8},{10,9},{11,1... | collective-permute-start | bytes 208904 | tf_op jit(solution)/shard_map/ppermute | solution.py:406
  23.0 3.6 %copy-start.12 = (f32[32,256]{1,0:T(8,128)S(1)}, f32[32,256]{1,0:T(8,128)}, u32[]{:S(2)}) copy-start(f32[32,256]{1,0:T(8,128)} %pipes.3) | copy-start | bytes 98308
  33.4 12.1 %copy-start.18 = (s32[256]{0:T(256)S(1)}, s32[256]{0:T(256)}, u32[]{:S(2)}) copy-start(s32[256]{0:T(256)} %param.20) | copy-start | bytes 3076
  33.4 24.1 %all-to-all-start.1 = ((f32[128,1,640]{2,1,0:T(1,128)}), f32[128,1,640]{2,1,0:T(1,128)S(1)}, u32[]{:S(2)}, u32[]{:S(2)}) async-start(f32[128,1,640]{2,1,0:T(1,128)} %copy.21), calls=%async_computation.1 | async-start | bytes 655360 | tf_op jit(solution)/shard_map/all_to_all | solution.py:452
  45.5 0.7 copy-start.17
  57.5 0.8 copy-start
  57.6 0.8 copy-start.13

commit v2 on v1

v2 whole, which is shorter than its diff:
```python
import functools

import jax
import jax.numpy as jnp
from jax import lax
from jax.experimental import pallas as pl
from jax.experimental.pallas import tpu as pltpu
from jax.sharding import PartitionSpec as P

CLASSES = 4
SWEEPS = 4
STEPS = 3
F32 = jnp.float32
BF16 = jnp.bfloat16

boundary_gain = 0.5

HALO_ROWS = 4
HALO_COLS = 12
ZONE = 8
ENDS = (0, 32, 31, 63)


def iota(shape, dim):
    return lax.broadcasted_iota(jnp.int32, shape, dim)


def packed(x):
    return jnp.concatenate([x[:64], x[64:]], axis=1)


def low_halves(block):
    lane = iota((64, 128), 1)
    return jnp.where(lane < 64, block[:64], pltpu.roll(block[64:], 64, 1))


def high_halves(block):
    lane = iota((64, 128), 1)
    return jnp.where(lane < 64, pltpu.roll(block[:64], 64, 1), block[64:])


def paired(low, high):
    lane = iota((64, 128), 1)
    top = jnp.where(lane < 64, low, pltpu.roll(high, 64, 1))
    bottom = jnp.where(lane < 64, pltpu.roll(low, 64, 1), high)
    return jnp.concatenate([top, bottom], axis=0)


def beside(values):
    lane = iota((128, 128), 1)
    both = paired(values, values)
    return jnp.where(lane < 64, pltpu.roll(both, 1, 0), pltpu.roll(both, 127, 0))


def gathered(table_ref, rows, high, low):
    low = jnp.bitwise_and(low, 127)

    found = jnp.zeros(high.shape, F32)
    for row in range(rows):
        line = jnp.broadcast_to(table_ref[row : row + 1, :], high.shape)
        found = jnp.where(high == row, jnp.take_along_axis(line, low, axis=1), found)
    return found


def summed(high_ref, low_ref, value_ref, high_size, low_size):
    rows = high_ref.shape[0]

    def step(index, total):
        start = pl.multiple_of(index * 8, 8)
        high = high_ref[pl.ds(start, 8), :]
        low = low_ref[pl.ds(start, 8), :]
        value = value_ref[pl.ds(start, 8), :]
        coarse = value.astype(BF16).astype(F32)
        fine = value - coarse
        row_hot, coarse_hot, fine_hot = [], [], []
        for j in range(8):
            row_hot.append(
                jnp.where(iota((high_size, 128), 0) == high[j : j + 1], 1.0, 0.0).astype(BF16)
            )
            same = iota((low_size, 128), 0) == low[j : j + 1]
            coarse_hot.append(jnp.where(same, coarse[j : j + 1], 0.0).astype(BF16))
            fine_hot.append(jnp.where(same, fine[j : j + 1], 0.0).astype(BF16))
        row_hot = jnp.concatenate(row_hot, axis=1)
        value_hot = jnp.concatenate(
            [jnp.concatenate(coarse_hot, axis=1), jnp.concatenate(fine_hot, axis=1)], axis=0
        )
        return total + lax.dot_general(
            row_hot, value_hot, (((1,), (1,)), ((), ())), preferred_element_type=F32
        )

    total = lax.fori_loop(0, rows // 8, step, jnp.zeros((high_size, 2 * low_size), F32))
    return total


def cell_place(cell):
    high = jnp.where(
        cell >= 0, jnp.bitwise_and(cell >> 7, 1) * 64 + (cell >> 8), -1
    )
    return high, jnp.bitwise_and(cell, 127)


def node_place(node):
    high = jnp.where(
        node >= 0, jnp.bitwise_and(node >> 7, 1) * 32 + (node >> 8), -1
    )
    return high, jnp.bitwise_and(node, 127)


def pipe_table(state):
    return jnp.concatenate([state[:, :128], state[:, 128:]], axis=0)


def strips(blocks, start):
    return jnp.concatenate([block[start : start + HALO_ROWS] for block in blocks], axis=0)


def start_kernel(surface, cond_x, cond_y, porosity, rainfall, fields, up, down, arrived):
    copies = [
        pltpu.make_async_copy(source, fields.at[index], arrived.at[index])
        for index, source in enumerate((surface, cond_x, cond_y, porosity, rainfall))
    ]
    for copy in copies:
        copy.start()
    for copy in copies:
        copy.wait()
    fields[3] = 1.0 / fields[3]
    for index in range(5):
        halves = [fields[index, :, 0:128], fields[index, :, 128:256]]
        up[pl.ds(index * 8, 8), :] = strips(halves, 0)
        down[pl.ds(index * 8, 8), :] = strips(halves, 60)


def tall_block(place_ref, block, above, below, start):
    over = jnp.where(place_ref[0] > 0, above[start : start + 4, :], 0.0)
    under = jnp.where(place_ref[0] < 7, below[start : start + 4, :], 0.0)
    return jnp.concatenate([block, under, over], axis=0)


def pack_cols_kernel(place_ref, above, below, fields, link_cell, tall_out, out):
    lane = iota((72, 128), 1)
    message = jnp.zeros((72, 128), F32)
    for index in range(5):
        tall = [
            tall_block(
                place_ref, fields[index, :, half * 128 : half * 128 + 128], above, below,
                index * 8 + half * 4,
            )
            for half in range(2)
        ]
        tall_out[index, :, 0:128] = tall[0]
        tall_out[index, :, 128:256] = tall[1]
        edges = jnp.where(
            lane < HALO_COLS, tall[0], jnp.where(lane >= 128 - HALO_COLS, tall[1], 0.0)
        )
        if index:
            edges = pltpu.roll(edges, index * 2 * HALO_COLS, 1)
        message = message + edges
    out[0:72, :] = message
    out[72:136, :] = packed(link_cell[...]).astype(F32)


def owner_start_kernel(
    pipes, link_node, link_coef, table, nodes, node_high, node_low, coef
):
    table[...] = pipe_table(pipes[...])
    high, low = node_place(packed(link_node[...]))
    node_high[...] = high
    node_low[...] = low
    coef[...] = packed(link_coef[...])
    nodes[...] = gathered(table, 64, high, low)


def swept(state, gains):
    def once(_, w):
        return (
            gains[0] * w
            + gains[1] * pltpu.roll(w, 1, 0)
            + gains[2] * pltpu.roll(w, 71, 0)
            + gains[3] * pltpu.roll(w, 1, 1)
            + gains[4] * pltpu.roll(w, 383, 1)
            + gains[5]
        )

    for i in range(SWEEPS):
        state = once(i, state)
    return state


def build_message(out, heads, nodes, table):
    out[:, 0:128] = paired(heads, nodes)
    out[:, 128:256] = beside(nodes)
    for index, row in enumerate(ENDS):
        block = jnp.broadcast_to(table[row : row + 1, :], (128, 128))
        out[:, 256 + index * 128 : 384 + index * 128] = block


def zone_heads(edge, zone_place, edge_ref, zone_ref):
    lane = iota((64, 128), 1)
    edge_ref[...] = jnp.where(lane < ZONE, edge, pltpu.roll(edge, 2 * ZONE, 1))
    lane8 = iota((8, 128), 1)
    table = jnp.zeros((8, 128), F32)
    for s in range(8):
        line = edge_ref[pl.ds(s, 8, stride=8), :]
        if s:
            line = pltpu.roll(line, s * 16, 1)
        table = jnp.where((lane8 >> 4) == s, line, table)
    zone_ref[...] = table
    zone_row, zone_col = zone_place
    high = jnp.where(zone_row >= 0, zone_row >> 3, -1)
    low = jnp.bitwise_and(zone_row, 7) * 16 + zone_col
    return gathered(zone_ref, 8, high, low)


def sweep_and_gather(
    state, gains, cell_high, cell_low, zone_place, surface_out, heads_out, zone_out, cell_table,
    edge_ref, zone_ref,
):
    state = swept(state, gains)
    surface_out[...] = state[:64]
    cell_table[0:64, :] = state[:64, 0:128]
    cell_table[64:128, :] = state[:64, 128:256]
    heads = gathered(cell_table, 128, cell_high, cell_low)
    heads_out[...] = heads
    if zone_place is not None:
        zone_out[...] = zone_heads(state[:64, 256:384], zone_place, edge_ref, zone_ref)
    return heads


def first_sweep_kernel(
    place_ref, tall, from_west, from_east, link_cell, table, nodes, coef,
    gains_out, inverse_out, cell_high, cell_low, zone_row_out, zone_col_out, surface_out, heads_out,
    zone_out, out, cell_table, edge_ref, zone_ref,
):
    lane = iota((72, 128), 1)
    wide = []
    for index in range(5):
        west = jnp.where(place_ref[1] > 0, from_west[0:72, :], 0.0)
        east = jnp.where(place_ref[1] < 15, from_east[0:72, :], 0.0)
        if index:
            west = pltpu.roll(west, 128 - index * 2 * HALO_COLS, 1)
            east = pltpu.roll(east, 128 - index * 2 * HALO_COLS, 1)
        edge = jnp.where(
            lane < HALO_COLS, east, jnp.where(lane >= 128 - HALO_COLS, west, 0.0)
        )
        wide.append(jnp.concatenate([tall[index], edge], axis=1))
    state, cond_x, cond_y, inverse, rainfall = wide
    north = pltpu.roll(cond_x, 1, 0)
    west = pltpu.roll(cond_y, 1, 1)
    gains = [
        1.0 - (north + cond_x + west + cond_y) * inverse,
        north * inverse, cond_x * inverse, west * inverse, cond_y * inverse, rainfall,
    ]
    for index, gain in enumerate(gains):
        gains_out[index] = gain
    inverse_out[...] = inverse[:64]
    cells = paired(from_west[72:136, :], from_east[72:136, :]).astype(jnp.int32)
    col = jnp.bitwise_and(cells, 255)
    is_west = iota((128, 128), 1) < 64
    zone_col = jnp.where(is_west, col - (256 - 2 * ZONE), col)
    inside = (zone_col >= 0) & (zone_col < 2 * ZONE)
    inside = inside & (jnp.where(is_west, zone_col, zone_col + ZONE) >= ZONE)
    zone_row = jnp.where((cells >= 0) & inside & (jnp.where(is_west, 0, zone_col) < ZONE), cells >> 8, -1)
    zone_row_out[...] = zone_row
    zone_col_out[...] = zone_col
    high, low = cell_place(packed(link_cell[...]))
    cell_high[...] = high
    cell_low[...] = low
    heads = sweep_and_gather(
        state, gains, high, low, (zone_row, zone_col), surface_out, heads_out, zone_out,
        cell_table, edge_ref, zone_ref,
    )
    build_message(out, heads, nodes[...], table)
    out[:, 768:896] = paired(coef[...], coef[...])
    out[:, 896:1024] = beside(coef[...])


def sweep_kernel(
    last, place_ref, surface, above, below, gains_ref, cell_high, cell_low, zone_row, zone_col,
    table, nodes, surface_out, heads_out, zone_out, out, cell_table, edge_ref, zone_ref,
):
    state = jnp.concatenate(
        [
            tall_block(
                place_ref, surface[:, block * 128 : block * 128 + 128], above, below, block * 4
            )
            for block in range(3)
        ],
        axis=1,
    )
    gains = [gains_ref[index] for index in range(6)]
    zone_place = None if last else (zone_row[...], zone_col[...])
    heads = sweep_and_gather(
        state, gains, cell_high[...], cell_low[...], zone_place, surface_out, heads_out, zone_out,
        cell_table, edge_ref, zone_ref,
    )
    build_message(out, heads, nodes[...], table)


def tile_kernel(
    first, last, got, surface, inverse, heads, zone, cell_high, cell_low, zone_row, zone_col, *rest
):
    rest = list(rest)
    if first:
        own_coef = low_halves(got[:, 768:896])
        zone_coef = got[:, 896:1024]
    else:
        own_coef = rest.pop(0)[...]
        zone_coef = rest.pop(0)[...]
    surface_out = rest.pop(0)
    if not last:
        up, down = rest.pop(0), rest.pop(0)
    if first:
        rest.pop(0)[...] = own_coef
        rest.pop(0)[...] = zone_coef
    value_ref, zone_value_ref = rest
    value_ref[...] = jnp.where(
        cell_high[...] >= 0, own_coef * (heads[...] - high_halves(got[:, 0:128])), 0.0
    )
    lost = summed(cell_high, cell_low, value_ref, 128, 128)
    lost = lost[:, :128] + lost[:, 128:]
    left = surface[:, 0:128] - inverse[:, 0:128] * lost[:64]
    right = surface[:, 128:256] - inverse[:, 128:256] * lost[64:]
    surface_out[:, 0:128] = left
    surface_out[:, 128:256] = right
    if last:
        return
    zone_value_ref[...] = jnp.where(
        zone_row[...] >= 0, zone_coef * (zone[...] - got[:, 128:256]), 0.0
    )
    lost = summed(zone_row, zone_col, zone_value_ref, 64, 64)
    lost = lost[:, :64] + lost[:, 64:]
    lost = jnp.concatenate([lost, jnp.zeros((64, 64), F32)], axis=1)
    lane = iota((64, 128), 1)
    lost = jnp.where(
        lane < ZONE, lost,
        jnp.where(lane >= 128 - ZONE, pltpu.roll(lost, 128 - 2 * ZONE, 1), 0.0),
    )
    edge = surface[:, 256:384] - inverse[:, 256:384] * lost
    surface_out[:, 256:384] = edge
    up[...] = strips([left, right, edge], 0)
    down[...] = strips([left, right, edge], 60)


def owner_kernel(
    last, place_ref, got, nodes, node_high, node_low, coef, table, meets, classes, matrices, *rest
):
    if last:
        pipes_out, value_ref, ends_ref = rest
    else:
        table_out, nodes_out, value_ref, ends_ref = rest
    value_ref[...] = jnp.where(
        node_high[...] >= 0, coef[...] * (low_halves(got[:, 0:128]) - nodes[...]), 0.0
    )
    inflow = summed(node_high, node_low, value_ref, 64, 128)
    balance = table[...] + (inflow[:, :128] + inflow[:, 128:])
    start = pl.multiple_of(place_ref[0] * 16, 16)
    for index in range(4):
        ends_ref[index * 16 : index * 16 + 16, :] = got[
            pl.ds(start, 16), 256 + index * 128 : 384 + index * 128
        ]
    meet = meets[...]
    meet_high = jnp.bitwise_and(meet >> 7, 1) * 16 + (meet >> 8)
    meet_high = jnp.where(iota((8, 128), 0) < 2, meet_high + 32, meet_high)
    met = gathered(ends_ref, 64, meet_high, meet) * boundary_gain
    node_row = iota((32, 128), 0)
    parts = []
    for half in range(2):
        part = balance[half * 32 : half * 32 + 32]
        part = part + jnp.where(
            node_row == 0, met[half : half + 1],
            jnp.where(node_row == 31, met[2 + half : 3 + half], 0.0),
        )
        products = jnp.dot(
            matrices[...], part, precision=lax.Precision.HIGHEST, preferred_element_type=F32
        )
        kind = classes[half : half + 1, :]
        updated = jnp.zeros((32, 128), F32)
        for index in range(CLASSES):
            updated = jnp.where(kind == index, products[index * 32 : index * 32 + 32], updated)
        parts.append(updated)
    if last:
        pipes_out[:, 0:128] = parts[0]
        pipes_out[:, 128:256] = parts[1]
        return
    table_out[0:32, :] = parts[0]
    table_out[32:64, :] = parts[1]
    nodes_out[...] = gathered(table_out, 64, node_high[...], node_low[...])


def shape(*dims, dtype=F32):
    return jax.ShapeDtypeStruct(dims, dtype)


def call(kernel, inputs, outputs, scratch=(), scalars=0, space=pltpu.VMEM, flops=10**9):
    smem = pl.BlockSpec(memory_space=pltpu.SMEM)
    vmem = pl.BlockSpec(memory_space=pltpu.VMEM)
    return pl.pallas_call(
        kernel,
        out_shape=outputs,
        in_specs=[smem] * scalars + [pl.BlockSpec(memory_space=space)] * (len(inputs) - scalars),
        out_specs=[vmem] * len(outputs),
        scratch_shapes=list(scratch),
        compiler_params=pltpu.CompilerParams(vmem_limit_bytes=32 << 20),
        cost_estimate=pl.CostEstimate(flops=flops, bytes_accessed=1 << 20, transcendentals=0),
    )(*inputs)


def ring(block, axis, distance):
    size = lax.axis_size(axis)
    return lax.ppermute(block, axis, [(i, (i + distance) % size) for i in range(size)])


def body(
    surface_head, conduct_x, conduct_y, porosity, rainfall, pipe_head, pipe_class, pipe_up,
    pipe_down, pipe_matrices, link_cell, link_node, link_coef,
):
    place = jnp.stack([lax.axis_index("row"), lax.axis_index("col")]).astype(jnp.int32)
    link_cell = link_cell[0]
    link_node = link_node[:, 0, :]
    link_coef = link_coef[:, 0, :]
    meets = jnp.concatenate(
        [pipe_up.reshape(2, 128), pipe_down.reshape(2, 128), jnp.zeros((4, 128), jnp.int32)], axis=0
    )
    classes = pipe_class.reshape(2, 128)
    matrices = pipe_matrices.reshape(CLASSES * 32, 32)
    ints = functools.partial(shape, dtype=jnp.int32)

    fields, up, down = call(
        start_kernel, (surface_head, conduct_x, conduct_y, porosity, rainfall),
        [shape(5, 64, 256), shape(40, 128), shape(40, 128)],
        [pltpu.SemaphoreType.DMA((5,))], space=pltpu.HBM,
    )
    above, below = ring(down, "row", 1), ring(up, "row", -1)
    tall, sent = call(
        pack_cols_kernel, (place, above, below, fields, link_cell),
        [shape(5, 72, 256), shape(136, 128)], scalars=1,
    )
    from_west, from_east = ring(sent, "col", 1), ring(sent, "col", -1)
    table, nodes, node_high, node_low, coef = call(
        owner_start_kernel, (pipe_head, link_node, link_coef),
        [shape(64, 128), shape(64, 128), ints(64, 128), ints(64, 128), shape(64, 128)],
    )
    gather_scratch = [
        pltpu.VMEM((128, 128), F32), pltpu.VMEM((64, 128), F32), pltpu.VMEM((8, 128), F32)
    ]
    swept_shapes = [shape(64, 384), shape(64, 128), shape(128, 128)]
    (gains, inverse, cell_high, cell_low, zone_row, zone_col, surface, heads, zone, sent) = call(
        first_sweep_kernel,
        (place, tall, from_west, from_east, link_cell, table, nodes, coef),
        [shape(6, 72, 384), shape(64, 384), ints(64, 128), ints(64, 128), ints(128, 128),
         ints(128, 128), *swept_shapes, shape(128, 1024)],
        gather_scratch, scalars=1,
    )
    sent, meets, classes, matrices = lax.optimization_barrier((sent, meets, classes, matrices))
    coefs = ()
    for step in range(STEPS):
        first, last = step == 0, step == STEPS - 1
        if step:
            surface, heads, zone, sent = call(
                functools.partial(sweep_kernel, last),
                (place, surface, above, below, gains, cell_high, cell_low, zone_row, zone_col,
                 table, nodes),
                [*swept_shapes, shape(128, 768)], gather_scratch, scalars=1,
            )
        got = lax.all_to_all(sent, ("row", "col"), split_axis=0, concat_axis=0, tiled=True)
        outputs = [shape(64, 256)] if last else [shape(64, 384), shape(12, 128), shape(12, 128)]
        if first:
            outputs += [shape(64, 128), shape(128, 128)]
        tile = call(
            functools.partial(tile_kernel, first, last),
            (got, surface, inverse, heads, zone, cell_high, cell_low, zone_row, zone_col, *coefs),
            outputs, [pltpu.VMEM((64, 128), F32), pltpu.VMEM((128, 128), F32)],
        )
        if not last:
            above, below = ring(tile[2], "row", 1), ring(tile[1], "row", -1)
        owner = call(
            functools.partial(owner_kernel, last),
            (place, got, nodes, node_high, node_low, coef, table, meets, classes, matrices),
            [shape(32, 256)] if last else [shape(64, 128), shape(64, 128)],
            [pltpu.VMEM((64, 128), F32), pltpu.VMEM((64, 128), F32)], scalars=1,
        )
        if last:
            return tile[0], owner[0]
        surface = tile[0]
        table, nodes = owner
        if first:
            coefs = tuple(tile[3:])


def solution(mesh):
    placed = (
        P("row", "col"),
        P("row", "col"),
        P("row", "col"),
        P("row", "col"),
        P("row", "col"),
        P(None, ("row", "col")),
        P(("row", "col")),
        P(("row", "col")),
        P(("row", "col")),
        P(),
        P(("row", "col"), None, None),
        P(None, ("row", "col"), None),
        P(None, ("row", "col"), None),
    )
    return jax.shard_map(
        body,
        mesh=mesh,
        in_specs=placed,
        out_specs=(P("row", "col"), P(None, ("row", "col"))),
        check_vma=False,
    )
```

time: 140 us -> 128 us (0.914)
  waiting for transfers between devices: 20.6 us -> 1.75 us
  blocking collectives: 44.9 us -> 59.9 us
  starting transfers between devices: 22.4 us -> 10.6 us
  Pallas kernels: 42.3 us -> 46 us
    all_to_all x2 -> x3, blocking collectives: 29.5 us -> 59.9 us  [body(): lax.all_to_all(sent, ('row', 'col'), split_axis=0, concat_axis=0, tiled=T...]
    all_to_all x2 -> x0, starting transfers between devices: 17.9 us -> none  [the longest x1 12 us: body(): lax.all_to_all(sent, ('row', 'col'), split_axis=0, concat_axis=0, tiled=T...]
    all_to_all x2 -> x0, waiting for transfers between devices: 17.1 us -> none  [the longest x1 11.3 us: body(): lax.all_to_all(sent, ('row', 'col'), split_axis=0, concat_axis=0, tiled=T...]
    all_to_all x2 -> x0, blocking collectives: 15.4 us -> none  [body(): got = lax.all_to_all(sent, 'row', split_axis=0, concat_axis=0, tiled=True)]
    ppermute x2 -> x8, starting transfers between devices: 4.5 us -> 10.6 us  [ring(): lax.ppermute(block, axis, [(i, (i + distance) % size) for i in range(size)])]
    pallas_call x8 -> x12, Pallas kernels: 42.3 us -> 46 us  [call(): pl.pallas_call(kernel, out_shape=outputs, in_specs=[smem] * scalars + [pl...]
    ppermute x2 -> x8, waiting for transfers between devices: 3.52 us -> 1.75 us  [ring(): lax.ppermute(block, axis, [(i, (i + distance) % size) for i in range(size)])]
    unnamed x44 -> x32, local copies, waits for them, and re-layouts: 6.8 us -> 6.63 us
  transfers between devices with their start and end apart: 4 -> 8, of which waited for: 3 -> 2; matrix products, arithmetic and copies ran while one was open for 0% -> 0% of each run, Pallas kernels for 0% -> 9%
where the time goes in v2:
time: 128 us; the launch traced here: 127 us
  blocking collectives  59.9 us (47%)
  Pallas kernels  46 us (36%)
  starting transfers between devices  10.6 us (8%)
  local copies, waits for them, and re-layouts  8.06 us (6%)
  waiting for transfers between devices  1.75 us (1%)
    all_to_all x3, blocking collectives, body(): lax.all_to_all(sent, ('row', 'col'), split_axis=0, concat_axis=0, tiled=T...  59.9 us
    pallas_call x12, Pallas kernels, call(): pl.pallas_call(kernel, out_shape=outputs, in_specs=[smem] * scalars + [pl...  46 us
    ppermute x8, starting transfers between devices, ring(): lax.ppermute(block, axis, [(i, (i + distance) % size) for i in range(size)])  10.6 us
    unnamed x32, local copies, waits for them, and re-layouts  6.63 us
  transfers between devices with their start and end apart: 8, of which 2 were waited for; matrix products, arithmetic and copies ran while one was open for 0% of the time, Pallas kernels for 9%

profile of v2, /device:TPU:1, one launch (start us, length us, event | category | flops | bytes accessed | tf_op | source)
XLA Modules:
  0.0 127.3 jit_solution(16515600249052088325)
XLA Ops:
  0.6 0.0 copy-start
  0.6 0.8 copy-done
  1.5 0.0 copy-start.1
  1.5 0.8 copy-done.1
  2.3 0.0 copy-start.2
  2.3 0.8 copy-done.2
  3.2 0.0 copy-start.3
  3.2 0.8 copy-done.3
  4.0 0.0 copy-start.4
  4.0 0.8 copy-done.4
  4.8 0.0 copy-start.11
  4.8 0.0 copy-start.12
  4.8 0.5 shard_map.140
  5.3 0.0 copy-start.8
  5.3 2.6 %collective-permute-start = (f32[40,128]{1,0:T(8,128)S(1)}, f32[40,128]{1,0:T(8,128)S(1)}, u32[]{:S(2)}, u32[]{:S(2)}) collective-permute-start(f32[40,128]{1,0:T(8,128)S(1)} %get-tuple-element.46), channel_id=1, source_target_pairs={{0,16},{16,32},{32,48},{48,64},{64,80},{80,96},{96,112},{112,0},{1... | collective-permute-start | bytes 61448 | tf_op jit(solution)/shard_map/ppermute | solution.py:410
  7.9 0.0 collective-permute-start.1
  7.9 0.1 pad.2.clone
  8.0 0.0 copy-done.11
  8.0 0.0 copy-done.12
  8.0 0.1 add_add_fusion.meets
  8.1 0.1 pad_add_fusion.place_ref
  8.2 0.0 copy-done.8
  8.2 0.0 copy-start.9
  8.2 0.1 copy.18
  8.3 0.7 copy-done.9
  8.9 0.1 copy.19
  9.0 0.7 copy-done.10
  9.7 0.1 copy.20
  9.8 0.0 collective-permute-done.above
  9.8 1.3 %collective-permute-done.1.below = f32[40,128]{1,0:T(8,128)S(1)} collective-permute-done((f32[40,128]{1,0:T(8,128)S(1)}, f32[40,128]{1,0:T(8,128)S(1)}, u32[]{:S(2)}, u32[]{:S(2)}) %collective-permute-start.1) | collective-permute-done | bytes 20512 | tf_op jit(solution)/shard_map/ppermute | solution.py:410
  11.2 0.7 shard_map.141
  11.8 1.4 %collective-permute-start.2 = (f32[136,128]{1,0:T(8,128)S(1)}, f32[136,128]{1,0:T(8,128)S(1)}, u32[]{:S(2)}, u32[]{:S(2)}) collective-permute-start(f32[136,128]{1,0:T(8,128)S(1)} %get-tuple-element.50), channel_id=1, source_target_pairs={{0,1},{1,2},{2,3},{3,4},{4,5},{5,6},{6,7},{7,8},{8,9},{9,10},{10,1... | collective-permute-start | bytes 208904 | tf_op jit(solution)/shard_map/ppermute | solution.py:410
  13.2 5.0 %collective-permute-start.3 = (f32[136,128]{1,0:T(8,128)S(1)}, f32[136,128]{1,0:T(8,128)S(1)}, u32[]{:S(2)}, u32[]{:S(2)}) collective-permute-start(f32[136,128]{1,0:T(8,128)S(1)} %get-tuple-element.50), channel_id=1, source_target_pairs={{0,15},{1,0},{2,1},{3,2},{4,3},{5,4},{6,5},{7,6},{8,7},{9,8},{10,9... | collective-permute-start | bytes 208904 | tf_op jit(solution)/shard_map/ppermute | solution.py:410
  18.2 0.0 copy-done.6
  18.2 1.6 %shard_map.142 = (f32[64,128]{1,0:T(8,128)S(1)}, f32[64,128]{1,0:T(8,128)S(1)}, s32[64,128]{1,0:T(8,128)S(1)}, s32[64,128]{1,0:T(8,128)S(1)}, f32[64,128]{1,0:T(8,128)S(1)}) custom-call(f32[32,256]{1,0:T(8,128)S(1)} %copy-done.6, s32[128,64]{1,0:T(8,128)S(1)} %bitcast.32, f32[128,64]{1,0:T(8,128)S(1)} %bitcast.33), custom_call_target="tpu_custom_call" | custom-call | flops 1000000000 | bytes 1048576 | tf_op jit(solution)/shard_map/pallas_call | solution.py:397
  19.8 0.4 collective-permute-done.2.from_west
  20.2 0.0 collective-permute-done.3.from_east
  20.2 4.8 %shard_map.143 = (f32[6,72,384]{2,1,0:T(8,128)S(1)}, f32[64,384]{1,0:T(8,128)S(1)}, s32[64,128]{1,0:T(8,128)S(1)}, s32[64,128]{1,0:T(8,128)S(1)}, s32[128,128]{1...) custom-call(s32[2]{0:T(128)S(1)} %pad_add_fusion.place_ref, ...), custom_call_target="tpu_custom_call" | custom-call | flops 1000000000 | bytes 1048576 | tf_op jit(solution)/shard_map/pallas_call | solution.py:397
  24.9 0.5 copy.21
  25.5 23.1 %all_to_all.33 = f32[128,1,1024]{2,1,0:T(1,128)S(1)} all-to-all(f32[128,1,1024]{2,1,0:T(1,128)S(1)} %copy.21), channel_id=1, replica_groups=mesh['row'=8,'col'=16] {'row','col'}, dimensions={0} | all-to-all | bytes 1048576 | tf_op jit(solution)/shard_map/all_to_all | solution.py:465
  48.6 0.1 copy.30
  48.7 0.0 copy-start.5
  48.7 6.4 %shard_map.144 = (f32[64,384]{1,0:T(8,128)S(1)}, f32[12,128]{1,0:T(8,128)S(1)}, f32[12,128]{1,0:T(8,128)S(1)}, f32[64,128]{1,0:T(8,128)S(1)}, f32[128,128]{1,0:T(8,128)S(1)}) custom-call(f32[128,1024]{1,0:T(8,128)S(1)} %bitcast.21, f32[64,384]{1,0:T(8,128)S(1)} %get-tuple-element.56.surface, f32[64,384]{1,0:T(8,128)S(1)} %get-tuple-element.57.inverse, ...), custom_call_target="tpu_custom_call" | custom-call | flops 1000000000 | bytes 1048576 | tf_op jit(solution)/shard_map/pallas_call | solution.py:397
  55.1 0.8 collective-permute-start.4
  55.9 0.0 collective-permute-start.5
  55.9 0.0 copy-done.5
  55.9 0.7 copy-done.7
  56.6 4.9 %shard_map.145 = (f32[64,128]{1,0:T(8,128)S(1)}, f32[64,128]{1,0:T(8,128)S(1)}) custom-call(s32[2]{0:T(128)S(1)} %pad_add_fusion.place_ref, f32[128,1024]{1,0:T(8,128)S(1)} %bitcast.22, f32[64,128]{1,0:T(8,128)S(1)} %get-tuple-element.52.nodes, s32[64,128]{1,0:T(8,128)S(1)} %get-tuple-element.68.node_high, s32[64,128]{1,0:T(8,128)S(1)} %get-tuple-element.69.node_low, ...), custom_call_target="tpu_custom_call" | custom-call | flops 1000000000 | bytes 1048576 | tf_op jit(solution)/shard_map/pallas_call | solution.py:397
  61.6 0.0 collective-permute-done.4.above
  61.6 0.0 collective-permute-done.5.below
  61.6 4.5 %shard_map.146 = (f32[64,384]{1,0:T(8,128)S(1)}, f32[64,128]{1,0:T(8,128)S(1)}, f32[128,128]{1,0:T(8,128)S(1)}, f32[128,768]{1,0:T(8,128)S(1)}) custom-call(s32[2]{0:T(128)S(1)} %pad_add_fusion.place_ref, f32[64,384]{1,0:T(8,128)S(1)} %get-tuple-element.64.surface, f32[12,128]{1,0:T(8,128)S(1)} %collective-permute-done.4.above, ...), custom_call_target="tpu_custom_call" | custom-call | flops 1000000000 | bytes 1048576 | tf_op jit(solution)/shard_map/pallas_call | solution.py:397
  66.1 0.4 copy.22
  66.5 18.4 %all_to_all.34 = f32[128,1,768]{2,1,0:T(1,128)S(1)} all-to-all(f32[128,1,768]{2,1,0:T(1,128)S(1)} %copy.22), channel_id=1, replica_groups=mesh['row'=8,'col'=16] {'row','col'}, dimensions={0} | all-to-all | bytes 786432 | tf_op jit(solution)/shard_map/all_to_all | solution.py:465
  84.9 6.4 %shard_map.147 = (f32[64,384]{1,0:T(8,128)S(1)}, f32[12,128]{1,0:T(8,128)S(1)}, f32[12,128]{1,0:T(8,128)S(1)}) custom-call(f32[128,768]{1,0:T(8,128)S(1)} %bitcast.24, f32[64,384]{1,0:T(8,128)S(1)} %get-tuple-element.76.surface, f32[64,384]{1,0:T(8,128)S(1)} %get-tuple-element.57.inverse, f32[64,128]{1,0:T(8,128)S(1)} %get-tuple-element.77.heads, ...), custom_call_target="tpu_custom_call" | custom-call | flops 1000000000 | bytes 1048576 | tf_op jit(solution)/shard_map/pallas_call | solution.py:397
  91.3 0.8 collective-permute-start.6
  92.1 0.0 collective-permute-start.7
  92.1 4.9 %shard_map.148 = (f32[64,128]{1,0:T(8,128)S(1)}, f32[64,128]{1,0:T(8,128)S(1)}) custom-call(s32[2]{0:T(128)S(1)} %pad_add_fusion.place_ref, f32[128,768]{1,0:T(8,128)S(1)} %bitcast.25, f32[64,128]{1,0:T(8,128)S(1)} %get-tuple-element.74.nodes, s32[64,128]{1,0:T(8,128)S(1)} %get-tuple-element.68.node_high, s32[64,128]{1,0:T(8,128)S(1)} %get-tuple-element.69.node_low, ...), custom_call_target="tpu_custom_call" | custom-call | flops 1000000000 | bytes 1048576 | tf_op jit(solution)/shard_map/pallas_call | solution.py:397
  97.0 0.0 collective-permute-done.6.above
  97.0 0.0 collective-permute-done.7.below
  97.0 4.0 %shard_map.149 = (f32[64,384]{1,0:T(8,128)S(1)}, f32[64,128]{1,0:T(8,128)S(1)}, f32[128,128]{1,0:T(8,128)S(1)}, f32[128,768]{1,0:T(8,128)S(1)}) custom-call(s32[2]{0:T(128)S(1)} %pad_add_fusion.place_ref, f32[64,384]{1,0:T(8,128)S(1)} %get-tuple-element.81.surface, f32[12,128]{1,0:T(8,128)S(1)} %collective-permute-done.6.above, ...), custom_call_target="tpu_custom_call" | custom-call | flops 1000000000 | bytes 1048576 | tf_op jit(solution)/shard_map/pallas_call | solution.py:397
  101.0 0.4 copy.23
  101.4 18.4 %all_to_all.35 = f32[128,1,768]{2,1,0:T(1,128)S(1)} all-to-all(f32[128,1,768]{2,1,0:T(1,128)S(1)} %copy.23), channel_id=1, replica_groups=mesh['row'=8,'col'=16] {'row','col'}, dimensions={0} | all-to-all | bytes 786432 | tf_op jit(solution)/shard_map/all_to_all | solution.py:465
  119.9 4.0 %shard_map.151 = f32[32,256]{1,0:T(8,128)} custom-call(s32[2]{0:T(128)S(1)} %pad_add_fusion.place_ref, f32[128,768]{1,0:T(8,128)S(1)} %bitcast.26, f32[64,128]{1,0:T(8,128)S(1)} %get-tuple-element.85.nodes, s32[64,128]{1,0:T(8,128)S(1)} %get-tuple-element.68.node_high, s32[64,128]{1,0:T(8,128)S(1)} %get-tuple-element.69.node_low, ...), custom_call_target="tpu_custom_call" | custom-call | flops 1000000000 | bytes 1048576 | tf_op jit(solution)/shard_map/pallas_call | solution.py:397
  123.9 3.3 %shard_map.150 = f32[64,256]{1,0:T(8,128)} custom-call(f32[128,768]{1,0:T(8,128)S(1)} %bitcast.27, f32[64,384]{1,0:T(8,128)S(1)} %get-tuple-element.87.surface, f32[64,384]{1,0:T(8,128)S(1)} %get-tuple-element.57.inverse, f32[64,128]{1,0:T(8,128)S(1)} %get-tuple-element.88.heads, f32[128,128]{1,0:T(8,128)S(1)} %get-tuple-element.89.zone, ...), custom_call_target="tpu_custom_call" | custom-call | flops 1000000000 | bytes 1048576 | tf_op jit(solution)/shard_map/pallas_call | solution.py:397
  (6 shorter events, 0.1 us)
Async XLA Ops:
  0.6 0.8 copy-start
  1.5 0.8 copy-start.1
  2.3 0.8 copy-start.2
  3.2 0.8 copy-start.3
  4.0 0.8 copy-start.4
  4.8 3.2 %copy-start.11 = (s32[256]{0:T(256)S(1)}, s32[256]{0:T(256)}, u32[]{:S(2)}) copy-start(s32[256]{0:T(256)} %param.21) | copy-start | bytes 3076
  4.8 3.2 %copy-start.12 = (s32[256]{0:T(256)S(1)}, s32[256]{0:T(256)}, u32[]{:S(2)}) copy-start(s32[256]{0:T(256)} %param.20) | copy-start | bytes 3076
  5.3 2.9 %copy-start.8 = (s32[1,128,64]{1,2,0:T(8,128)S(1)}, s32[1,128,64]{1,2,0:T(8,128)}, u32[]{:S(2)}) copy-start(s32[1,128,64]{1,2,0:T(8,128)} %param.23) | copy-start | bytes 98308
  5.3 4.5 %collective-permute-start = (f32[40,128]{1,0:T(8,128)S(1)}, f32[40,128]{1,0:T(8,128)S(1)}, u32[]{:S(2)}, u32[]{:S(2)}) collective-permute-start(f32[40,128]{1,0:T(8,128)S(1)} %get-tuple-element.46), channel_id=1, source_target_pairs={{0,16},{16,32},{32,48},{48,64},{64,80},{80,96},{96,112},{112,0},{1... | collective-permute-start | bytes 61448 | tf_op jit(solution)/shard_map/ppermute | solution.py:410
  7.9 3.2 %collective-permute-start.1 = (f32[40,128]{1,0:T(8,128)S(1)}, f32[40,128]{1,0:T(8,128)S(1)}, u32[]{:S(2)}, u32[]{:S(2)}) collective-permute-start(f32[40,128]{1,0:T(8,128)S(1)} %get-tuple-element.47), channel_id=1, source_target_pairs={{0,112},{16,0},{32,16},{48,32},{64,48},{80,64},{96,80},{112,96},{1... | collective-permute-start | bytes 61448 | tf_op jit(solution)/shard_map/ppermute | solution.py:410
  8.2 0.8 copy-start.9
  8.9 0.8 copy-start.10
  11.2 7.0 %copy-start.6 = (f32[32,256]{1,0:T(8,128)S(1)}, f32[32,256]{1,0:T(8,128)}, u32[]{:S(2)}) copy-start(f32[32,256]{1,0:T(8,128)} %pipes.1) | copy-start | bytes 98308
  11.8 8.3 %collective-permute-start.2 = (f32[136,128]{1,0:T(8,128)S(1)}, f32[136,128]{1,0:T(8,128)S(1)}, u32[]{:S(2)}, u32[]{:S(2)}) collective-permute-start(f32[136,128]{1,0:T(8,128)S(1)} %get-tuple-element.50), channel_id=1, source_target_pairs={{0,1},{1,2},{2,3},{3,4},{4,5},{5,6},{6,7},{7,8},{8,9},{9,10},{10,1... | collective-permute-start | bytes 208904 | tf_op jit(solution)/shard_map/ppermute | solution.py:410
  13.2 7.0 %collective-permute-start.3 = (f32[136,128]{1,0:T(8,128)S(1)}, f32[136,128]{1,0:T(8,128)S(1)}, u32[]{:S(2)}, u32[]{:S(2)}) collective-permute-start(f32[136,128]{1,0:T(8,128)S(1)} %get-tuple-element.50), channel_id=1, source_target_pairs={{0,15},{1,0},{2,1},{3,2},{4,3},{5,4},{6,5},{7,6},{8,7},{9,8},{10,9... | collective-permute-start | bytes 208904 | tf_op jit(solution)/shard_map/ppermute | solution.py:410
  48.7 7.2 %copy-start.5 = (f32[4,32,32]{2,1,0:T(8,128)S(1)}, f32[4,32,32]{2,1,0:T(8,128)}, u32[]{:S(2)}) copy-start(f32[4,32,32]{2,1,0:T(8,128)} %param.22) | copy-start | bytes 49156
  55.1 6.4 %collective-permute-start.4 = (f32[12,128]{1,0:T(8,128)S(1)}, f32[12,128]{1,0:T(8,128)S(1)}, u32[]{:S(2)}, u32[]{:S(2)}) collective-permute-start(f32[12,128]{1,0:T(8,128)S(1)} %get-tuple-element.65), channel_id=1, source_target_pairs={{0,16},{16,32},{32,48},{48,64},{64,80},{80,96},{96,112},{112,0},{1... | collective-permute-start | bytes 18440 | tf_op jit(solution)/shard_map/ppermute | solution.py:410
  55.9 5.6 %collective-permute-start.5 = (f32[12,128]{1,0:T(8,128)S(1)}, f32[12,128]{1,0:T(8,128)S(1)}, u32[]{:S(2)}, u32[]{:S(2)}) collective-permute-start(f32[12,128]{1,0:T(8,128)S(1)} %get-tuple-element.66), channel_id=1, source_target_pairs={{0,112},{16,0},{32,16},{48,32},{64,48},{80,64},{96,80},{112,96},{1... | collective-permute-start | bytes 18440 | tf_op jit(solution)/shard_map/ppermute | solution.py:410
  55.9 0.7 copy-start.7
  91.3 5.7 %collective-permute-start.6 = (f32[12,128]{1,0:T(8,128)S(1)}, f32[12,128]{1,0:T(8,128)S(1)}, u32[]{:S(2)}, u32[]{:S(2)}) collective-permute-start(f32[12,128]{1,0:T(8,128)S(1)} %get-tuple-element.82), channel_id=1, source_target_pairs={{0,16},{16,32},{32,48},{48,64},{64,80},{80,96},{96,112},{112,0},{1... | collective-permute-start | bytes 18440 | tf_op jit(solution)/shard_map/ppermute | solution.py:410
  92.1 4.9 %collective-permute-start.7 = (f32[12,128]{1,0:T(8,128)S(1)}, f32[12,128]{1,0:T(8,128)S(1)}, u32[]{:S(2)}, u32[]{:S(2)}) collective-permute-start(f32[12,128]{1,0:T(8,128)S(1)} %get-tuple-element.83), channel_id=1, source_target_pairs={{0,112},{16,0},{32,16},{48,32},{64,48},{80,64},{96,80},{112,96},{1... | collective-permute-start | bytes 18440 | tf_op jit(solution)/shard_map/ppermute | solution.py:410

commit v3 on v2

--- a/solution.py
+++ b/solution.py
@@ -54,42 +54,51 @@
 
 def gathered(table_ref, rows, high, low):
     low = jnp.bitwise_and(low, 127)
-
-    found = jnp.zeros(high.shape, F32)
-    for row in range(rows):
-        line = jnp.broadcast_to(table_ref[row : row + 1, :], high.shape)
-        found = jnp.where(high == row, jnp.take_along_axis(line, low, axis=1), found)
-    return found
+    tiles = []
+    for start in range(0, high.shape[0], 8):
+        tile_high, tile_low = high[start : start + 8], low[start : start + 8]
+        found = jnp.zeros((8, 128), F32)
+        for row in range(rows):
+            line = jnp.broadcast_to(table_ref[row : row + 1, :], (8, 128))
+            values = jnp.take_along_axis(line, tile_low, axis=1)
+            found = jnp.where(tile_high == row, values, found)
+        tiles.append(found)
+    return jnp.concatenate(tiles, axis=0) if len(tiles) > 1 else tiles[0]
+
+
+def repeated(line, size):
+    block = jnp.broadcast_to(line, (16, 128)).astype(BF16)
+    return jnp.concatenate([block] * (size // 16), axis=0) if size > 16 else block
 
 
 def summed(high_ref, low_ref, value_ref, high_size, low_size):
-    rows = high_ref.shape[0]
-
-    def step(index, total):
-        start = pl.multiple_of(index * 8, 8)
-        high = high_ref[pl.ds(start, 8), :]
-        low = low_ref[pl.ds(start, 8), :]
-        value = value_ref[pl.ds(start, 8), :]
+    high_iota = iota((high_size, 128), 0).astype(F32).astype(BF16)
+    low_iota = iota((low_size, 128), 0).astype(F32).astype(BF16)
+    high_zero = jnp.zeros((high_size, 128), BF16)
+    low_zero = jnp.zeros((low_size, 128), BF16)
+    low_one = jnp.ones((low_size, 128), BF16)
+    total = jnp.zeros((2 * high_size, low_size), F32)
+    for start in range(0, high_ref.shape[0], 8):
+        high = high_ref[start : start + 8, :].astype(F32)
+        low = low_ref[start : start + 8, :].astype(F32)
+        value = value_ref[start : start + 8, :]
         coarse = value.astype(BF16).astype(F32)
         fine = value - coarse
-        row_hot, coarse_hot, fine_hot = [], [], []
+        coarse_hot, fine_hot, low_hot = [], [], []
         for j in range(8):
-            row_hot.append(
-                jnp.where(iota((high_size, 128), 0) == high[j : j + 1], 1.0, 0.0).astype(BF16)
-            )
-            same = iota((low_size, 128), 0) == low[j : j + 1]
-            coarse_hot.append(jnp.where(same, coarse[j : j + 1], 0.0).astype(BF16))
-            fine_hot.append(jnp.where(same, fine[j : j + 1], 0.0).astype(BF16))
-        row_hot = jnp.concatenate(row_hot, axis=1)
+            same = repeated(high[j : j + 1], high_size) == high_iota
+            coarse_hot.append(jnp.where(same, repeated(coarse[j : j + 1], high_size), high_zero))
+            fine_hot.append(jnp.where(same, repeated(fine[j : j + 1], high_size), high_zero))
+            same = repeated(low[j : j + 1], low_size) == low_iota
+            low_hot.append(jnp.where(same, low_one, low_zero))
         value_hot = jnp.concatenate(
             [jnp.concatenate(coarse_hot, axis=1), jnp.concatenate(fine_hot, axis=1)], axis=0
         )
-        return total + lax.dot_general(
-            row_hot, value_hot, (((1,), (1,)), ((), ())), preferred_element_type=F32
-        )
-
-    total = lax.fori_loop(0, rows // 8, step, jnp.zeros((high_size, 2 * low_size), F32))
-    return total
+        total = total + lax.dot_general(
+            value_hot, jnp.concatenate(low_hot, axis=1), (((1,), (1,)), ((), ())),
+            preferred_element_type=F32,
+        )
+    return total[:high_size] + total[high_size:]
 
 
 def cell_place(cell):
@@ -317,7 +326,6 @@
         cell_high[...] >= 0, own_coef * (heads[...] - high_halves(got[:, 0:128])), 0.0
     )
     lost = summed(cell_high, cell_low, value_ref, 128, 128)
-    lost = lost[:, :128] + lost[:, 128:]
     left = surface[:, 0:128] - inverse[:, 0:128] * lost[:64]
     right = surface[:, 128:256] - inverse[:, 128:256] * lost[64:]
     surface_out[:, 0:128] = left
@@ -327,9 +335,8 @@
     zone_value_ref[...] = jnp.where(
         zone_row[...] >= 0, zone_coef * (zone[...] - got[:, 128:256]), 0.0
     )
-    lost = summed(zone_row, zone_col, zone_value_ref, 64, 64)
-    lost = lost[:, :64] + lost[:, 64:]
-    lost = jnp.concatenate([lost, jnp.zeros((64, 64), F32)], axis=1)
+    lost = summed(zone_row, zone_col, zone_value_ref, 64, 2 * ZONE)
+    lost = jnp.concatenate([lost, jnp.zeros((64, 128 - 2 * ZONE), F32)], axis=1)
     lane = iota((64, 128), 1)
     lost = jnp.where(
         lane < ZONE, lost,
@@ -352,7 +359,7 @@
         node_high[...] >= 0, coef[...] * (low_halves(got[:, 0:128]) - nodes[...]), 0.0
     )
     inflow = summed(node_high, node_low, value_ref, 64, 128)
-    balance = table[...] + (inflow[:, :128] + inflow[:, 128:])
+    balance = table[...] + inflow
     start = pl.multiple_of(place_ref[0] * 16, 16)
     for index in range(4):
         ends_ref[index * 16 : index * 16 + 16, :] = got[
@@ -391,7 +398,7 @@
     return jax.ShapeDtypeStruct(dims, dtype)
 
 
-def call(kernel, inputs, outputs, scratch=(), scalars=0, space=pltpu.VMEM, flops=10**9):
+def call(kernel, inputs, outputs, scratch=(), scalars=0, space=pltpu.VMEM, grant=32):
     smem = pl.BlockSpec(memory_space=pltpu.SMEM)
     vmem = pl.BlockSpec(memory_space=pltpu.VMEM)
     return pl.pallas_call(
@@ -400,8 +407,8 @@
         in_specs=[smem] * scalars + [pl.BlockSpec(memory_space=space)] * (len(inputs) - scalars),
         out_specs=[vmem] * len(outputs),
         scratch_shapes=list(scratch),
-        compiler_params=pltpu.CompilerParams(vmem_limit_bytes=32 << 20),
-        cost_estimate=pl.CostEstimate(flops=flops, bytes_accessed=1 << 20, transcendentals=0),
+        compiler_params=pltpu.CompilerParams(vmem_limit_bytes=grant << 20),
+        cost_estimate=pl.CostEstimate(flops=10**9, bytes_accessed=1 << 20, transcendentals=0),
     )(*inputs)
 
 
@@ -428,7 +435,7 @@
     fields, up, down = call(
         start_kernel, (surface_head, conduct_x, conduct_y, porosity, rainfall),
         [shape(5, 64, 256), shape(40, 128), shape(40, 128)],
-        [pltpu.SemaphoreType.DMA((5,))], space=pltpu.HBM,
+        [pltpu.SemaphoreType.DMA((5,))], space=pl.ANY, grant=60,
     )
     above, below = ring(down, "row", 1), ring(up, "row", -1)
     tall, sent = call(

time: 128 us -> 102 us (0.80)
  Pallas kernels: 46 us -> 24.1 us
  local copies, waits for them, and re-layouts: 8.06 us -> 2.56 us
  waiting for transfers between devices: 1.75 us -> 5.93 us
  blocking collectives: 59.9 us -> 58.1 us
    pallas_call x12, Pallas kernels: 46 us -> 24.1 us  [call(): pl.pallas_call(kernel, out_shape=outputs, in_specs=[smem] * scalars + [pl...]
    unnamed x32 -> x24, local copies, waits for them, and re-layouts: 6.63 us -> 1.13 us
    ppermute x8, waiting for transfers between devices: 1.75 us -> 5.93 us  [ring(): lax.ppermute(block, axis, [(i, (i + distance) % size) for i in range(size)])]
    all_to_all x3, blocking collectives: 59.9 us -> 58.1 us  [body(): lax.all_to_all(sent, ('row', 'col'), split_axis=0, concat_axis=0, tiled=T...]
  transfers between devices with their start and end apart: 8 -> 8, of which waited for: 2 -> 5; matrix products, arithmetic and copies ran while one was open for 0% -> 0% of each run, Pallas kernels for 9% -> 5%
where the time goes in v3:
time: 102 us
  blocking collectives  58.1 us (57%)
  Pallas kernels  24.1 us (24%)
  starting transfers between devices  10.6 us (10%)
  waiting for transfers between devices  5.93 us (6%)
  local copies, waits for them, and re-layouts  2.56 us (3%)
    all_to_all x3, blocking collectives, body(): lax.all_to_all(sent, ('row', 'col'), split_axis=0, concat_axis=0, tiled=T...  58.1 us
    pallas_call x12, Pallas kernels, call(): pl.pallas_call(kernel, out_shape=outputs, in_specs=[smem] * scalars + [pl...  24.1 us
    ppermute x8, starting transfers between devices, ring(): lax.ppermute(block, axis, [(i, (i + distance) % size) for i in range(size)])  10.6 us
    ppermute x8, waiting for transfers between devices, ring(): lax.ppermute(block, axis, [(i, (i + distance) % size) for i in range(size)])  5.93 us
  transfers between devices with their start and end apart: 8, of which 5 were waited for; matrix products, arithmetic and copies ran while one was open for 0% of the time, Pallas kernels for 5%

profile of v3, /device:TPU:1, one launch (start us, length us, event | category | flops | bytes accessed | tf_op | source)
XLA Modules:
  0.0 102.2 jit_solution(9169840505672770064)
XLA Ops:
  0.6 0.0 copy-start.7
  0.6 0.0 copy-start.8
  0.7 0.0 copy-start.4
  0.7 0.0 copy-start.5
  0.7 0.0 copy-start.6
  0.7 1.8 %shard_map.140 = (f32[5,64,256]{2,1,0:T(8,128)}, f32[40,128]{1,0:T(8,128)}, f32[40,128]{1,0:T(8,128)}) custom-call(f32[64,256]{1,0:T(8,128)} %surface.1, f32[64,256]{1,0:T(8,128)} %cond_x.1, f32[64,256]{1,0:T(8,128)} %cond_y.1, f32[64,256]{1,0:T(8,128)} %porosity.1, f32[64,256]{1,0:T(8,128)} %rainfall.1), custom_call_target="tpu_custom_call" | custom-call | flops 1000000000 | bytes 1048576 | tf_op jit(solution)/shard_map/pallas_call | solution.py:404
  2.5 0.0 copy-start.3
  2.5 2.6 %collective-permute-start = (f32[40,128]{1,0:T(8,128)}, f32[40,128]{1,0:T(8,128)S(1)}, u32[]{:S(2)}, u32[]{:S(2)}) collective-permute-start(f32[40,128]{1,0:T(8,128)} %get-tuple-element.46), channel_id=1, source_target_pairs={{0,16},{16,32},{32,48},{48,64},{64,80},{80,96},{96,112},{112,0},{1... | collective-permute-start | bytes 61448 | tf_op jit(solution)/shard_map/ppermute | solution.py:417
  5.1 0.0 collective-permute-start.1
  5.1 0.1 pad.2.clone
  5.2 0.0 copy-done.7
  5.2 0.0 copy-done.8
  5.2 0.1 add_add_fusion.meets
  5.3 0.1 pad_add_fusion.place_ref
  5.3 0.0 copy-done.4
  5.3 0.1 copy.18
  5.4 0.0 copy-done.5
  5.4 0.1 copy.19
  5.5 0.0 copy-done.6
  5.5 0.1 copy.20
  5.6 0.6 collective-permute-done.above
  6.2 2.3 %collective-permute-done.1.below = f32[40,128]{1,0:T(8,128)S(1)} collective-permute-done((f32[40,128]{1,0:T(8,128)}, f32[40,128]{1,0:T(8,128)S(1)}, u32[]{:S(2)}, u32[]{:S(2)}) %collective-permute-start.1) | collective-permute-done | bytes 20512 | tf_op jit(solution)/shard_map/ppermute | solution.py:417
  8.5 0.0 copy-done.3
  8.5 0.0 copy-start.1
  8.5 0.7 shard_map.141
  9.2 1.4 %collective-permute-start.2 = (f32[136,128]{1,0:T(8,128)S(1)}, f32[136,128]{1,0:T(8,128)S(1)}, u32[]{:S(2)}, u32[]{:S(2)}) collective-permute-start(f32[136,128]{1,0:T(8,128)S(1)} %get-tuple-element.50), channel_id=1, source_target_pairs={{0,1},{1,2},{2,3},{3,4},{4,5},{5,6},{6,7},{7,8},{8,9},{9,10},{10,1... | collective-permute-start | bytes 208904 | tf_op jit(solution)/shard_map/ppermute | solution.py:417
  10.6 5.0 %collective-permute-start.3 = (f32[136,128]{1,0:T(8,128)S(1)}, f32[136,128]{1,0:T(8,128)S(1)}, u32[]{:S(2)}, u32[]{:S(2)}) collective-permute-start(f32[136,128]{1,0:T(8,128)S(1)} %get-tuple-element.50), channel_id=1, source_target_pairs={{0,15},{1,0},{2,1},{3,2},{4,3},{5,4},{6,5},{7,6},{8,7},{9,8},{10,9... | collective-permute-start | bytes 208904 | tf_op jit(solution)/shard_map/ppermute | solution.py:417
  15.5 0.0 copy-done.1
  15.6 0.7 shard_map.142
  16.3 1.6 %collective-permute-done.2.from_west = f32[136,128]{1,0:T(8,128)S(1)} collective-permute-done((f32[136,128]{1,0:T(8,128)S(1)}, f32[136,128]{1,0:T(8,128)S(1)}, u32[]{:S(2)}, u32[]{:S(2)}) %collective-permute-start.2) | collective-permute-done | bytes 69664 | tf_op jit(solution)/shard_map/ppermute | solution.py:417
  17.9 0.0 collective-permute-done.3.from_east
  17.9 2.7 %shard_map.143 = (f32[6,72,384]{2,1,0:T(8,128)S(1)}, f32[64,384]{1,0:T(8,128)S(1)}, s32[64,128]{1,0:T(8,128)S(1)}, s32[64,128]{1,0:T(8,128)S(1)}, s32[128,128]{1...) custom-call(s32[2]{0:T(128)S(1)} %pad_add_fusion.place_ref, ...), custom_call_target="tpu_custom_call" | custom-call | flops 1000000000 | bytes 1048576 | tf_op jit(solution)/shard_map/pallas_call | solution.py:404
  20.6 0.5 copy.21
  21.2 22.2 %all_to_all.33 = f32[128,1,1024]{2,1,0:T(1,128)S(1)} all-to-all(f32[128,1,1024]{2,1,0:T(1,128)S(1)} %copy.21), channel_id=1, replica_groups=mesh['row'=8,'col'=16] {'row','col'}, dimensions={0} | all-to-all | bytes 1048576 | tf_op jit(solution)/shard_map/all_to_all | solution.py:472
  43.4 0.1 copy.30
  43.5 0.0 copy-start
  43.5 2.4 %shard_map.144 = (f32[64,384]{1,0:T(8,128)S(1)}, f32[12,128]{1,0:T(8,128)S(1)}, f32[12,128]{1,0:T(8,128)S(1)}, f32[64,128]{1,0:T(8,128)S(1)}, f32[128,128]{1,0:T(8,128)S(1)}) custom-call(f32[128,1024]{1,0:T(8,128)S(1)} %bitcast.21, f32[64,384]{1,0:T(8,128)S(1)} %get-tuple-element.56.surface, f32[64,384]{1,0:T(8,128)S(1)} %get-tuple-element.57.inverse, ...), custom_call_target="tpu_custom_call" | custom-call | flops 1000000000 | bytes 1048576 | tf_op jit(solution)/shard_map/pallas_call | solution.py:404
  45.9 0.8 collective-permute-start.4
  46.7 0.0 collective-permute-start.5
  46.7 0.0 copy-start.2
  46.7 0.0 copy-done
  46.7 0.7 copy-done.2
  47.4 2.3 %shard_map.145 = (f32[64,128]{1,0:T(8,128)S(1)}, f32[64,128]{1,0:T(8,128)S(1)}) custom-call(s32[2]{0:T(128)S(1)} %pad_add_fusion.place_ref, f32[128,1024]{1,0:T(8,128)S(1)} %bitcast.22, f32[64,128]{1,0:T(8,128)S(1)} %get-tuple-element.52.nodes, s32[64,128]{1,0:T(8,128)S(1)} %get-tuple-element.68.node_high, s32[64,128]{1,0:T(8,128)S(1)} %get-tuple-element.69.node_low, ...), custom_call_target="tpu_custom_call" | custom-call | flops 1000000000 | bytes 1048576 | tf_op jit(solution)/shard_map/pallas_call | solution.py:404
  49.7 0.0 collective-permute-done.4.above
  49.7 0.4 collective-permute-done.5.below
  50.1 2.5 %shard_map.146 = (f32[64,384]{1,0:T(8,128)S(1)}, f32[64,128]{1,0:T(8,128)S(1)}, f32[128,128]{1,0:T(8,128)S(1)}, f32[128,768]{1,0:T(8,128)S(1)}) custom-call(s32[2]{0:T(128)S(1)} %pad_add_fusion.place_ref, f32[64,384]{1,0:T(8,128)S(1)} %get-tuple-element.64.surface, f32[12,128]{1,0:T(8,128)S(1)} %collective-permute-done.4.above, ...), custom_call_target="tpu_custom_call" | custom-call | flops 1000000000 | bytes 1048576 | tf_op jit(solution)/shard_map/pallas_call | solution.py:404
  52.6 0.4 copy.22
  53.0 18.0 %all_to_all.34 = f32[128,1,768]{2,1,0:T(1,128)S(1)} all-to-all(f32[128,1,768]{2,1,0:T(1,128)S(1)} %copy.22), channel_id=1, replica_groups=mesh['row'=8,'col'=16] {'row','col'}, dimensions={0} | all-to-all | bytes 786432 | tf_op jit(solution)/shard_map/all_to_all | solution.py:472
  71.1 2.4 %shard_map.147 = (f32[64,384]{1,0:T(8,128)S(1)}, f32[12,128]{1,0:T(8,128)S(1)}, f32[12,128]{1,0:T(8,128)S(1)}) custom-call(f32[128,768]{1,0:T(8,128)S(1)} %bitcast.24, f32[64,384]{1,0:T(8,128)S(1)} %get-tuple-element.76.surface, f32[64,384]{1,0:T(8,128)S(1)} %get-tuple-element.57.inverse, f32[64,128]{1,0:T(8,128)S(1)} %get-tuple-element.77.heads, ...), custom_call_target="tpu_custom_call" | custom-call | flops 1000000000 | bytes 1048576 | tf_op jit(solution)/shard_map/pallas_call | solution.py:404
  73.5 0.8 collective-permute-start.6
  74.3 0.0 collective-permute-start.7
  74.3 2.3 %shard_map.148 = (f32[64,128]{1,0:T(8,128)S(1)}, f32[64,128]{1,0:T(8,128)S(1)}) custom-call(s32[2]{0:T(128)S(1)} %pad_add_fusion.place_ref, f32[128,768]{1,0:T(8,128)S(1)} %bitcast.25, f32[64,128]{1,0:T(8,128)S(1)} %get-tuple-element.74.nodes, s32[64,128]{1,0:T(8,128)S(1)} %get-tuple-element.68.node_high, s32[64,128]{1,0:T(8,128)S(1)} %get-tuple-element.69.node_low, ...), custom_call_target="tpu_custom_call" | custom-call | flops 1000000000 | bytes 1048576 | tf_op jit(solution)/shard_map/pallas_call | solution.py:404
  76.6 0.0 collective-permute-done.6.above
  76.6 1.0 %collective-permute-done.7.below = f32[12,128]{1,0:T(8,128)S(1)} collective-permute-done((f32[12,128]{1,0:T(8,128)S(1)}, f32[12,128]{1,0:T(8,128)S(1)}, u32[]{:S(2)}, u32[]{:S(2)}) %collective-permute-start.7) | collective-permute-done | bytes 6176 | tf_op jit(solution)/shard_map/ppermute | solution.py:417
  77.6 2.2 %shard_map.149 = (f32[64,384]{1,0:T(8,128)S(1)}, f32[64,128]{1,0:T(8,128)S(1)}, f32[128,128]{1,0:T(8,128)S(1)}, f32[128,768]{1,0:T(8,128)S(1)}) custom-call(s32[2]{0:T(128)S(1)} %pad_add_fusion.place_ref, f32[64,384]{1,0:T(8,128)S(1)} %get-tuple-element.81.surface, f32[12,128]{1,0:T(8,128)S(1)} %collective-permute-done.6.above, ...), custom_call_target="tpu_custom_call" | custom-call | flops 1000000000 | bytes 1048576 | tf_op jit(solution)/shard_map/pallas_call | solution.py:404
  79.9 0.4 copy.23
  80.3 17.8 %all_to_all.35 = f32[128,1,768]{2,1,0:T(1,128)S(1)} all-to-all(f32[128,1,768]{2,1,0:T(1,128)S(1)} %copy.23), channel_id=1, replica_groups=mesh['row'=8,'col'=16] {'row','col'}, dimensions={0} | all-to-all | bytes 786432 | tf_op jit(solution)/shard_map/all_to_all | solution.py:472
  98.1 2.2 %shard_map.151 = f32[32,256]{1,0:T(8,128)} custom-call(s32[2]{0:T(128)S(1)} %pad_add_fusion.place_ref, f32[128,768]{1,0:T(8,128)S(1)} %bitcast.26, f32[64,128]{1,0:T(8,128)S(1)} %get-tuple-element.85.nodes, s32[64,128]{1,0:T(8,128)S(1)} %get-tuple-element.68.node_high, s32[64,128]{1,0:T(8,128)S(1)} %get-tuple-element.69.node_low, ...), custom_call_target="tpu_custom_call" | custom-call | flops 1000000000 | bytes 1048576 | tf_op jit(solution)/shard_map/pallas_call | solution.py:404
  100.3 1.9 %shard_map.150 = f32[64,256]{1,0:T(8,128)} custom-call(f32[128,768]{1,0:T(8,128)S(1)} %bitcast.27, f32[64,384]{1,0:T(8,128)S(1)} %get-tuple-element.87.surface, f32[64,384]{1,0:T(8,128)S(1)} %get-tuple-element.57.inverse, f32[64,128]{1,0:T(8,128)S(1)} %get-tuple-element.88.heads, f32[128,128]{1,0:T(8,128)S(1)} %get-tuple-element.89.zone, ...), custom_call_target="tpu_custom_call" | custom-call | flops 1000000000 | bytes 1048576 | tf_op jit(solution)/shard_map/pallas_call | solution.py:404
  (3 shorter events, 0.1 us)
Async XLA Ops:
  0.6 4.6 %copy-start.7 = (s32[256]{0:T(256)S(1)}, s32[256]{0:T(256)}, u32[]{:S(2)}) copy-start(s32[256]{0:T(256)} %param.21) | copy-start | bytes 3076
  0.6 4.5 %copy-start.8 = (s32[256]{0:T(256)S(1)}, s32[256]{0:T(256)}, u32[]{:S(2)}) copy-start(s32[256]{0:T(256)} %param.20) | copy-start | bytes 3076
  0.7 4.7 %copy-start.4 = (s32[1,128,64]{1,2,0:T(8,128)S(1)}, s32[1,128,64]{1,2,0:T(8,128)}, u32[]{:S(2)}) copy-start(s32[1,128,64]{1,2,0:T(8,128)} %param.23) | copy-start | bytes 98308
  0.7 4.8 %copy-start.5 = (s32[128,1,64]{0,2,1:T(8,128)S(1)}, s32[128,1,64]{0,2,1:T(8,128)}, u32[]{:S(2)}) copy-start(s32[128,1,64]{0,2,1:T(8,128)} %param.24) | copy-start | bytes 98308
  0.7 4.9 %copy-start.6 = (f32[128,1,64]{0,2,1:T(8,128)S(1)}, f32[128,1,64]{0,2,1:T(8,128)}, u32[]{:S(2)}) copy-start(f32[128,1,64]{0,2,1:T(8,128)} %param.25) | copy-start | bytes 98308
  2.5 6.0 %copy-start.3 = (f32[5,64,256]{2,1,0:T(8,128)S(1)}, f32[5,64,256]{2,1,0:T(8,128)}, u32[]{:S(2)}) copy-start(f32[5,64,256]{2,1,0:T(8,128)} %get-tuple-element.48.fields) | copy-start | bytes 983044
  2.5 3.7 %collective-permute-start = (f32[40,128]{1,0:T(8,128)}, f32[40,128]{1,0:T(8,128)S(1)}, u32[]{:S(2)}, u32[]{:S(2)}) collective-permute-start(f32[40,128]{1,0:T(8,128)} %get-tuple-element.46), channel_id=1, source_target_pairs={{0,16},{16,32},{32,48},{48,64},{64,80},{80,96},{96,112},{112,0},{1... | collective-permute-start | bytes 61448 | tf_op jit(solution)/shard_map/ppermute | solution.py:417
  5.1 3.4 %collective-permute-start.1 = (f32[40,128]{1,0:T(8,128)}, f32[40,128]{1,0:T(8,128)S(1)}, u32[]{:S(2)}, u32[]{:S(2)}) collective-permute-start(f32[40,128]{1,0:T(8,128)} %get-tuple-element.47), channel_id=1, source_target_pairs={{0,112},{16,0},{32,16},{48,32},{64,48},{80,64},{96,80},{112,96},{1... | collective-permute-start | bytes 61448 | tf_op jit(solution)/shard_map/ppermute | solution.py:417
  8.5 7.0 %copy-start.1 = (f32[32,256]{1,0:T(8,128)S(1)}, f32[32,256]{1,0:T(8,128)}, u32[]{:S(2)}) copy-start(f32[32,256]{1,0:T(8,128)} %pipes.1) | copy-start | bytes 98308
  9.2 8.7 %collective-permute-start.2 = (f32[136,128]{1,0:T(8,128)S(1)}, f32[136,128]{1,0:T(8,128)S(1)}, u32[]{:S(2)}, u32[]{:S(2)}) collective-permute-start(f32[136,128]{1,0:T(8,128)S(1)} %get-tuple-element.50), channel_id=1, source_target_pairs={{0,1},{1,2},{2,3},{3,4},{4,5},{5,6},{6,7},{7,8},{8,9},{9,10},{10,1... | collective-permute-start | bytes 208904 | tf_op jit(solution)/shard_map/ppermute | solution.py:417
  10.6 7.3 %collective-permute-start.3 = (f32[136,128]{1,0:T(8,128)S(1)}, f32[136,128]{1,0:T(8,128)S(1)}, u32[]{:S(2)}, u32[]{:S(2)}) collective-permute-start(f32[136,128]{1,0:T(8,128)S(1)} %get-tuple-element.50), channel_id=1, source_target_pairs={{0,15},{1,0},{2,1},{3,2},{4,3},{5,4},{6,5},{7,6},{8,7},{9,8},{10,9... | collective-permute-start | bytes 208904 | tf_op jit(solution)/shard_map/ppermute | solution.py:417
  43.5 3.2 %copy-start = (f32[4,32,32]{2,1,0:T(8,128)S(1)}, f32[4,32,32]{2,1,0:T(8,128)}, u32[]{:S(2)}) copy-start(f32[4,32,32]{2,1,0:T(8,128)} %param.22) | copy-start | bytes 49156
  45.9 3.8 %collective-permute-start.4 = (f32[12,128]{1,0:T(8,128)S(1)}, f32[12,128]{1,0:T(8,128)S(1)}, u32[]{:S(2)}, u32[]{:S(2)}) collective-permute-start(f32[12,128]{1,0:T(8,128)S(1)} %get-tuple-element.65), channel_id=1, source_target_pairs={{0,16},{16,32},{32,48},{48,64},{64,80},{80,96},{96,112},{112,0},{1... | collective-permute-start | bytes 18440 | tf_op jit(solution)/shard_map/ppermute | solution.py:417
  46.7 3.4 %collective-permute-start.5 = (f32[12,128]{1,0:T(8,128)S(1)}, f32[12,128]{1,0:T(8,128)S(1)}, u32[]{:S(2)}, u32[]{:S(2)}) collective-permute-start(f32[12,128]{1,0:T(8,128)S(1)} %get-tuple-element.66), channel_id=1, source_target_pairs={{0,112},{16,0},{32,16},{48,32},{64,48},{80,64},{96,80},{112,96},{1... | collective-permute-start | bytes 18440 | tf_op jit(solution)/shard_map/ppermute | solution.py:417
  46.7 0.7 copy-start.2
  73.5 3.1 %collective-permute-start.6 = (f32[12,128]{1,0:T(8,128)S(1)}, f32[12,128]{1,0:T(8,128)S(1)}, u32[]{:S(2)}, u32[]{:S(2)}) collective-permute-start(f32[12,128]{1,0:T(8,128)S(1)} %get-tuple-element.82), channel_id=1, source_target_pairs={{0,16},{16,32},{32,48},{48,64},{64,80},{80,96},{96,112},{112,0},{1... | collective-permute-start | bytes 18440 | tf_op jit(solution)/shard_map/ppermute | solution.py:417
  74.3 3.4 %collective-permute-start.7 = (f32[12,128]{1,0:T(8,128)S(1)}, f32[12,128]{1,0:T(8,128)S(1)}, u32[]{:S(2)}, u32[]{:S(2)}) collective-permute-start(f32[12,128]{1,0:T(8,128)S(1)} %get-tuple-element.83), channel_id=1, source_target_pairs={{0,112},{16,0},{32,16},{48,32},{64,48},{80,64},{96,80},{112,96},{1... | collective-permute-start | bytes 18440 | tf_op jit(solution)/shard_map/ppermute | solution.py:417

commit v4 on v3

--- a/solution.py
+++ b/solution.py
@@ -169,8 +169,11 @@
 
 
 def owner_start_kernel(
-    pipes, link_node, link_coef, table, nodes, node_high, node_low, coef
-):
+    pipes, link_node, link_coef, kinds, laws, table, nodes, node_high, node_low, coef, classes,
+    matrices,
+):
+    classes[...] = kinds[...]
+    matrices[...] = laws[...]
     table[...] = pipe_table(pipes[...])
     high, low = node_place(packed(link_node[...]))
     node_high[...] = high
@@ -195,12 +198,19 @@
     return state
 
 
-def build_message(out, heads, nodes, table):
-    out[:, 0:128] = paired(heads, nodes)
-    out[:, 128:256] = beside(nodes)
+def put(out, blocks, index, value):
+    out[pl.ds(index, 128, stride=blocks), :] = value
+
+
+def taken(got, blocks, index):
+    return got[pl.ds(index, 128, stride=blocks), :]
+
+
+def build_message(out, blocks, heads, nodes, table):
+    put(out, blocks, 0, paired(heads, nodes))
+    put(out, blocks, 1, beside(nodes))
     for index, row in enumerate(ENDS):
-        block = jnp.broadcast_to(table[row : row + 1, :], (128, 128))
-        out[:, 256 + index * 128 : 384 + index * 128] = block
+        put(out, blocks, 2 + index, jnp.broadcast_to(table[row : row + 1, :], (128, 128)))
 
 
 def zone_heads(edge, zone_place, edge_ref, zone_ref):
@@ -278,9 +288,9 @@
         state, gains, high, low, (zone_row, zone_col), surface_out, heads_out, zone_out,
         cell_table, edge_ref, zone_ref,
     )
-    build_message(out, heads, nodes[...], table)
-    out[:, 768:896] = paired(coef[...], coef[...])
-    out[:, 896:1024] = beside(coef[...])
+    build_message(out, 8, heads, nodes[...], table)
+    put(out, 8, 6, paired(coef[...], coef[...]))
+    put(out, 8, 7, beside(coef[...]))
 
 
 def sweep_kernel(
@@ -302,16 +312,17 @@
         state, gains, cell_high[...], cell_low[...], zone_place, surface_out, heads_out, zone_out,
         cell_table, edge_ref, zone_ref,
     )
-    build_message(out, heads, nodes[...], table)
+    build_message(out, 6, heads, nodes[...], table)
 
 
 def tile_kernel(
     first, last, got, surface, inverse, heads, zone, cell_high, cell_low, zone_row, zone_col, *rest
 ):
     rest = list(rest)
+    blocks = 8 if first else 6
     if first:
-        own_coef = low_halves(got[:, 768:896])
-        zone_coef = got[:, 896:1024]
+        own_coef = low_halves(taken(got, blocks, 6))
+        zone_coef = taken(got, blocks, 7)
     else:
         own_coef = rest.pop(0)[...]
         zone_coef = rest.pop(0)[...]
@@ -323,7 +334,7 @@
         rest.pop(0)[...] = zone_coef
     value_ref, zone_value_ref = rest
     value_ref[...] = jnp.where(
-        cell_high[...] >= 0, own_coef * (heads[...] - high_halves(got[:, 0:128])), 0.0
+        cell_high[...] >= 0, own_coef * (heads[...] - high_halves(taken(got, blocks, 0))), 0.0
     )
     lost = summed(cell_high, cell_low, value_ref, 128, 128)
     left = surface[:, 0:128] - inverse[:, 0:128] * lost[:64]
@@ -333,7 +344,7 @@
     if last:
         return
     zone_value_ref[...] = jnp.where(
-        zone_row[...] >= 0, zone_coef * (zone[...] - got[:, 128:256]), 0.0
+        zone_row[...] >= 0, zone_coef * (zone[...] - taken(got, blocks, 1)), 0.0
     )
     lost = summed(zone_row, zone_col, zone_value_ref, 64, 2 * ZONE)
     lost = jnp.concatenate([lost, jnp.zeros((64, 128 - 2 * ZONE), F32)], axis=1)
@@ -349,21 +360,22 @@
 
 
 def owner_kernel(
-    last, place_ref, got, nodes, node_high, node_low, coef, table, meets, classes, matrices, *rest
-):
+    first, last, place_ref, got, nodes, node_high, node_low, coef, table, meets, classes, matrices, *rest
+):
+    blocks = 8 if first else 6
     if last:
         pipes_out, value_ref, ends_ref = rest
     else:
         table_out, nodes_out, value_ref, ends_ref = rest
     value_ref[...] = jnp.where(
-        node_high[...] >= 0, coef[...] * (low_halves(got[:, 0:128]) - nodes[...]), 0.0
+        node_high[...] >= 0, coef[...] * (low_halves(taken(got, blocks, 0)) - nodes[...]), 0.0
     )
     inflow = summed(node_high, node_low, value_ref, 64, 128)
     balance = table[...] + inflow
-    start = pl.multiple_of(place_ref[0] * 16, 16)
+    start = pl.multiple_of(place_ref[0] * 16 * blocks, 32)
     for index in range(4):
         ends_ref[index * 16 : index * 16 + 16, :] = got[
-            pl.ds(start, 16), 256 + index * 128 : 384 + index * 128
+            pl.ds(start + 2 + index, 16, stride=blocks), :
         ]
     meet = meets[...]
     meet_high = jnp.bitwise_and(meet >> 7, 1) * 16 + (meet >> 8)
@@ -394,6 +406,21 @@
     nodes_out[...] = gathered(table_out, 64, node_high[...], node_low[...])
 
 
+def final_kernel(
+    place_ref, got, surface, inverse, heads, zone, cell_high, cell_low, zone_row, zone_col, own_coef,
+    zone_coef, nodes, node_high, node_low, coef, table, meets, classes, matrices, surface_out,
+    pipes_out, cell_value_ref, zone_value_ref, node_value_ref, ends_ref,
+):
+    owner_kernel(
+        False, True, place_ref, got, nodes, node_high, node_low, coef, table, meets, classes,
+        matrices, pipes_out, node_value_ref, ends_ref,
+    )
+    tile_kernel(
+        False, True, got, surface, inverse, heads, zone, cell_high, cell_low, zone_row, zone_col,
+        own_coef, zone_coef, surface_out, cell_value_ref, zone_value_ref,
+    )
+
+
 def shape(*dims, dtype=F32):
     return jax.ShapeDtypeStruct(dims, dtype)
 
@@ -443,9 +470,10 @@
         [shape(5, 72, 256), shape(136, 128)], scalars=1,
     )
     from_west, from_east = ring(sent, "col", 1), ring(sent, "col", -1)
-    table, nodes, node_high, node_low, coef = call(
-        owner_start_kernel, (pipe_head, link_node, link_coef),
-        [shape(64, 128), shape(64, 128), ints(64, 128), ints(64, 128), shape(64, 128)],
+    table, nodes, node_high, node_low, coef, classes, matrices = call(
+        owner_start_kernel, (pipe_head, link_node, link_coef, classes, matrices),
+        [shape(64, 128), shape(64, 128), ints(64, 128), ints(64, 128), shape(64, 128),
+         ints(2, 128), shape(128, 32)],
     )
     gather_scratch = [
         pltpu.VMEM((128, 128), F32), pltpu.VMEM((64, 128), F32), pltpu.VMEM((8, 128), F32)
@@ -455,10 +483,10 @@
         first_sweep_kernel,
         (place, tall, from_west, from_east, link_cell, table, nodes, coef),
         [shape(6, 72, 384), shape(64, 384), ints(64, 128), ints(64, 128), ints(128, 128),
-         ints(128, 128), *swept_shapes, shape(128, 1024)],
+         ints(128, 128), *swept_shapes, shape(1024, 128)],
         gather_scratch, scalars=1,
     )
-    sent, meets, classes, matrices = lax.optimization_barrier((sent, meets, classes, matrices))
+    sent, meets = lax.optimization_barrier((sent, meets))
     coefs = ()
     for step in range(STEPS):
         first, last = step == 0, step == STEPS - 1
@@ -467,31 +495,33 @@
                 functools.partial(sweep_kernel, last),
                 (place, surface, above, below, gains, cell_high, cell_low, zone_row, zone_col,
                  table, nodes),
-                [*swept_shapes, shape(128, 768)], gather_scratch, scalars=1,
+                [*swept_shapes, shape(768, 128)], gather_scratch, scalars=1,
             )
-        got = lax.all_to_all(sent, ("row", "col"), split_axis=0, concat_axis=0, tiled=True)
-        outputs = [shape(64, 256)] if last else [shape(64, 384), shape(12, 128), shape(12, 128)]
+        got = lax.all_to_all(
+            sent.reshape(128, 1, -1), ("row", "col"), split_axis=0, concat_axis=0, tiled=True
+        ).reshape(-1, 128)
+        tile_inputs = (surface, inverse, heads, zone, cell_high, cell_low, zone_row, zone_col, *coefs)
+        owner_inputs = (nodes, node_high, node_low, coef, table, meets, classes, matrices)
+        tile_scratch = [pltpu.VMEM((64, 128), F32), pltpu.VMEM((128, 128), F32)]
+        owner_scratch = [pltpu.VMEM((64, 128), F32), pltpu.VMEM((64, 128), F32)]
+        if last:
+            return tuple(call(
+                final_kernel, (place, got, *tile_inputs, *owner_inputs),
+                [shape(64, 256), shape(32, 256)], tile_scratch + owner_scratch, scalars=1,
+            ))
+        outputs = [shape(64, 384), shape(12, 128), shape(12, 128)]
         if first:
             outputs += [shape(64, 128), shape(128, 128)]
-        tile = call(
-            functools.partial(tile_kernel, first, last),
-            (got, surface, inverse, heads, zone, cell_high, cell_low, zone_row, zone_col, *coefs),
-            outputs, [pltpu.VMEM((64, 128), F32), pltpu.VMEM((128, 128), F32)],
-        )
-        if not last:
-            above, below = ring(tile[2], "row", 1), ring(tile[1], "row", -1)
-        owner = call(
-            functools.partial(owner_kernel, last),
-            (place, got, nodes, node_high, node_low, coef, table, meets, classes, matrices),
-            [shape(32, 256)] if last else [shape(64, 128), shape(64, 128)],
-            [pltpu.VMEM((64, 128), F32), pltpu.VMEM((64, 128), F32)], scalars=1,
-        )
-        if last:
-            return tile[0], owner[0]
-        surface = tile[0]
-        table, nodes = owner
+        surface, up, down, *new_coefs = call(
+            functools.partial(tile_kernel, first, False), (got, *tile_inputs), outputs, tile_scratch
+        )
+        above, below = ring(down, "row", 1), ring(up, "row", -1)
+        table, nodes = call(
+            functools.partial(owner_kernel, first, False), (place, got, *owner_inputs),
+            [shape(64, 128), shape(64, 128)], owner_scratch, scalars=1,
+        )
         if first:
-            coefs = tuple(tile[3:])
+            coefs = tuple(new_coefs)
 
 
 def solution(mesh):

time: 102 us -> 99.9 us (0.979)
  local copies, waits for them, and re-layouts: 2.56 us -> 1.06 us
    all_to_all x3 -> x0, local copies, waits for them, and re-layouts: 1.35 us -> none  [body(): lax.all_to_all(sent, ('row', 'col'), split_axis=0, concat_axis=0, tiled=T...]
    pallas_call x12 -> x11, Pallas kernels: 24.1 us -> 23.3 us  [call(): pl.pallas_call(kernel, out_shape=outputs, in_specs=[smem] * scalars + [pl...]
where the time goes in v4:
time: 99.9 us; the launch traced here: 99.7 us
  blocking collectives  57.8 us (58%)
  Pallas kernels  23.3 us (23%)
  starting transfers between devices  10.6 us (11%)
  waiting for transfers between devices  5.93 us (6%)
  local copies, waits for them, and re-layouts  1.06 us (1%)
    all_to_all x3, blocking collectives, body(): lax.all_to_all(sent.reshape(128, 1, -1), ('row', 'col'), split_axis=0, co...  57.8 us
    pallas_call x11, Pallas kernels, call(): pl.pallas_call(kernel, out_shape=outputs, in_specs=[smem] * scalars + [pl...  23.3 us
    ppermute x8, starting transfers between devices, ring(): lax.ppermute(block, axis, [(i, (i + distance) % size) for i in range(size)])  10.6 us
    ppermute x8, waiting for transfers between devices, ring(): lax.ppermute(block, axis, [(i, (i + distance) % size) for i in range(size)])  5.93 us
  transfers between devices with their start and end apart: 8, of which 5 were waited for; matrix products, arithmetic and copies ran while one was open for 0% of the time, Pallas kernels for 5%

profile of v4, /device:TPU:1, one launch (start us, length us, event | category | flops | bytes accessed | tf_op | source)
XLA Modules:
  0.0 99.7 jit_solution(8273718513118081574)
XLA Ops:
  0.6 0.0 copy-start.7
  0.6 0.0 copy-start.8
  0.7 0.0 copy-start.4
  0.7 0.0 copy-start.5
  0.7 0.0 copy-start.6
  0.7 1.8 %shard_map.140 = (f32[5,64,256]{2,1,0:T(8,128)}, f32[40,128]{1,0:T(8,128)}, f32[40,128]{1,0:T(8,128)}) custom-call(f32[64,256]{1,0:T(8,128)} %surface.1, f32[64,256]{1,0:T(8,128)} %cond_x.1, f32[64,256]{1,0:T(8,128)} %cond_y.1, f32[64,256]{1,0:T(8,128)} %porosity.1, f32[64,256]{1,0:T(8,128)} %rainfall.1), custom_call_target="tpu_custom_call" | custom-call | flops 1000000000 | bytes 1048576 | tf_op jit(solution)/shard_map/pallas_call | solution.py:431
  2.5 0.0 copy-start.3
  2.5 2.6 %collective-permute-start = (f32[40,128]{1,0:T(8,128)}, f32[40,128]{1,0:T(8,128)S(1)}, u32[]{:S(2)}, u32[]{:S(2)}) collective-permute-start(f32[40,128]{1,0:T(8,128)} %get-tuple-element.46), channel_id=1, source_target_pairs={{0,16},{16,32},{32,48},{48,64},{64,80},{80,96},{96,112},{112,0},{1... | collective-permute-start | bytes 61448 | tf_op jit(solution)/shard_map/ppermute | solution.py:444
  5.1 0.0 collective-permute-start.1
  5.1 0.1 pad.2.clone
  5.2 0.0 copy-done.7
  5.2 0.0 copy-done.8
  5.2 0.1 add_add_fusion.meets
  5.3 0.1 pad_add_fusion.place_ref
  5.3 0.0 copy-done.4
  5.3 0.1 copy.18
  5.4 0.0 copy-done.5
  5.4 0.1 copy.19
  5.5 0.0 copy-done.6
  5.5 0.1 copy.20
  5.6 0.6 collective-permute-done.above
  6.2 2.3 %collective-permute-done.1.below = f32[40,128]{1,0:T(8,128)S(1)} collective-permute-done((f32[40,128]{1,0:T(8,128)}, f32[40,128]{1,0:T(8,128)S(1)}, u32[]{:S(2)}, u32[]{:S(2)}) %collective-permute-start.1) | collective-permute-done | bytes 20512 | tf_op jit(solution)/shard_map/ppermute | solution.py:444
  8.5 0.0 copy-done.3
  8.5 0.0 copy-start
  8.5 0.0 copy-start.1
  8.5 0.7 shard_map.141
  9.2 1.4 %collective-permute-start.2 = (f32[136,128]{1,0:T(8,128)S(1)}, f32[136,128]{1,0:T(8,128)S(1)}, u32[]{:S(2)}, u32[]{:S(2)}) collective-permute-start(f32[136,128]{1,0:T(8,128)S(1)} %get-tuple-element.50), channel_id=1, source_target_pairs={{0,1},{1,2},{2,3},{3,4},{4,5},{5,6},{6,7},{7,8},{8,9},{9,10},{10,1... | collective-permute-start | bytes 208904 | tf_op jit(solution)/shard_map/ppermute | solution.py:444
  10.6 5.0 %collective-permute-start.3 = (f32[136,128]{1,0:T(8,128)S(1)}, f32[136,128]{1,0:T(8,128)S(1)}, u32[]{:S(2)}, u32[]{:S(2)}) collective-permute-start(f32[136,128]{1,0:T(8,128)S(1)} %get-tuple-element.50), channel_id=1, source_target_pairs={{0,15},{1,0},{2,1},{3,2},{4,3},{5,4},{6,5},{7,6},{8,7},{9,8},{10,9... | collective-permute-start | bytes 208904 | tf_op jit(solution)/shard_map/ppermute | solution.py:444
  15.6 0.0 copy-start.2
  15.6 0.0 copy-done
  15.6 0.0 copy-done.1
  15.6 0.7 copy-done.2
  16.2 0.7 shard_map.142
  16.9 1.0 collective-permute-done.2.from_west
  17.9 0.0 collective-permute-done.3.from_east
  17.9 2.8 %shard_map.143 = (f32[6,72,384]{2,1,0:T(8,128)S(1)}, f32[64,384]{1,0:T(8,128)S(1)}, s32[64,128]{1,0:T(8,128)S(1)}, s32[64,128]{1,0:T(8,128)S(1)}, s32[128,128]{1...) custom-call(s32[2]{0:T(128)S(1)} %pad_add_fusion.place_ref, ...), custom_call_target="tpu_custom_call" | custom-call | flops 1000000000 | bytes 1048576 | tf_op jit(solution)/shard_map/pallas_call | solution.py:431
  20.7 22.2 %all_to_all.15 = f32[128,1,1024]{2,1,0:T(1,128)S(1)} all-to-all(f32[128,1,1024]{2,1,0:T(1,128)S(1)} %bitcast.17), channel_id=1, replica_groups=mesh['row'=8,'col'=16] {'row','col'}, dimensions={0} | all-to-all | bytes 1048576 | tf_op jit(solution)/shard_map/all_to_all | solution.py:500
  42.9 2.4 %shard_map.144 = (f32[64,384]{1,0:T(8,128)S(1)}, f32[12,128]{1,0:T(8,128)S(1)}, f32[12,128]{1,0:T(8,128)S(1)}, f32[64,128]{1,0:T(8,128)S(1)}, f32[128,128]{1,0:T(8,128)S(1)}) custom-call(f32[1024,128]{1,0:T(8,128)S(1)} %bitcast.15, f32[64,384]{1,0:T(8,128)S(1)} %get-tuple-element.56.surface, f32[64,384]{1,0:T(8,128)S(1)} %get-tuple-element.57.inverse, ...), custom_call_target="tpu_custom_call" | custom-call | flops 1000000000 | bytes 1048576 | tf_op jit(solution)/shard_map/pallas_call | solution.py:431
  45.3 0.8 collective-permute-start.4
  46.1 0.0 collective-permute-start.5
  46.1 2.3 %shard_map.145 = (f32[64,128]{1,0:T(8,128)S(1)}, f32[64,128]{1,0:T(8,128)S(1)}) custom-call(s32[2]{0:T(128)S(1)} %pad_add_fusion.place_ref, f32[1024,128]{1,0:T(8,128)S(1)} %bitcast.16, f32[64,128]{1,0:T(8,128)S(1)} %get-tuple-element.52.nodes, s32[64,128]{1,0:T(8,128)S(1)} %get-tuple-element.68.node_high, s32[64,128]{1,0:T(8,128)S(1)} %get-tuple-element.69.node_low, ...), custom_call_target="tpu_custom_call" | custom-call | flops 1000000000 | bytes 1048576 | tf_op jit(solution)/shard_map/pallas_call | solution.py:431
  48.4 0.0 collective-permute-done.4.above
  48.4 1.0 %collective-permute-done.5.below = f32[12,128]{1,0:T(8,128)S(1)} collective-permute-done((f32[12,128]{1,0:T(8,128)S(1)}, f32[12,128]{1,0:T(8,128)S(1)}, u32[]{:S(2)}, u32[]{:S(2)}) %collective-permute-start.5) | collective-permute-done | bytes 6176 | tf_op jit(solution)/shard_map/ppermute | solution.py:444
  49.5 2.5 %shard_map.146 = (f32[64,384]{1,0:T(8,128)S(1)}, f32[64,128]{1,0:T(8,128)S(1)}, f32[128,128]{1,0:T(8,128)S(1)}, f32[768,128]{1,0:T(8,128)S(1)}) custom-call(s32[2]{0:T(128)S(1)} %pad_add_fusion.place_ref, f32[64,384]{1,0:T(8,128)S(1)} %get-tuple-element.64.surface, f32[12,128]{1,0:T(8,128)S(1)} %collective-permute-done.4.above, ...), custom_call_target="tpu_custom_call" | custom-call | flops 1000000000 | bytes 1048576 | tf_op jit(solution)/shard_map/pallas_call | solution.py:431
  52.0 17.8 %all_to_all.16 = f32[128,1,768]{2,1,0:T(1,128)S(1)} all-to-all(f32[128,1,768]{2,1,0:T(1,128)S(1)} %bitcast.22), channel_id=1, replica_groups=mesh['row'=8,'col'=16] {'row','col'}, dimensions={0} | all-to-all | bytes 786432 | tf_op jit(solution)/shard_map/all_to_all | solution.py:500
  69.8 2.4 %shard_map.147 = (f32[64,384]{1,0:T(8,128)S(1)}, f32[12,128]{1,0:T(8,128)S(1)}, f32[12,128]{1,0:T(8,128)S(1)}) custom-call(f32[768,128]{1,0:T(8,128)S(1)} %bitcast.19, f32[64,384]{1,0:T(8,128)S(1)} %get-tuple-element.76.surface, f32[64,384]{1,0:T(8,128)S(1)} %get-tuple-element.57.inverse, f32[64,128]{1,0:T(8,128)S(1)} %get-tuple-element.77.heads, ...), custom_call_target="tpu_custom_call" | custom-call | flops 1000000000 | bytes 1048576 | tf_op jit(solution)/shard_map/pallas_call | solution.py:431
  72.2 0.8 collective-permute-start.6
  73.0 0.0 collective-permute-start.7
  73.0 2.3 %shard_map.148 = (f32[64,128]{1,0:T(8,128)S(1)}, f32[64,128]{1,0:T(8,128)S(1)}) custom-call(s32[2]{0:T(128)S(1)} %pad_add_fusion.place_ref, f32[768,128]{1,0:T(8,128)S(1)} %bitcast.20, f32[64,128]{1,0:T(8,128)S(1)} %get-tuple-element.74.nodes, s32[64,128]{1,0:T(8,128)S(1)} %get-tuple-element.68.node_high, s32[64,128]{1,0:T(8,128)S(1)} %get-tuple-element.69.node_low, ...), custom_call_target="tpu_custom_call" | custom-call | flops 1000000000 | bytes 1048576 | tf_op jit(solution)/shard_map/pallas_call | solution.py:431
  75.3 0.0 collective-permute-done.6.above
  75.3 1.0 %collective-permute-done.7.below = f32[12,128]{1,0:T(8,128)S(1)} collective-permute-done((f32[12,128]{1,0:T(8,128)S(1)}, f32[12,128]{1,0:T(8,128)S(1)}, u32[]{:S(2)}, u32[]{:S(2)}) %collective-permute-start.7) | collective-permute-done | bytes 6176 | tf_op jit(solution)/shard_map/ppermute | solution.py:444
  76.3 2.2 %shard_map.149 = (f32[64,384]{1,0:T(8,128)S(1)}, f32[64,128]{1,0:T(8,128)S(1)}, f32[128,128]{1,0:T(8,128)S(1)}, f32[768,128]{1,0:T(8,128)S(1)}) custom-call(s32[2]{0:T(128)S(1)} %pad_add_fusion.place_ref, f32[64,384]{1,0:T(8,128)S(1)} %get-tuple-element.81.surface, f32[12,128]{1,0:T(8,128)S(1)} %collective-permute-done.6.above, ...), custom_call_target="tpu_custom_call" | custom-call | flops 1000000000 | bytes 1048576 | tf_op jit(solution)/shard_map/pallas_call | solution.py:431
  78.6 17.8 %all_to_all.17 = f32[128,1,768]{2,1,0:T(1,128)S(1)} all-to-all(f32[128,1,768]{2,1,0:T(1,128)S(1)} %bitcast.21), channel_id=1, replica_groups=mesh['row'=8,'col'=16] {'row','col'}, dimensions={0} | all-to-all | bytes 786432 | tf_op jit(solution)/shard_map/all_to_all | solution.py:500
  96.3 3.3 %shard_map.150 = (f32[64,256]{1,0:T(8,128)}, f32[32,256]{1,0:T(8,128)}) custom-call(s32[2]{0:T(128)S(1)} %pad_add_fusion.place_ref, f32[768,128]{1,0:T(8,128)S(1)} %bitcast.18, f32[64,384]{1,0:T(8,128)S(1)} %get-tuple-element.87.surface, f32[64,384]{1,0:T(8,128)S(1)} %get-tuple-element.57.inverse, f32[64,128]{1,0:T(8,128)S(1)} %get-tuple-element.88.heads, ...), custom_call_target="tpu_custom_call" | custom-call | flops 1000000000 | bytes 1048576 | tf_op jit(solution)/shard_map/pallas_call | solution.py:431
  (1 shorter events, 0.0 us)
Async XLA Ops:
  0.6 4.6 %copy-start.7 = (s32[256]{0:T(256)S(1)}, s32[256]{0:T(256)}, u32[]{:S(2)}) copy-start(s32[256]{0:T(256)} %param.21) | copy-start | bytes 3076
  0.6 4.5 %copy-start.8 = (s32[256]{0:T(256)S(1)}, s32[256]{0:T(256)}, u32[]{:S(2)}) copy-start(s32[256]{0:T(256)} %param.20) | copy-start | bytes 3076
  0.7 4.7 %copy-start.4 = (s32[1,128,64]{1,2,0:T(8,128)S(1)}, s32[1,128,64]{1,2,0:T(8,128)}, u32[]{:S(2)}) copy-start(s32[1,128,64]{1,2,0:T(8,128)} %param.23) | copy-start | bytes 98308
  0.7 4.8 %copy-start.5 = (s32[128,1,64]{0,2,1:T(8,128)S(1)}, s32[128,1,64]{0,2,1:T(8,128)}, u32[]{:S(2)}) copy-start(s32[128,1,64]{0,2,1:T(8,128)} %param.24) | copy-start | bytes 98308
  0.7 4.9 %copy-start.6 = (f32[128,1,64]{0,2,1:T(8,128)S(1)}, f32[128,1,64]{0,2,1:T(8,128)}, u32[]{:S(2)}) copy-start(f32[128,1,64]{0,2,1:T(8,128)} %param.25) | copy-start | bytes 98308
  2.5 6.0 %copy-start.3 = (f32[5,64,256]{2,1,0:T(8,128)S(1)}, f32[5,64,256]{2,1,0:T(8,128)}, u32[]{:S(2)}) copy-start(f32[5,64,256]{2,1,0:T(8,128)} %get-tuple-element.48.fields) | copy-start | bytes 983044
  2.5 3.7 %collective-permute-start = (f32[40,128]{1,0:T(8,128)}, f32[40,128]{1,0:T(8,128)S(1)}, u32[]{:S(2)}, u32[]{:S(2)}) collective-permute-start(f32[40,128]{1,0:T(8,128)} %get-tuple-element.46), channel_id=1, source_target_pairs={{0,16},{16,32},{32,48},{48,64},{64,80},{80,96},{96,112},{112,0},{1... | collective-permute-start | bytes 61448 | tf_op jit(solution)/shard_map/ppermute | solution.py:444
  5.1 3.4 %collective-permute-start.1 = (f32[40,128]{1,0:T(8,128)}, f32[40,128]{1,0:T(8,128)S(1)}, u32[]{:S(2)}, u32[]{:S(2)}) collective-permute-start(f32[40,128]{1,0:T(8,128)} %get-tuple-element.47), channel_id=1, source_target_pairs={{0,112},{16,0},{32,16},{48,32},{64,48},{80,64},{96,80},{112,96},{1... | collective-permute-start | bytes 61448 | tf_op jit(solution)/shard_map/ppermute | solution.py:444
  8.5 7.0 %copy-start = (f32[4,32,32]{2,1,0:T(8,128)S(1)}, f32[4,32,32]{2,1,0:T(8,128)}, u32[]{:S(2)}) copy-start(f32[4,32,32]{2,1,0:T(8,128)} %param.22) | copy-start | bytes 49156
  8.5 7.0 %copy-start.1 = (f32[32,256]{1,0:T(8,128)S(1)}, f32[32,256]{1,0:T(8,128)}, u32[]{:S(2)}) copy-start(f32[32,256]{1,0:T(8,128)} %pipes.1) | copy-start | bytes 98308
  9.2 8.7 %collective-permute-start.2 = (f32[136,128]{1,0:T(8,128)S(1)}, f32[136,128]{1,0:T(8,128)S(1)}, u32[]{:S(2)}, u32[]{:S(2)}) collective-permute-start(f32[136,128]{1,0:T(8,128)S(1)} %get-tuple-element.50), channel_id=1, source_target_pairs={{0,1},{1,2},{2,3},{3,4},{4,5},{5,6},{6,7},{7,8},{8,9},{9,10},{10,1... | collective-permute-start | bytes 208904 | tf_op jit(solution)/shard_map/ppermute | solution.py:444
  10.6 7.3 %collective-permute-start.3 = (f32[136,128]{1,0:T(8,128)S(1)}, f32[136,128]{1,0:T(8,128)S(1)}, u32[]{:S(2)}, u32[]{:S(2)}) collective-permute-start(f32[136,128]{1,0:T(8,128)S(1)} %get-tuple-element.50), channel_id=1, source_target_pairs={{0,15},{1,0},{2,1},{3,2},{4,3},{5,4},{6,5},{7,6},{8,7},{9,8},{10,9... | collective-permute-start | bytes 208904 | tf_op jit(solution)/shard_map/ppermute | solution.py:444
  15.6 0.7 copy-start.2
  45.3 3.2 %collective-permute-start.4 = (f32[12,128]{1,0:T(8,128)S(1)}, f32[12,128]{1,0:T(8,128)S(1)}, u32[]{:S(2)}, u32[]{:S(2)}) collective-permute-start(f32[12,128]{1,0:T(8,128)S(1)} %get-tuple-element.65), channel_id=1, source_target_pairs={{0,16},{16,32},{32,48},{48,64},{64,80},{80,96},{96,112},{112,0},{1... | collective-permute-start | bytes 18440 | tf_op jit(solution)/shard_map/ppermute | solution.py:444
  46.1 3.4 %collective-permute-start.5 = (f32[12,128]{1,0:T(8,128)S(1)}, f32[12,128]{1,0:T(8,128)S(1)}, u32[]{:S(2)}, u32[]{:S(2)}) collective-permute-start(f32[12,128]{1,0:T(8,128)S(1)} %get-tuple-element.66), channel_id=1, source_target_pairs={{0,112},{16,0},{32,16},{48,32},{64,48},{80,64},{96,80},{112,96},{1... | collective-permute-start | bytes 18440 | tf_op jit(solution)/shard_map/ppermute | solution.py:444
  72.2 3.1 %collective-permute-start.6 = (f32[12,128]{1,0:T(8,128)S(1)}, f32[12,128]{1,0:T(8,128)S(1)}, u32[]{:S(2)}, u32[]{:S(2)}) collective-permute-start(f32[12,128]{1,0:T(8,128)S(1)} %get-tuple-element.82), channel_id=1, source_target_pairs={{0,16},{16,32},{32,48},{48,64},{64,80},{80,96},{96,112},{112,0},{1... | collective-permute-start | bytes 18440 | tf_op jit(solution)/shard_map/ppermute | solution.py:444
  73.0 3.4 %collective-permute-start.7 = (f32[12,128]{1,0:T(8,128)S(1)}, f32[12,128]{1,0:T(8,128)S(1)}, u32[]{:S(2)}, u32[]{:S(2)}) collective-permute-start(f32[12,128]{1,0:T(8,128)S(1)} %get-tuple-element.83), channel_id=1, source_target_pairs={{0,112},{16,0},{32,16},{48,32},{64,48},{80,64},{96,80},{112,96},{1... | collective-permute-start | bytes 18440 | tf_op jit(solution)/shard_map/ppermute | solution.py:444

commit v5 on v4

--- a/solution.py
+++ b/solution.py
@@ -123,11 +123,18 @@
     return jnp.concatenate([block[start : start + HALO_ROWS] for block in blocks], axis=0)
 
 
-def start_kernel(surface, cond_x, cond_y, porosity, rainfall, fields, up, down, arrived):
+def even(place_ref, dim):
+    return jnp.bitwise_and(place_ref[dim], 1) == 0
+
+
+def start_kernel(
+    place_ref, surface, cond_x, cond_y, porosity, rainfall, pipes, fields, near, far, tips, arrived
+):
     copies = [
         pltpu.make_async_copy(source, fields.at[index], arrived.at[index])
         for index, source in enumerate((surface, cond_x, cond_y, porosity, rainfall))
     ]
+    copies.append(pltpu.make_async_copy(pipes.at[24:32, :], tips, arrived.at[5]))
     for copy in copies:
         copy.start()
     for copy in copies:
@@ -135,23 +142,30 @@
     fields[3] = 1.0 / fields[3]
     for index in range(5):
         halves = [fields[index, :, 0:128], fields[index, :, 128:256]]
-        up[pl.ds(index * 8, 8), :] = strips(halves, 0)
-        down[pl.ds(index * 8, 8), :] = strips(halves, 60)
-
-
-def tall_block(place_ref, block, above, below, start):
-    over = jnp.where(place_ref[0] > 0, above[start : start + 4, :], 0.0)
-    under = jnp.where(place_ref[0] < 7, below[start : start + 4, :], 0.0)
+        top, bottom = strips(halves, 0), strips(halves, 60)
+        near[pl.ds(index * 8, 8), :] = jnp.where(even(place_ref, 0), bottom, top)
+        far[pl.ds(index * 8, 8), :] = jnp.where(even(place_ref, 0), top, bottom)
+    near[40:48, :] = jnp.concatenate(
+        [tips[7:8, 0:128], tips[7:8, 128:256], jnp.zeros((6, 128), F32)], axis=0
+    )
+
+
+def tall_block(place_ref, block, near, far, start):
+    near, far = near[start : start + 4, :], far[start : start + 4, :]
+    over = jnp.where(even(place_ref, 0), far, near)
+    under = jnp.where(even(place_ref, 0), near, far)
+    over = jnp.where(place_ref[0] > 0, over, 0.0)
+    under = jnp.where(place_ref[0] < 7, under, 0.0)
     return jnp.concatenate([block, under, over], axis=0)
 
 
-def pack_cols_kernel(place_ref, above, below, fields, link_cell, tall_out, out):
+def pack_cols_kernel(place_ref, near, far, fields, link_cell, tall_out, out):
     lane = iota((72, 128), 1)
     message = jnp.zeros((72, 128), F32)
     for index in range(5):
         tall = [
             tall_block(
-                place_ref, fields[index, :, half * 128 : half * 128 + 128], above, below,
+                place_ref, fields[index, :, half * 128 : half * 128 + 128], near, far,
                 index * 8 + half * 4,
             )
             for half in range(2)
@@ -206,11 +220,9 @@
     return got[pl.ds(index, 128, stride=blocks), :]
 
 
-def build_message(out, blocks, heads, nodes, table):
-    put(out, blocks, 0, paired(heads, nodes))
-    put(out, blocks, 1, beside(nodes))
-    for index, row in enumerate(ENDS):
-        put(out, blocks, 2 + index, jnp.broadcast_to(table[row : row + 1, :], (128, 128)))
+def build_message(out, heads, nodes):
+    put(out, 6, 0, paired(heads, nodes))
+    put(out, 6, 1, beside(nodes))
 
 
 def zone_heads(edge, zone_place, edge_ref, zone_ref):
@@ -246,12 +258,14 @@
 
 
 def first_sweep_kernel(
-    place_ref, tall, from_west, from_east, link_cell, table, nodes, coef,
+    place_ref, tall, near_col, far_col, near, link_cell, table, nodes, coef,
     gains_out, inverse_out, cell_high, cell_low, zone_row_out, zone_col_out, surface_out, heads_out,
     zone_out, out, cell_table, edge_ref, zone_ref,
 ):
     lane = iota((72, 128), 1)
     wide = []
+    from_west = jnp.where(even(place_ref, 1), far_col[...], near_col[...])
+    from_east = jnp.where(even(place_ref, 1), near_col[...], far_col[...])
     for index in range(5):
         west = jnp.where(place_ref[1] > 0, from_west[0:72, :], 0.0)
         east = jnp.where(place_ref[1] < 15, from_east[0:72, :], 0.0)
@@ -288,19 +302,24 @@
         state, gains, high, low, (zone_row, zone_col), surface_out, heads_out, zone_out,
         cell_table, edge_ref, zone_ref,
     )
-    build_message(out, 8, heads, nodes[...], table)
-    put(out, 8, 6, paired(coef[...], coef[...]))
-    put(out, 8, 7, beside(coef[...]))
+    build_message(out, heads, nodes[...])
+    own_rows = (iota((128, 128), 0) >> 4) == place_ref[0]
+    for half in range(2):
+        own = jnp.broadcast_to(table[half * 32 : half * 32 + 1, :], (128, 128))
+        other = jnp.broadcast_to(near[40 + half : 41 + half, :], (128, 128))
+        put(out, 6, 2 + half, jnp.where(own_rows, own, other))
+    put(out, 6, 4, paired(coef[...], coef[...]))
+    put(out, 6, 5, beside(coef[...]))
 
 
 def sweep_kernel(
-    last, place_ref, surface, above, below, gains_ref, cell_high, cell_low, zone_row, zone_col,
+    last, place_ref, surface, near, far, gains_ref, cell_high, cell_low, zone_row, zone_col,
     table, nodes, surface_out, heads_out, zone_out, out, cell_table, edge_ref, zone_ref,
 ):
     state = jnp.concatenate(
         [
             tall_block(
-                place_ref, surface[:, block * 128 : block * 128 + 128], above, below, block * 4
+                place_ref, surface[:, block * 128 : block * 128 + 128], near, far, block * 4
             )
             for block in range(3)
         ],
@@ -312,29 +331,30 @@
         state, gains, cell_high[...], cell_low[...], zone_place, surface_out, heads_out, zone_out,
         cell_table, edge_ref, zone_ref,
     )
-    build_message(out, 6, heads, nodes[...], table)
+    build_message(out, heads, nodes[...])
+    for index, row in enumerate(ENDS):
+        put(out, 6, 2 + index, jnp.broadcast_to(table[row : row + 1, :], (128, 128)))
 
 
 def tile_kernel(
-    first, last, got, surface, inverse, heads, zone, cell_high, cell_low, zone_row, zone_col, *rest
+    first, last, place_ref, got, surface, inverse, heads, zone, cell_high, cell_low, zone_row, zone_col, *rest
 ):
     rest = list(rest)
-    blocks = 8 if first else 6
     if first:
-        own_coef = low_halves(taken(got, blocks, 6))
-        zone_coef = taken(got, blocks, 7)
+        own_coef = low_halves(taken(got, 6, 4))
+        zone_coef = taken(got, 6, 5)
     else:
         own_coef = rest.pop(0)[...]
         zone_coef = rest.pop(0)[...]
     surface_out = rest.pop(0)
     if not last:
-        up, down = rest.pop(0), rest.pop(0)
+        near, far = rest.pop(0), rest.pop(0)
     if first:
         rest.pop(0)[...] = own_coef
         rest.pop(0)[...] = zone_coef
     value_ref, zone_value_ref = rest
     value_ref[...] = jnp.where(
-        cell_high[...] >= 0, own_coef * (heads[...] - high_halves(taken(got, blocks, 0))), 0.0
+        cell_high[...] >= 0, own_coef * (heads[...] - high_halves(taken(got, 6, 0))), 0.0
     )
     lost = summed(cell_high, cell_low, value_ref, 128, 128)
     left = surface[:, 0:128] - inverse[:, 0:128] * lost[:64]
@@ -344,7 +364,7 @@
     if last:
         return
     zone_value_ref[...] = jnp.where(
-        zone_row[...] >= 0, zone_coef * (zone[...] - taken(got, blocks, 1)), 0.0
+        zone_row[...] >= 0, zone_coef * (zone[...] - taken(got, 6, 1)), 0.0
     )
     lost = summed(zone_row, zone_col, zone_value_ref, 64, 2 * ZONE)
     lost = jnp.concatenate([lost, jnp.zeros((64, 128 - 2 * ZONE), F32)], axis=1)
@@ -355,28 +375,28 @@
     )
     edge = surface[:, 256:384] - inverse[:, 256:384] * lost
     surface_out[:, 256:384] = edge
-    up[...] = strips([left, right, edge], 0)
-    down[...] = strips([left, right, edge], 60)
+    top, bottom = strips([left, right, edge], 0), strips([left, right, edge], 60)
+    near[...] = jnp.where(even(place_ref, 0), bottom, top)
+    far[...] = jnp.where(even(place_ref, 0), top, bottom)
 
 
 def owner_kernel(
     first, last, place_ref, got, nodes, node_high, node_low, coef, table, meets, classes, matrices, *rest
 ):
-    blocks = 8 if first else 6
     if last:
         pipes_out, value_ref, ends_ref = rest
     else:
         table_out, nodes_out, value_ref, ends_ref = rest
     value_ref[...] = jnp.where(
-        node_high[...] >= 0, coef[...] * (low_halves(taken(got, blocks, 0)) - nodes[...]), 0.0
+        node_high[...] >= 0, coef[...] * (low_halves(taken(got, 6, 0)) - nodes[...]), 0.0
     )
     inflow = summed(node_high, node_low, value_ref, 64, 128)
     balance = table[...] + inflow
-    start = pl.multiple_of(place_ref[0] * 16 * blocks, 32)
+    start = pl.multiple_of(place_ref[0] * 96, 32)
+    other = pl.multiple_of((place_ref[0] ^ 1) * 96, 32) if first else start
     for index in range(4):
-        ends_ref[index * 16 : index * 16 + 16, :] = got[
-            pl.ds(start + 2 + index, 16, stride=blocks), :
-        ]
+        source, block = (other, index) if first and index >= 2 else (start, 2 + index)
+        ends_ref[index * 16 : index * 16 + 16, :] = got[pl.ds(source + block, 16, stride=6), :]
     meet = meets[...]
     meet_high = jnp.bitwise_and(meet >> 7, 1) * 16 + (meet >> 8)
     meet_high = jnp.where(iota((8, 128), 0) < 2, meet_high + 32, meet_high)
@@ -416,7 +436,7 @@
         matrices, pipes_out, node_value_ref, ends_ref,
     )
     tile_kernel(
-        False, True, got, surface, inverse, heads, zone, cell_high, cell_low, zone_row, zone_col,
+        False, True, place_ref, got, surface, inverse, heads, zone, cell_high, cell_low, zone_row, zone_col,
         own_coef, zone_coef, surface_out, cell_value_ref, zone_value_ref,
     )
 
@@ -439,9 +459,25 @@
     )(*inputs)
 
 
-def ring(block, axis, distance):
-    size = lax.axis_size(axis)
-    return lax.ppermute(block, axis, [(i, (i + distance) % size) for i in range(size)])
+def swapped(near, far, dim):
+    sizes = lax.axis_size("row"), lax.axis_size("col")
+    routes = [], []
+    for row in range(sizes[0]):
+        for col in range(sizes[1]):
+            here = [row, col]
+            partner = list(here)
+            partner[dim] ^= 1
+            other = list(here)
+            other[dim] += 1 if here[dim] % 2 else -1
+            if not 0 <= other[dim] < sizes[dim]:
+                other = list(here)
+                other[1 - dim] ^= 1
+            for route, there in zip(routes, (partner, other)):
+                route.append((row * sizes[1] + col, there[0] * sizes[1] + there[1]))
+    return (
+        lax.ppermute(near, ("row", "col"), routes[0]),
+        lax.ppermute(far, ("row", "col"), routes[1]),
+    )
 
 
 def body(
@@ -459,17 +495,20 @@
     matrices = pipe_matrices.reshape(CLASSES * 32, 32)
     ints = functools.partial(shape, dtype=jnp.int32)
 
-    fields, up, down = call(
-        start_kernel, (surface_head, conduct_x, conduct_y, porosity, rainfall),
-        [shape(5, 64, 256), shape(40, 128), shape(40, 128)],
-        [pltpu.SemaphoreType.DMA((5,))], space=pl.ANY, grant=60,
-    )
-    above, below = ring(down, "row", 1), ring(up, "row", -1)
+    fields, near, far = call(
+        start_kernel,
+        (place, *(pltpu.with_memory_space_constraint(x, pltpu.HBM) for x in (
+            surface_head, conduct_x, conduct_y, porosity, rainfall, pipe_head
+        ))),
+        [shape(5, 64, 256), shape(48, 128), shape(40, 128)],
+        [pltpu.VMEM((8, 256), F32), pltpu.SemaphoreType.DMA((6,))], scalars=1, space=pltpu.HBM,
+    )
+    near, far = swapped(near, far, 0)
     tall, sent = call(
-        pack_cols_kernel, (place, above, below, fields, link_cell),
+        pack_cols_kernel, (place, near, far, fields, link_cell),
         [shape(5, 72, 256), shape(136, 128)], scalars=1,
     )
-    from_west, from_east = ring(sent, "col", 1), ring(sent, "col", -1)
+    near_col, far_col = swapped(sent, sent, 1)
     table, nodes, node_high, node_low, coef, classes, matrices = call(
         owner_start_kernel, (pipe_head, link_node, link_coef, classes, matrices),
         [shape(64, 128), shape(64, 128), ints(64, 128), ints(64, 128), shape(64, 128),
@@ -481,9 +520,9 @@
     swept_shapes = [shape(64, 384), shape(64, 128), shape(128, 128)]
     (gains, inverse, cell_high, cell_low, zone_row, zone_col, surface, heads, zone, sent) = call(
         first_sweep_kernel,
-        (place, tall, from_west, from_east, link_cell, table, nodes, coef),
+        (place, tall, near_col, far_col, near, link_cell, table, nodes, coef),
         [shape(6, 72, 384), shape(64, 384), ints(64, 128), ints(64, 128), ints(128, 128),
-         ints(128, 128), *swept_shapes, shape(1024, 128)],
+         ints(128, 128), *swept_shapes, shape(768, 128)],
         gather_scratch, scalars=1,
     )
     sent, meets = lax.optimization_barrier((sent, meets))
@@ -493,7 +532,7 @@
         if step:
             surface, heads, zone, sent = call(
                 functools.partial(sweep_kernel, last),
-                (place, surface, above, below, gains, cell_high, cell_low, zone_row, zone_col,
+                (place, surface, near, far, gains, cell_high, cell_low, zone_row, zone_col,
                  table, nodes),
                 [*swept_shapes, shape(768, 128)], gather_scratch, scalars=1,
             )
@@ -512,10 +551,11 @@
         outputs = [shape(64, 384), shape(12, 128), shape(12, 128)]
         if first:
             outputs += [shape(64, 128), shape(128, 128)]
-        surface, up, down, *new_coefs = call(
-            functools.partial(tile_kernel, first, False), (got, *tile_inputs), outputs, tile_scratch
-        )
-        above, below = ring(down, "row", 1), ring(up, "row", -1)
+        surface, near, far, *new_coefs = call(
+            functools.partial(tile_kernel, first, False), (place, got, *tile_inputs), outputs,
+            tile_scratch, scalars=1,
+        )
+        near, far = swapped(near, far, 0)
         table, nodes = call(
             functools.partial(owner_kernel, first, False), (place, got, *owner_inputs),
             [shape(64, 128), shape(64, 128)], owner_scratch, scalars=1,

time: 99.9 us -> 94.5 us (0.946)
  waiting for transfers between devices: 5.93 us -> 1.45 us
  starting transfers between devices: 10.6 us -> 6.51 us
  local copies, waits for them, and re-layouts: 1.06 us -> 3.04 us
    ppermute x8, waiting for transfers between devices: 5.93 us -> 1.45 us  [the longest x4 1.44 us: swapped(): lax.ppermute(far, ('row', 'col'), routes[1])]
    ppermute x8, starting transfers between devices: 10.6 us -> 6.51 us  [the longest x4 4.14 us: swapped(): lax.ppermute(near, ('row', 'col'), routes[0])]
    unnamed x21 -> x19, local copies, waits for them, and re-layouts: 0.98 us -> 2.97 us
  transfers between devices with their start and end apart: 8 -> 8, of which waited for: 5 -> 2; matrix products, arithmetic and copies ran while one was open for 0% -> 0% of each run, Pallas kernels for 5% -> 6%
where the time goes in v5:
time: 94.5 us; the launch traced here: 94.2 us
  blocking collectives  58 us (61%)
  Pallas kernels  24.2 us (26%)
  starting transfers between devices  6.51 us (7%)
  local copies, waits for them, and re-layouts  3.04 us (3%)
  waiting for transfers between devices  1.45 us (2%)
    all_to_all x3, blocking collectives, body(): lax.all_to_all(sent.reshape(128, 1, -1), ('row', 'col'), split_axis=0, co...  58 us
    pallas_call x11, Pallas kernels, call(): pl.pallas_call(kernel, out_shape=outputs, in_specs=[smem] * scalars + [pl...  24.2 us
    ppermute x4, starting transfers between devices, swapped(): lax.ppermute(near, ('row', 'col'), routes[0])  4.14 us
    unnamed x19, local copies, waits for them, and re-layouts  2.97 us
    ppermute x4, starting transfers between devices, swapped(): lax.ppermute(far, ('row', 'col'), routes[1])  2.37 us
  transfers between devices with their start and end apart: 8, of which 2 were waited for; matrix products, arithmetic and copies ran while one was open for 0% of the time, Pallas kernels for 6%

profile of v5, /device:TPU:1, one launch (start us, length us, event | category | flops | bytes accessed | tf_op | source)
XLA Modules:
  0.0 94.2 jit_solution(10419737168651256792)
XLA Ops:
  0.6 0.1 pad_add_fusion.place_ref
  0.7 0.0 copy-start.7
  0.7 0.0 copy-start.3
  0.7 1.6 %shard_map.140 = (f32[5,64,256]{2,1,0:T(8,128)S(1)}, f32[48,128]{1,0:T(8,128)S(1)}, f32[40,128]{1,0:T(8,128)S(1)}) custom-call(s32[2]{0:T(128)S(1)} %pad_add_fusion.place_ref, f32[64,256]{1,0:T(8,128)} %surface.1, f32[64,256]{1,0:T(8,128)} %cond_x.1, f32[64,256]{1,0:T(8,128)} %cond_y.1, f32[64,256]{1,0:T(8,128)} %porosity.1, f32[64,256]{1,0:T(8,128)} %rainfall.1, ...), custom_call_target="tpu_custom_call" | custom-call | flops 1000000000 | bytes 1048576 | tf_op jit(solution)/shard_map/pallas_call | solution.py:451
  2.3 1.5 %collective-permute-start = (f32[48,128]{1,0:T(8,128)S(1)}, f32[48,128]{1,0:T(8,128)S(1)}, u32[]{:S(2)}, u32[]{:S(2)}) collective-permute-start(f32[48,128]{1,0:T(8,128)S(1)} %get-tuple-element.46), channel_id=1, source_target_pairs={{0,16},{1,17},{2,18},{3,19},{4,20},{5,21},{6,22},{7,23},{8,24},{9,... | collective-permute-start | bytes 73736 | tf_op jit(solution)/shard_map/ppermute | solution.py:478
  3.8 1.3 %collective-permute-start.1 = (f32[40,128]{1,0:T(8,128)S(1)}, f32[40,128]{1,0:T(8,128)S(1)}, u32[]{:S(2)}, u32[]{:S(2)}) collective-permute-start(f32[40,128]{1,0:T(8,128)S(1)} %get-tuple-element.47), channel_id=1, source_target_pairs={{0,1},{1,0},{2,3},{3,2},{4,5},{5,4},{6,7},{7,6},{8,9},{9,8},{10,11... | collective-permute-start | bytes 61448 | tf_op jit(solution)/shard_map/ppermute | solution.py:479
  5.1 0.1 pad.2.clone
  5.2 0.0 copy-start.6
  5.2 0.0 copy-done.7
  5.2 0.7 copy-done.6
  5.8 0.1 add_add_fusion.meets
  5.9 0.0 copy-done.3
  5.9 0.0 copy-start.4
  5.9 0.1 copy.18
  6.0 0.7 copy-done.4
  6.7 0.0 copy-start.5
  6.7 0.1 copy.19
  6.8 0.7 copy-done.5
  7.4 0.1 copy.20
  7.5 0.0 collective-permute-done.1.far
  7.5 0.0 collective-permute-done.near
  7.5 0.0 copy-start
  7.5 0.0 copy-start.1
  7.6 0.7 shard_map.141
  8.2 1.4 %collective-permute-start.2 = (f32[136,128]{1,0:T(8,128)S(1)}, f32[136,128]{1,0:T(8,128)S(1)}, u32[]{:S(2)}, u32[]{:S(2)}) collective-permute-start(f32[136,128]{1,0:T(8,128)S(1)} %get-tuple-element.50), channel_id=1, source_target_pairs={{0,1},{1,0},{2,3},{3,2},{4,5},{5,4},{6,7},{7,6},{8,9},{9,8},{10,11... | collective-permute-start | bytes 208904 | tf_op jit(solution)/shard_map/ppermute | solution.py:478
  9.6 0.5 collective-permute-start.3
  10.1 0.0 copy-start.2
  10.1 0.0 copy-done
  10.1 0.0 copy-done.1
  10.1 0.7 copy-done.2
  10.8 0.7 shard_map.142
  11.5 0.0 collective-permute-done.2.near_col
  11.5 0.0 collective-permute-done.3.far_col
  11.5 2.8 %shard_map.143 = (f32[6,72,384]{2,1,0:T(8,128)S(1)}, f32[64,384]{1,0:T(8,128)S(1)}, s32[64,128]{1,0:T(8,128)S(1)}, s32[64,128]{1,0:T(8,128)S(1)}, s32[128,128]{1...) custom-call(s32[2]{0:T(128)S(1)} %pad_add_fusion.place_ref, ...), custom_call_target="tpu_custom_call" | custom-call | flops 1000000000 | bytes 1048576 | tf_op jit(solution)/shard_map/pallas_call | solution.py:451
  14.3 25.9 %all_to_all.15 = f32[128,1,768]{2,1,0:T(1,128)S(1)} all-to-all(f32[128,1,768]{2,1,0:T(1,128)S(1)} %bitcast.20), channel_id=1, replica_groups=mesh['row'=8,'col'=16] {'row','col'}, dimensions={0} | all-to-all | bytes 786432 | tf_op jit(solution)/shard_map/all_to_all | solution.py:539
  40.2 2.9 %shard_map.144 = (f32[64,384]{1,0:T(8,128)S(1)}, f32[12,128]{1,0:T(8,128)S(1)}, f32[12,128]{1,0:T(8,128)S(1)}, f32[64,128]{1,0:T(8,128)S(1)}, f32[128,128]{1,0:T(8,128)S(1)}) custom-call(s32[2]{0:T(128)S(1)} %pad_add_fusion.place_ref, f32[768,128]{1,0:T(8,128)S(1)} %bitcast.15, f32[64,384]{1,0:T(8,128)S(1)} %get-tuple-element.56.surface, ...), custom_call_target="tpu_custom_call" | custom-call | flops 1000000000 | bytes 1048576 | tf_op jit(solution)/shard_map/pallas_call | solution.py:451
  43.1 0.6 collective-permute-start.4
  43.7 0.3 collective-permute-start.5
  44.0 2.3 %shard_map.145 = (f32[64,128]{1,0:T(8,128)S(1)}, f32[64,128]{1,0:T(8,128)S(1)}) custom-call(s32[2]{0:T(128)S(1)} %pad_add_fusion.place_ref, f32[768,128]{1,0:T(8,128)S(1)} %bitcast.16, f32[64,128]{1,0:T(8,128)S(1)} %get-tuple-element.52.nodes, s32[64,128]{1,0:T(8,128)S(1)} %get-tuple-element.68.node_high, s32[64,128]{1,0:T(8,128)S(1)} %get-tuple-element.69.node_low, ...), custom_call_target="tpu_custom_call" | custom-call | flops 1000000000 | bytes 1048576 | tf_op jit(solution)/shard_map/pallas_call | solution.py:451
  46.3 0.0 collective-permute-done.4.near
  46.3 0.7 collective-permute-done.5.far
  47.0 2.5 %shard_map.146 = (f32[64,384]{1,0:T(8,128)S(1)}, f32[64,128]{1,0:T(8,128)S(1)}, f32[128,128]{1,0:T(8,128)S(1)}, f32[768,128]{1,0:T(8,128)S(1)}) custom-call(s32[2]{0:T(128)S(1)} %pad_add_fusion.place_ref, f32[64,384]{1,0:T(8,128)S(1)} %get-tuple-element.64.surface, f32[12,128]{1,0:T(8,128)S(1)} %collective-permute-done.4.near, ...), custom_call_target="tpu_custom_call" | custom-call | flops 1000000000 | bytes 1048576 | tf_op jit(solution)/shard_map/pallas_call | solution.py:451
  49.6 16.1 %all_to_all.16 = f32[128,1,768]{2,1,0:T(1,128)S(1)} all-to-all(f32[128,1,768]{2,1,0:T(1,128)S(1)} %bitcast.22), channel_id=1, replica_groups=mesh['row'=8,'col'=16] {'row','col'}, dimensions={0} | all-to-all | bytes 786432 | tf_op jit(solution)/shard_map/all_to_all | solution.py:539
  65.7 2.9 %shard_map.147 = (f32[64,384]{1,0:T(8,128)S(1)}, f32[12,128]{1,0:T(8,128)S(1)}, f32[12,128]{1,0:T(8,128)S(1)}) custom-call(s32[2]{0:T(128)S(1)} %pad_add_fusion.place_ref, f32[768,128]{1,0:T(8,128)S(1)} %bitcast.18, f32[64,384]{1,0:T(8,128)S(1)} %get-tuple-element.76.surface, f32[64,384]{1,0:T(8,128)S(1)} %get-tuple-element.57.inverse, ...), custom_call_target="tpu_custom_call" | custom-call | flops 1000000000 | bytes 1048576 | tf_op jit(solution)/shard_map/pallas_call | solution.py:451
  68.6 0.6 collective-permute-start.6
  69.2 0.3 collective-permute-start.7
  69.5 2.3 %shard_map.148 = (f32[64,128]{1,0:T(8,128)S(1)}, f32[64,128]{1,0:T(8,128)S(1)}) custom-call(s32[2]{0:T(128)S(1)} %pad_add_fusion.place_ref, f32[768,128]{1,0:T(8,128)S(1)} %bitcast.19, f32[64,128]{1,0:T(8,128)S(1)} %get-tuple-element.74.nodes, s32[64,128]{1,0:T(8,128)S(1)} %get-tuple-element.68.node_high, s32[64,128]{1,0:T(8,128)S(1)} %get-tuple-element.69.node_low, ...), custom_call_target="tpu_custom_call" | custom-call | flops 1000000000 | bytes 1048576 | tf_op jit(solution)/shard_map/pallas_call | solution.py:451
  71.8 0.0 collective-permute-done.6.near
  71.8 0.7 collective-permute-done.7.far
  72.6 2.2 %shard_map.149 = (f32[64,384]{1,0:T(8,128)S(1)}, f32[64,128]{1,0:T(8,128)S(1)}, f32[128,128]{1,0:T(8,128)S(1)}, f32[768,128]{1,0:T(8,128)S(1)}) custom-call(s32[2]{0:T(128)S(1)} %pad_add_fusion.place_ref, f32[64,384]{1,0:T(8,128)S(1)} %get-tuple-element.81.surface, f32[12,128]{1,0:T(8,128)S(1)} %collective-permute-done.6.near, ...), custom_call_target="tpu_custom_call" | custom-call | flops 1000000000 | bytes 1048576 | tf_op jit(solution)/shard_map/pallas_call | solution.py:451
  74.8 16.0 %all_to_all.17 = f32[128,1,768]{2,1,0:T(1,128)S(1)} all-to-all(f32[128,1,768]{2,1,0:T(1,128)S(1)} %bitcast.21), channel_id=1, replica_groups=mesh['row'=8,'col'=16] {'row','col'}, dimensions={0} | all-to-all | bytes 786432 | tf_op jit(solution)/shard_map/all_to_all | solution.py:539
  90.8 3.3 %shard_map.150 = (f32[64,256]{1,0:T(8,128)}, f32[32,256]{1,0:T(8,128)}) custom-call(s32[2]{0:T(128)S(1)} %pad_add_fusion.place_ref, f32[768,128]{1,0:T(8,128)S(1)} %bitcast.17, f32[64,384]{1,0:T(8,128)S(1)} %get-tuple-element.87.surface, f32[64,384]{1,0:T(8,128)S(1)} %get-tuple-element.57.inverse, f32[64,128]{1,0:T(8,128)S(1)} %get-tuple-element.88.heads, ...), custom_call_target="tpu_custom_call" | custom-call | flops 1000000000 | bytes 1048576 | tf_op jit(solution)/shard_map/pallas_call | solution.py:451
  (1 shorter events, 0.0 us)
Async XLA Ops:
  0.7 4.4 %copy-start.7 = (s32[256]{0:T(256)S(1)}, s32[256]{0:T(256)}, u32[]{:S(2)}) copy-start(s32[256]{0:T(256)} %param.20) | copy-start | bytes 3076
  0.7 5.2 %copy-start.3 = (s32[1,128,64]{1,2,0:T(8,128)S(1)}, s32[1,128,64]{1,2,0:T(8,128)}, u32[]{:S(2)}) copy-start(s32[1,128,64]{1,2,0:T(8,128)} %param.23) | copy-start | bytes 98308
  2.3 5.2 %collective-permute-start = (f32[48,128]{1,0:T(8,128)S(1)}, f32[48,128]{1,0:T(8,128)S(1)}, u32[]{:S(2)}, u32[]{:S(2)}) collective-permute-start(f32[48,128]{1,0:T(8,128)S(1)} %get-tuple-element.46), channel_id=1, source_target_pairs={{0,16},{1,17},{2,18},{3,19},{4,20},{5,21},{6,22},{7,23},{8,24},{9,... | collective-permute-start | bytes 73736 | tf_op jit(solution)/shard_map/ppermute | solution.py:478
  3.8 3.7 %collective-permute-start.1 = (f32[40,128]{1,0:T(8,128)S(1)}, f32[40,128]{1,0:T(8,128)S(1)}, u32[]{:S(2)}, u32[]{:S(2)}) collective-permute-start(f32[40,128]{1,0:T(8,128)S(1)} %get-tuple-element.47), channel_id=1, source_target_pairs={{0,1},{1,0},{2,3},{3,2},{4,5},{5,4},{6,7},{7,6},{8,9},{9,8},{10,11... | collective-permute-start | bytes 61448 | tf_op jit(solution)/shard_map/ppermute | solution.py:479
  5.2 0.7 copy-start.6
  5.9 0.8 copy-start.4
  6.7 0.8 copy-start.5
  7.5 2.6 %copy-start = (f32[4,32,32]{2,1,0:T(8,128)S(1)}, f32[4,32,32]{2,1,0:T(8,128)}, u32[]{:S(2)}) copy-start(f32[4,32,32]{2,1,0:T(8,128)} %param.22) | copy-start | bytes 49156
  7.5 2.5 %copy-start.1 = (f32[32,256]{1,0:T(8,128)S(1)}, f32[32,256]{1,0:T(8,128)}, u32[]{:S(2)}) copy-start(f32[32,256]{1,0:T(8,128)} %pipes.3) | copy-start | bytes 98308
  8.2 3.2 %collective-permute-start.2 = (f32[136,128]{1,0:T(8,128)S(1)}, f32[136,128]{1,0:T(8,128)S(1)}, u32[]{:S(2)}, u32[]{:S(2)}) collective-permute-start(f32[136,128]{1,0:T(8,128)S(1)} %get-tuple-element.50), channel_id=1, source_target_pairs={{0,1},{1,0},{2,3},{3,2},{4,5},{5,4},{6,7},{7,6},{8,9},{9,8},{10,11... | collective-permute-start | bytes 208904 | tf_op jit(solution)/shard_map/ppermute | solution.py:478
  9.6 1.9 %collective-permute-start.3 = (f32[136,128]{1,0:T(8,128)S(1)}, f32[136,128]{1,0:T(8,128)S(1)}, u32[]{:S(2)}, u32[]{:S(2)}) collective-permute-start(f32[136,128]{1,0:T(8,128)S(1)} %get-tuple-element.50), channel_id=1, source_target_pairs={{0,16},{1,2},{2,1},{3,4},{4,3},{5,6},{6,5},{7,8},{8,7},{9,10},{10,... | collective-permute-start | bytes 208904 | tf_op jit(solution)/shard_map/ppermute | solution.py:479
  10.1 0.7 copy-start.2
  43.1 3.3 %collective-permute-start.4 = (f32[12,128]{1,0:T(8,128)S(1)}, f32[12,128]{1,0:T(8,128)S(1)}, u32[]{:S(2)}, u32[]{:S(2)}) collective-permute-start(f32[12,128]{1,0:T(8,128)S(1)} %get-tuple-element.65), channel_id=1, source_target_pairs={{0,16},{1,17},{2,18},{3,19},{4,20},{5,21},{6,22},{7,23},{8,24},{9,... | collective-permute-start | bytes 18440 | tf_op jit(solution)/shard_map/ppermute | solution.py:478
  43.7 3.3 %collective-permute-start.5 = (f32[12,128]{1,0:T(8,128)S(1)}, f32[12,128]{1,0:T(8,128)S(1)}, u32[]{:S(2)}, u32[]{:S(2)}) collective-permute-start(f32[12,128]{1,0:T(8,128)S(1)} %get-tuple-element.66), channel_id=1, source_target_pairs={{0,1},{1,0},{2,3},{3,2},{4,5},{5,4},{6,7},{7,6},{8,9},{9,8},{10,11... | collective-permute-start | bytes 18440 | tf_op jit(solution)/shard_map/ppermute | solution.py:479
  68.6 3.3 %collective-permute-start.6 = (f32[12,128]{1,0:T(8,128)S(1)}, f32[12,128]{1,0:T(8,128)S(1)}, u32[]{:S(2)}, u32[]{:S(2)}) collective-permute-start(f32[12,128]{1,0:T(8,128)S(1)} %get-tuple-element.82), channel_id=1, source_target_pairs={{0,16},{1,17},{2,18},{3,19},{4,20},{5,21},{6,22},{7,23},{8,24},{9,... | collective-permute-start | bytes 18440 | tf_op jit(solution)/shard_map/ppermute | solution.py:478
  69.2 3.3 %collective-permute-start.7 = (f32[12,128]{1,0:T(8,128)S(1)}, f32[12,128]{1,0:T(8,128)S(1)}, u32[]{:S(2)}, u32[]{:S(2)}) collective-permute-start(f32[12,128]{1,0:T(8,128)S(1)} %get-tuple-element.83), channel_id=1, source_target_pairs={{0,1},{1,0},{2,3},{3,2},{4,5},{5,4},{6,7},{7,6},{8,9},{9,8},{10,11... | collective-permute-start | bytes 18440 | tf_op jit(solution)/shard_map/ppermute | solution.py:479

commit v6 on v5

--- a/solution.py
+++ b/solution.py
@@ -66,38 +66,73 @@
     return jnp.concatenate(tiles, axis=0) if len(tiles) > 1 else tiles[0]
 
 
+def gathered_by_product(table, high_ref, low_ref, tiles):
+    coarse = table.astype(BF16)
+    fine = (table - coarse.astype(F32)).astype(BF16)
+    parts = jnp.concatenate([coarse, fine], axis=1)
+    row_iota = iota((128, 128), 0)
+    high_iota = row_iota.astype(F32).astype(BF16)
+    one, zero = jnp.ones((128, 128), BF16), jnp.zeros((128, 128), BF16)
+    found = []
+    for start in range(0, 8 * tiles, 8):
+        high = high_ref[start : start + 8, :].astype(F32)
+        low = low_ref[start : start + 8, :]
+        hot = jnp.concatenate(
+            [
+                jnp.where(repeated(high[j : j + 1], 128) == high_iota, one, zero)
+                for j in range(8)
+            ],
+            axis=1,
+        )
+        lines = lax.dot_general(
+            parts, hot, (((0,), (0,)), ((), ())), preferred_element_type=F32
+        )
+        lines = lines[:128] + lines[128:]
+        for j in range(8):
+            line = jnp.where(
+                row_iota == low[j : j + 1], lines[:, j * 128 : j * 128 + 128], 0.0
+            )
+            found.append(jnp.sum(line, axis=0, keepdims=True))
+    return jnp.concatenate(found, axis=0)
+
+
 def repeated(line, size):
     block = jnp.broadcast_to(line, (16, 128)).astype(BF16)
     return jnp.concatenate([block] * (size // 16), axis=0) if size > 16 else block
 
 
-def summed(high_ref, low_ref, value_ref, high_size, low_size):
-    high_iota = iota((high_size, 128), 0).astype(F32).astype(BF16)
-    low_iota = iota((low_size, 128), 0).astype(F32).astype(BF16)
-    high_zero = jnp.zeros((high_size, 128), BF16)
-    low_zero = jnp.zeros((low_size, 128), BF16)
-    low_one = jnp.ones((low_size, 128), BF16)
-    total = jnp.zeros((2 * high_size, low_size), F32)
+def summed(high_ref, low_ref, value_ref, high_size, low_size, by_low=False):
+    refs, sizes = (high_ref, low_ref), (high_size, low_size)
+    bearer = 1 if by_low else 0
+    iotas = [iota((size, 128), 0).astype(F32).astype(BF16) for size in sizes]
+    zeros = [jnp.zeros((size, 128), BF16) for size in sizes]
+    one = jnp.ones((sizes[1 - bearer], 128), BF16)
+    total = None
     for start in range(0, high_ref.shape[0], 8):
-        high = high_ref[start : start + 8, :].astype(F32)
-        low = low_ref[start : start + 8, :].astype(F32)
+        places = [ref[start : start + 8, :].astype(F32) for ref in refs]
         value = value_ref[start : start + 8, :]
         coarse = value.astype(BF16).astype(F32)
         fine = value - coarse
-        coarse_hot, fine_hot, low_hot = [], [], []
+        size, zero = sizes[bearer], zeros[bearer]
+        coarse_hot, fine_hot, plain_hot = [], [], []
         for j in range(8):
-            same = repeated(high[j : j + 1], high_size) == high_iota
-            coarse_hot.append(jnp.where(same, repeated(coarse[j : j + 1], high_size), high_zero))
-            fine_hot.append(jnp.where(same, repeated(fine[j : j + 1], high_size), high_zero))
-            same = repeated(low[j : j + 1], low_size) == low_iota
-            low_hot.append(jnp.where(same, low_one, low_zero))
+            same = [
+                repeated(places[side][j : j + 1], sizes[side]) == iotas[side] for side in range(2)
+            ]
+            coarse_hot.append(jnp.where(same[bearer], repeated(coarse[j : j + 1], size), zero))
+            fine_hot.append(jnp.where(same[bearer], repeated(fine[j : j + 1], size), zero))
+            plain_hot.append(jnp.where(same[1 - bearer], one, zeros[1 - bearer]))
         value_hot = jnp.concatenate(
             [jnp.concatenate(coarse_hot, axis=1), jnp.concatenate(fine_hot, axis=1)], axis=0
         )
-        total = total + lax.dot_general(
-            value_hot, jnp.concatenate(low_hot, axis=1), (((1,), (1,)), ((), ())),
-            preferred_element_type=F32,
-        )
+        plain_hot = jnp.concatenate(plain_hot, axis=1)
+        sides = (plain_hot, value_hot) if by_low else (value_hot, plain_hot)
+        product = lax.dot_general(
+            *sides, (((1,), (1,)), ((), ())), preferred_element_type=F32
+        )
+        total = product if total is None else total + product
+    if by_low:
+        return total[:, :low_size] + total[:, low_size:]
     return total[:high_size] + total[high_size:]
 
 
@@ -123,12 +158,16 @@
     return jnp.concatenate([block[start : start + HALO_ROWS] for block in blocks], axis=0)
 
 
-def even(place_ref, dim):
-    return jnp.bitwise_and(place_ref[dim], 1) == 0
+def row_col():
+    return lax.axis_index("row"), lax.axis_index("col")
+
+
+def even(dim):
+    return jnp.bitwise_and(row_col()[dim], 1) == 0
 
 
 def start_kernel(
-    place_ref, surface, cond_x, cond_y, porosity, rainfall, pipes, fields, near, far, tips, arrived
+    surface, cond_x, cond_y, porosity, rainfall, pipes, fields, near, far, tips, arrived
 ):
     copies = [
         pltpu.make_async_copy(source, fields.at[index], arrived.at[index])
@@ -143,29 +182,29 @@
     for index in range(5):
         halves = [fields[index, :, 0:128], fields[index, :, 128:256]]
         top, bottom = strips(halves, 0), strips(halves, 60)
-        near[pl.ds(index * 8, 8), :] = jnp.where(even(place_ref, 0), bottom, top)
-        far[pl.ds(index * 8, 8), :] = jnp.where(even(place_ref, 0), top, bottom)
+        near[pl.ds(index * 8, 8), :] = jnp.where(even(0), bottom, top)
+        far[pl.ds(index * 8, 8), :] = jnp.where(even(0), top, bottom)
     near[40:48, :] = jnp.concatenate(
         [tips[7:8, 0:128], tips[7:8, 128:256], jnp.zeros((6, 128), F32)], axis=0
     )
 
 
-def tall_block(place_ref, block, near, far, start):
+def tall_block(block, near, far, start):
     near, far = near[start : start + 4, :], far[start : start + 4, :]
-    over = jnp.where(even(place_ref, 0), far, near)
-    under = jnp.where(even(place_ref, 0), near, far)
-    over = jnp.where(place_ref[0] > 0, over, 0.0)
-    under = jnp.where(place_ref[0] < 7, under, 0.0)
+    over = jnp.where(even(0), far, near)
+    under = jnp.where(even(0), near, far)
+    over = jnp.where(row_col()[0] > 0, over, 0.0)
+    under = jnp.where(row_col()[0] < 7, under, 0.0)
     return jnp.concatenate([block, under, over], axis=0)
 
 
-def pack_cols_kernel(place_ref, near, far, fields, link_cell, tall_out, out):
+def pack_cols_kernel(near, far, fields, link_cell, tall_out, out):
     lane = iota((72, 128), 1)
     message = jnp.zeros((72, 128), F32)
     for index in range(5):
         tall = [
             tall_block(
-                place_ref, fields[index, :, half * 128 : half * 128 + 128], near, far,
+                fields[index, :, half * 128 : half * 128 + 128], near, far,
                 index * 8 + half * 4,
             )
             for half in range(2)
@@ -250,7 +289,13 @@
     surface_out[...] = state[:64]
     cell_table[0:64, :] = state[:64, 0:128]
     cell_table[64:128, :] = state[:64, 128:256]
-    heads = gathered(cell_table, 128, cell_high, cell_low)
+    heads = jnp.concatenate(
+        [
+            gathered_by_product(cell_table[...], cell_high, cell_low, 4),
+            gathered(cell_table, 128, cell_high[32:64, :], cell_low[32:64, :]),
+        ],
+        axis=0,
+    )
     heads_out[...] = heads
     if zone_place is not None:
         zone_out[...] = zone_heads(state[:64, 256:384], zone_place, edge_ref, zone_ref)
@@ -258,17 +303,17 @@
 
 
 def first_sweep_kernel(
-    place_ref, tall, near_col, far_col, near, link_cell, table, nodes, coef,
+    tall, near_col, far_col, near, link_cell, table, nodes, coef,
     gains_out, inverse_out, cell_high, cell_low, zone_row_out, zone_col_out, surface_out, heads_out,
     zone_out, out, cell_table, edge_ref, zone_ref,
 ):
     lane = iota((72, 128), 1)
     wide = []
-    from_west = jnp.where(even(place_ref, 1), far_col[...], near_col[...])
-    from_east = jnp.where(even(place_ref, 1), near_col[...], far_col[...])
+    from_west = jnp.where(even(1), far_col[...], near_col[...])
+    from_east = jnp.where(even(1), near_col[...], far_col[...])
     for index in range(5):
-        west = jnp.where(place_ref[1] > 0, from_west[0:72, :], 0.0)
-        east = jnp.where(place_ref[1] < 15, from_east[0:72, :], 0.0)
+        west = jnp.where(row_col()[1] > 0, from_west[0:72, :], 0.0)
+        east = jnp.where(row_col()[1] < 15, from_east[0:72, :], 0.0)
         if index:
             west = pltpu.roll(west, 128 - index * 2 * HALO_COLS, 1)
             east = pltpu.roll(east, 128 - index * 2 * HALO_COLS, 1)
@@ -299,11 +344,11 @@
     cell_high[...] = high
     cell_low[...] = low
     heads = sweep_and_gather(
-        state, gains, high, low, (zone_row, zone_col), surface_out, heads_out, zone_out,
+        state, gains, cell_high, cell_low, (zone_row, zone_col), surface_out, heads_out, zone_out,
         cell_table, edge_ref, zone_ref,
     )
     build_message(out, heads, nodes[...])
-    own_rows = (iota((128, 128), 0) >> 4) == place_ref[0]
+    own_rows = (iota((128, 128), 0) >> 4) == row_col()[0]
     for half in range(2):
         own = jnp.broadcast_to(table[half * 32 : half * 32 + 1, :], (128, 128))
         other = jnp.broadcast_to(near[40 + half : 41 + half, :], (128, 128))
@@ -313,13 +358,13 @@
 
 
 def sweep_kernel(
-    last, place_ref, surface, near, far, gains_ref, cell_high, cell_low, zone_row, zone_col,
+    last, surface, near, far, gains_ref, cell_high, cell_low, zone_row, zone_col,
     table, nodes, surface_out, heads_out, zone_out, out, cell_table, edge_ref, zone_ref,
 ):
     state = jnp.concatenate(
         [
             tall_block(
-                place_ref, surface[:, block * 128 : block * 128 + 128], near, far, block * 4
+                surface[:, block * 128 : block * 128 + 128], near, far, block * 4
             )
             for block in range(3)
         ],
@@ -328,7 +373,7 @@
     gains = [gains_ref[index] for index in range(6)]
     zone_place = None if last else (zone_row[...], zone_col[...])
     heads = sweep_and_gather(
-        state, gains, cell_high[...], cell_low[...], zone_place, surface_out, heads_out, zone_out,
+        state, gains, cell_high, cell_low, zone_place, surface_out, heads_out, zone_out,
         cell_table, edge_ref, zone_ref,
     )
     build_message(out, heads, nodes[...])
@@ -337,7 +382,7 @@
 
 
 def tile_kernel(
-    first, last, place_ref, got, surface, inverse, heads, zone, cell_high, cell_low, zone_row, zone_col, *rest
+    first, last, got, surface, inverse, heads, zone, cell_high, cell_low, zone_row, zone_col, *rest
 ):
     rest = list(rest)
     if first:
@@ -366,7 +411,7 @@
     zone_value_ref[...] = jnp.where(
         zone_row[...] >= 0, zone_coef * (zone[...] - taken(got, 6, 1)), 0.0
     )
-    lost = summed(zone_row, zone_col, zone_value_ref, 64, 2 * ZONE)
+    lost = summed(zone_row, zone_col, zone_value_ref, 64, 2 * ZONE, by_low=True)
     lost = jnp.concatenate([lost, jnp.zeros((64, 128 - 2 * ZONE), F32)], axis=1)
     lane = iota((64, 128), 1)
     lost = jnp.where(
@@ -376,12 +421,12 @@
     edge = surface[:, 256:384] - inverse[:, 256:384] * lost
     surface_out[:, 256:384] = edge
     top, bottom = strips([left, right, edge], 0), strips([left, right, edge], 60)
-    near[...] = jnp.where(even(place_ref, 0), bottom, top)
-    far[...] = jnp.where(even(place_ref, 0), top, bottom)
+    near[...] = jnp.where(even(0), bottom, top)
+    far[...] = jnp.where(even(0), top, bottom)
 
 
 def owner_kernel(
-    first, last, place_ref, got, nodes, node_high, node_low, coef, table, meets, classes, matrices, *rest
+    first, last, got, nodes, node_high, node_low, coef, table, meets, classes, matrices, *rest
 ):
     if last:
         pipes_out, value_ref, ends_ref = rest
@@ -392,8 +437,8 @@
     )
     inflow = summed(node_high, node_low, value_ref, 64, 128)
     balance = table[...] + inflow
-    start = pl.multiple_of(place_ref[0] * 96, 32)
-    other = pl.multiple_of((place_ref[0] ^ 1) * 96, 32) if first else start
+    start = pl.multiple_of(row_col()[0] * 96, 32)
+    other = pl.multiple_of((row_col()[0] ^ 1) * 96, 32) if first else start
     for index in range(4):
         source, block = (other, index) if first and index >= 2 else (start, 2 + index)
         ends_ref[index * 16 : index * 16 + 16, :] = got[pl.ds(source + block, 16, stride=6), :]
@@ -427,16 +472,16 @@
 
 
 def final_kernel(
-    place_ref, got, surface, inverse, heads, zone, cell_high, cell_low, zone_row, zone_col, own_coef,
+    got, surface, inverse, heads, zone, cell_high, cell_low, zone_row, zone_col, own_coef,
     zone_coef, nodes, node_high, node_low, coef, table, meets, classes, matrices, surface_out,
     pipes_out, cell_value_ref, zone_value_ref, node_value_ref, ends_ref,
 ):
     owner_kernel(
-        False, True, place_ref, got, nodes, node_high, node_low, coef, table, meets, classes,
+        False, True, got, nodes, node_high, node_low, coef, table, meets, classes,
         matrices, pipes_out, node_value_ref, ends_ref,
     )
     tile_kernel(
-        False, True, place_ref, got, surface, inverse, heads, zone, cell_high, cell_low, zone_row, zone_col,
+        False, True, got, surface, inverse, heads, zone, cell_high, cell_low, zone_row, zone_col,
         own_coef, zone_coef, surface_out, cell_value_ref, zone_value_ref,
     )
 
@@ -445,16 +490,15 @@
     return jax.ShapeDtypeStruct(dims, dtype)
 
 
-def call(kernel, inputs, outputs, scratch=(), scalars=0, space=pltpu.VMEM, grant=32):
-    smem = pl.BlockSpec(memory_space=pltpu.SMEM)
+def call(kernel, inputs, outputs, scratch=(), space=pltpu.VMEM):
     vmem = pl.BlockSpec(memory_space=pltpu.VMEM)
     return pl.pallas_call(
         kernel,
         out_shape=outputs,
-        in_specs=[smem] * scalars + [pl.BlockSpec(memory_space=space)] * (len(inputs) - scalars),
+        in_specs=[pl.BlockSpec(memory_space=space)] * len(inputs),
         out_specs=[vmem] * len(outputs),
         scratch_shapes=list(scratch),
-        compiler_params=pltpu.CompilerParams(vmem_limit_bytes=grant << 20),
+        compiler_params=pltpu.CompilerParams(vmem_limit_bytes=32 << 20),
         cost_estimate=pl.CostEstimate(flops=10**9, bytes_accessed=1 << 20, transcendentals=0),
     )(*inputs)
 
@@ -484,10 +528,7 @@
     surface_head, conduct_x, conduct_y, porosity, rainfall, pipe_head, pipe_class, pipe_up,
     pipe_down, pipe_matrices, link_cell, link_node, link_coef,
 ):
-    place = jnp.stack([lax.axis_index("row"), lax.axis_index("col")]).astype(jnp.int32)
     link_cell = link_cell[0]
-    link_node = link_node[:, 0, :]
-    link_coef = link_coef[:, 0, :]
     meets = jnp.concatenate(
         [pipe_up.reshape(2, 128), pipe_down.reshape(2, 128), jnp.zeros((4, 128), jnp.int32)], axis=0
     )
@@ -497,17 +538,20 @@
 
     fields, near, far = call(
         start_kernel,
-        (place, *(pltpu.with_memory_space_constraint(x, pltpu.HBM) for x in (
+        [pltpu.with_memory_space_constraint(x, pltpu.HBM) for x in (
             surface_head, conduct_x, conduct_y, porosity, rainfall, pipe_head
-        ))),
+        )],
         [shape(5, 64, 256), shape(48, 128), shape(40, 128)],
-        [pltpu.VMEM((8, 256), F32), pltpu.SemaphoreType.DMA((6,))], scalars=1, space=pltpu.HBM,
+        [pltpu.VMEM((8, 256), F32), pltpu.SemaphoreType.DMA((6,))], space=pltpu.HBM,
     )
     near, far = swapped(near, far, 0)
     tall, sent = call(
-        pack_cols_kernel, (place, near, far, fields, link_cell),
-        [shape(5, 72, 256), shape(136, 128)], scalars=1,
-    )
+        pack_cols_kernel, (near, far, fields, link_cell),
+        [shape(5, 72, 256), shape(136, 128)],
+    )
+    sent, link_node, link_coef = lax.optimization_barrier((sent, link_node, link_coef))
+    link_node = link_node[:, 0, :]
+    link_coef = link_coef[:, 0, :]
     near_col, far_col = swapped(sent, sent, 1)
     table, nodes, node_high, node_low, coef, classes, matrices = call(
         owner_start_kernel, (pipe_head, link_node, link_coef, classes, matrices),
@@ -520,10 +564,10 @@
     swept_shapes = [shape(64, 384), shape(64, 128), shape(128, 128)]
     (gains, inverse, cell_high, cell_low, zone_row, zone_col, surface, heads, zone, sent) = call(
         first_sweep_kernel,
-        (place, tall, near_col, far_col, near, link_cell, table, nodes, coef),
+        (tall, near_col, far_col, near, link_cell, table, nodes, coef),
         [shape(6, 72, 384), shape(64, 384), ints(64, 128), ints(64, 128), ints(128, 128),
          ints(128, 128), *swept_shapes, shape(768, 128)],
-        gather_scratch, scalars=1,
+        gather_scratch,
     )
     sent, meets = lax.optimization_barrier((sent, meets))
     coefs = ()
@@ -532,9 +576,9 @@
         if step:
             surface, heads, zone, sent = call(
                 functools.partial(sweep_kernel, last),
-                (place, surface, near, far, gains, cell_high, cell_low, zone_row, zone_col,
+                (surface, near, far, gains, cell_high, cell_low, zone_row, zone_col,
                  table, nodes),
-                [*swept_shapes, shape(768, 128)], gather_scratch, scalars=1,
+                [*swept_shapes, shape(768, 128)], gather_scratch,
             )
         got = lax.all_to_all(
             sent.reshape(128, 1, -1), ("row", "col"), split_axis=0, concat_axis=0, tiled=True
@@ -545,20 +589,20 @@
         owner_scratch = [pltpu.VMEM((64, 128), F32), pltpu.VMEM((64, 128), F32)]
         if last:
             return tuple(call(
-                final_kernel, (place, got, *tile_inputs, *owner_inputs),
-                [shape(64, 256), shape(32, 256)], tile_scratch + owner_scratch, scalars=1,
+                final_kernel, (got, *tile_inputs, *owner_inputs),
+                [shape(64, 256), shape(32, 256)], tile_scratch + owner_scratch,
             ))
         outputs = [shape(64, 384), shape(12, 128), shape(12, 128)]
         if first:
             outputs += [shape(64, 128), shape(128, 128)]
         surface, near, far, *new_coefs = call(
-            functools.partial(tile_kernel, first, False), (place, got, *tile_inputs), outputs,
-            tile_scratch, scalars=1,
+            functools.partial(tile_kernel, first, False), (got, *tile_inputs), outputs,
+            tile_scratch,
         )
         near, far = swapped(near, far, 0)
         table, nodes = call(
-            functools.partial(owner_kernel, first, False), (place, got, *owner_inputs),
-            [shape(64, 128), shape(64, 128)], owner_scratch, scalars=1,
+            functools.partial(owner_kernel, first, False), (got, *owner_inputs),
+            [shape(64, 128), shape(64, 128)], owner_scratch,
         )
         if first:
             coefs = tuple(new_coefs)

time: 94.5 us -> 88.1 us (0.932)
  Pallas kernels: 24.2 us -> 16.7 us
  waiting for transfers between devices: 1.45 us -> 3.36 us
  local copies, waits for them, and re-layouts: 3.04 us -> 1.77 us
    pallas_call x11, Pallas kernels: 24.2 us -> 16.7 us  [call(): pl.pallas_call(kernel, out_shape=outputs, in_specs=[pl.BlockSpec(memory_s...]
    ppermute x4, waiting for transfers between devices: 1.44 us -> 3.35 us  [swapped(): lax.ppermute(far, ('row', 'col'), routes[1])]
    unnamed x19 -> x17, local copies, waits for them, and re-layouts: 2.97 us -> 1.51 us
  transfers between devices with their start and end apart: 8 -> 8, of which waited for: 2 -> 3; matrix products, arithmetic and copies ran while one was open for 0% -> 0% of each run, Pallas kernels for 6% -> 5%
where the time goes in v6:
time: 88.1 us; the launch traced here: 87.8 us
  blocking collectives  58.1 us (66%)
  Pallas kernels  16.7 us (19%)
  starting transfers between devices  6.98 us (8%)
  waiting for transfers between devices  3.36 us (4%)
  local copies, waits for them, and re-layouts  1.77 us (2%)
    all_to_all x3, blocking collectives, body(): lax.all_to_all(sent.reshape(128, 1, -1), ('row', 'col'), split_axis=0, co...  58.1 us
    pallas_call x11, Pallas kernels, call(): pl.pallas_call(kernel, out_shape=outputs, in_specs=[pl.BlockSpec(memory_s...  16.7 us
    ppermute x4, starting transfers between devices, swapped(): lax.ppermute(near, ('row', 'col'), routes[0])  4.23 us
    ppermute x4, waiting for transfers between devices, swapped(): lax.ppermute(far, ('row', 'col'), routes[1])  3.35 us
    ppermute x4, starting transfers between devices, swapped(): lax.ppermute(far, ('row', 'col'), routes[1])  2.75 us
  transfers between devices with their start and end apart: 8, of which 3 were waited for; matrix products, arithmetic and copies ran while one was open for 0% of the time, Pallas kernels for 5%

profile of v6, /device:TPU:1, one launch (start us, length us, event | category | flops | bytes accessed | tf_op | source)
XLA Modules:
  0.0 87.8 jit_solution(11921179149827647920)
XLA Ops:
  0.6 0.0 copy-start.7
  0.6 0.0 copy-start.3
  0.7 1.0 %shard_map.140 = (f32[5,64,256]{2,1,0:T(8,128)S(1)}, f32[48,128]{1,0:T(8,128)S(1)}, f32[40,128]{1,0:T(8,128)S(1)}) custom-call(f32[64,256]{1,0:T(8,128)} %surface.1, f32[64,256]{1,0:T(8,128)} %cond_x.1, f32[64,256]{1,0:T(8,128)} %cond_y.1, f32[64,256]{1,0:T(8,128)} %porosity.1, f32[64,256]{1,0:T(8,128)} %rainfall.1, f32[32,256]{1,0:T(8,128)} %pipes.3), custom_call_target="tpu_custom_call" | custom-call | flops 1000000000 | bytes 1048576 | tf_op jit(solution)/shard_map/pallas_call | solution.py:495
  1.7 1.5 %collective-permute-start = (f32[48,128]{1,0:T(8,128)S(1)}, f32[48,128]{1,0:T(8,128)S(1)}, u32[]{:S(2)}, u32[]{:S(2)}) collective-permute-start(f32[48,128]{1,0:T(8,128)S(1)} %get-tuple-element.49), channel_id=1, source_target_pairs={{0,16},{1,17},{2,18},{3,19},{4,20},{5,21},{6,22},{7,23},{8,24},{9,... | collective-permute-start | bytes 73736 | tf_op jit(solution)/shard_map/ppermute | solution.py:522
  3.2 1.3 %collective-permute-start.1 = (f32[40,128]{1,0:T(8,128)S(1)}, f32[40,128]{1,0:T(8,128)S(1)}, u32[]{:S(2)}, u32[]{:S(2)}) collective-permute-start(f32[40,128]{1,0:T(8,128)S(1)} %get-tuple-element.50), channel_id=1, source_target_pairs={{0,1},{1,0},{2,3},{3,2},{4,5},{5,4},{6,7},{7,6},{8,9},{9,8},{10,11... | collective-permute-start | bytes 61448 | tf_op jit(solution)/shard_map/ppermute | solution.py:523
  4.5 0.1 pad.2.clone
  4.6 0.0 copy-start.6
  4.6 0.0 copy-done.7
  4.6 0.7 copy-done.6
  5.2 0.1 add_add_fusion.meets
  5.3 0.0 copy-done.3
  5.3 0.1 copy.18
  5.4 1.3 %collective-permute-done.1.far = f32[40,128]{1,0:T(8,128)S(1)} collective-permute-done((f32[40,128]{1,0:T(8,128)S(1)}, f32[40,128]{1,0:T(8,128)S(1)}, u32[]{:S(2)}, u32[]{:S(2)}) %collective-permute-start.1) | collective-permute-done | bytes 20512 | tf_op jit(solution)/shard_map/ppermute | solution.py:523
  6.7 0.0 collective-permute-done.near
  6.7 0.0 copy-start.4
  6.7 0.1 shard_map.141
  6.8 0.0 copy-start.5
  6.8 1.5 %collective-permute-start.2 = (f32[136,128]{1,0:T(8,128)S(1)}, f32[136,128]{1,0:T(8,128)S(1)}, u32[]{:S(2)}, u32[]{:S(2)}) collective-permute-start(f32[136,128]{1,0:T(8,128)S(1)} %get-tuple-element.54), channel_id=1, source_target_pairs={{0,1},{1,0},{2,3},{3,2},{4,5},{5,4},{6,7},{7,6},{8,9},{9,8},{10,11... | collective-permute-start | bytes 208904 | tf_op jit(solution)/shard_map/ppermute | solution.py:522
  8.3 0.7 collective-permute-start.3
  9.0 0.0 copy-done.4
  9.0 0.1 copy.19
  9.1 0.0 copy-done.5
  9.1 0.0 copy-start
  9.1 0.0 copy-start.1
  9.1 0.1 copy.20
  9.2 0.0 copy-start.2
  9.2 0.7 copy-done
  9.9 0.0 copy-done.1
  9.9 0.0 copy-done.2
  9.9 0.7 shard_map.142
  10.6 0.0 collective-permute-done.2.near_col
  10.6 0.0 collective-permute-done.3.far_col
  10.7 1.8 %shard_map.143 = (f32[6,72,384]{2,1,0:T(8,128)S(1)}, f32[64,384]{1,0:T(8,128)S(1)}, s32[64,128]{1,0:T(8,128)S(1)}, s32[64,128]{1,0:T(8,128)S(1)}, s32[128,128]{1...) custom-call(f32[5,72,256]{2,1,0:T(8,128)S(1)} %get-tuple-element.52., ...), custom_call_target="tpu_custom_call" | custom-call | flops 1000000000 | bytes 1048576 | tf_op jit(solution)/shard_map/pallas_call | solution.py:495
  12.5 25.5 %all_to_all.15 = f32[128,1,768]{2,1,0:T(1,128)S(1)} all-to-all(f32[128,1,768]{2,1,0:T(1,128)S(1)} %bitcast.18), channel_id=1, replica_groups=mesh['row'=8,'col'=16] {'row','col'}, dimensions={0} | all-to-all | bytes 786432 | tf_op jit(solution)/shard_map/all_to_all | solution.py:583
  38.0 2.0 %shard_map.144 = (f32[64,384]{1,0:T(8,128)S(1)}, f32[12,128]{1,0:T(8,128)S(1)}, f32[12,128]{1,0:T(8,128)S(1)}, f32[64,128]{1,0:T(8,128)S(1)}, f32[128,128]{1,0:T(8,128)S(1)}) custom-call(f32[768,128]{1,0:T(8,128)S(1)} %bitcast.13, f32[64,384]{1,0:T(8,128)S(1)} %get-tuple-element.62.surface, f32[64,384]{1,0:T(8,128)S(1)} %get-tuple-element.63.inverse, ...), custom_call_target="tpu_custom_call" | custom-call | flops 1000000000 | bytes 1048576 | tf_op jit(solution)/shard_map/pallas_call | solution.py:495
  40.0 0.6 collective-permute-start.4
  40.6 0.3 collective-permute-start.5
  40.9 1.8 %shard_map.145 = (f32[64,128]{1,0:T(8,128)S(1)}, f32[64,128]{1,0:T(8,128)S(1)}) custom-call(f32[768,128]{1,0:T(8,128)S(1)} %bitcast.14, f32[64,128]{1,0:T(8,128)S(1)} %get-tuple-element.58.nodes, s32[64,128]{1,0:T(8,128)S(1)} %get-tuple-element.74.node_high, s32[64,128]{1,0:T(8,128)S(1)} %get-tuple-element.75.node_low, ...), custom_call_target="tpu_custom_call" | custom-call | flops 1000000000 | bytes 1048576 | tf_op jit(solution)/shard_map/pallas_call | solution.py:495
  42.7 0.0 collective-permute-done.4.near
  42.7 1.3 %collective-permute-done.5.far = f32[12,128]{1,0:T(8,128)S(1)} collective-permute-done((f32[12,128]{1,0:T(8,128)S(1)}, f32[12,128]{1,0:T(8,128)S(1)}, u32[]{:S(2)}, u32[]{:S(2)}) %collective-permute-start.5) | collective-permute-done | bytes 6176 | tf_op jit(solution)/shard_map/ppermute | solution.py:523
  44.0 1.5 %shard_map.146 = (f32[64,384]{1,0:T(8,128)S(1)}, f32[64,128]{1,0:T(8,128)S(1)}, f32[128,128]{1,0:T(8,128)S(1)}, f32[768,128]{1,0:T(8,128)S(1)}) custom-call(f32[64,384]{1,0:T(8,128)S(1)} %get-tuple-element.70.surface, f32[12,128]{1,0:T(8,128)S(1)} %collective-permute-done.4.near, f32[12,128]{1,0:T(8,128)S(1)} %collective-permute-done.5.far, ...), custom_call_target="tpu_custom_call" | custom-call | flops 1000000000 | bytes 1048576 | tf_op jit(solution)/shard_map/pallas_call | solution.py:495
  45.5 16.1 %all_to_all.16 = f32[128,1,768]{2,1,0:T(1,128)S(1)} all-to-all(f32[128,1,768]{2,1,0:T(1,128)S(1)} %bitcast.20), channel_id=1, replica_groups=mesh['row'=8,'col'=16] {'row','col'}, dimensions={0} | all-to-all | bytes 786432 | tf_op jit(solution)/shard_map/all_to_all | solution.py:583
  61.6 2.0 %shard_map.147 = (f32[64,384]{1,0:T(8,128)S(1)}, f32[12,128]{1,0:T(8,128)S(1)}, f32[12,128]{1,0:T(8,128)S(1)}) custom-call(f32[768,128]{1,0:T(8,128)S(1)} %bitcast.15, f32[64,384]{1,0:T(8,128)S(1)} %get-tuple-element.82.surface, f32[64,384]{1,0:T(8,128)S(1)} %get-tuple-element.63.inverse, f32[64,128]{1,0:T(8,128)S(1)} %get-tuple-element.83.heads, ...), custom_call_target="tpu_custom_call" | custom-call | flops 1000000000 | bytes 1048576 | tf_op jit(solution)/shard_map/pallas_call | solution.py:495
  63.6 0.6 collective-permute-start.6
  64.2 0.5 collective-permute-start.7
  64.7 1.8 %shard_map.148 = (f32[64,128]{1,0:T(8,128)S(1)}, f32[64,128]{1,0:T(8,128)S(1)}) custom-call(f32[768,128]{1,0:T(8,128)S(1)} %bitcast.16, f32[64,128]{1,0:T(8,128)S(1)} %get-tuple-element.80.nodes, s32[64,128]{1,0:T(8,128)S(1)} %get-tuple-element.74.node_high, s32[64,128]{1,0:T(8,128)S(1)} %get-tuple-element.75.node_low, ...), custom_call_target="tpu_custom_call" | custom-call | flops 1000000000 | bytes 1048576 | tf_op jit(solution)/shard_map/pallas_call | solution.py:495
  66.4 0.0 collective-permute-done.6.near
  66.5 0.8 collective-permute-done.7.far
  67.3 1.3 %shard_map.149 = (f32[64,384]{1,0:T(8,128)S(1)}, f32[64,128]{1,0:T(8,128)S(1)}, f32[128,128]{1,0:T(8,128)S(1)}, f32[768,128]{1,0:T(8,128)S(1)}) custom-call(f32[64,384]{1,0:T(8,128)S(1)} %get-tuple-element.87.surface, f32[12,128]{1,0:T(8,128)S(1)} %collective-permute-done.6.near, f32[12,128]{1,0:T(8,128)S(1)} %collective-permute-done.7.far, ...), custom_call_target="tpu_custom_call" | custom-call | flops 1000000000 | bytes 1048576 | tf_op jit(solution)/shard_map/pallas_call | solution.py:495
  68.6 16.5 %all_to_all.17 = f32[128,1,768]{2,1,0:T(1,128)S(1)} all-to-all(f32[128,1,768]{2,1,0:T(1,128)S(1)} %bitcast.19), channel_id=1, replica_groups=mesh['row'=8,'col'=16] {'row','col'}, dimensions={0} | all-to-all | bytes 786432 | tf_op jit(solution)/shard_map/all_to_all | solution.py:583
  85.1 2.8 %shard_map.150 = (f32[64,256]{1,0:T(8,128)}, f32[32,256]{1,0:T(8,128)}) custom-call(f32[768,128]{1,0:T(8,128)S(1)} %bitcast.17, f32[64,384]{1,0:T(8,128)S(1)} %get-tuple-element.93.surface, f32[64,384]{1,0:T(8,128)S(1)} %get-tuple-element.63.inverse, f32[64,128]{1,0:T(8,128)S(1)} %get-tuple-element.94.heads, f32[128,128]{1,0:T(8,128)S(1)} %get-tuple-element.95.zone, ...), custom_call_target="tpu_custom_call" | custom-call | flops 1000000000 | bytes 1048576 | tf_op jit(solution)/shard_map/pallas_call | solution.py:495
  (1 shorter events, 0.0 us)
Async XLA Ops:
  0.6 3.9 %copy-start.7 = (s32[256]{0:T(256)S(1)}, s32[256]{0:T(256)}, u32[]{:S(2)}) copy-start(s32[256]{0:T(256)} %param.20) | copy-start | bytes 3076
  0.6 4.7 %copy-start.3 = (s32[1,128,64]{1,2,0:T(8,128)S(1)}, s32[1,128,64]{1,2,0:T(8,128)}, u32[]{:S(2)}) copy-start(s32[1,128,64]{1,2,0:T(8,128)} %param.23) | copy-start | bytes 98308
  1.7 5.0 %collective-permute-start = (f32[48,128]{1,0:T(8,128)S(1)}, f32[48,128]{1,0:T(8,128)S(1)}, u32[]{:S(2)}, u32[]{:S(2)}) collective-permute-start(f32[48,128]{1,0:T(8,128)S(1)} %get-tuple-element.49), channel_id=1, source_target_pairs={{0,16},{1,17},{2,18},{3,19},{4,20},{5,21},{6,22},{7,23},{8,24},{9,... | collective-permute-start | bytes 73736 | tf_op jit(solution)/shard_map/ppermute | solution.py:522
  3.2 3.5 %collective-permute-start.1 = (f32[40,128]{1,0:T(8,128)S(1)}, f32[40,128]{1,0:T(8,128)S(1)}, u32[]{:S(2)}, u32[]{:S(2)}) collective-permute-start(f32[40,128]{1,0:T(8,128)S(1)} %get-tuple-element.50), channel_id=1, source_target_pairs={{0,1},{1,0},{2,3},{3,2},{4,5},{5,4},{6,7},{7,6},{8,9},{9,8},{10,11... | collective-permute-start | bytes 61448 | tf_op jit(solution)/shard_map/ppermute | solution.py:523
  4.6 0.7 copy-start.6
  6.7 2.3 %copy-start.4 = (s32[128,1,64]{0,2,1:T(8,128)S(1)}, s32[128,1,64]{0,2,1:T(8,128)}, u32[]{:S(2)}) copy-start(s32[128,1,64]{0,2,1:T(8,128)} %param.24) | copy-start | bytes 98308
  6.8 2.2 %copy-start.5 = (f32[128,1,64]{0,2,1:T(8,128)S(1)}, f32[128,1,64]{0,2,1:T(8,128)}, u32[]{:S(2)}) copy-start(f32[128,1,64]{0,2,1:T(8,128)} %param.25) | copy-start | bytes 98308
  6.8 3.8 %collective-permute-start.2 = (f32[136,128]{1,0:T(8,128)S(1)}, f32[136,128]{1,0:T(8,128)S(1)}, u32[]{:S(2)}, u32[]{:S(2)}) collective-permute-start(f32[136,128]{1,0:T(8,128)S(1)} %get-tuple-element.54), channel_id=1, source_target_pairs={{0,1},{1,0},{2,3},{3,2},{4,5},{5,4},{6,7},{7,6},{8,9},{9,8},{10,11... | collective-permute-start | bytes 208904 | tf_op jit(solution)/shard_map/ppermute | solution.py:522
  8.3 2.4 %collective-permute-start.3 = (f32[136,128]{1,0:T(8,128)S(1)}, f32[136,128]{1,0:T(8,128)S(1)}, u32[]{:S(2)}, u32[]{:S(2)}) collective-permute-start(f32[136,128]{1,0:T(8,128)S(1)} %get-tuple-element.54), channel_id=1, source_target_pairs={{0,16},{1,2},{2,1},{3,4},{4,3},{5,6},{6,5},{7,8},{8,7},{9,10},{10,... | collective-permute-start | bytes 208904 | tf_op jit(solution)/shard_map/ppermute | solution.py:523
  9.1 0.8 copy-start
  9.1 0.8 copy-start.1
  9.2 0.7 copy-start.2
  40.0 2.7 %collective-permute-start.4 = (f32[12,128]{1,0:T(8,128)S(1)}, f32[12,128]{1,0:T(8,128)S(1)}, u32[]{:S(2)}, u32[]{:S(2)}) collective-permute-start(f32[12,128]{1,0:T(8,128)S(1)} %get-tuple-element.71), channel_id=1, source_target_pairs={{0,16},{1,17},{2,18},{3,19},{4,20},{5,21},{6,22},{7,23},{8,24},{9,... | collective-permute-start | bytes 18440 | tf_op jit(solution)/shard_map/ppermute | solution.py:522
  40.6 3.3 %collective-permute-start.5 = (f32[12,128]{1,0:T(8,128)S(1)}, f32[12,128]{1,0:T(8,128)S(1)}, u32[]{:S(2)}, u32[]{:S(2)}) collective-permute-start(f32[12,128]{1,0:T(8,128)S(1)} %get-tuple-element.72), channel_id=1, source_target_pairs={{0,1},{1,0},{2,3},{3,2},{4,5},{5,4},{6,7},{7,6},{8,9},{9,8},{10,11... | collective-permute-start | bytes 18440 | tf_op jit(solution)/shard_map/ppermute | solution.py:523
  63.6 2.9 %collective-permute-start.6 = (f32[12,128]{1,0:T(8,128)S(1)}, f32[12,128]{1,0:T(8,128)S(1)}, u32[]{:S(2)}, u32[]{:S(2)}) collective-permute-start(f32[12,128]{1,0:T(8,128)S(1)} %get-tuple-element.88), channel_id=1, source_target_pairs={{0,16},{1,17},{2,18},{3,19},{4,20},{5,21},{6,22},{7,23},{8,24},{9,... | collective-permute-start | bytes 18440 | tf_op jit(solution)/shard_map/ppermute | solution.py:522
  64.2 3.1 %collective-permute-start.7 = (f32[12,128]{1,0:T(8,128)S(1)}, f32[12,128]{1,0:T(8,128)S(1)}, u32[]{:S(2)}, u32[]{:S(2)}) collective-permute-start(f32[12,128]{1,0:T(8,128)S(1)} %get-tuple-element.89), channel_id=1, source_target_pairs={{0,1},{1,0},{2,3},{3,2},{4,5},{5,4},{6,7},{7,6},{8,9},{9,8},{10,11... | collective-permute-start | bytes 18440 | tf_op jit(solution)/shard_map/ppermute | solution.py:523

commit v7 on v6

--- a/solution.py
+++ b/solution.py
@@ -136,6 +136,37 @@
     return total[:high_size] + total[high_size:]
 
 
+def summed_by_columns(row_ref, value_ref, hot_ref):
+    row_iota = iota((64, 128), 0).astype(F32).astype(BF16)
+    zero = jnp.zeros((64, 128), BF16)
+    total = jnp.zeros((128, 256), F32)
+    for start in range(0, 64, 8):
+        rows = row_ref[start : start + 8, :].astype(F32)
+        value = value_ref[start : start + 8, :]
+        coarse = value.astype(BF16).astype(F32)
+        fine = value - coarse
+        coarse_hot, fine_hot = [], []
+        for j in range(8):
+            same = repeated(rows[j : j + 1], 64) == row_iota
+            coarse_hot.append(jnp.where(same, repeated(coarse[j : j + 1], 64), zero))
+            fine_hot.append(jnp.where(same, repeated(fine[j : j + 1], 64), zero))
+        value_hot = jnp.concatenate(
+            [jnp.concatenate(coarse_hot, axis=1), jnp.concatenate(fine_hot, axis=1)], axis=0
+        )
+        total = total + jnp.dot(
+            value_hot, hot_ref[start * 128 : start * 128 + 1024, :], preferred_element_type=F32
+        )
+    return total[:64] + total[64:]
+
+
+def columns_kernel(link_cell, hot):
+    cols = jnp.bitwise_and(packed(link_cell[...]), 255).astype(F32).T
+    lane = iota((128, 256), 1).astype(F32)
+    for j in range(64):
+        same = jnp.broadcast_to(cols[:, j : j + 1], (128, 256)) == lane
+        hot[j * 128 : j * 128 + 128, :] = jnp.where(same, 1.0, 0.0).astype(BF16)
+
+
 def cell_place(cell):
     high = jnp.where(
         cell >= 0, jnp.bitwise_and(cell >> 7, 1) * 64 + (cell >> 8), -1
@@ -259,9 +290,10 @@
     return got[pl.ds(index, 128, stride=blocks), :]
 
 
-def build_message(out, heads, nodes):
-    put(out, 6, 0, paired(heads, nodes))
-    put(out, 6, 1, beside(nodes))
+def build_message(out, blocks, heads, nodes):
+    put(out, blocks, 0, paired(heads, nodes))
+    if blocks == 6:
+        put(out, blocks, 5, beside(nodes))
 
 
 def zone_heads(edge, zone_place, edge_ref, zone_ref):
@@ -347,14 +379,14 @@
         state, gains, cell_high, cell_low, (zone_row, zone_col), surface_out, heads_out, zone_out,
         cell_table, edge_ref, zone_ref,
     )
-    build_message(out, heads, nodes[...])
+    build_message(out, 6, heads, nodes[...])
     own_rows = (iota((128, 128), 0) >> 4) == row_col()[0]
     for half in range(2):
         own = jnp.broadcast_to(table[half * 32 : half * 32 + 1, :], (128, 128))
         other = jnp.broadcast_to(near[40 + half : 41 + half, :], (128, 128))
-        put(out, 6, 2 + half, jnp.where(own_rows, own, other))
-    put(out, 6, 4, paired(coef[...], coef[...]))
-    put(out, 6, 5, beside(coef[...]))
+        put(out, 6, 1 + half, jnp.where(own_rows, own, other))
+    put(out, 6, 3, paired(coef[...], coef[...]))
+    put(out, 6, 4, beside(coef[...]))
 
 
 def sweep_kernel(
@@ -376,18 +408,19 @@
         state, gains, cell_high, cell_low, zone_place, surface_out, heads_out, zone_out,
         cell_table, edge_ref, zone_ref,
     )
-    build_message(out, heads, nodes[...])
+    blocks = 5 if last else 6
+    build_message(out, blocks, heads, nodes[...])
     for index, row in enumerate(ENDS):
-        put(out, 6, 2 + index, jnp.broadcast_to(table[row : row + 1, :], (128, 128)))
+        put(out, blocks, 1 + index, jnp.broadcast_to(table[row : row + 1, :], (128, 128)))
 
 
 def tile_kernel(
-    first, last, got, surface, inverse, heads, zone, cell_high, cell_low, zone_row, zone_col, *rest
+    first, last, got, surface, inverse, heads, zone, cell_high, hot, zone_row, zone_col, *rest
 ):
     rest = list(rest)
     if first:
-        own_coef = low_halves(taken(got, 6, 4))
-        zone_coef = taken(got, 6, 5)
+        own_coef = low_halves(taken(got, 6, 3))
+        zone_coef = taken(got, 6, 4)
     else:
         own_coef = rest.pop(0)[...]
         zone_coef = rest.pop(0)[...]
@@ -397,19 +430,20 @@
     if first:
         rest.pop(0)[...] = own_coef
         rest.pop(0)[...] = zone_coef
-    value_ref, zone_value_ref = rest
+    value_ref, zone_value_ref, row_ref = rest
     value_ref[...] = jnp.where(
-        cell_high[...] >= 0, own_coef * (heads[...] - high_halves(taken(got, 6, 0))), 0.0
-    )
-    lost = summed(cell_high, cell_low, value_ref, 128, 128)
-    left = surface[:, 0:128] - inverse[:, 0:128] * lost[:64]
-    right = surface[:, 128:256] - inverse[:, 128:256] * lost[64:]
+        cell_high[...] >= 0, own_coef * (heads[...] - high_halves(taken(got, 5 if last else 6, 0))), 0.0
+    )
+    row_ref[...] = jnp.where(cell_high[...] >= 0, jnp.bitwise_and(cell_high[...], 63), -1)
+    lost = summed_by_columns(row_ref, value_ref, hot)
+    left = surface[:, 0:128] - inverse[:, 0:128] * lost[:, 0:128]
+    right = surface[:, 128:256] - inverse[:, 128:256] * lost[:, 128:256]
     surface_out[:, 0:128] = left
     surface_out[:, 128:256] = right
     if last:
         return
     zone_value_ref[...] = jnp.where(
-        zone_row[...] >= 0, zone_coef * (zone[...] - taken(got, 6, 1)), 0.0
+        zone_row[...] >= 0, zone_coef * (zone[...] - taken(got, 6, 5)), 0.0
     )
     lost = summed(zone_row, zone_col, zone_value_ref, 64, 2 * ZONE, by_low=True)
     lost = jnp.concatenate([lost, jnp.zeros((64, 128 - 2 * ZONE), F32)], axis=1)
@@ -428,20 +462,21 @@
 def owner_kernel(
     first, last, got, nodes, node_high, node_low, coef, table, meets, classes, matrices, *rest
 ):
+    blocks = 5 if last else 6
     if last:
         pipes_out, value_ref, ends_ref = rest
     else:
         table_out, nodes_out, value_ref, ends_ref = rest
     value_ref[...] = jnp.where(
-        node_high[...] >= 0, coef[...] * (low_halves(taken(got, 6, 0)) - nodes[...]), 0.0
+        node_high[...] >= 0, coef[...] * (low_halves(taken(got, blocks, 0)) - nodes[...]), 0.0
     )
     inflow = summed(node_high, node_low, value_ref, 64, 128)
     balance = table[...] + inflow
-    start = pl.multiple_of(row_col()[0] * 96, 32)
+    start = pl.multiple_of(row_col()[0] * (16 * blocks), 16)
     other = pl.multiple_of((row_col()[0] ^ 1) * 96, 32) if first else start
     for index in range(4):
-        source, block = (other, index) if first and index >= 2 else (start, 2 + index)
-        ends_ref[index * 16 : index * 16 + 16, :] = got[pl.ds(source + block, 16, stride=6), :]
+        source, block = (other, index - 1) if first and index >= 2 else (start, 1 + index)
+        ends_ref[index * 16 : index * 16 + 16, :] = got[pl.ds(source + block, 16, stride=blocks), :]
     meet = meets[...]
     meet_high = jnp.bitwise_and(meet >> 7, 1) * 16 + (meet >> 8)
     meet_high = jnp.where(iota((8, 128), 0) < 2, meet_high + 32, meet_high)
@@ -472,17 +507,17 @@
 
 
 def final_kernel(
-    got, surface, inverse, heads, zone, cell_high, cell_low, zone_row, zone_col, own_coef,
-    zone_coef, nodes, node_high, node_low, coef, table, meets, classes, matrices, surface_out,
-    pipes_out, cell_value_ref, zone_value_ref, node_value_ref, ends_ref,
+    got, surface, inverse, heads, zone, cell_high, hot, zone_row, zone_col, own_coef, zone_coef,
+    nodes, node_high, node_low, coef, table, meets, classes, matrices, surface_out,
+    pipes_out, cell_value_ref, zone_value_ref, row_ref, node_value_ref, ends_ref,
 ):
     owner_kernel(
         False, True, got, nodes, node_high, node_low, coef, table, meets, classes,
         matrices, pipes_out, node_value_ref, ends_ref,
     )
     tile_kernel(
-        False, True, got, surface, inverse, heads, zone, cell_high, cell_low, zone_row, zone_col,
-        own_coef, zone_coef, surface_out, cell_value_ref, zone_value_ref,
+        False, True, got, surface, inverse, heads, zone, cell_high, hot, zone_row, zone_col,
+        own_coef, zone_coef, surface_out, cell_value_ref, zone_value_ref, row_ref,
     )
 
 
@@ -498,7 +533,7 @@
         in_specs=[pl.BlockSpec(memory_space=space)] * len(inputs),
         out_specs=[vmem] * len(outputs),
         scratch_shapes=list(scratch),
-        compiler_params=pltpu.CompilerParams(vmem_limit_bytes=32 << 20),
+        compiler_params=pltpu.CompilerParams(vmem_limit_bytes=16 << 20),
         cost_estimate=pl.CostEstimate(flops=10**9, bytes_accessed=1 << 20, transcendentals=0),
     )(*inputs)
 
@@ -549,7 +584,9 @@
         pack_cols_kernel, (near, far, fields, link_cell),
         [shape(5, 72, 256), shape(136, 128)],
     )
-    sent, link_node, link_coef = lax.optimization_barrier((sent, link_node, link_coef))
+    sent, link_node, link_coef, cells = lax.optimization_barrier(
+        (sent, link_node, link_coef, link_cell)
+    )
     link_node = link_node[:, 0, :]
     link_coef = link_coef[:, 0, :]
     near_col, far_col = swapped(sent, sent, 1)
@@ -558,6 +595,7 @@
         [shape(64, 128), shape(64, 128), ints(64, 128), ints(64, 128), shape(64, 128),
          ints(2, 128), shape(128, 32)],
     )
+    (hot,) = call(columns_kernel, (cells,), [shape(8192, 256, dtype=BF16)])
     gather_scratch = [
         pltpu.VMEM((128, 128), F32), pltpu.VMEM((64, 128), F32), pltpu.VMEM((8, 128), F32)
     ]
@@ -569,7 +607,7 @@
          ints(128, 128), *swept_shapes, shape(768, 128)],
         gather_scratch,
     )
-    sent, meets = lax.optimization_barrier((sent, meets))
+    sent, meets, hot = lax.optimization_barrier((sent, meets, hot))
     coefs = ()
     for step in range(STEPS):
         first, last = step == 0, step == STEPS - 1
@@ -578,14 +616,16 @@
                 functools.partial(sweep_kernel, last),
                 (surface, near, far, gains, cell_high, cell_low, zone_row, zone_col,
                  table, nodes),
-                [*swept_shapes, shape(768, 128)], gather_scratch,
+                [*swept_shapes, shape(640 if last else 768, 128)], gather_scratch,
             )
         got = lax.all_to_all(
             sent.reshape(128, 1, -1), ("row", "col"), split_axis=0, concat_axis=0, tiled=True
         ).reshape(-1, 128)
-        tile_inputs = (surface, inverse, heads, zone, cell_high, cell_low, zone_row, zone_col, *coefs)
+        tile_inputs = (surface, inverse, heads, zone, cell_high, hot, zone_row, zone_col, *coefs)
         owner_inputs = (nodes, node_high, node_low, coef, table, meets, classes, matrices)
-        tile_scratch = [pltpu.VMEM((64, 128), F32), pltpu.VMEM((128, 128), F32)]
+        tile_scratch = [
+            pltpu.VMEM((64, 128), F32), pltpu.VMEM((128, 128), F32), pltpu.VMEM((64, 128), jnp.int32)
+        ]
         owner_scratch = [pltpu.VMEM((64, 128), F32), pltpu.VMEM((64, 128), F32)]
         if last:
             return tuple(call(

time: 88.1 us -> 85.9 us (0.975)
  blocking collectives: 58.1 us -> 55.3 us
    all_to_all x3, blocking collectives: 58.1 us -> 55.3 us  [body(): lax.all_to_all(sent.reshape(128, 1, -1), ('row', 'col'), split_axis=0, co...]
    ppermute x4, starting transfers between devices: 2.75 us -> 3.79 us  [swapped(): lax.ppermute(far, ('row', 'col'), routes[1])]
    pallas_call x11 -> x12, Pallas kernels: 16.7 us -> 17.4 us  [call(): pl.pallas_call(kernel, out_shape=outputs, in_specs=[pl.BlockSpec(memory_s...]
  transfers between devices with their start and end apart: 8 -> 8, of which waited for: 3 -> 2; matrix products, arithmetic and copies ran while one was open for 0% -> 2% of each run, Pallas kernels for 5% -> 7%
where the time goes in v7:
time: 85.9 us; the launch traced here: 85.6 us
  blocking collectives  55.3 us (64%)
  Pallas kernels  17.4 us (20%)
  starting transfers between devices  7.6 us (9%)
  waiting for transfers between devices  2.52 us (3%)
  local copies, waits for them, and re-layouts  1.13 us (1%)
    all_to_all x3, blocking collectives, body(): lax.all_to_all(sent.reshape(128, 1, -1), ('row', 'col'), split_axis=0, co...  55.3 us
    pallas_call x12, Pallas kernels, call(): pl.pallas_call(kernel, out_shape=outputs, in_specs=[pl.BlockSpec(memory_s...  17.4 us
    ppermute x4, starting transfers between devices, swapped(): lax.ppermute(near, ('row', 'col'), routes[0])  3.81 us
    ppermute x4, starting transfers between devices, swapped(): lax.ppermute(far, ('row', 'col'), routes[1])  3.79 us
    ppermute x4, waiting for transfers between devices, swapped(): lax.ppermute(far, ('row', 'col'), routes[1])  2.51 us
  transfers between devices with their start and end apart: 8, of which 2 were waited for; matrix products, arithmetic and copies ran while one was open for 2% of the time, Pallas kernels for 7%

profile of v7, /device:TPU:1, one launch (start us, length us, event | category | flops | bytes accessed | tf_op | source)
XLA Modules:
  0.0 85.6 jit_solution(6207004429282143268)
XLA Ops:
  0.6 0.0 copy-start.4
  0.6 0.0 copy-start.3
  0.7 1.0 %shard_map.140 = (f32[5,64,256]{2,1,0:T(8,128)S(1)}, f32[48,128]{1,0:T(8,128)S(1)}, f32[40,128]{1,0:T(8,128)S(1)}) custom-call(f32[64,256]{1,0:T(8,128)} %surface.1, f32[64,256]{1,0:T(8,128)} %cond_x.1, f32[64,256]{1,0:T(8,128)} %cond_y.1, f32[64,256]{1,0:T(8,128)} %porosity.1, f32[64,256]{1,0:T(8,128)} %rainfall.1, f32[32,256]{1,0:T(8,128)} %pipes.3), custom_call_target="tpu_custom_call" | custom-call | flops 1000000000 | bytes 1048576 | tf_op jit(solution)/shard_map/pallas_call | solution.py:530
  1.7 0.0 copy-start
  1.7 0.0 copy-start.1
  1.7 0.0 copy-start.2
  1.7 2.7 %collective-permute-start.1 = (f32[40,128]{1,0:T(8,128)S(1)}, f32[40,128]{1,0:T(8,128)S(1)}, u32[]{:S(2)}, u32[]{:S(2)}) collective-permute-start(f32[40,128]{1,0:T(8,128)S(1)} %get-tuple-element.52), channel_id=1, source_target_pairs={{0,1},{1,0},{2,3},{3,2},{4,5},{5,4},{6,7},{7,6},{8,9},{9,8},{10,11... | collective-permute-start | bytes 61448 | tf_op jit(solution)/shard_map/ppermute | solution.py:558
  4.4 0.5 collective-permute-start
  4.9 0.1 pad.2.clone
  5.0 0.8 add_add_fusion.meets
  5.7 0.8 copy.18
  6.6 0.0 collective-permute-done.1.far
  6.6 0.0 collective-permute-done.near
  6.6 0.1 shard_map.141
  6.8 0.5 collective-permute-start.3
  7.2 1.9 %collective-permute-start.2 = (f32[136,128]{1,0:T(8,128)S(1)}, f32[136,128]{1,0:T(8,128)S(1)}, u32[]{:S(2)}, u32[]{:S(2)}) collective-permute-start(f32[136,128]{1,0:T(8,128)S(1)} %get-tuple-element.56), channel_id=1, source_target_pairs={{0,1},{1,0},{2,3},{3,2},{4,5},{5,4},{6,7},{7,6},{8,9},{9,8},{10,11... | collective-permute-start | bytes 208904 | tf_op jit(solution)/shard_map/ppermute | solution.py:557
  9.1 0.0 copy-done.3
  9.1 0.1 copy.19
  9.2 0.0 copy-done.4
  9.2 0.1 copy.20
  9.3 1.5 %shard_map.144.hot = bf16[8192,256]{1,0:T(8,128)(2,1)S(1)} custom-call(s32[128,64]{1,0:T(8,128)S(1)} %bitcast.22), custom_call_target="tpu_custom_call" | custom-call | flops 1000000000 | bytes 1048576 | tf_op jit(solution)/shard_map/pallas_call | solution.py:530
  10.8 0.0 copy-done
  10.8 0.0 copy-done.1
  10.8 0.0 copy-done.2
  10.8 0.7 shard_map.142
  11.5 0.0 collective-permute-done.3.far_col
  11.5 0.0 collective-permute-done.2.near_col
  11.6 1.8 %shard_map.143 = (f32[6,72,384]{2,1,0:T(8,128)S(1)}, f32[64,384]{1,0:T(8,128)S(1)}, s32[64,128]{1,0:T(8,128)S(1)}, s32[64,128]{1,0:T(8,128)S(1)}, s32[128,128]{1...) custom-call(f32[5,72,256]{2,1,0:T(8,128)S(1)} %get-tuple-element.54., ...), custom_call_target="tpu_custom_call" | custom-call | flops 1000000000 | bytes 1048576 | tf_op jit(solution)/shard_map/pallas_call | solution.py:530
  13.4 23.8 %all_to_all.15 = f32[128,1,768]{2,1,0:T(1,128)S(1)} all-to-all(f32[128,1,768]{2,1,0:T(1,128)S(1)} %bitcast.18), channel_id=1, replica_groups=mesh['row'=8,'col'=16] {'row','col'}, dimensions={0} | all-to-all | bytes 786432 | tf_op jit(solution)/shard_map/all_to_all | solution.py:621
  37.2 1.4 %shard_map.145 = (f32[64,384]{1,0:T(8,128)S(1)}, f32[12,128]{1,0:T(8,128)S(1)}, f32[12,128]{1,0:T(8,128)S(1)}, f32[64,128]{1,0:T(8,128)S(1)}, f32[128,128]{1,0:T(8,128)S(1)}) custom-call(f32[768,128]{1,0:T(8,128)S(1)} %bitcast.13, f32[64,384]{1,0:T(8,128)S(1)} %get-tuple-element.65.surface, f32[64,384]{1,0:T(8,128)S(1)} %get-tuple-element.66.inverse, ...), custom_call_target="tpu_custom_call" | custom-call | flops 1000000000 | bytes 1048576 | tf_op jit(solution)/shard_map/pallas_call | solution.py:530
  38.6 0.6 collective-permute-start.4
  39.2 0.3 collective-permute-start.5
  39.5 1.8 %shard_map.146 = (f32[64,128]{1,0:T(8,128)S(1)}, f32[64,128]{1,0:T(8,128)S(1)}) custom-call(f32[768,128]{1,0:T(8,128)S(1)} %bitcast.14, f32[64,128]{1,0:T(8,128)S(1)} %get-tuple-element.60.nodes, s32[64,128]{1,0:T(8,128)S(1)} %get-tuple-element.78.node_high, s32[64,128]{1,0:T(8,128)S(1)} %get-tuple-element.79.node_low, ...), custom_call_target="tpu_custom_call" | custom-call | flops 1000000000 | bytes 1048576 | tf_op jit(solution)/shard_map/pallas_call | solution.py:530
  41.3 0.0 collective-permute-done.4.near
  41.3 1.3 %collective-permute-done.5.far = f32[12,128]{1,0:T(8,128)S(1)} collective-permute-done((f32[12,128]{1,0:T(8,128)S(1)}, f32[12,128]{1,0:T(8,128)S(1)}, u32[]{:S(2)}, u32[]{:S(2)}) %collective-permute-start.5) | collective-permute-done | bytes 6176 | tf_op jit(solution)/shard_map/ppermute | solution.py:558
  42.5 1.5 %shard_map.147 = (f32[64,384]{1,0:T(8,128)S(1)}, f32[64,128]{1,0:T(8,128)S(1)}, f32[128,128]{1,0:T(8,128)S(1)}, f32[768,128]{1,0:T(8,128)S(1)}) custom-call(f32[64,384]{1,0:T(8,128)S(1)} %get-tuple-element.73.surface, f32[12,128]{1,0:T(8,128)S(1)} %collective-permute-done.4.near, f32[12,128]{1,0:T(8,128)S(1)} %collective-permute-done.5.far, ...), custom_call_target="tpu_custom_call" | custom-call | flops 1000000000 | bytes 1048576 | tf_op jit(solution)/shard_map/pallas_call | solution.py:530
  44.1 16.1 %all_to_all.16 = f32[128,1,768]{2,1,0:T(1,128)S(1)} all-to-all(f32[128,1,768]{2,1,0:T(1,128)S(1)} %bitcast.19), channel_id=1, replica_groups=mesh['row'=8,'col'=16] {'row','col'}, dimensions={0} | all-to-all | bytes 786432 | tf_op jit(solution)/shard_map/all_to_all | solution.py:621
  60.1 1.4 %shard_map.148 = (f32[64,384]{1,0:T(8,128)S(1)}, f32[12,128]{1,0:T(8,128)S(1)}, f32[12,128]{1,0:T(8,128)S(1)}) custom-call(f32[768,128]{1,0:T(8,128)S(1)} %bitcast.15, f32[64,384]{1,0:T(8,128)S(1)} %get-tuple-element.86.surface, f32[64,384]{1,0:T(8,128)S(1)} %get-tuple-element.66.inverse, f32[64,128]{1,0:T(8,128)S(1)} %get-tuple-element.87.heads, ...), custom_call_target="tpu_custom_call" | custom-call | flops 1000000000 | bytes 1048576 | tf_op jit(solution)/shard_map/pallas_call | solution.py:530
  61.5 0.8 collective-permute-start.6
  62.3 0.3 collective-permute-start.7
  62.6 1.8 %shard_map.149 = (f32[64,128]{1,0:T(8,128)S(1)}, f32[64,128]{1,0:T(8,128)S(1)}) custom-call(f32[768,128]{1,0:T(8,128)S(1)} %bitcast.16, f32[64,128]{1,0:T(8,128)S(1)} %get-tuple-element.84.nodes, s32[64,128]{1,0:T(8,128)S(1)} %get-tuple-element.78.node_high, s32[64,128]{1,0:T(8,128)S(1)} %get-tuple-element.79.node_low, ...), custom_call_target="tpu_custom_call" | custom-call | flops 1000000000 | bytes 1048576 | tf_op jit(solution)/shard_map/pallas_call | solution.py:530
  64.4 0.0 collective-permute-done.6.near
  64.4 1.3 %collective-permute-done.7.far = f32[12,128]{1,0:T(8,128)S(1)} collective-permute-done((f32[12,128]{1,0:T(8,128)S(1)}, f32[12,128]{1,0:T(8,128)S(1)}, u32[]{:S(2)}, u32[]{:S(2)}) %collective-permute-start.7) | collective-permute-done | bytes 6176 | tf_op jit(solution)/shard_map/ppermute | solution.py:558
  65.6 1.3 %shard_map.150 = (f32[64,384]{1,0:T(8,128)S(1)}, f32[64,128]{1,0:T(8,128)S(1)}, f32[128,128]{1,0:T(8,128)S(1)}, f32[640,128]{1,0:T(8,128)S(1)}) custom-call(f32[64,384]{1,0:T(8,128)S(1)} %get-tuple-element.91.surface, f32[12,128]{1,0:T(8,128)S(1)} %collective-permute-done.6.near, f32[12,128]{1,0:T(8,128)S(1)} %collective-permute-done.7.far, ...), custom_call_target="tpu_custom_call" | custom-call | flops 1000000000 | bytes 1048576 | tf_op jit(solution)/shard_map/pallas_call | solution.py:530
  66.9 15.4 %all_to_all.17 = f32[128,1,640]{2,1,0:T(1,128)S(1)} all-to-all(f32[128,1,640]{2,1,0:T(1,128)S(1)} %bitcast.20), channel_id=1, replica_groups=mesh['row'=8,'col'=16] {'row','col'}, dimensions={0} | all-to-all | bytes 655360 | tf_op jit(solution)/shard_map/all_to_all | solution.py:621
  82.3 3.2 %shard_map.151 = (f32[64,256]{1,0:T(8,128)}, f32[32,256]{1,0:T(8,128)}) custom-call(f32[640,128]{1,0:T(8,128)S(1)} %bitcast.17, f32[64,384]{1,0:T(8,128)S(1)} %get-tuple-element.97.surface, f32[64,384]{1,0:T(8,128)S(1)} %get-tuple-element.66.inverse, f32[64,128]{1,0:T(8,128)S(1)} %get-tuple-element.98.heads, f32[128,128]{1,0:T(8,128)S(1)} %get-tuple-element.99.zone, ...), custom_call_target="tpu_custom_call" | custom-call | flops 1000000000 | bytes 1048576 | tf_op jit(solution)/shard_map/pallas_call | solution.py:530
  (1 shorter events, 0.0 us)
Async XLA Ops:
  0.6 8.6 %copy-start.4 = (f32[128,1,64]{0,2,1:T(8,128)S(1)}, f32[128,1,64]{0,2,1:T(8,128)}, u32[]{:S(2)}) copy-start(f32[128,1,64]{0,2,1:T(8,128)} %param.25) | copy-start | bytes 98308
  0.6 8.5 %copy-start.3 = (s32[128,1,64]{0,2,1:T(8,128)S(1)}, s32[128,1,64]{0,2,1:T(8,128)}, u32[]{:S(2)}) copy-start(s32[128,1,64]{0,2,1:T(8,128)} %param.24) | copy-start | bytes 98308
  1.7 9.1 %copy-start = (f32[4,32,32]{2,1,0:T(8,128)S(1)}, f32[4,32,32]{2,1,0:T(8,128)}, u32[]{:S(2)}) copy-start(f32[4,32,32]{2,1,0:T(8,128)} %param.22) | copy-start | bytes 49156
  1.7 9.1 %copy-start.1 = (f32[32,256]{1,0:T(8,128)S(1)}, f32[32,256]{1,0:T(8,128)}, u32[]{:S(2)}) copy-start(f32[32,256]{1,0:T(8,128)} %pipes.3) | copy-start | bytes 98308
  1.7 9.1 %copy-start.2 = (s32[256]{0:T(256)S(1)}, s32[256]{0:T(256)}, u32[]{:S(2)}) copy-start(s32[256]{0:T(256)} %param.19) | copy-start | bytes 3076
  1.7 4.9 %collective-permute-start.1 = (f32[40,128]{1,0:T(8,128)S(1)}, f32[40,128]{1,0:T(8,128)S(1)}, u32[]{:S(2)}, u32[]{:S(2)}) collective-permute-start(f32[40,128]{1,0:T(8,128)S(1)} %get-tuple-element.52), channel_id=1, source_target_pairs={{0,1},{1,0},{2,3},{3,2},{4,5},{5,4},{6,7},{7,6},{8,9},{9,8},{10,11... | collective-permute-start | bytes 61448 | tf_op jit(solution)/shard_map/ppermute | solution.py:558
  4.4 2.2 %collective-permute-start = (f32[48,128]{1,0:T(8,128)S(1)}, f32[48,128]{1,0:T(8,128)S(1)}, u32[]{:S(2)}, u32[]{:S(2)}) collective-permute-start(f32[48,128]{1,0:T(8,128)S(1)} %get-tuple-element.51), channel_id=1, source_target_pairs={{0,16},{1,17},{2,18},{3,19},{4,20},{5,21},{6,22},{7,23},{8,24},{9,... | collective-permute-start | bytes 73736 | tf_op jit(solution)/shard_map/ppermute | solution.py:557
  6.8 4.8 %collective-permute-start.3 = (f32[136,128]{1,0:T(8,128)S(1)}, f32[136,128]{1,0:T(8,128)S(1)}, u32[]{:S(2)}, u32[]{:S(2)}) collective-permute-start(f32[136,128]{1,0:T(8,128)S(1)} %get-tuple-element.56), channel_id=1, source_target_pairs={{0,16},{1,2},{2,1},{3,4},{4,3},{5,6},{6,5},{7,8},{8,7},{9,10},{10,... | collective-permute-start | bytes 208904 | tf_op jit(solution)/shard_map/ppermute | solution.py:558
  7.2 4.3 %collective-permute-start.2 = (f32[136,128]{1,0:T(8,128)S(1)}, f32[136,128]{1,0:T(8,128)S(1)}, u32[]{:S(2)}, u32[]{:S(2)}) collective-permute-start(f32[136,128]{1,0:T(8,128)S(1)} %get-tuple-element.56), channel_id=1, source_target_pairs={{0,1},{1,0},{2,3},{3,2},{4,5},{5,4},{6,7},{7,6},{8,9},{9,8},{10,11... | collective-permute-start | bytes 208904 | tf_op jit(solution)/shard_map/ppermute | solution.py:557
  38.6 2.7 %collective-permute-start.4 = (f32[12,128]{1,0:T(8,128)S(1)}, f32[12,128]{1,0:T(8,128)S(1)}, u32[]{:S(2)}, u32[]{:S(2)}) collective-permute-start(f32[12,128]{1,0:T(8,128)S(1)} %get-tuple-element.74), channel_id=1, source_target_pairs={{0,16},{1,17},{2,18},{3,19},{4,20},{5,21},{6,22},{7,23},{8,24},{9,... | collective-permute-start | bytes 18440 | tf_op jit(solution)/shard_map/ppermute | solution.py:557
  39.2 3.3 %collective-permute-start.5 = (f32[12,128]{1,0:T(8,128)S(1)}, f32[12,128]{1,0:T(8,128)S(1)}, u32[]{:S(2)}, u32[]{:S(2)}) collective-permute-start(f32[12,128]{1,0:T(8,128)S(1)} %get-tuple-element.75), channel_id=1, source_target_pairs={{0,1},{1,0},{2,3},{3,2},{4,5},{5,4},{6,7},{7,6},{8,9},{9,8},{10,11... | collective-permute-start | bytes 18440 | tf_op jit(solution)/shard_map/ppermute | solution.py:558
  61.5 2.9 %collective-permute-start.6 = (f32[12,128]{1,0:T(8,128)S(1)}, f32[12,128]{1,0:T(8,128)S(1)}, u32[]{:S(2)}, u32[]{:S(2)}) collective-permute-start(f32[12,128]{1,0:T(8,128)S(1)} %get-tuple-element.92), channel_id=1, source_target_pairs={{0,16},{1,17},{2,18},{3,19},{4,20},{5,21},{6,22},{7,23},{8,24},{9,... | collective-permute-start | bytes 18440 | tf_op jit(solution)/shard_map/ppermute | solution.py:557
  62.3 3.3 %collective-permute-start.7 = (f32[12,128]{1,0:T(8,128)S(1)}, f32[12,128]{1,0:T(8,128)S(1)}, u32[]{:S(2)}, u32[]{:S(2)}) collective-permute-start(f32[12,128]{1,0:T(8,128)S(1)} %get-tuple-element.93), channel_id=1, source_target_pairs={{0,1},{1,0},{2,3},{3,2},{4,5},{5,4},{6,7},{7,6},{8,9},{9,8},{10,11... | collective-permute-start | bytes 18440 | tf_op jit(solution)/shard_map/ppermute | solution.py:558

commit v8 on v7

--- a/solution.py
+++ b/solution.py
@@ -253,9 +253,12 @@
 
 
 def owner_start_kernel(
-    pipes, link_node, link_coef, kinds, laws, table, nodes, node_high, node_low, coef, classes,
-    matrices,
-):
+    pipes, link_node, link_coef, kinds, laws, uppers, lowers, table, nodes, node_high, node_low,
+    coef, classes, matrices, meets,
+):
+    meets[...] = jnp.concatenate(
+        [uppers[...], lowers[...], jnp.zeros((4, 128), jnp.int32)], axis=0
+    )
     classes[...] = kinds[...]
     matrices[...] = laws[...]
     table[...] = pipe_table(pipes[...])
@@ -506,21 +509,6 @@
     nodes_out[...] = gathered(table_out, 64, node_high[...], node_low[...])
 
 
-def final_kernel(
-    got, surface, inverse, heads, zone, cell_high, hot, zone_row, zone_col, own_coef, zone_coef,
-    nodes, node_high, node_low, coef, table, meets, classes, matrices, surface_out,
-    pipes_out, cell_value_ref, zone_value_ref, row_ref, node_value_ref, ends_ref,
-):
-    owner_kernel(
-        False, True, got, nodes, node_high, node_low, coef, table, meets, classes,
-        matrices, pipes_out, node_value_ref, ends_ref,
-    )
-    tile_kernel(
-        False, True, got, surface, inverse, heads, zone, cell_high, hot, zone_row, zone_col,
-        own_coef, zone_coef, surface_out, cell_value_ref, zone_value_ref, row_ref,
-    )
-
-
 def shape(*dims, dtype=F32):
     return jax.ShapeDtypeStruct(dims, dtype)
 
@@ -564,9 +552,7 @@
     pipe_down, pipe_matrices, link_cell, link_node, link_coef,
 ):
     link_cell = link_cell[0]
-    meets = jnp.concatenate(
-        [pipe_up.reshape(2, 128), pipe_down.reshape(2, 128), jnp.zeros((4, 128), jnp.int32)], axis=0
-    )
+    uppers, lowers = pipe_up.reshape(2, 128), pipe_down.reshape(2, 128)
     classes = pipe_class.reshape(2, 128)
     matrices = pipe_matrices.reshape(CLASSES * 32, 32)
     ints = functools.partial(shape, dtype=jnp.int32)
@@ -590,10 +576,10 @@
     link_node = link_node[:, 0, :]
     link_coef = link_coef[:, 0, :]
     near_col, far_col = swapped(sent, sent, 1)
-    table, nodes, node_high, node_low, coef, classes, matrices = call(
-        owner_start_kernel, (pipe_head, link_node, link_coef, classes, matrices),
+    table, nodes, node_high, node_low, coef, classes, matrices, meets = call(
+        owner_start_kernel, (pipe_head, link_node, link_coef, classes, matrices, uppers, lowers),
         [shape(64, 128), shape(64, 128), ints(64, 128), ints(64, 128), shape(64, 128),
-         ints(2, 128), shape(128, 32)],
+         ints(2, 128), shape(128, 32), ints(8, 128)],
     )
     (hot,) = call(columns_kernel, (cells,), [shape(8192, 256, dtype=BF16)])
     gather_scratch = [
@@ -607,7 +593,7 @@
          ints(128, 128), *swept_shapes, shape(768, 128)],
         gather_scratch,
     )
-    sent, meets, hot = lax.optimization_barrier((sent, meets, hot))
+    sent, hot = lax.optimization_barrier((sent, hot))
     coefs = ()
     for step in range(STEPS):
         first, last = step == 0, step == STEPS - 1
@@ -628,10 +614,15 @@
         ]
         owner_scratch = [pltpu.VMEM((64, 128), F32), pltpu.VMEM((64, 128), F32)]
         if last:
-            return tuple(call(
-                final_kernel, (got, *tile_inputs, *owner_inputs),
-                [shape(64, 256), shape(32, 256)], tile_scratch + owner_scratch,
-            ))
+            (pipes_out,) = call(
+                functools.partial(owner_kernel, False, True), (got, *owner_inputs),
+                [shape(32, 256)], owner_scratch,
+            )
+            (surface_out,) = call(
+                functools.partial(tile_kernel, False, True), (got, *tile_inputs), [shape(64, 256)],
+                tile_scratch,
+            )
+            return surface_out, pipes_out
         outputs = [shape(64, 384), shape(12, 128), shape(12, 128)]
         if first:
             outputs += [shape(64, 128), shape(128, 128)]

time: 85.9 us -> 86 us (level)
  waiting for transfers between devices: 2.52 us -> 3.43 us
    ppermute x4, starting transfers between devices: 3.79 us -> 2.55 us  [swapped(): lax.ppermute(far, ('row', 'col'), routes[1])]
    ppermute x4, starting transfers between devices: 3.81 us -> 5.04 us  [swapped(): lax.ppermute(near, ('row', 'col'), routes[0])]
    ppermute x4, waiting for transfers between devices: 2.51 us -> 3.42 us  [swapped(): lax.ppermute(far, ('row', 'col'), routes[1])]
    pallas_call x12 -> x13, Pallas kernels: 17.4 us -> 17.2 us  [call(): pl.pallas_call(kernel, out_shape=outputs, in_specs=[pl.BlockSpec(memory_s...]
  transfers between devices with their start and end apart: 8 -> 8, of which waited for: 2 -> 3; matrix products, arithmetic and copies ran while one was open for 2% -> 1% of each run, Pallas kernels for 7% -> 7%
where the time goes in v8:
time: 86 us; the launch traced here: 85.7 us
  blocking collectives  55.5 us (65%)
  Pallas kernels  17.2 us (20%)
  starting transfers between devices  7.59 us (9%)
  waiting for transfers between devices  3.43 us (4%)
  local copies, waits for them, and re-layouts  1.07 us (1%)
  between operations  0.86 us (1%)
    all_to_all x3, blocking collectives, body(): lax.all_to_all(sent.reshape(128, 1, -1), ('row', 'col'), split_axis=0, co...  55.5 us
    pallas_call x13, Pallas kernels, call(): pl.pallas_call(kernel, out_shape=outputs, in_specs=[pl.BlockSpec(memory_s...  17.2 us
    ppermute x4, starting transfers between devices, swapped(): lax.ppermute(near, ('row', 'col'), routes[0])  5.04 us
    ppermute x4, waiting for transfers between devices, swapped(): lax.ppermute(far, ('row', 'col'), routes[1])  3.42 us
    ppermute x4, starting transfers between devices, swapped(): lax.ppermute(far, ('row', 'col'), routes[1])  2.55 us
  transfers between devices with their start and end apart: 8, of which 3 were waited for; matrix products, arithmetic and copies ran while one was open for 1% of the time, Pallas kernels for 7%

profile of v8, /device:TPU:1, one launch (start us, length us, event | category | flops | bytes accessed | tf_op | source)
XLA Modules:
  0.0 85.7 jit_solution(17989348208415268583)
XLA Ops:
  0.6 0.0 copy-start.6
  0.6 0.0 copy-start.5
  0.7 1.0 %shard_map.140 = (f32[5,64,256]{2,1,0:T(8,128)S(1)}, f32[48,128]{1,0:T(8,128)S(1)}, f32[40,128]{1,0:T(8,128)S(1)}) custom-call(f32[64,256]{1,0:T(8,128)} %surface.1, f32[64,256]{1,0:T(8,128)} %cond_x.1, f32[64,256]{1,0:T(8,128)} %cond_y.1, f32[64,256]{1,0:T(8,128)} %porosity.1, f32[64,256]{1,0:T(8,128)} %rainfall.1, f32[32,256]{1,0:T(8,128)} %pipes.3), custom_call_target="tpu_custom_call" | custom-call | flops 1000000000 | bytes 1048576 | tf_op jit(solution)/shard_map/pallas_call | solution.py:518
  1.7 0.0 copy-start
  1.7 0.0 copy-start.1
  1.7 0.0 copy-start.2
  1.7 0.0 copy-start.3
  1.8 0.0 copy-start.4
  1.8 1.5 %collective-permute-start = (f32[48,128]{1,0:T(8,128)S(1)}, f32[48,128]{1,0:T(8,128)S(1)}, u32[]{:S(2)}, u32[]{:S(2)}) collective-permute-start(f32[48,128]{1,0:T(8,128)S(1)} %get-tuple-element.51), channel_id=1, source_target_pairs={{0,16},{1,17},{2,18},{3,19},{4,20},{5,21},{6,22},{7,23},{8,24},{9,... | collective-permute-start | bytes 73736 | tf_op jit(solution)/shard_map/ppermute | solution.py:545
  3.3 1.3 %collective-permute-start.1 = (f32[40,128]{1,0:T(8,128)S(1)}, f32[40,128]{1,0:T(8,128)S(1)}, u32[]{:S(2)}, u32[]{:S(2)}) collective-permute-start(f32[40,128]{1,0:T(8,128)S(1)} %get-tuple-element.52), channel_id=1, source_target_pairs={{0,1},{1,0},{2,3},{3,2},{4,5},{5,4},{6,7},{7,6},{8,9},{9,8},{10,11... | collective-permute-start | bytes 61448 | tf_op jit(solution)/shard_map/ppermute | solution.py:546
  4.5 0.8 copy.18
  5.4 1.4 %collective-permute-done.1.far = f32[40,128]{1,0:T(8,128)S(1)} collective-permute-done((f32[40,128]{1,0:T(8,128)S(1)}, f32[40,128]{1,0:T(8,128)S(1)}, u32[]{:S(2)}, u32[]{:S(2)}) %collective-permute-start.1) | collective-permute-done | bytes 20512 | tf_op jit(solution)/shard_map/ppermute | solution.py:546
  6.8 0.0 collective-permute-done.near
  6.8 0.1 shard_map.141
  6.9 0.5 collective-permute-start.3
  7.4 2.3 %collective-permute-start.2 = (f32[136,128]{1,0:T(8,128)S(1)}, f32[136,128]{1,0:T(8,128)S(1)}, u32[]{:S(2)}, u32[]{:S(2)}) collective-permute-start(f32[136,128]{1,0:T(8,128)S(1)} %get-tuple-element.56), channel_id=1, source_target_pairs={{0,1},{1,0},{2,3},{3,2},{4,5},{5,4},{6,7},{7,6},{8,9},{9,8},{10,11... | collective-permute-start | bytes 208904 | tf_op jit(solution)/shard_map/ppermute | solution.py:545
  9.6 0.0 copy-done.5
  9.6 0.1 copy.19
  9.7 0.0 copy-done.6
  9.7 0.1 copy.20
  9.8 1.5 %shard_map.144.hot = bf16[8192,256]{1,0:T(8,128)(2,1)S(1)} custom-call(s32[128,64]{1,0:T(8,128)S(1)} %bitcast.23), custom_call_target="tpu_custom_call" | custom-call | flops 1000000000 | bytes 1048576 | tf_op jit(solution)/shard_map/pallas_call | solution.py:518
  11.3 0.0 copy-done
  11.3 0.0 copy-done.1
  11.3 0.0 copy-done.2
  11.3 0.0 copy-done.3
  11.3 0.0 copy-done.4
  11.4 0.7 shard_map.142
  12.1 0.0 collective-permute-done.3.far_col
  12.1 0.0 collective-permute-done.2.near_col
  12.1 1.8 %shard_map.143 = (f32[6,72,384]{2,1,0:T(8,128)S(1)}, f32[64,384]{1,0:T(8,128)S(1)}, s32[64,128]{1,0:T(8,128)S(1)}, s32[64,128]{1,0:T(8,128)S(1)}, s32[128,128]{1...) custom-call(f32[5,72,256]{2,1,0:T(8,128)S(1)} %get-tuple-element.54., ...), custom_call_target="tpu_custom_call" | custom-call | flops 1000000000 | bytes 1048576 | tf_op jit(solution)/shard_map/pallas_call | solution.py:518
  13.9 23.6 %all_to_all.15 = f32[128,1,768]{2,1,0:T(1,128)S(1)} all-to-all(f32[128,1,768]{2,1,0:T(1,128)S(1)} %bitcast.19), channel_id=1, replica_groups=mesh['row'=8,'col'=16] {'row','col'}, dimensions={0} | all-to-all | bytes 786432 | tf_op jit(solution)/shard_map/all_to_all | solution.py:607
  37.5 1.4 %shard_map.145 = (f32[64,384]{1,0:T(8,128)S(1)}, f32[12,128]{1,0:T(8,128)S(1)}, f32[12,128]{1,0:T(8,128)S(1)}, f32[64,128]{1,0:T(8,128)S(1)}, f32[128,128]{1,0:T(8,128)S(1)}) custom-call(f32[768,128]{1,0:T(8,128)S(1)} %bitcast.13, f32[64,384]{1,0:T(8,128)S(1)} %get-tuple-element.65.surface, f32[64,384]{1,0:T(8,128)S(1)} %get-tuple-element.66.inverse, ...), custom_call_target="tpu_custom_call" | custom-call | flops 1000000000 | bytes 1048576 | tf_op jit(solution)/shard_map/pallas_call | solution.py:518
  38.9 0.6 collective-permute-start.4
  39.5 0.3 collective-permute-start.5
  39.8 1.8 %shard_map.146 = (f32[64,128]{1,0:T(8,128)S(1)}, f32[64,128]{1,0:T(8,128)S(1)}) custom-call(f32[768,128]{1,0:T(8,128)S(1)} %bitcast.14, f32[64,128]{1,0:T(8,128)S(1)} %get-tuple-element.60.nodes, s32[64,128]{1,0:T(8,128)S(1)} %get-tuple-element.78.node_high, s32[64,128]{1,0:T(8,128)S(1)} %get-tuple-element.79.node_low, ...), custom_call_target="tpu_custom_call" | custom-call | flops 1000000000 | bytes 1048576 | tf_op jit(solution)/shard_map/pallas_call | solution.py:518
  41.6 0.0 collective-permute-done.4.near
  41.6 1.3 %collective-permute-done.5.far = f32[12,128]{1,0:T(8,128)S(1)} collective-permute-done((f32[12,128]{1,0:T(8,128)S(1)}, f32[12,128]{1,0:T(8,128)S(1)}, u32[]{:S(2)}, u32[]{:S(2)}) %collective-permute-start.5) | collective-permute-done | bytes 6176 | tf_op jit(solution)/shard_map/ppermute | solution.py:546
  42.8 1.5 %shard_map.147 = (f32[64,384]{1,0:T(8,128)S(1)}, f32[64,128]{1,0:T(8,128)S(1)}, f32[128,128]{1,0:T(8,128)S(1)}, f32[768,128]{1,0:T(8,128)S(1)}) custom-call(f32[64,384]{1,0:T(8,128)S(1)} %get-tuple-element.73.surface, f32[12,128]{1,0:T(8,128)S(1)} %collective-permute-done.4.near, f32[12,128]{1,0:T(8,128)S(1)} %collective-permute-done.5.far, ...), custom_call_target="tpu_custom_call" | custom-call | flops 1000000000 | bytes 1048576 | tf_op jit(solution)/shard_map/pallas_call | solution.py:518
  44.4 16.1 %all_to_all.16 = f32[128,1,768]{2,1,0:T(1,128)S(1)} all-to-all(f32[128,1,768]{2,1,0:T(1,128)S(1)} %bitcast.20), channel_id=1, replica_groups=mesh['row'=8,'col'=16] {'row','col'}, dimensions={0} | all-to-all | bytes 786432 | tf_op jit(solution)/shard_map/all_to_all | solution.py:607
  60.4 1.4 %shard_map.148 = (f32[64,384]{1,0:T(8,128)S(1)}, f32[12,128]{1,0:T(8,128)S(1)}, f32[12,128]{1,0:T(8,128)S(1)}) custom-call(f32[768,128]{1,0:T(8,128)S(1)} %bitcast.15, f32[64,384]{1,0:T(8,128)S(1)} %get-tuple-element.86.surface, f32[64,384]{1,0:T(8,128)S(1)} %get-tuple-element.66.inverse, f32[64,128]{1,0:T(8,128)S(1)} %get-tuple-element.87.heads, ...), custom_call_target="tpu_custom_call" | custom-call | flops 1000000000 | bytes 1048576 | tf_op jit(solution)/shard_map/pallas_call | solution.py:518
  61.8 0.6 collective-permute-start.6
  62.4 0.5 collective-permute-start.7
  62.9 1.8 %shard_map.149 = (f32[64,128]{1,0:T(8,128)S(1)}, f32[64,128]{1,0:T(8,128)S(1)}) custom-call(f32[768,128]{1,0:T(8,128)S(1)} %bitcast.16, f32[64,128]{1,0:T(8,128)S(1)} %get-tuple-element.84.nodes, s32[64,128]{1,0:T(8,128)S(1)} %get-tuple-element.78.node_high, s32[64,128]{1,0:T(8,128)S(1)} %get-tuple-element.79.node_low, ...), custom_call_target="tpu_custom_call" | custom-call | flops 1000000000 | bytes 1048576 | tf_op jit(solution)/shard_map/pallas_call | solution.py:518
  64.7 0.0 collective-permute-done.6.near
  64.7 0.8 collective-permute-done.7.far
  65.5 1.3 %shard_map.150 = (f32[64,384]{1,0:T(8,128)S(1)}, f32[64,128]{1,0:T(8,128)S(1)}, f32[128,128]{1,0:T(8,128)S(1)}, f32[640,128]{1,0:T(8,128)S(1)}) custom-call(f32[64,384]{1,0:T(8,128)S(1)} %get-tuple-element.91.surface, f32[12,128]{1,0:T(8,128)S(1)} %collective-permute-done.6.near, f32[12,128]{1,0:T(8,128)S(1)} %collective-permute-done.7.far, ...), custom_call_target="tpu_custom_call" | custom-call | flops 1000000000 | bytes 1048576 | tf_op jit(solution)/shard_map/pallas_call | solution.py:518
  66.8 15.8 %all_to_all.17 = f32[128,1,640]{2,1,0:T(1,128)S(1)} all-to-all(f32[128,1,640]{2,1,0:T(1,128)S(1)} %bitcast.21), channel_id=1, replica_groups=mesh['row'=8,'col'=16] {'row','col'}, dimensions={0} | all-to-all | bytes 655360 | tf_op jit(solution)/shard_map/all_to_all | solution.py:607
  82.6 1.6 %shard_map.152 = f32[32,256]{1,0:T(8,128)} custom-call(f32[640,128]{1,0:T(8,128)S(1)} %bitcast.17, f32[64,128]{1,0:T(8,128)S(1)} %get-tuple-element.95.nodes, s32[64,128]{1,0:T(8,128)S(1)} %get-tuple-element.78.node_high, s32[64,128]{1,0:T(8,128)S(1)} %get-tuple-element.79.node_low, f32[64,128]{1,0:T(8,128)S(1)} %get-tuple-element.61.coef, ...), custom_call_target="tpu_custom_call" | custom-call | flops 1000000000 | bytes 1048576 | tf_op jit(solution)/shard_map/pallas_call | solution.py:518
  84.3 1.4 %shard_map.151 = f32[64,256]{1,0:T(8,128)} custom-call(f32[640,128]{1,0:T(8,128)S(1)} %bitcast.18, f32[64,384]{1,0:T(8,128)S(1)} %get-tuple-element.97.surface, f32[64,384]{1,0:T(8,128)S(1)} %get-tuple-element.66.inverse, f32[64,128]{1,0:T(8,128)S(1)} %get-tuple-element.98.heads, f32[128,128]{1,0:T(8,128)S(1)} %get-tuple-element.99.zone, ...), custom_call_target="tpu_custom_call" | custom-call | flops 1000000000 | bytes 1048576 | tf_op jit(solution)/shard_map/pallas_call | solution.py:518
Async XLA Ops:
  0.6 9.1 %copy-start.6 = (f32[128,1,64]{0,2,1:T(8,128)S(1)}, f32[128,1,64]{0,2,1:T(8,128)}, u32[]{:S(2)}) copy-start(f32[128,1,64]{0,2,1:T(8,128)} %param.25) | copy-start | bytes 98308
  0.6 9.0 %copy-start.5 = (s32[128,1,64]{0,2,1:T(8,128)S(1)}, s32[128,1,64]{0,2,1:T(8,128)}, u32[]{:S(2)}) copy-start(s32[128,1,64]{0,2,1:T(8,128)} %param.24) | copy-start | bytes 98308
  1.7 9.6 %copy-start = (f32[4,32,32]{2,1,0:T(8,128)S(1)}, f32[4,32,32]{2,1,0:T(8,128)}, u32[]{:S(2)}) copy-start(f32[4,32,32]{2,1,0:T(8,128)} %param.22) | copy-start | bytes 49156
  1.7 9.6 %copy-start.1 = (f32[32,256]{1,0:T(8,128)S(1)}, f32[32,256]{1,0:T(8,128)}, u32[]{:S(2)}) copy-start(f32[32,256]{1,0:T(8,128)} %pipes.3) | copy-start | bytes 98308
  1.7 9.6 %copy-start.2 = (s32[256]{0:T(256)S(1)}, s32[256]{0:T(256)}, u32[]{:S(2)}) copy-start(s32[256]{0:T(256)} %param.19) | copy-start | bytes 3076
  1.7 9.6 %copy-start.3 = (s32[256]{0:T(256)S(1)}, s32[256]{0:T(256)}, u32[]{:S(2)}) copy-start(s32[256]{0:T(256)} %param.20) | copy-start | bytes 3076
  1.8 9.6 %copy-start.4 = (s32[256]{0:T(256)S(1)}, s32[256]{0:T(256)}, u32[]{:S(2)}) copy-start(s32[256]{0:T(256)} %param.21) | copy-start | bytes 3076
  1.8 5.0 %collective-permute-start = (f32[48,128]{1,0:T(8,128)S(1)}, f32[48,128]{1,0:T(8,128)S(1)}, u32[]{:S(2)}, u32[]{:S(2)}) collective-permute-start(f32[48,128]{1,0:T(8,128)S(1)} %get-tuple-element.51), channel_id=1, source_target_pairs={{0,16},{1,17},{2,18},{3,19},{4,20},{5,21},{6,22},{7,23},{8,24},{9,... | collective-permute-start | bytes 73736 | tf_op jit(solution)/shard_map/ppermute | solution.py:545
  3.3 3.5 %collective-permute-start.1 = (f32[40,128]{1,0:T(8,128)S(1)}, f32[40,128]{1,0:T(8,128)S(1)}, u32[]{:S(2)}, u32[]{:S(2)}) collective-permute-start(f32[40,128]{1,0:T(8,128)S(1)} %get-tuple-element.52), channel_id=1, source_target_pairs={{0,1},{1,0},{2,3},{3,2},{4,5},{5,4},{6,7},{7,6},{8,9},{9,8},{10,11... | collective-permute-start | bytes 61448 | tf_op jit(solution)/shard_map/ppermute | solution.py:546
  6.9 5.2 %collective-permute-start.3 = (f32[136,128]{1,0:T(8,128)S(1)}, f32[136,128]{1,0:T(8,128)S(1)}, u32[]{:S(2)}, u32[]{:S(2)}) collective-permute-start(f32[136,128]{1,0:T(8,128)S(1)} %get-tuple-element.56), channel_id=1, source_target_pairs={{0,16},{1,2},{2,1},{3,4},{4,3},{5,6},{6,5},{7,8},{8,7},{9,10},{10,... | collective-permute-start | bytes 208904 | tf_op jit(solution)/shard_map/ppermute | solution.py:546
  7.4 4.7 %collective-permute-start.2 = (f32[136,128]{1,0:T(8,128)S(1)}, f32[136,128]{1,0:T(8,128)S(1)}, u32[]{:S(2)}, u32[]{:S(2)}) collective-permute-start(f32[136,128]{1,0:T(8,128)S(1)} %get-tuple-element.56), channel_id=1, source_target_pairs={{0,1},{1,0},{2,3},{3,2},{4,5},{5,4},{6,7},{7,6},{8,9},{9,8},{10,11... | collective-permute-start | bytes 208904 | tf_op jit(solution)/shard_map/ppermute | solution.py:545
  38.9 2.7 %collective-permute-start.4 = (f32[12,128]{1,0:T(8,128)S(1)}, f32[12,128]{1,0:T(8,128)S(1)}, u32[]{:S(2)}, u32[]{:S(2)}) collective-permute-start(f32[12,128]{1,0:T(8,128)S(1)} %get-tuple-element.74), channel_id=1, source_target_pairs={{0,16},{1,17},{2,18},{3,19},{4,20},{5,21},{6,22},{7,23},{8,24},{9,... | collective-permute-start | bytes 18440 | tf_op jit(solution)/shard_map/ppermute | solution.py:545
  39.5 3.3 %collective-permute-start.5 = (f32[12,128]{1,0:T(8,128)S(1)}, f32[12,128]{1,0:T(8,128)S(1)}, u32[]{:S(2)}, u32[]{:S(2)}) collective-permute-start(f32[12,128]{1,0:T(8,128)S(1)} %get-tuple-element.75), channel_id=1, source_target_pairs={{0,1},{1,0},{2,3},{3,2},{4,5},{5,4},{6,7},{7,6},{8,9},{9,8},{10,11... | collective-permute-start | bytes 18440 | tf_op jit(solution)/shard_map/ppermute | solution.py:546
  61.8 2.9 %collective-permute-start.6 = (f32[12,128]{1,0:T(8,128)S(1)}, f32[12,128]{1,0:T(8,128)S(1)}, u32[]{:S(2)}, u32[]{:S(2)}) collective-permute-start(f32[12,128]{1,0:T(8,128)S(1)} %get-tuple-element.92), channel_id=1, source_target_pairs={{0,16},{1,17},{2,18},{3,19},{4,20},{5,21},{6,22},{7,23},{8,24},{9,... | collective-permute-start | bytes 18440 | tf_op jit(solution)/shard_map/ppermute | solution.py:545
  62.4 3.1 %collective-permute-start.7 = (f32[12,128]{1,0:T(8,128)S(1)}, f32[12,128]{1,0:T(8,128)S(1)}, u32[]{:S(2)}, u32[]{:S(2)}) collective-permute-start(f32[12,128]{1,0:T(8,128)S(1)} %get-tuple-element.93), channel_id=1, source_target_pairs={{0,1},{1,0},{2,3},{3,2},{4,5},{5,4},{6,7},{7,6},{8,9},{9,8},{10,11... | collective-permute-start | bytes 18440 | tf_op jit(solution)/shard_map/ppermute | solution.py:546

commit v9 on v8

--- a/solution.py
+++ b/solution.py
@@ -526,7 +526,11 @@
     )(*inputs)
 
 
-def swapped(near, far, dim):
+def copy_kernel(source, out):
+    out[...] = source[...]
+
+
+def swapped(near, far, dim, copied=None):
     sizes = lax.axis_size("row"), lax.axis_size("col")
     routes = [], []
     for row in range(sizes[0]):
@@ -541,10 +545,12 @@
                 other[1 - dim] ^= 1
             for route, there in zip(routes, (partner, other)):
                 route.append((row * sizes[1] + col, there[0] * sizes[1] + there[1]))
-    return (
-        lax.ppermute(near, ("row", "col"), routes[0]),
-        lax.ppermute(far, ("row", "col"), routes[1]),
-    )
+    if copied == "near":
+        (near,) = call(copy_kernel, (near,), [shape(*near.shape)])
+    if copied == "far":
+        (far,) = call(copy_kernel, (far,), [shape(*far.shape)])
+    far = lax.ppermute(far, ("row", "col"), routes[1])
+    return lax.ppermute(near, ("row", "col"), routes[0]), far
 
 
 def body(
@@ -565,22 +571,21 @@
         [shape(5, 64, 256), shape(48, 128), shape(40, 128)],
         [pltpu.VMEM((8, 256), F32), pltpu.SemaphoreType.DMA((6,))], space=pltpu.HBM,
     )
-    near, far = swapped(near, far, 0)
-    tall, sent = call(
-        pack_cols_kernel, (near, far, fields, link_cell),
-        [shape(5, 72, 256), shape(136, 128)],
-    )
-    sent, link_node, link_coef, cells = lax.optimization_barrier(
-        (sent, link_node, link_coef, link_cell)
-    )
+    near, far = swapped(near, far, 0, "near")
     link_node = link_node[:, 0, :]
     link_coef = link_coef[:, 0, :]
-    near_col, far_col = swapped(sent, sent, 1)
     table, nodes, node_high, node_low, coef, classes, matrices, meets = call(
         owner_start_kernel, (pipe_head, link_node, link_coef, classes, matrices, uppers, lowers),
         [shape(64, 128), shape(64, 128), ints(64, 128), ints(64, 128), shape(64, 128),
          ints(2, 128), shape(128, 32), ints(8, 128)],
     )
+    near, far, nodes = lax.optimization_barrier((near, far, nodes))
+    tall, sent = call(
+        pack_cols_kernel, (near, far, fields, link_cell),
+        [shape(5, 72, 256), shape(136, 128)],
+    )
+    sent, cells = lax.optimization_barrier((sent, link_cell))
+    near_col, far_col = swapped(sent, sent, 1)
     (hot,) = call(columns_kernel, (cells,), [shape(8192, 256, dtype=BF16)])
     gather_scratch = [
         pltpu.VMEM((128, 128), F32), pltpu.VMEM((64, 128), F32), pltpu.VMEM((8, 128), F32)
@@ -630,7 +635,7 @@
             functools.partial(tile_kernel, first, False), (got, *tile_inputs), outputs,
             tile_scratch,
         )
-        near, far = swapped(near, far, 0)
+        near, far = swapped(near, far, 0, "far")
         table, nodes = call(
             functools.partial(owner_kernel, first, False), (got, *owner_inputs),
             [shape(64, 128), shape(64, 128)], owner_scratch,

time: 86 us -> 85.5 us (level)
  waiting for transfers between devices: 3.43 us -> 0.5 us
  blocking collectives: 55.5 us -> 57.9 us
    ppermute x8, waiting for transfers between devices: 3.43 us -> 0.5 us  [the longest x4 0.26 us: swapped(): return (lax.ppermute(near, ('row', 'col'), routes[0]), far)]
    all_to_all x3, blocking collectives: 55.5 us -> 57.9 us  [body(): lax.all_to_all(sent.reshape(128, 1, -1), ('row', 'col'), split_axis=0, co...]
    pallas_call x13 -> x16, Pallas kernels: 17.2 us -> 17.3 us  [call(): pl.pallas_call(kernel, out_shape=outputs, in_specs=[pl.BlockSpec(memory_s...]
  transfers between devices with their start and end apart: 8 -> 8, of which waited for: 3 -> 3; matrix products, arithmetic and copies ran while one was open for 1% -> 0% of each run, Pallas kernels for 7% -> 7%
where the time goes in v9:
time: 85.5 us; the launch traced here: 85.3 us
  blocking collectives  57.9 us (68%)
  Pallas kernels  17.3 us (20%)
  starting transfers between devices  8.43 us (10%)
  between operations  0.89 us (1%)
    all_to_all x3, blocking collectives, body(): lax.all_to_all(sent.reshape(128, 1, -1), ('row', 'col'), split_axis=0, co...  57.9 us
    pallas_call x16, Pallas kernels, call(): pl.pallas_call(kernel, out_shape=outputs, in_specs=[pl.BlockSpec(memory_s...  17.3 us
    ppermute x4, starting transfers between devices, swapped(): far = lax.ppermute(far, ('row', 'col'), routes[1])  5.67 us
    ppermute x4, starting transfers between devices, swapped(): return (lax.ppermute(near, ('row', 'col'), routes[0]), far)  2.76 us
  transfers between devices with their start and end apart: 8, of which 3 were waited for; matrix products, arithmetic and copies ran while one was open for 0% of the time, Pallas kernels for 7%

profile of v9, /device:TPU:1, one launch (start us, length us, event | category | flops | bytes accessed | tf_op | source)
XLA Modules:
  0.0 85.3 jit_solution(398211654893454454)
XLA Ops:
  0.6 0.0 copy-start.1
  0.6 0.0 copy-start.5
  0.7 0.0 copy-start.6
  0.7 0.0 copy-start
  0.7 0.0 copy-start.4
  0.7 0.0 copy-start.3
  0.7 0.0 copy-start.2
  0.7 1.1 %shard_map.140 = (f32[5,64,256]{2,1,0:T(8,128)S(1)}, f32[48,128]{1,0:T(8,128)S(1)}, f32[40,128]{1,0:T(8,128)S(1)}) custom-call(f32[64,256]{1,0:T(8,128)} %surface.1, f32[64,256]{1,0:T(8,128)} %cond_x.1, f32[64,256]{1,0:T(8,128)} %cond_y.1, f32[64,256]{1,0:T(8,128)} %porosity.1, f32[64,256]{1,0:T(8,128)} %rainfall.1, f32[32,256]{1,0:T(8,128)} %pipes.3), custom_call_target="tpu_custom_call" | custom-call | flops 1000000000 | bytes 1048576 | tf_op jit(solution)/shard_map/pallas_call | solution.py:518
  1.8 0.0 copy-start.7
  1.8 2.7 %collective-permute-start.1 = (f32[40,128]{1,0:T(8,128)S(1)}, f32[40,128]{1,0:T(8,128)S(1)}, u32[]{:S(2)}, u32[]{:S(2)}) collective-permute-start(f32[40,128]{1,0:T(8,128)S(1)} %get-tuple-element.53), channel_id=1, source_target_pairs={{0,1},{1,0},{2,3},{3,2},{4,5},{5,4},{6,7},{7,6},{8,9},{9,8},{10,11... | collective-permute-start | bytes 61448 | tf_op jit(solution)/shard_map/ppermute | solution.py:552
  4.5 0.5 collective-permute-start
  5.0 0.0 copy-done.5
  5.0 0.1 copy.18
  5.1 0.0 copy-done.6
  5.1 0.1 copy.19
  5.2 0.0 copy-done.1
  5.2 0.0 copy-done
  5.2 0.0 copy-done.4
  5.2 0.0 copy-done.3
  5.2 0.0 copy-done.2
  5.3 0.7 shard_map.142
  6.0 0.0 copy-done.7
  6.0 0.1 copy.20
  6.1 0.0 collective-permute-done.1.far
  6.1 0.0 collective-permute-done.near
  6.1 0.1 shard_map.143
  6.2 1.1 %collective-permute-start.3 = (f32[136,128]{1,0:T(8,128)S(1)}, f32[136,128]{1,0:T(8,128)S(1)}, u32[]{:S(2)}, u32[]{:S(2)}) collective-permute-start(f32[136,128]{1,0:T(8,128)S(1)} %get-tuple-element.60), channel_id=1, source_target_pairs={{0,16},{1,2},{2,1},{3,4},{4,3},{5,6},{6,5},{7,8},{8,7},{9,10},{10,... | collective-permute-start | bytes 208904 | tf_op jit(solution)/shard_map/ppermute | solution.py:552
  7.3 1.5 %collective-permute-start.2 = (f32[136,128]{1,0:T(8,128)S(1)}, f32[136,128]{1,0:T(8,128)S(1)}, u32[]{:S(2)}, u32[]{:S(2)}) collective-permute-start(f32[136,128]{1,0:T(8,128)S(1)} %get-tuple-element.60), channel_id=1, source_target_pairs={{0,1},{1,0},{2,3},{3,2},{4,5},{5,4},{6,7},{7,6},{8,9},{9,8},{10,11... | collective-permute-start | bytes 208904 | tf_op jit(solution)/shard_map/ppermute | solution.py:553
  8.8 1.4 %shard_map.145.hot = bf16[8192,256]{1,0:T(8,128)(2,1)S(1)} custom-call(s32[128,64]{1,0:T(8,128)S(1)} %bitcast.23), custom_call_target="tpu_custom_call" | custom-call | flops 1000000000 | bytes 1048576 | tf_op jit(solution)/shard_map/pallas_call | solution.py:518
  10.2 0.0 collective-permute-done.3.far_col
  10.3 0.3 collective-permute-done.2.near_col
  10.5 1.8 %shard_map.144 = (f32[6,72,384]{2,1,0:T(8,128)S(1)}, f32[64,384]{1,0:T(8,128)S(1)}, s32[64,128]{1,0:T(8,128)S(1)}, s32[64,128]{1,0:T(8,128)S(1)}, s32[128,128]{1...) custom-call(f32[5,72,256]{2,1,0:T(8,128)S(1)} %get-tuple-element.58., ...), custom_call_target="tpu_custom_call" | custom-call | flops 1000000000 | bytes 1048576 | tf_op jit(solution)/shard_map/pallas_call | solution.py:518
  12.3 25.0 %all_to_all.15 = f32[128,1,768]{2,1,0:T(1,128)S(1)} all-to-all(f32[128,1,768]{2,1,0:T(1,128)S(1)} %bitcast.19), channel_id=1, replica_groups=mesh['row'=8,'col'=16] {'row','col'}, dimensions={0} | all-to-all | bytes 786432 | tf_op jit(solution)/shard_map/all_to_all | solution.py:612
  37.3 1.4 %shard_map.146 = (f32[64,384]{1,0:T(8,128)S(1)}, f32[12,128]{1,0:T(8,128)S(1)}, f32[12,128]{1,0:T(8,128)S(1)}, f32[64,128]{1,0:T(8,128)S(1)}, f32[128,128]{1,0:T(8,128)S(1)}) custom-call(f32[768,128]{1,0:T(8,128)S(1)} %bitcast.13, f32[64,384]{1,0:T(8,128)S(1)} %get-tuple-element.67.surface, f32[64,384]{1,0:T(8,128)S(1)} %get-tuple-element.68.inverse, ...), custom_call_target="tpu_custom_call" | custom-call | flops 1000000000 | bytes 1048576 | tf_op jit(solution)/shard_map/pallas_call | solution.py:518
  38.7 0.8 collective-permute-start.5
  39.5 0.4 collective-permute-start.4
  39.9 1.8 %shard_map.148 = (f32[64,128]{1,0:T(8,128)S(1)}, f32[64,128]{1,0:T(8,128)S(1)}) custom-call(f32[768,128]{1,0:T(8,128)S(1)} %bitcast.14, f32[64,128]{1,0:T(8,128)S(1)} %get-tuple-element.62.nodes, s32[64,128]{1,0:T(8,128)S(1)} %get-tuple-element.80.node_high, s32[64,128]{1,0:T(8,128)S(1)} %get-tuple-element.81.node_low, ...), custom_call_target="tpu_custom_call" | custom-call | flops 1000000000 | bytes 1048576 | tf_op jit(solution)/shard_map/pallas_call | solution.py:518
  41.7 0.1 collective-permute-done.5.far
  41.8 0.0 collective-permute-done.4.near
  41.8 1.5 %shard_map.149 = (f32[64,384]{1,0:T(8,128)S(1)}, f32[64,128]{1,0:T(8,128)S(1)}, f32[128,128]{1,0:T(8,128)S(1)}, f32[768,128]{1,0:T(8,128)S(1)}) custom-call(f32[64,384]{1,0:T(8,128)S(1)} %get-tuple-element.75.surface, f32[12,128]{1,0:T(8,128)S(1)} %collective-permute-done.4.near, f32[12,128]{1,0:T(8,128)S(1)} %collective-permute-done.5.far, ...), custom_call_target="tpu_custom_call" | custom-call | flops 1000000000 | bytes 1048576 | tf_op jit(solution)/shard_map/pallas_call | solution.py:518
  43.3 16.8 %all_to_all.16 = f32[128,1,768]{2,1,0:T(1,128)S(1)} all-to-all(f32[128,1,768]{2,1,0:T(1,128)S(1)} %bitcast.20), channel_id=1, replica_groups=mesh['row'=8,'col'=16] {'row','col'}, dimensions={0} | all-to-all | bytes 786432 | tf_op jit(solution)/shard_map/all_to_all | solution.py:612
  60.1 1.4 %shard_map.150 = (f32[64,384]{1,0:T(8,128)S(1)}, f32[12,128]{1,0:T(8,128)S(1)}, f32[12,128]{1,0:T(8,128)S(1)}) custom-call(f32[768,128]{1,0:T(8,128)S(1)} %bitcast.15, f32[64,384]{1,0:T(8,128)S(1)} %get-tuple-element.88.surface, f32[64,384]{1,0:T(8,128)S(1)} %get-tuple-element.68.inverse, f32[64,128]{1,0:T(8,128)S(1)} %get-tuple-element.89.heads, ...), custom_call_target="tpu_custom_call" | custom-call | flops 1000000000 | bytes 1048576 | tf_op jit(solution)/shard_map/pallas_call | solution.py:518
  61.5 1.0 %collective-permute-start.7 = (f32[12,128]{1,0:T(8,128)S(1)}, f32[12,128]{1,0:T(8,128)S(1)}, u32[]{:S(2)}, u32[]{:S(2)}) collective-permute-start(f32[12,128]{1,0:T(8,128)S(1)} %shard_map.151), channel_id=1, source_target_pairs={{0,1},{1,0},{2,3},{3,2},{4,5},{5,4},{6,7},{7,6},{8,9},{9,8},{10,11... | collective-permute-start | bytes 18440 | tf_op jit(solution)/shard_map/ppermute | solution.py:552
  62.5 0.4 collective-permute-start.6
  63.0 1.8 %shard_map.152 = (f32[64,128]{1,0:T(8,128)S(1)}, f32[64,128]{1,0:T(8,128)S(1)}) custom-call(f32[768,128]{1,0:T(8,128)S(1)} %bitcast.16, f32[64,128]{1,0:T(8,128)S(1)} %get-tuple-element.86.nodes, s32[64,128]{1,0:T(8,128)S(1)} %get-tuple-element.80.node_high, s32[64,128]{1,0:T(8,128)S(1)} %get-tuple-element.81.node_low, ...), custom_call_target="tpu_custom_call" | custom-call | flops 1000000000 | bytes 1048576 | tf_op jit(solution)/shard_map/pallas_call | solution.py:518
  64.7 0.1 collective-permute-done.7.far
  64.9 0.0 collective-permute-done.6.near
  64.9 1.3 %shard_map.153 = (f32[64,384]{1,0:T(8,128)S(1)}, f32[64,128]{1,0:T(8,128)S(1)}, f32[128,128]{1,0:T(8,128)S(1)}, f32[640,128]{1,0:T(8,128)S(1)}) custom-call(f32[64,384]{1,0:T(8,128)S(1)} %get-tuple-element.93.surface, f32[12,128]{1,0:T(8,128)S(1)} %collective-permute-done.6.near, f32[12,128]{1,0:T(8,128)S(1)} %collective-permute-done.7.far, ...), custom_call_target="tpu_custom_call" | custom-call | flops 1000000000 | bytes 1048576 | tf_op jit(solution)/shard_map/pallas_call | solution.py:518
  66.1 16.1 %all_to_all.17 = f32[128,1,640]{2,1,0:T(1,128)S(1)} all-to-all(f32[128,1,640]{2,1,0:T(1,128)S(1)} %bitcast.21), channel_id=1, replica_groups=mesh['row'=8,'col'=16] {'row','col'}, dimensions={0} | all-to-all | bytes 655360 | tf_op jit(solution)/shard_map/all_to_all | solution.py:612
  82.3 1.6 %shard_map.155 = f32[32,256]{1,0:T(8,128)} custom-call(f32[640,128]{1,0:T(8,128)S(1)} %bitcast.17, f32[64,128]{1,0:T(8,128)S(1)} %get-tuple-element.97.nodes, s32[64,128]{1,0:T(8,128)S(1)} %get-tuple-element.80.node_high, s32[64,128]{1,0:T(8,128)S(1)} %get-tuple-element.81.node_low, f32[64,128]{1,0:T(8,128)S(1)} %get-tuple-element.63.coef, ...), custom_call_target="tpu_custom_call" | custom-call | flops 1000000000 | bytes 1048576 | tf_op jit(solution)/shard_map/pallas_call | solution.py:518
  83.9 1.4 %shard_map.154 = f32[64,256]{1,0:T(8,128)} custom-call(f32[640,128]{1,0:T(8,128)S(1)} %bitcast.18, f32[64,384]{1,0:T(8,128)S(1)} %get-tuple-element.99.surface, f32[64,384]{1,0:T(8,128)S(1)} %get-tuple-element.68.inverse, f32[64,128]{1,0:T(8,128)S(1)} %get-tuple-element.100.heads, f32[128,128]{1,0:T(8,128)S(1)} %get-tuple-element.101.zone, ...), custom_call_target="tpu_custom_call" | custom-call | flops 1000000000 | bytes 1048576 | tf_op jit(solution)/shard_map/pallas_call | solution.py:518
  (3 shorter events, 0.0 us)
Async XLA Ops:
  0.6 4.6 %copy-start.1 = (f32[32,256]{1,0:T(8,128)S(1)}, f32[32,256]{1,0:T(8,128)}, u32[]{:S(2)}) copy-start(f32[32,256]{1,0:T(8,128)} %pipes.3) | copy-start | bytes 98308
  0.6 4.4 %copy-start.5 = (s32[128,1,64]{0,2,1:T(8,128)S(1)}, s32[128,1,64]{0,2,1:T(8,128)}, u32[]{:S(2)}) copy-start(s32[128,1,64]{0,2,1:T(8,128)} %param.24) | copy-start | bytes 98308
  0.7 4.4 %copy-start.6 = (f32[128,1,64]{0,2,1:T(8,128)S(1)}, f32[128,1,64]{0,2,1:T(8,128)}, u32[]{:S(2)}) copy-start(f32[128,1,64]{0,2,1:T(8,128)} %param.25) | copy-start | bytes 98308
  0.7 4.6 %copy-start = (f32[4,32,32]{2,1,0:T(8,128)S(1)}, f32[4,32,32]{2,1,0:T(8,128)}, u32[]{:S(2)}) copy-start(f32[4,32,32]{2,1,0:T(8,128)} %param.22) | copy-start | bytes 49156
  0.7 4.6 %copy-start.4 = (s32[256]{0:T(256)S(1)}, s32[256]{0:T(256)}, u32[]{:S(2)}) copy-start(s32[256]{0:T(256)} %param.21) | copy-start | bytes 3076
  0.7 4.6 %copy-start.3 = (s32[256]{0:T(256)S(1)}, s32[256]{0:T(256)}, u32[]{:S(2)}) copy-start(s32[256]{0:T(256)} %param.20) | copy-start | bytes 3076
  0.7 4.6 %copy-start.2 = (s32[256]{0:T(256)S(1)}, s32[256]{0:T(256)}, u32[]{:S(2)}) copy-start(s32[256]{0:T(256)} %param.19) | copy-start | bytes 3076
  1.8 4.1 %copy-start.7 = (s32[1,128,64]{1,2,0:T(8,128)S(1)}, s32[1,128,64]{1,2,0:T(8,128)}, u32[]{:S(2)}) copy-start(s32[1,128,64]{1,2,0:T(8,128)} %param.23) | copy-start | bytes 98308
  1.8 4.2 %collective-permute-start.1 = (f32[40,128]{1,0:T(8,128)S(1)}, f32[40,128]{1,0:T(8,128)S(1)}, u32[]{:S(2)}, u32[]{:S(2)}) collective-permute-start(f32[40,128]{1,0:T(8,128)S(1)} %get-tuple-element.53), channel_id=1, source_target_pairs={{0,1},{1,0},{2,3},{3,2},{4,5},{5,4},{6,7},{7,6},{8,9},{9,8},{10,11... | collective-permute-start | bytes 61448 | tf_op jit(solution)/shard_map/ppermute | solution.py:552
  4.5 1.6 %collective-permute-start = (f32[48,128]{1,0:T(8,128)S(1)}, f32[48,128]{1,0:T(8,128)S(1)}, u32[]{:S(2)}, u32[]{:S(2)}) collective-permute-start(f32[48,128]{1,0:T(8,128)S(1)} %shard_map.141), channel_id=1, source_target_pairs={{0,16},{1,17},{2,18},{3,19},{4,20},{5,21},{6,22},{7,23},{8,24},{9,... | collective-permute-start | bytes 73736 | tf_op jit(solution)/shard_map/ppermute | solution.py:553
  6.2 4.0 %collective-permute-start.3 = (f32[136,128]{1,0:T(8,128)S(1)}, f32[136,128]{1,0:T(8,128)S(1)}, u32[]{:S(2)}, u32[]{:S(2)}) collective-permute-start(f32[136,128]{1,0:T(8,128)S(1)} %get-tuple-element.60), channel_id=1, source_target_pairs={{0,16},{1,2},{2,1},{3,4},{4,3},{5,6},{6,5},{7,8},{8,7},{9,10},{10,... | collective-permute-start | bytes 208904 | tf_op jit(solution)/shard_map/ppermute | solution.py:552
  7.3 3.2 %collective-permute-start.2 = (f32[136,128]{1,0:T(8,128)S(1)}, f32[136,128]{1,0:T(8,128)S(1)}, u32[]{:S(2)}, u32[]{:S(2)}) collective-permute-start(f32[136,128]{1,0:T(8,128)S(1)} %get-tuple-element.60), channel_id=1, source_target_pairs={{0,1},{1,0},{2,3},{3,2},{4,5},{5,4},{6,7},{7,6},{8,9},{9,8},{10,11... | collective-permute-start | bytes 208904 | tf_op jit(solution)/shard_map/ppermute | solution.py:553
  38.7 3.2 %collective-permute-start.5 = (f32[12,128]{1,0:T(8,128)S(1)}, f32[12,128]{1,0:T(8,128)S(1)}, u32[]{:S(2)}, u32[]{:S(2)}) collective-permute-start(f32[12,128]{1,0:T(8,128)S(1)} %shard_map.147), channel_id=1, source_target_pairs={{0,1},{1,0},{2,3},{3,2},{4,5},{5,4},{6,7},{7,6},{8,9},{9,8},{10,11... | collective-permute-start | bytes 18440 | tf_op jit(solution)/shard_map/ppermute | solution.py:552
  39.5 2.3 %collective-permute-start.4 = (f32[12,128]{1,0:T(8,128)S(1)}, f32[12,128]{1,0:T(8,128)S(1)}, u32[]{:S(2)}, u32[]{:S(2)}) collective-permute-start(f32[12,128]{1,0:T(8,128)S(1)} %get-tuple-element.76), channel_id=1, source_target_pairs={{0,16},{1,17},{2,18},{3,19},{4,20},{5,21},{6,22},{7,23},{8,24},{9,... | collective-permute-start | bytes 18440 | tf_op jit(solution)/shard_map/ppermute | solution.py:553
  61.5 3.3 %collective-permute-start.7 = (f32[12,128]{1,0:T(8,128)S(1)}, f32[12,128]{1,0:T(8,128)S(1)}, u32[]{:S(2)}, u32[]{:S(2)}) collective-permute-start(f32[12,128]{1,0:T(8,128)S(1)} %shard_map.151), channel_id=1, source_target_pairs={{0,1},{1,0},{2,3},{3,2},{4,5},{5,4},{6,7},{7,6},{8,9},{9,8},{10,11... | collective-permute-start | bytes 18440 | tf_op jit(solution)/shard_map/ppermute | solution.py:552
  62.5 2.3 %collective-permute-start.6 = (f32[12,128]{1,0:T(8,128)S(1)}, f32[12,128]{1,0:T(8,128)S(1)}, u32[]{:S(2)}, u32[]{:S(2)}) collective-permute-start(f32[12,128]{1,0:T(8,128)S(1)} %get-tuple-element.94), channel_id=1, source_target_pairs={{0,16},{1,17},{2,18},{3,19},{4,20},{5,21},{6,22},{7,23},{8,24},{9,... | collective-permute-start | bytes 18440 | tf_op jit(solution)/shard_map/ppermute | solution.py:553

commit v10 on v9

--- a/solution.py
+++ b/solution.py
@@ -293,10 +293,19 @@
     return got[pl.ds(index, 128, stride=blocks), :]
 
 
-def build_message(out, blocks, heads, nodes):
+def build_message(out, blocks, heads, nodes, own_ends, other_ends):
     put(out, blocks, 0, paired(heads, nodes))
-    if blocks == 6:
-        put(out, blocks, 5, beside(nodes))
+    own_rows = (iota((128, 128), 0) >> 4) == row_col()[0]
+    for half in range(2):
+        own = jnp.broadcast_to(own_ends[half], (128, 128))
+        other = jnp.broadcast_to(other_ends[half], (128, 128))
+        put(out, blocks, 1 + half, jnp.where(own_rows, own, other))
+    if blocks > 3:
+        put(out, blocks, blocks - 1, beside(nodes))
+
+
+def partner_rows(blocks):
+    return pl.multiple_of((row_col()[0] ^ 1) * (16 * blocks), 16)
 
 
 def zone_heads(edge, zone_place, edge_ref, zone_ref):
@@ -382,12 +391,9 @@
         state, gains, cell_high, cell_low, (zone_row, zone_col), surface_out, heads_out, zone_out,
         cell_table, edge_ref, zone_ref,
     )
-    build_message(out, 6, heads, nodes[...])
-    own_rows = (iota((128, 128), 0) >> 4) == row_col()[0]
-    for half in range(2):
-        own = jnp.broadcast_to(table[half * 32 : half * 32 + 1, :], (128, 128))
-        other = jnp.broadcast_to(near[40 + half : 41 + half, :], (128, 128))
-        put(out, 6, 1 + half, jnp.where(own_rows, own, other))
+    build_message(
+        out, 6, heads, nodes[...], (table[0:1, :], table[32:33, :]), (near[40:41, :], near[41:42, :])
+    )
     put(out, 6, 3, paired(coef[...], coef[...]))
     put(out, 6, 4, beside(coef[...]))
 
@@ -411,16 +417,27 @@
         state, gains, cell_high, cell_low, zone_place, surface_out, heads_out, zone_out,
         cell_table, edge_ref, zone_ref,
     )
-    blocks = 5 if last else 6
-    build_message(out, blocks, heads, nodes[...])
-    for index, row in enumerate(ENDS):
-        put(out, blocks, 1 + index, jnp.broadcast_to(table[row : row + 1, :], (128, 128)))
+    build_message(
+        out, 3 if last else 4, heads, nodes[...], (table[0:1, :], table[32:33, :]),
+        (table[31:32, :], table[63:64, :]),
+    )
+
+
+def relayed(got, blocks):
+    return jnp.concatenate(
+        [got[pl.ds(partner_rows(blocks) + block, 16, stride=blocks), :] for block in (1, 2)], axis=0
+    )
+
+
+def relay_kernel(got, out):
+    out[...] = relayed(got, 3)
 
 
 def tile_kernel(
     first, last, got, surface, inverse, heads, zone, cell_high, hot, zone_row, zone_col, *rest
 ):
     rest = list(rest)
+    blocks = 6 if first else 3 if last else 4
     if first:
         own_coef = low_halves(taken(got, 6, 3))
         zone_coef = taken(got, 6, 4)
@@ -435,7 +452,7 @@
         rest.pop(0)[...] = zone_coef
     value_ref, zone_value_ref, row_ref = rest
     value_ref[...] = jnp.where(
-        cell_high[...] >= 0, own_coef * (heads[...] - high_halves(taken(got, 5 if last else 6, 0))), 0.0
+        cell_high[...] >= 0, own_coef * (heads[...] - high_halves(taken(got, blocks, 0))), 0.0
     )
     row_ref[...] = jnp.where(cell_high[...] >= 0, jnp.bitwise_and(cell_high[...], 63), -1)
     lost = summed_by_columns(row_ref, value_ref, hot)
@@ -446,7 +463,7 @@
     if last:
         return
     zone_value_ref[...] = jnp.where(
-        zone_row[...] >= 0, zone_coef * (zone[...] - taken(got, 6, 5)), 0.0
+        zone_row[...] >= 0, zone_coef * (zone[...] - taken(got, blocks, blocks - 1)), 0.0
     )
     lost = summed(zone_row, zone_col, zone_value_ref, 64, 2 * ZONE, by_low=True)
     lost = jnp.concatenate([lost, jnp.zeros((64, 128 - 2 * ZONE), F32)], axis=1)
@@ -458,28 +475,46 @@
     edge = surface[:, 256:384] - inverse[:, 256:384] * lost
     surface_out[:, 256:384] = edge
     top, bottom = strips([left, right, edge], 0), strips([left, right, edge], 60)
-    near[...] = jnp.where(even(0), bottom, top)
+    near[0:12, :] = jnp.where(even(0), bottom, top)
     far[...] = jnp.where(even(0), top, bottom)
+    if not first:
+        near[16:48, :] = relayed(got, blocks)
+
+
+def inflow_of(blocks, got, nodes, node_high, node_low, coef, value_ref):
+    value_ref[...] = jnp.where(
+        node_high[...] >= 0, coef[...] * (low_halves(taken(got, blocks, 0)) - nodes[...]), 0.0
+    )
+    return summed(node_high, node_low, value_ref, 64, 128)
+
+
+def inflow_kernel(got, nodes, node_high, node_low, coef, out, value_ref):
+    out[...] = inflow_of(4, got, nodes, node_high, node_low, coef, value_ref)
 
 
 def owner_kernel(
     first, last, got, nodes, node_high, node_low, coef, table, meets, classes, matrices, *rest
 ):
-    blocks = 5 if last else 6
+    blocks = 6 if first else 3 if last else 4
+    rest = list(rest)
+    relay = None if first else rest.pop(0)
+    inflow = None if first or last else rest.pop(0)[...]
     if last:
         pipes_out, value_ref, ends_ref = rest
     else:
         table_out, nodes_out, value_ref, ends_ref = rest
-    value_ref[...] = jnp.where(
-        node_high[...] >= 0, coef[...] * (low_halves(taken(got, blocks, 0)) - nodes[...]), 0.0
-    )
-    inflow = summed(node_high, node_low, value_ref, 64, 128)
+    if inflow is None:
+        inflow = inflow_of(blocks, got, nodes, node_high, node_low, coef, value_ref)
     balance = table[...] + inflow
     start = pl.multiple_of(row_col()[0] * (16 * blocks), 16)
-    other = pl.multiple_of((row_col()[0] ^ 1) * 96, 32) if first else start
-    for index in range(4):
-        source, block = (other, index - 1) if first and index >= 2 else (start, 1 + index)
-        ends_ref[index * 16 : index * 16 + 16, :] = got[pl.ds(source + block, 16, stride=blocks), :]
+    for half in range(2):
+        ends_ref[half * 16 : half * 16 + 16, :] = got[
+            pl.ds(start + 1 + half, 16, stride=blocks), :
+        ]
+    if first:
+        ends_ref[32:64, :] = relayed(got, blocks)
+    else:
+        ends_ref[32:64, :] = relay[0:32, :] if last else relay[16:48, :]
     meet = meets[...]
     meet_high = jnp.bitwise_and(meet >> 7, 1) * 16 + (meet >> 8)
     meet_high = jnp.where(iota((8, 128), 0) < 2, meet_high + 32, meet_high)
@@ -513,7 +548,7 @@
     return jax.ShapeDtypeStruct(dims, dtype)
 
 
-def call(kernel, inputs, outputs, scratch=(), space=pltpu.VMEM):
+def call(kernel, inputs, outputs, scratch=(), space=pltpu.VMEM, flops=10**9):
     vmem = pl.BlockSpec(memory_space=pltpu.VMEM)
     return pl.pallas_call(
         kernel,
@@ -522,7 +557,7 @@
         out_specs=[vmem] * len(outputs),
         scratch_shapes=list(scratch),
         compiler_params=pltpu.CompilerParams(vmem_limit_bytes=16 << 20),
-        cost_estimate=pl.CostEstimate(flops=10**9, bytes_accessed=1 << 20, transcendentals=0),
+        cost_estimate=pl.CostEstimate(flops=flops, bytes_accessed=1 << 20, transcendentals=0),
     )(*inputs)
 
 
@@ -545,6 +580,8 @@
                 other[1 - dim] ^= 1
             for route, there in zip(routes, (partner, other)):
                 route.append((row * sizes[1] + col, there[0] * sizes[1] + there[1]))
+    if far is None:
+        return lax.ppermute(near, ("row", "col"), routes[0])
     if copied == "near":
         (near,) = call(copy_kernel, (near,), [shape(*near.shape)])
     if copied == "far":
@@ -607,7 +644,7 @@
                 functools.partial(sweep_kernel, last),
                 (surface, near, far, gains, cell_high, cell_low, zone_row, zone_col,
                  table, nodes),
-                [*swept_shapes, shape(640 if last else 768, 128)], gather_scratch,
+                [*swept_shapes, shape(384 if last else 512, 128)], gather_scratch,
             )
         got = lax.all_to_all(
             sent.reshape(128, 1, -1), ("row", "col"), split_axis=0, concat_axis=0, tiled=True
@@ -619,23 +656,31 @@
         ]
         owner_scratch = [pltpu.VMEM((64, 128), F32), pltpu.VMEM((64, 128), F32)]
         if last:
-            (pipes_out,) = call(
-                functools.partial(owner_kernel, False, True), (got, *owner_inputs),
-                [shape(32, 256)], owner_scratch,
-            )
+            (relay,) = call(relay_kernel, (got,), [shape(32, 128)])
+            relay = swapped(relay, None, 0)
             (surface_out,) = call(
                 functools.partial(tile_kernel, False, True), (got, *tile_inputs), [shape(64, 256)],
                 tile_scratch,
             )
+            (pipes_out,) = call(
+                functools.partial(owner_kernel, False, True), (got, *owner_inputs, relay),
+                [shape(32, 256)], owner_scratch,
+            )
             return surface_out, pipes_out
-        outputs = [shape(64, 384), shape(12, 128), shape(12, 128)]
+        outputs = [shape(64, 384), shape(12 if first else 48, 128), shape(12, 128)]
         if first:
             outputs += [shape(64, 128), shape(128, 128)]
         surface, near, far, *new_coefs = call(
             functools.partial(tile_kernel, first, False), (got, *tile_inputs), outputs,
             tile_scratch,
         )
-        near, far = swapped(near, far, 0, "far")
+        near, far = swapped(near, far, 0, "far" if first else None)
+        if not first:
+            (inflow,) = call(
+                inflow_kernel, (got, nodes, node_high, node_low, coef), [shape(64, 128)],
+                owner_scratch[:1], flops=10**6,
+            )
+            owner_inputs += (near, inflow)
         table, nodes = call(
             functools.partial(owner_kernel, first, False), (got, *owner_inputs),
             [shape(64, 128), shape(64, 128)], owner_scratch,

time: 85.5 us -> 83.4 us (0.975)
  blocking collectives: 57.9 us -> 54.5 us
  waiting for transfers between devices: 0.5 us -> 1.61 us
    all_to_all x3, blocking collectives: 57.9 us -> 54.5 us  [body(): lax.all_to_all(sent.reshape(128, 1, -1), ('row', 'col'), split_axis=0, co...]
    ppermute x4, waiting for transfers between devices: 0.24 us -> 1.35 us  [swapped(): far = lax.ppermute(far, ('row', 'col'), routes[1])]
    pallas_call x16 -> x17, Pallas kernels: 17.3 us -> 17.3 us  [call(): pl.pallas_call(kernel, out_shape=outputs, in_specs=[pl.BlockSpec(memory_s...]
  transfers between devices with their start and end apart: 8 -> 9, of which waited for: 3 -> 3; matrix products, arithmetic and copies ran while one was open for 0% -> 0% of each run, Pallas kernels for 7% -> 9%
where the time goes in v10:
time: 83.4 us; the launch traced here: 83.2 us
  blocking collectives  54.5 us (65%)
  Pallas kernels  17.3 us (21%)
  starting transfers between devices  8.53 us (10%)
  waiting for transfers between devices  1.61 us (2%)
  between operations  0.89 us (1%)
    all_to_all x3, blocking collectives, body(): lax.all_to_all(sent.reshape(128, 1, -1), ('row', 'col'), split_axis=0, co...  54.5 us
    pallas_call x17, Pallas kernels, call(): pl.pallas_call(kernel, out_shape=outputs, in_specs=[pl.BlockSpec(memory_s...  17.3 us
    ppermute x4, starting transfers between devices, swapped(): far = lax.ppermute(far, ('row', 'col'), routes[1])  4.94 us
    ppermute x4, starting transfers between devices, swapped(): return (lax.ppermute(near, ('row', 'col'), routes[0]), far)  3.12 us
  transfers between devices with their start and end apart: 9, of which 3 were waited for; matrix products, arithmetic and copies ran while one was open for 0% of the time, Pallas kernels for 9%

profile of v10, /device:TPU:1, one launch (start us, length us, event | category | flops | bytes accessed | tf_op | source)
XLA Modules:
  0.0 83.2 jit_solution(4783406799507473585)
XLA Ops:
  0.6 0.0 copy-start.1
  0.6 0.0 copy-start.5
  0.7 0.0 copy-start.6
  0.7 0.0 copy-start
  0.7 0.0 copy-start.4
  0.7 0.0 copy-start.3
  0.7 0.0 copy-start.2
  0.7 1.1 %shard_map.140 = (f32[5,64,256]{2,1,0:T(8,128)S(1)}, f32[48,128]{1,0:T(8,128)S(1)}, f32[40,128]{1,0:T(8,128)S(1)}) custom-call(f32[64,256]{1,0:T(8,128)} %surface.1, f32[64,256]{1,0:T(8,128)} %cond_x.1, f32[64,256]{1,0:T(8,128)} %cond_y.1, f32[64,256]{1,0:T(8,128)} %porosity.1, f32[64,256]{1,0:T(8,128)} %rainfall.1, f32[32,256]{1,0:T(8,128)} %pipes.3), custom_call_target="tpu_custom_call" | custom-call | flops 1000000000 | bytes 1048576 | tf_op jit(solution)/shard_map/pallas_call | solution.py:553
  1.8 0.0 copy-start.7
  1.8 2.7 %collective-permute-start.1 = (f32[40,128]{1,0:T(8,128)S(1)}, f32[40,128]{1,0:T(8,128)S(1)}, u32[]{:S(2)}, u32[]{:S(2)}) collective-permute-start(f32[40,128]{1,0:T(8,128)S(1)} %get-tuple-element.53), channel_id=1, source_target_pairs={{0,1},{1,0},{2,3},{3,2},{4,5},{5,4},{6,7},{7,6},{8,9},{9,8},{10,11... | collective-permute-start | bytes 61448 | tf_op jit(solution)/shard_map/ppermute | solution.py:589
  4.5 0.5 collective-permute-start
  5.0 0.0 copy-done.5
  5.0 0.1 copy.18
  5.1 0.0 copy-done.6
  5.1 0.1 copy.19
  5.2 0.0 copy-done.1
  5.2 0.0 copy-done
  5.2 0.0 copy-done.4
  5.2 0.0 copy-done.3
  5.2 0.0 copy-done.2
  5.3 0.7 shard_map.142
  6.0 0.0 copy-done.7
  6.0 0.1 copy.20
  6.1 0.0 collective-permute-done.1.far
  6.1 0.0 collective-permute-done.near
  6.1 0.1 shard_map.143
  6.2 1.1 %collective-permute-start.3 = (f32[136,128]{1,0:T(8,128)S(1)}, f32[136,128]{1,0:T(8,128)S(1)}, u32[]{:S(2)}, u32[]{:S(2)}) collective-permute-start(f32[136,128]{1,0:T(8,128)S(1)} %get-tuple-element.60), channel_id=1, source_target_pairs={{0,16},{1,2},{2,1},{3,4},{4,3},{5,6},{6,5},{7,8},{8,7},{9,10},{10,... | collective-permute-start | bytes 208904 | tf_op jit(solution)/shard_map/ppermute | solution.py:589
  7.3 1.5 %collective-permute-start.2 = (f32[136,128]{1,0:T(8,128)S(1)}, f32[136,128]{1,0:T(8,128)S(1)}, u32[]{:S(2)}, u32[]{:S(2)}) collective-permute-start(f32[136,128]{1,0:T(8,128)S(1)} %get-tuple-element.60), channel_id=1, source_target_pairs={{0,1},{1,0},{2,3},{3,2},{4,5},{5,4},{6,7},{7,6},{8,9},{9,8},{10,11... | collective-permute-start | bytes 208904 | tf_op jit(solution)/shard_map/ppermute | solution.py:590
  8.8 1.4 %shard_map.145.hot = bf16[8192,256]{1,0:T(8,128)(2,1)S(1)} custom-call(s32[128,64]{1,0:T(8,128)S(1)} %bitcast.23), custom_call_target="tpu_custom_call" | custom-call | flops 1000000000 | bytes 1048576 | tf_op jit(solution)/shard_map/pallas_call | solution.py:553
  10.2 0.0 collective-permute-done.3.far_col
  10.3 0.3 collective-permute-done.2.near_col
  10.5 1.8 %shard_map.144 = (f32[6,72,384]{2,1,0:T(8,128)S(1)}, f32[64,384]{1,0:T(8,128)S(1)}, s32[64,128]{1,0:T(8,128)S(1)}, s32[64,128]{1,0:T(8,128)S(1)}, s32[128,128]{1...) custom-call(f32[5,72,256]{2,1,0:T(8,128)S(1)} %get-tuple-element.58., ...), custom_call_target="tpu_custom_call" | custom-call | flops 1000000000 | bytes 1048576 | tf_op jit(solution)/shard_map/pallas_call | solution.py:553
  12.3 25.0 %all_to_all.15 = f32[128,1,768]{2,1,0:T(1,128)S(1)} all-to-all(f32[128,1,768]{2,1,0:T(1,128)S(1)} %bitcast.21), channel_id=1, replica_groups=mesh['row'=8,'col'=16] {'row','col'}, dimensions={0} | all-to-all | bytes 786432 | tf_op jit(solution)/shard_map/all_to_all | solution.py:649
  37.3 1.4 %shard_map.146 = (f32[64,384]{1,0:T(8,128)S(1)}, f32[12,128]{1,0:T(8,128)S(1)}, f32[12,128]{1,0:T(8,128)S(1)}, f32[64,128]{1,0:T(8,128)S(1)}, f32[128,128]{1,0:T(8,128)S(1)}) custom-call(f32[768,128]{1,0:T(8,128)S(1)} %bitcast.16, f32[64,384]{1,0:T(8,128)S(1)} %get-tuple-element.67.surface, f32[64,384]{1,0:T(8,128)S(1)} %get-tuple-element.68.inverse, ...), custom_call_target="tpu_custom_call" | custom-call | flops 1000000000 | bytes 1048576 | tf_op jit(solution)/shard_map/pallas_call | solution.py:553
  38.7 0.8 %collective-permute-start.5 = (f32[12,128]{1,0:T(8,128)S(1)}, f32[12,128]{1,0:T(8,128)S(1)}, u32[]{:S(2)}, u32[]{:S(2)}) collective-permute-start(f32[12,128]{1,0:T(8,128)S(1)} %shard_map.147), channel_id=1, source_target_pairs={{0,1},{1,0},{2,3},{3,2},{4,5},{5,4},{6,7},{7,6},{8,9},{9,8},{10,11... | collective-permute-start | bytes 18440 | tf_op jit(solution)/shard_map/ppermute | solution.py:589
  39.5 0.4 collective-permute-start.4
  39.9 1.8 %shard_map.148 = (f32[64,128]{1,0:T(8,128)S(1)}, f32[64,128]{1,0:T(8,128)S(1)}) custom-call(f32[768,128]{1,0:T(8,128)S(1)} %bitcast.17, f32[64,128]{1,0:T(8,128)S(1)} %get-tuple-element.62.nodes, s32[64,128]{1,0:T(8,128)S(1)} %get-tuple-element.80.node_high, s32[64,128]{1,0:T(8,128)S(1)} %get-tuple-element.81.node_low, ...), custom_call_target="tpu_custom_call" | custom-call | flops 1000000000 | bytes 1048576 | tf_op jit(solution)/shard_map/pallas_call | solution.py:553
  41.7 0.1 collective-permute-done.5.far
  41.8 0.0 collective-permute-done.4.near
  41.8 1.5 %shard_map.149 = (f32[64,384]{1,0:T(8,128)S(1)}, f32[64,128]{1,0:T(8,128)S(1)}, f32[128,128]{1,0:T(8,128)S(1)}, f32[512,128]{1,0:T(8,128)S(1)}) custom-call(f32[64,384]{1,0:T(8,128)S(1)} %get-tuple-element.75.surface, f32[12,128]{1,0:T(8,128)S(1)} %collective-permute-done.4.near, f32[12,128]{1,0:T(8,128)S(1)} %collective-permute-done.5.far, ...), custom_call_target="tpu_custom_call" | custom-call | flops 1000000000 | bytes 1048576 | tf_op jit(solution)/shard_map/pallas_call | solution.py:553
  43.4 15.5 %all_to_all.16 = f32[128,1,512]{2,1,0:T(1,128)S(1)} all-to-all(f32[128,1,512]{2,1,0:T(1,128)S(1)} %bitcast.25), channel_id=1, replica_groups=mesh['row'=8,'col'=16] {'row','col'}, dimensions={0} | all-to-all | bytes 524288 | tf_op jit(solution)/shard_map/all_to_all | solution.py:649
  58.8 1.4 %shard_map.150 = (f32[64,384]{1,0:T(8,128)S(1)}, f32[48,128]{1,0:T(8,128)S(1)}, f32[12,128]{1,0:T(8,128)S(1)}) custom-call(f32[512,128]{1,0:T(8,128)S(1)} %bitcast.13, f32[64,384]{1,0:T(8,128)S(1)} %get-tuple-element.88.surface, f32[64,384]{1,0:T(8,128)S(1)} %get-tuple-element.68.inverse, f32[64,128]{1,0:T(8,128)S(1)} %get-tuple-element.89.heads, ...), custom_call_target="tpu_custom_call" | custom-call | flops 1000000000 | bytes 1048576 | tf_op jit(solution)/shard_map/pallas_call | solution.py:553
  60.2 0.8 collective-permute-start.6
  61.0 0.3 collective-permute-start.7
  61.3 0.7 shard_map.151.rest_1_
  62.0 0.0 collective-permute-done.6.rest_0_.near
  62.0 1.1 %shard_map.152 = (f32[64,128]{1,0:T(8,128)S(1)}, f32[64,128]{1,0:T(8,128)S(1)}) custom-call(f32[512,128]{1,0:T(8,128)S(1)} %bitcast.15, f32[64,128]{1,0:T(8,128)S(1)} %get-tuple-element.86.nodes, s32[64,128]{1,0:T(8,128)S(1)} %get-tuple-element.80.node_high, s32[64,128]{1,0:T(8,128)S(1)} %get-tuple-element.81.node_low, ...), custom_call_target="tpu_custom_call" | custom-call | flops 1000000000 | bytes 1048576 | tf_op jit(solution)/shard_map/pallas_call | solution.py:553
  63.1 1.2 %collective-permute-done.7.far = f32[12,128]{1,0:T(8,128)S(1)} collective-permute-done((f32[12,128]{1,0:T(8,128)S(1)}, f32[12,128]{1,0:T(8,128)S(1)}, u32[]{:S(2)}, u32[]{:S(2)}) %collective-permute-start.7) | collective-permute-done | bytes 6176 | tf_op jit(solution)/shard_map/ppermute | solution.py:589
  64.3 1.3 %shard_map.153 = (f32[64,384]{1,0:T(8,128)S(1)}, f32[64,128]{1,0:T(8,128)S(1)}, f32[128,128]{1,0:T(8,128)S(1)}, f32[384,128]{1,0:T(8,128)S(1)}) custom-call(f32[64,384]{1,0:T(8,128)S(1)} %get-tuple-element.93.surface, f32[48,128]{1,0:T(8,128)S(1)} %collective-permute-done.6.rest_0_.near, f32[12,128]{1,0:T(8,128)S(1)} %collective-permute-done.7.far, ...), custom_call_target="tpu_custom_call" | custom-call | flops 1000000000 | bytes 1048576 | tf_op jit(solution)/shard_map/pallas_call | solution.py:553
  65.6 14.1 %all_to_all.17 = f32[128,1,384]{2,1,0:T(1,128)S(1)} all-to-all(f32[128,1,384]{2,1,0:T(1,128)S(1)} %bitcast.26), channel_id=1, replica_groups=mesh['row'=8,'col'=16] {'row','col'}, dimensions={0} | all-to-all | bytes 393216 | tf_op jit(solution)/shard_map/all_to_all | solution.py:649
  79.7 0.5 collective-permute-start.8
  80.2 1.4 %shard_map.154 = f32[64,256]{1,0:T(8,128)} custom-call(f32[384,128]{1,0:T(8,128)S(1)} %bitcast.19, f32[64,384]{1,0:T(8,128)S(1)} %get-tuple-element.99.surface, f32[64,384]{1,0:T(8,128)S(1)} %get-tuple-element.68.inverse, f32[64,128]{1,0:T(8,128)S(1)} %get-tuple-element.100.heads, f32[128,128]{1,0:T(8,128)S(1)} %get-tuple-element.101.zone, ...), custom_call_target="tpu_custom_call" | custom-call | flops 1000000000 | bytes 1048576 | tf_op jit(solution)/shard_map/pallas_call | solution.py:553
  81.6 0.0 collective-permute-done.8.rest_0_
  81.6 1.6 %shard_map.156 = f32[32,256]{1,0:T(8,128)} custom-call(f32[384,128]{1,0:T(8,128)S(1)} %bitcast.20, f32[64,128]{1,0:T(8,128)S(1)} %get-tuple-element.97.nodes, s32[64,128]{1,0:T(8,128)S(1)} %get-tuple-element.80.node_high, s32[64,128]{1,0:T(8,128)S(1)} %get-tuple-element.81.node_low, f32[64,128]{1,0:T(8,128)S(1)} %get-tuple-element.63.coef, ...), custom_call_target="tpu_custom_call" | custom-call | flops 1000000000 | bytes 1048576 | tf_op jit(solution)/shard_map/pallas_call | solution.py:553
  (3 shorter events, 0.0 us)
Async XLA Ops:
  0.6 4.6 %copy-start.1 = (f32[32,256]{1,0:T(8,128)S(1)}, f32[32,256]{1,0:T(8,128)}, u32[]{:S(2)}) copy-start(f32[32,256]{1,0:T(8,128)} %pipes.3) | copy-start | bytes 98308
  0.6 4.4 %copy-start.5 = (s32[128,1,64]{0,2,1:T(8,128)S(1)}, s32[128,1,64]{0,2,1:T(8,128)}, u32[]{:S(2)}) copy-start(s32[128,1,64]{0,2,1:T(8,128)} %param.24) | copy-start | bytes 98308
  0.7 4.4 %copy-start.6 = (f32[128,1,64]{0,2,1:T(8,128)S(1)}, f32[128,1,64]{0,2,1:T(8,128)}, u32[]{:S(2)}) copy-start(f32[128,1,64]{0,2,1:T(8,128)} %param.25) | copy-start | bytes 98308
  0.7 4.6 %copy-start = (f32[4,32,32]{2,1,0:T(8,128)S(1)}, f32[4,32,32]{2,1,0:T(8,128)}, u32[]{:S(2)}) copy-start(f32[4,32,32]{2,1,0:T(8,128)} %param.22) | copy-start | bytes 49156
  0.7 4.6 %copy-start.4 = (s32[256]{0:T(256)S(1)}, s32[256]{0:T(256)}, u32[]{:S(2)}) copy-start(s32[256]{0:T(256)} %param.21) | copy-start | bytes 3076
  0.7 4.6 %copy-start.3 = (s32[256]{0:T(256)S(1)}, s32[256]{0:T(256)}, u32[]{:S(2)}) copy-start(s32[256]{0:T(256)} %param.20) | copy-start | bytes 3076
  0.7 4.6 %copy-start.2 = (s32[256]{0:T(256)S(1)}, s32[256]{0:T(256)}, u32[]{:S(2)}) copy-start(s32[256]{0:T(256)} %param.19) | copy-start | bytes 3076
  1.8 4.1 %copy-start.7 = (s32[1,128,64]{1,2,0:T(8,128)S(1)}, s32[1,128,64]{1,2,0:T(8,128)}, u32[]{:S(2)}) copy-start(s32[1,128,64]{1,2,0:T(8,128)} %param.23) | copy-start | bytes 98308
  1.8 4.2 %collective-permute-start.1 = (f32[40,128]{1,0:T(8,128)S(1)}, f32[40,128]{1,0:T(8,128)S(1)}, u32[]{:S(2)}, u32[]{:S(2)}) collective-permute-start(f32[40,128]{1,0:T(8,128)S(1)} %get-tuple-element.53), channel_id=1, source_target_pairs={{0,1},{1,0},{2,3},{3,2},{4,5},{5,4},{6,7},{7,6},{8,9},{9,8},{10,11... | collective-permute-start | bytes 61448 | tf_op jit(solution)/shard_map/ppermute | solution.py:589
  4.5 1.6 %collective-permute-start = (f32[48,128]{1,0:T(8,128)S(1)}, f32[48,128]{1,0:T(8,128)S(1)}, u32[]{:S(2)}, u32[]{:S(2)}) collective-permute-start(f32[48,128]{1,0:T(8,128)S(1)} %shard_map.141), channel_id=1, source_target_pairs={{0,16},{1,17},{2,18},{3,19},{4,20},{5,21},{6,22},{7,23},{8,24},{9,... | collective-permute-start | bytes 73736 | tf_op jit(solution)/shard_map/ppermute | solution.py:590
  6.2 4.0 %collective-permute-start.3 = (f32[136,128]{1,0:T(8,128)S(1)}, f32[136,128]{1,0:T(8,128)S(1)}, u32[]{:S(2)}, u32[]{:S(2)}) collective-permute-start(f32[136,128]{1,0:T(8,128)S(1)} %get-tuple-element.60), channel_id=1, source_target_pairs={{0,16},{1,2},{2,1},{3,4},{4,3},{5,6},{6,5},{7,8},{8,7},{9,10},{10,... | collective-permute-start | bytes 208904 | tf_op jit(solution)/shard_map/ppermute | solution.py:589
  7.3 3.2 %collective-permute-start.2 = (f32[136,128]{1,0:T(8,128)S(1)}, f32[136,128]{1,0:T(8,128)S(1)}, u32[]{:S(2)}, u32[]{:S(2)}) collective-permute-start(f32[136,128]{1,0:T(8,128)S(1)} %get-tuple-element.60), channel_id=1, source_target_pairs={{0,1},{1,0},{2,3},{3,2},{4,5},{5,4},{6,7},{7,6},{8,9},{9,8},{10,11... | collective-permute-start | bytes 208904 | tf_op jit(solution)/shard_map/ppermute | solution.py:590
  38.7 3.2 %collective-permute-start.5 = (f32[12,128]{1,0:T(8,128)S(1)}, f32[12,128]{1,0:T(8,128)S(1)}, u32[]{:S(2)}, u32[]{:S(2)}) collective-permute-start(f32[12,128]{1,0:T(8,128)S(1)} %shard_map.147), channel_id=1, source_target_pairs={{0,1},{1,0},{2,3},{3,2},{4,5},{5,4},{6,7},{7,6},{8,9},{9,8},{10,11... | collective-permute-start | bytes 18440 | tf_op jit(solution)/shard_map/ppermute | solution.py:589
  39.5 2.3 %collective-permute-start.4 = (f32[12,128]{1,0:T(8,128)S(1)}, f32[12,128]{1,0:T(8,128)S(1)}, u32[]{:S(2)}, u32[]{:S(2)}) collective-permute-start(f32[12,128]{1,0:T(8,128)S(1)} %get-tuple-element.76), channel_id=1, source_target_pairs={{0,16},{1,17},{2,18},{3,19},{4,20},{5,21},{6,22},{7,23},{8,24},{9,... | collective-permute-start | bytes 18440 | tf_op jit(solution)/shard_map/ppermute | solution.py:590
  60.2 1.8 %collective-permute-start.6 = (f32[48,128]{1,0:T(8,128)S(1)}, f32[48,128]{1,0:T(8,128)S(1)}, u32[]{:S(2)}, u32[]{:S(2)}) collective-permute-start(f32[48,128]{1,0:T(8,128)S(1)} %get-tuple-element.94), channel_id=1, source_target_pairs={{0,16},{1,17},{2,18},{3,19},{4,20},{5,21},{6,22},{7,23},{8,24},{9,... | collective-permute-start | bytes 73736 | tf_op jit(solution)/shard_map/ppermute | solution.py:590
  61.0 3.3 %collective-permute-start.7 = (f32[12,128]{1,0:T(8,128)S(1)}, f32[12,128]{1,0:T(8,128)S(1)}, u32[]{:S(2)}, u32[]{:S(2)}) collective-permute-start(f32[12,128]{1,0:T(8,128)S(1)} %get-tuple-element.95), channel_id=1, source_target_pairs={{0,1},{1,0},{2,3},{3,2},{4,5},{5,4},{6,7},{7,6},{8,9},{9,8},{10,11... | collective-permute-start | bytes 18440 | tf_op jit(solution)/shard_map/ppermute | solution.py:589
  79.7 1.9 %collective-permute-start.8 = (f32[32,128]{1,0:T(8,128)S(1)}, f32[32,128]{1,0:T(8,128)S(1)}, u32[]{:S(2)}, u32[]{:S(2)}) collective-permute-start(f32[32,128]{1,0:T(8,128)S(1)} %shard_map.155), channel_id=1, source_target_pairs={{0,16},{1,17},{2,18},{3,19},{4,20},{5,21},{6,22},{7,23},{8,24},{9,... | collective-permute-start | bytes 49160 | tf_op jit(solution)/shard_map/ppermute | solution.py:584

commit v11 on v10

--- a/solution.py
+++ b/solution.py
@@ -293,8 +293,7 @@
     return got[pl.ds(index, 128, stride=blocks), :]
 
 
-def build_message(out, blocks, heads, nodes, own_ends, other_ends):
-    put(out, blocks, 0, paired(heads, nodes))
+def build_rest(out, blocks, nodes, own_ends, other_ends):
     own_rows = (iota((128, 128), 0) >> 4) == row_col()[0]
     for half in range(2):
         own = jnp.broadcast_to(own_ends[half], (128, 128))
@@ -302,6 +301,11 @@
         put(out, blocks, 1 + half, jnp.where(own_rows, own, other))
     if blocks > 3:
         put(out, blocks, blocks - 1, beside(nodes))
+
+
+def build_message(out, blocks, heads, nodes, own_ends, other_ends):
+    put(out, blocks, 0, paired(heads, nodes))
+    build_rest(out, blocks, nodes, own_ends, other_ends)
 
 
 def partner_rows(blocks):
@@ -400,7 +404,7 @@
 
 def sweep_kernel(
     last, surface, near, far, gains_ref, cell_high, cell_low, zone_row, zone_col,
-    table, nodes, surface_out, heads_out, zone_out, out, cell_table, edge_ref, zone_ref,
+    message, nodes, surface_out, heads_out, zone_out, out, cell_table, edge_ref, zone_ref,
 ):
     state = jnp.concatenate(
         [
@@ -417,10 +421,7 @@
         state, gains, cell_high, cell_low, zone_place, surface_out, heads_out, zone_out,
         cell_table, edge_ref, zone_ref,
     )
-    build_message(
-        out, 3 if last else 4, heads, nodes[...], (table[0:1, :], table[32:33, :]),
-        (table[31:32, :], table[63:64, :]),
-    )
+    put(out, 3 if last else 4, 0, paired(heads, nodes[...]))
 
 
 def relayed(got, blocks):
@@ -502,7 +503,7 @@
     if last:
         pipes_out, value_ref, ends_ref = rest
     else:
-        table_out, nodes_out, value_ref, ends_ref = rest
+        table_out, nodes_out, out, value_ref, ends_ref = rest
     if inflow is None:
         inflow = inflow_of(blocks, got, nodes, node_high, node_low, coef, value_ref)
     balance = table[...] + inflow
@@ -541,14 +542,19 @@
         return
     table_out[0:32, :] = parts[0]
     table_out[32:64, :] = parts[1]
-    nodes_out[...] = gathered(table_out, 64, node_high[...], node_low[...])
+    heads = gathered(table_out, 64, node_high[...], node_low[...])
+    nodes_out[...] = heads
+    build_rest(
+        out, 4 if first else 3, heads, (parts[0][0:1], parts[1][0:1]),
+        (parts[0][31:32], parts[1][31:32]),
+    )
 
 
 def shape(*dims, dtype=F32):
     return jax.ShapeDtypeStruct(dims, dtype)
 
 
-def call(kernel, inputs, outputs, scratch=(), space=pltpu.VMEM, flops=10**9):
+def call(kernel, inputs, outputs, scratch=(), space=pltpu.VMEM, flops=10**9, aliases=()):
     vmem = pl.BlockSpec(memory_space=pltpu.VMEM)
     return pl.pallas_call(
         kernel,
@@ -556,6 +562,7 @@
         in_specs=[pl.BlockSpec(memory_space=space)] * len(inputs),
         out_specs=[vmem] * len(outputs),
         scratch_shapes=list(scratch),
+        input_output_aliases=dict(aliases),
         compiler_params=pltpu.CompilerParams(vmem_limit_bytes=16 << 20),
         cost_estimate=pl.CostEstimate(flops=flops, bytes_accessed=1 << 20, transcendentals=0),
     )(*inputs)
@@ -643,8 +650,8 @@
             surface, heads, zone, sent = call(
                 functools.partial(sweep_kernel, last),
                 (surface, near, far, gains, cell_high, cell_low, zone_row, zone_col,
-                 table, nodes),
-                [*swept_shapes, shape(384 if last else 512, 128)], gather_scratch,
+                 sent, nodes),
+                [*swept_shapes, shape(384 if last else 512, 128)], gather_scratch, aliases={8: 3},
             )
         got = lax.all_to_all(
             sent.reshape(128, 1, -1), ("row", "col"), split_axis=0, concat_axis=0, tiled=True
@@ -681,9 +688,9 @@
                 owner_scratch[:1], flops=10**6,
             )
             owner_inputs += (near, inflow)
-        table, nodes = call(
+        table, nodes, sent = call(
             functools.partial(owner_kernel, first, False), (got, *owner_inputs),
-            [shape(64, 128), shape(64, 128)], owner_scratch,
+            [shape(64, 128), shape(64, 128), shape(512 if first else 384, 128)], owner_scratch,
         )
         if first:
             coefs = tuple(new_coefs)

time: 83.4 us -> 83.4 us (level)
  transfers between devices with their start and end apart: 9 -> 9, of which waited for: 3 -> 2; matrix products, arithmetic and copies ran while one was open for 0% -> 0% of each run, Pallas kernels for 9% -> 9%
where the time goes in v11:
time: 83.4 us; the launch traced here: 83.2 us
  blocking collectives  54.5 us (65%)
  Pallas kernels  17.4 us (21%)
  starting transfers between devices  8.53 us (10%)
  waiting for transfers between devices  1.53 us (2%)
  between operations  0.89 us (1%)
    all_to_all x3, blocking collectives, body(): lax.all_to_all(sent.reshape(128, 1, -1), ('row', 'col'), split_axis=0, co...  54.5 us
    pallas_call x17, Pallas kernels, call(): pl.pallas_call(kernel, out_shape=outputs, in_specs=[pl.BlockSpec(memory_s...  17.4 us
    ppermute x4, starting transfers between devices, swapped(): far = lax.ppermute(far, ('row', 'col'), routes[1])  4.94 us
    ppermute x4, starting transfers between devices, swapped(): return (lax.ppermute(near, ('row', 'col'), routes[0]), far)  3.12 us
  transfers between devices with their start and end apart: 9, of which 2 were waited for; matrix products, arithmetic and copies ran while one was open for 0% of the time, Pallas kernels for 9%

profile of v11, /device:TPU:1, one launch (start us, length us, event | category | flops | bytes accessed | tf_op | source)
XLA Modules:
  0.0 83.2 jit_solution(3266706173542614112)
XLA Ops:
  0.6 0.0 copy-start.1
  0.6 0.0 copy-start.5
  0.7 0.0 copy-start.6
  0.7 0.0 copy-start
  0.7 0.0 copy-start.4
  0.7 0.0 copy-start.3
  0.7 0.0 copy-start.2
  0.7 1.1 %shard_map.140 = (f32[5,64,256]{2,1,0:T(8,128)S(1)}, f32[48,128]{1,0:T(8,128)S(1)}, f32[40,128]{1,0:T(8,128)S(1)}) custom-call(f32[64,256]{1,0:T(8,128)} %surface.1, f32[64,256]{1,0:T(8,128)} %cond_x.1, f32[64,256]{1,0:T(8,128)} %cond_y.1, f32[64,256]{1,0:T(8,128)} %porosity.1, f32[64,256]{1,0:T(8,128)} %rainfall.1, f32[32,256]{1,0:T(8,128)} %pipes.3), custom_call_target="tpu_custom_call" | custom-call | flops 1000000000 | bytes 1048576 | tf_op jit(solution)/shard_map/pallas_call | solution.py:559
  1.8 0.0 copy-start.7
  1.8 2.7 %collective-permute-start.1 = (f32[40,128]{1,0:T(8,128)S(1)}, f32[40,128]{1,0:T(8,128)S(1)}, u32[]{:S(2)}, u32[]{:S(2)}) collective-permute-start(f32[40,128]{1,0:T(8,128)S(1)} %get-tuple-element.55), channel_id=1, source_target_pairs={{0,1},{1,0},{2,3},{3,2},{4,5},{5,4},{6,7},{7,6},{8,9},{9,8},{10,11... | collective-permute-start | bytes 61448 | tf_op jit(solution)/shard_map/ppermute | solution.py:596
  4.5 0.5 collective-permute-start
  5.0 0.0 copy-done.5
  5.0 0.1 copy.20
  5.1 0.0 copy-done.6
  5.1 0.1 copy.21
  5.2 0.0 copy-done.1
  5.2 0.0 copy-done
  5.2 0.0 copy-done.4
  5.2 0.0 copy-done.3
  5.2 0.0 copy-done.2
  5.3 0.7 shard_map.142
  6.0 0.0 copy-done.7
  6.0 0.1 copy.22
  6.1 0.0 collective-permute-done.1.far
  6.1 0.0 collective-permute-done.near
  6.1 0.1 shard_map.143
  6.2 1.1 %collective-permute-start.3 = (f32[136,128]{1,0:T(8,128)S(1)}, f32[136,128]{1,0:T(8,128)S(1)}, u32[]{:S(2)}, u32[]{:S(2)}) collective-permute-start(f32[136,128]{1,0:T(8,128)S(1)} %get-tuple-element.62), channel_id=1, source_target_pairs={{0,16},{1,2},{2,1},{3,4},{4,3},{5,6},{6,5},{7,8},{8,7},{9,10},{10,... | collective-permute-start | bytes 208904 | tf_op jit(solution)/shard_map/ppermute | solution.py:596
  7.3 1.5 %collective-permute-start.2 = (f32[136,128]{1,0:T(8,128)S(1)}, f32[136,128]{1,0:T(8,128)S(1)}, u32[]{:S(2)}, u32[]{:S(2)}) collective-permute-start(f32[136,128]{1,0:T(8,128)S(1)} %get-tuple-element.62), channel_id=1, source_target_pairs={{0,1},{1,0},{2,3},{3,2},{4,5},{5,4},{6,7},{7,6},{8,9},{9,8},{10,11... | collective-permute-start | bytes 208904 | tf_op jit(solution)/shard_map/ppermute | solution.py:597
  8.8 1.4 %shard_map.145.hot = bf16[8192,256]{1,0:T(8,128)(2,1)S(1)} custom-call(s32[128,64]{1,0:T(8,128)S(1)} %bitcast.23), custom_call_target="tpu_custom_call" | custom-call | flops 1000000000 | bytes 1048576 | tf_op jit(solution)/shard_map/pallas_call | solution.py:559
  10.2 0.0 collective-permute-done.3.far_col
  10.3 0.3 collective-permute-done.2.near_col
  10.5 1.8 %shard_map.144 = (f32[6,72,384]{2,1,0:T(8,128)S(1)}, f32[64,384]{1,0:T(8,128)S(1)}, s32[64,128]{1,0:T(8,128)S(1)}, s32[64,128]{1,0:T(8,128)S(1)}, s32[128,128]{1...) custom-call(f32[5,72,256]{2,1,0:T(8,128)S(1)} %get-tuple-element.60., ...), custom_call_target="tpu_custom_call" | custom-call | flops 1000000000 | bytes 1048576 | tf_op jit(solution)/shard_map/pallas_call | solution.py:559
  12.3 25.0 %all_to_all.15 = f32[128,1,768]{2,1,0:T(1,128)S(1)} all-to-all(f32[128,1,768]{2,1,0:T(1,128)S(1)} %bitcast.21), channel_id=1, replica_groups=mesh['row'=8,'col'=16] {'row','col'}, dimensions={0} | all-to-all | bytes 786432 | tf_op jit(solution)/shard_map/all_to_all | solution.py:656
  37.3 1.4 %shard_map.146 = (f32[64,384]{1,0:T(8,128)S(1)}, f32[12,128]{1,0:T(8,128)S(1)}, f32[12,128]{1,0:T(8,128)S(1)}, f32[64,128]{1,0:T(8,128)S(1)}, f32[128,128]{1,0:T(8,128)S(1)}) custom-call(f32[768,128]{1,0:T(8,128)S(1)} %bitcast.16, f32[64,384]{1,0:T(8,128)S(1)} %get-tuple-element.69.surface, f32[64,384]{1,0:T(8,128)S(1)} %get-tuple-element.70.inverse, ...), custom_call_target="tpu_custom_call" | custom-call | flops 1000000000 | bytes 1048576 | tf_op jit(solution)/shard_map/pallas_call | solution.py:559
  38.7 0.8 %collective-permute-start.5 = (f32[12,128]{1,0:T(8,128)S(1)}, f32[12,128]{1,0:T(8,128)S(1)}, u32[]{:S(2)}, u32[]{:S(2)}) collective-permute-start(f32[12,128]{1,0:T(8,128)S(1)} %shard_map.147), channel_id=1, source_target_pairs={{0,1},{1,0},{2,3},{3,2},{4,5},{5,4},{6,7},{7,6},{8,9},{9,8},{10,11... | collective-permute-start | bytes 18440 | tf_op jit(solution)/shard_map/ppermute | solution.py:596
  39.5 0.4 collective-permute-start.4
  39.9 1.8 %shard_map.148 = (f32[64,128]{1,0:T(8,128)S(1)}, f32[64,128]{1,0:T(8,128)S(1)}, f32[512,128]{1,0:T(8,128)S(1)}) custom-call(f32[768,128]{1,0:T(8,128)S(1)} %bitcast.17, f32[64,128]{1,0:T(8,128)S(1)} %get-tuple-element.64.nodes, s32[64,128]{1,0:T(8,128)S(1)} %get-tuple-element.82.node_high, s32[64,128]{1,0:T(8,128)S(1)} %get-tuple-element.83.node_low, ...), custom_call_target="tpu_custom_call" | custom-call | flops 1000000000 | bytes 1048576 | tf_op jit(solution)/shard_map/pallas_call | solution.py:559
  41.8 0.0 collective-permute-done.5.far
  41.8 0.0 collective-permute-done.4.near
  41.8 1.5 %shard_map.149 = (f32[64,384]{1,0:T(8,128)S(1)}, f32[64,128]{1,0:T(8,128)S(1)}, f32[128,128]{1,0:T(8,128)S(1)}, f32[512,128]{1,0:T(8,128)S(1)}) custom-call(f32[64,384]{1,0:T(8,128)S(1)} %get-tuple-element.77.surface, f32[12,128]{1,0:T(8,128)S(1)} %collective-permute-done.4.near, ...), custom_call_target="tpu_custom_call", output_to_operand_aliasing={{3}: (8, {})} | custom-call | flops 1000000000 | bytes 1048576 | tf_op jit(solution)/shard_map/pallas_call | solution.py:559
  43.3 15.5 %all_to_all.16 = f32[128,1,512]{2,1,0:T(1,128)S(1)} all-to-all(f32[128,1,512]{2,1,0:T(1,128)S(1)} %bitcast.25), channel_id=1, replica_groups=mesh['row'=8,'col'=16] {'row','col'}, dimensions={0} | all-to-all | bytes 524288 | tf_op jit(solution)/shard_map/all_to_all | solution.py:656
  58.8 1.4 %shard_map.150 = (f32[64,384]{1,0:T(8,128)S(1)}, f32[48,128]{1,0:T(8,128)S(1)}, f32[12,128]{1,0:T(8,128)S(1)}) custom-call(f32[512,128]{1,0:T(8,128)S(1)} %bitcast.13, f32[64,384]{1,0:T(8,128)S(1)} %get-tuple-element.90.surface, f32[64,384]{1,0:T(8,128)S(1)} %get-tuple-element.70.inverse, f32[64,128]{1,0:T(8,128)S(1)} %get-tuple-element.91.heads, ...), custom_call_target="tpu_custom_call" | custom-call | flops 1000000000 | bytes 1048576 | tf_op jit(solution)/shard_map/pallas_call | solution.py:559
  60.2 0.8 collective-permute-start.6
  61.0 0.3 collective-permute-start.7
  61.3 0.8 shard_map.151.rest_1_
  62.0 0.0 collective-permute-done.6.rest_0_.near
  62.0 1.1 %shard_map.152 = (f32[64,128]{1,0:T(8,128)S(1)}, f32[64,128]{1,0:T(8,128)S(1)}, f32[384,128]{1,0:T(8,128)S(1)}) custom-call(f32[512,128]{1,0:T(8,128)S(1)} %bitcast.15, f32[64,128]{1,0:T(8,128)S(1)} %get-tuple-element.88.nodes, s32[64,128]{1,0:T(8,128)S(1)} %get-tuple-element.82.node_high, s32[64,128]{1,0:T(8,128)S(1)} %get-tuple-element.83.node_low, ...), custom_call_target="tpu_custom_call" | custom-call | flops 1000000000 | bytes 1048576 | tf_op jit(solution)/shard_map/pallas_call | solution.py:559
  63.1 1.2 %collective-permute-done.7.far = f32[12,128]{1,0:T(8,128)S(1)} collective-permute-done((f32[12,128]{1,0:T(8,128)S(1)}, f32[12,128]{1,0:T(8,128)S(1)}, u32[]{:S(2)}, u32[]{:S(2)}) %collective-permute-start.7) | collective-permute-done | bytes 6176 | tf_op jit(solution)/shard_map/ppermute | solution.py:596
  64.3 1.3 %shard_map.153 = (f32[64,384]{1,0:T(8,128)S(1)}, f32[64,128]{1,0:T(8,128)S(1)}, f32[128,128]{1,0:T(8,128)S(1)}, f32[384,128]{1,0:T(8,128)S(1)}) custom-call(f32[64,384]{1,0:T(8,128)S(1)} %get-tuple-element.95.surface, f32[48,128]{1,0:T(8,128)S(1)} %collective-permute-done.6.rest_0_.near, ...), custom_call_target="tpu_custom_call", output_to_operand_aliasing={{3}: (8, {})} | custom-call | flops 1000000000 | bytes 1048576 | tf_op jit(solution)/shard_map/pallas_call | solution.py:559
  65.6 14.1 %all_to_all.17 = f32[128,1,384]{2,1,0:T(1,128)S(1)} all-to-all(f32[128,1,384]{2,1,0:T(1,128)S(1)} %bitcast.26), channel_id=1, replica_groups=mesh['row'=8,'col'=16] {'row','col'}, dimensions={0} | all-to-all | bytes 393216 | tf_op jit(solution)/shard_map/all_to_all | solution.py:656
  79.7 0.5 collective-permute-start.8
  80.2 1.4 %shard_map.154 = f32[64,256]{1,0:T(8,128)} custom-call(f32[384,128]{1,0:T(8,128)S(1)} %bitcast.19, f32[64,384]{1,0:T(8,128)S(1)} %get-tuple-element.102.surface, f32[64,384]{1,0:T(8,128)S(1)} %get-tuple-element.70.inverse, f32[64,128]{1,0:T(8,128)S(1)} %get-tuple-element.103.heads, f32[128,128]{1,0:T(8,128)S(1)} %get-tuple-element.104.zone, ...), custom_call_target="tpu_custom_call" | custom-call | flops 1000000000 | bytes 1048576 | tf_op jit(solution)/shard_map/pallas_call | solution.py:559
  81.6 0.0 collective-permute-done.8.rest_0_
  81.6 1.6 %shard_map.156 = f32[32,256]{1,0:T(8,128)} custom-call(f32[384,128]{1,0:T(8,128)S(1)} %bitcast.20, f32[64,128]{1,0:T(8,128)S(1)} %get-tuple-element.100.nodes, s32[64,128]{1,0:T(8,128)S(1)} %get-tuple-element.82.node_high, s32[64,128]{1,0:T(8,128)S(1)} %get-tuple-element.83.node_low, f32[64,128]{1,0:T(8,128)S(1)} %get-tuple-element.65.coef, ...), custom_call_target="tpu_custom_call" | custom-call | flops 1000000000 | bytes 1048576 | tf_op jit(solution)/shard_map/pallas_call | solution.py:559
  (3 shorter events, 0.0 us)
Async XLA Ops:
  0.6 4.6 %copy-start.1 = (f32[32,256]{1,0:T(8,128)S(1)}, f32[32,256]{1,0:T(8,128)}, u32[]{:S(2)}) copy-start(f32[32,256]{1,0:T(8,128)} %pipes.3) | copy-start | bytes 98308
  0.6 4.4 %copy-start.5 = (s32[128,1,64]{0,2,1:T(8,128)S(1)}, s32[128,1,64]{0,2,1:T(8,128)}, u32[]{:S(2)}) copy-start(s32[128,1,64]{0,2,1:T(8,128)} %param.24) | copy-start | bytes 98308
  0.7 4.4 %copy-start.6 = (f32[128,1,64]{0,2,1:T(8,128)S(1)}, f32[128,1,64]{0,2,1:T(8,128)}, u32[]{:S(2)}) copy-start(f32[128,1,64]{0,2,1:T(8,128)} %param.25) | copy-start | bytes 98308
  0.7 4.6 %copy-start = (f32[4,32,32]{2,1,0:T(8,128)S(1)}, f32[4,32,32]{2,1,0:T(8,128)}, u32[]{:S(2)}) copy-start(f32[4,32,32]{2,1,0:T(8,128)} %param.22) | copy-start | bytes 49156
  0.7 4.6 %copy-start.4 = (s32[256]{0:T(256)S(1)}, s32[256]{0:T(256)}, u32[]{:S(2)}) copy-start(s32[256]{0:T(256)} %param.21) | copy-start | bytes 3076
  0.7 4.6 %copy-start.3 = (s32[256]{0:T(256)S(1)}, s32[256]{0:T(256)}, u32[]{:S(2)}) copy-start(s32[256]{0:T(256)} %param.20) | copy-start | bytes 3076
  0.7 4.6 %copy-start.2 = (s32[256]{0:T(256)S(1)}, s32[256]{0:T(256)}, u32[]{:S(2)}) copy-start(s32[256]{0:T(256)} %param.19) | copy-start | bytes 3076
  1.8 4.1 %copy-start.7 = (s32[1,128,64]{1,2,0:T(8,128)S(1)}, s32[1,128,64]{1,2,0:T(8,128)}, u32[]{:S(2)}) copy-start(s32[1,128,64]{1,2,0:T(8,128)} %param.23) | copy-start | bytes 98308
  1.8 4.2 %collective-permute-start.1 = (f32[40,128]{1,0:T(8,128)S(1)}, f32[40,128]{1,0:T(8,128)S(1)}, u32[]{:S(2)}, u32[]{:S(2)}) collective-permute-start(f32[40,128]{1,0:T(8,128)S(1)} %get-tuple-element.55), channel_id=1, source_target_pairs={{0,1},{1,0},{2,3},{3,2},{4,5},{5,4},{6,7},{7,6},{8,9},{9,8},{10,11... | collective-permute-start | bytes 61448 | tf_op jit(solution)/shard_map/ppermute | solution.py:596
  4.5 1.6 %collective-permute-start = (f32[48,128]{1,0:T(8,128)S(1)}, f32[48,128]{1,0:T(8,128)S(1)}, u32[]{:S(2)}, u32[]{:S(2)}) collective-permute-start(f32[48,128]{1,0:T(8,128)S(1)} %shard_map.141), channel_id=1, source_target_pairs={{0,16},{1,17},{2,18},{3,19},{4,20},{5,21},{6,22},{7,23},{8,24},{9,... | collective-permute-start | bytes 73736 | tf_op jit(solution)/shard_map/ppermute | solution.py:597
  6.2 4.0 %collective-permute-start.3 = (f32[136,128]{1,0:T(8,128)S(1)}, f32[136,128]{1,0:T(8,128)S(1)}, u32[]{:S(2)}, u32[]{:S(2)}) collective-permute-start(f32[136,128]{1,0:T(8,128)S(1)} %get-tuple-element.62), channel_id=1, source_target_pairs={{0,16},{1,2},{2,1},{3,4},{4,3},{5,6},{6,5},{7,8},{8,7},{9,10},{10,... | collective-permute-start | bytes 208904 | tf_op jit(solution)/shard_map/ppermute | solution.py:596
  7.3 3.2 %collective-permute-start.2 = (f32[136,128]{1,0:T(8,128)S(1)}, f32[136,128]{1,0:T(8,128)S(1)}, u32[]{:S(2)}, u32[]{:S(2)}) collective-permute-start(f32[136,128]{1,0:T(8,128)S(1)} %get-tuple-element.62), channel_id=1, source_target_pairs={{0,1},{1,0},{2,3},{3,2},{4,5},{5,4},{6,7},{7,6},{8,9},{9,8},{10,11... | collective-permute-start | bytes 208904 | tf_op jit(solution)/shard_map/ppermute | solution.py:597
  38.7 3.2 %collective-permute-start.5 = (f32[12,128]{1,0:T(8,128)S(1)}, f32[12,128]{1,0:T(8,128)S(1)}, u32[]{:S(2)}, u32[]{:S(2)}) collective-permute-start(f32[12,128]{1,0:T(8,128)S(1)} %shard_map.147), channel_id=1, source_target_pairs={{0,1},{1,0},{2,3},{3,2},{4,5},{5,4},{6,7},{7,6},{8,9},{9,8},{10,11... | collective-permute-start | bytes 18440 | tf_op jit(solution)/shard_map/ppermute | solution.py:596
  39.5 2.3 %collective-permute-start.4 = (f32[12,128]{1,0:T(8,128)S(1)}, f32[12,128]{1,0:T(8,128)S(1)}, u32[]{:S(2)}, u32[]{:S(2)}) collective-permute-start(f32[12,128]{1,0:T(8,128)S(1)} %get-tuple-element.78), channel_id=1, source_target_pairs={{0,16},{1,17},{2,18},{3,19},{4,20},{5,21},{6,22},{7,23},{8,24},{9,... | collective-permute-start | bytes 18440 | tf_op jit(solution)/shard_map/ppermute | solution.py:597
  60.2 1.8 %collective-permute-start.6 = (f32[48,128]{1,0:T(8,128)S(1)}, f32[48,128]{1,0:T(8,128)S(1)}, u32[]{:S(2)}, u32[]{:S(2)}) collective-permute-start(f32[48,128]{1,0:T(8,128)S(1)} %get-tuple-element.96), channel_id=1, source_target_pairs={{0,16},{1,17},{2,18},{3,19},{4,20},{5,21},{6,22},{7,23},{8,24},{9,... | collective-permute-start | bytes 73736 | tf_op jit(solution)/shard_map/ppermute | solution.py:597
  61.0 3.3 %collective-permute-start.7 = (f32[12,128]{1,0:T(8,128)S(1)}, f32[12,128]{1,0:T(8,128)S(1)}, u32[]{:S(2)}, u32[]{:S(2)}) collective-permute-start(f32[12,128]{1,0:T(8,128)S(1)} %get-tuple-element.97), channel_id=1, source_target_pairs={{0,1},{1,0},{2,3},{3,2},{4,5},{5,4},{6,7},{7,6},{8,9},{9,8},{10,11... | collective-permute-start | bytes 18440 | tf_op jit(solution)/shard_map/ppermute | solution.py:596
  79.7 1.9 %collective-permute-start.8 = (f32[32,128]{1,0:T(8,128)S(1)}, f32[32,128]{1,0:T(8,128)S(1)}, u32[]{:S(2)}, u32[]{:S(2)}) collective-permute-start(f32[32,128]{1,0:T(8,128)S(1)} %shard_map.155), channel_id=1, source_target_pairs={{0,16},{1,17},{2,18},{3,19},{4,20},{5,21},{6,22},{7,23},{8,24},{9,... | collective-permute-start | bytes 49160 | tf_op jit(solution)/shard_map/ppermute | solution.py:591

commit v12 on v10

--- a/solution.py
+++ b/solution.py
@@ -492,13 +492,28 @@
     out[...] = inflow_of(4, got, nodes, node_high, node_low, coef, value_ref)
 
 
+def last_kernel(
+    got, surface, inverse, heads, zone, cell_high, hot, zone_row, zone_col, own_coef, zone_coef,
+    nodes, node_high, node_low, coef, surface_out, inflow, value_ref, zone_value_ref, row_ref,
+    node_value_ref, held, sent,
+):
+    tile_kernel(
+        False, True, got, surface, inverse, heads, zone, cell_high, hot, zone_row, zone_col,
+        own_coef, zone_coef, held, value_ref, zone_value_ref, row_ref,
+    )
+    copy = pltpu.make_async_copy(held, surface_out, sent)
+    copy.start()
+    inflow[...] = inflow_of(3, got, nodes, node_high, node_low, coef, node_value_ref)
+    copy.wait()
+
+
 def owner_kernel(
     first, last, got, nodes, node_high, node_low, coef, table, meets, classes, matrices, *rest
 ):
     blocks = 6 if first else 3 if last else 4
     rest = list(rest)
     relay = None if first else rest.pop(0)
-    inflow = None if first or last else rest.pop(0)[...]
+    inflow = None if first else rest.pop(0)[...]
     if last:
         pipes_out, value_ref, ends_ref = rest
     else:
@@ -548,13 +563,13 @@
     return jax.ShapeDtypeStruct(dims, dtype)
 
 
-def call(kernel, inputs, outputs, scratch=(), space=pltpu.VMEM, flops=10**9):
-    vmem = pl.BlockSpec(memory_space=pltpu.VMEM)
+def call(kernel, inputs, outputs, scratch=(), space=pltpu.VMEM, flops=10**9, spaces=None):
+    spaces = spaces or [pltpu.VMEM] * len(outputs)
     return pl.pallas_call(
         kernel,
         out_shape=outputs,
         in_specs=[pl.BlockSpec(memory_space=space)] * len(inputs),
-        out_specs=[vmem] * len(outputs),
+        out_specs=[pl.BlockSpec(memory_space=out) for out in spaces],
         scratch_shapes=list(scratch),
         compiler_params=pltpu.CompilerParams(vmem_limit_bytes=16 << 20),
         cost_estimate=pl.CostEstimate(flops=flops, bytes_accessed=1 << 20, transcendentals=0),
@@ -658,12 +673,16 @@
         if last:
             (relay,) = call(relay_kernel, (got,), [shape(32, 128)])
             relay = swapped(relay, None, 0)
-            (surface_out,) = call(
-                functools.partial(tile_kernel, False, True), (got, *tile_inputs), [shape(64, 256)],
-                tile_scratch,
+            surface_out, inflow = call(
+                last_kernel, (got, *tile_inputs, nodes, node_high, node_low, coef),
+                [shape(64, 256), shape(64, 128)],
+                tile_scratch + [
+                    pltpu.VMEM((64, 128), F32), pltpu.VMEM((64, 256), F32), pltpu.SemaphoreType.DMA
+                ],
+                spaces=[pltpu.HBM, pltpu.VMEM],
             )
             (pipes_out,) = call(
-                functools.partial(owner_kernel, False, True), (got, *owner_inputs, relay),
+                functools.partial(owner_kernel, False, True), (got, *owner_inputs, relay, inflow),
                 [shape(32, 256)], owner_scratch,
             )
             return surface_out, pipes_out

time: 83.4 us -> 83.4 us (level)
  no operation moved by 1% of the time
where the time goes in v12:
time: 83.4 us; the launch traced here: 83.1 us
  blocking collectives  54.5 us (65%)
  Pallas kernels  17.2 us (21%)
  starting transfers between devices  8.53 us (10%)
  waiting for transfers between devices  1.6 us (2%)
  between operations  0.91 us (1%)
    all_to_all x3, blocking collectives, body(): lax.all_to_all(sent.reshape(128, 1, -1), ('row', 'col'), split_axis=0, co...  54.5 us
    pallas_call x17, Pallas kernels, call(): pl.pallas_call(kernel, out_shape=outputs, in_specs=[pl.BlockSpec(memory_s...  17.2 us
    ppermute x4, starting transfers between devices, swapped(): far = lax.ppermute(far, ('row', 'col'), routes[1])  4.94 us
    ppermute x4, starting transfers between devices, swapped(): return (lax.ppermute(near, ('row', 'col'), routes[0]), far)  3.12 us
  transfers between devices with their start and end apart: 9, of which 3 were waited for; matrix products, arithmetic and copies ran while one was open for 0% of the time, Pallas kernels for 9%

profile of v12, /device:TPU:1, one launch (start us, length us, event | category | flops | bytes accessed | tf_op | source)
XLA Modules:
  0.0 83.1 jit_solution(8143534292355189454)
XLA Ops:
  0.6 0.0 copy-start.1
  0.6 0.0 copy-start.5
  0.7 0.0 copy-start.6
  0.7 0.0 copy-start
  0.7 0.0 copy-start.4
  0.7 0.0 copy-start.3
  0.7 0.0 copy-start.2
  0.7 1.1 %shard_map.140 = (f32[5,64,256]{2,1,0:T(8,128)S(1)}, f32[48,128]{1,0:T(8,128)S(1)}, f32[40,128]{1,0:T(8,128)S(1)}) custom-call(f32[64,256]{1,0:T(8,128)} %surface.1, f32[64,256]{1,0:T(8,128)} %cond_x.1, f32[64,256]{1,0:T(8,128)} %cond_y.1, f32[64,256]{1,0:T(8,128)} %porosity.1, f32[64,256]{1,0:T(8,128)} %rainfall.1, f32[32,256]{1,0:T(8,128)} %pipes.3), custom_call_target="tpu_custom_call" | custom-call | flops 1000000000 | bytes 1048576 | tf_op jit(solution)/shard_map/pallas_call | solution.py:568
  1.8 0.0 copy-start.7
  1.8 2.7 %collective-permute-start.1 = (f32[40,128]{1,0:T(8,128)S(1)}, f32[40,128]{1,0:T(8,128)S(1)}, u32[]{:S(2)}, u32[]{:S(2)}) collective-permute-start(f32[40,128]{1,0:T(8,128)S(1)} %get-tuple-element.55), channel_id=1, source_target_pairs={{0,1},{1,0},{2,3},{3,2},{4,5},{5,4},{6,7},{7,6},{8,9},{9,8},{10,11... | collective-permute-start | bytes 61448 | tf_op jit(solution)/shard_map/ppermute | solution.py:604
  4.5 0.5 collective-permute-start
  5.0 0.0 copy-done.5
  5.0 0.1 copy.18
  5.1 0.0 copy-done.6
  5.1 0.1 copy.19
  5.2 0.0 copy-done.1
  5.2 0.0 copy-done
  5.2 0.0 copy-done.4
  5.2 0.0 copy-done.3
  5.2 0.0 copy-done.2
  5.3 0.7 shard_map.142
  6.0 0.0 copy-done.7
  6.0 0.1 copy.20
  6.1 0.0 collective-permute-done.1.far
  6.1 0.0 collective-permute-done.near
  6.1 0.1 shard_map.143
  6.2 1.1 %collective-permute-start.3 = (f32[136,128]{1,0:T(8,128)S(1)}, f32[136,128]{1,0:T(8,128)S(1)}, u32[]{:S(2)}, u32[]{:S(2)}) collective-permute-start(f32[136,128]{1,0:T(8,128)S(1)} %get-tuple-element.62), channel_id=1, source_target_pairs={{0,16},{1,2},{2,1},{3,4},{4,3},{5,6},{6,5},{7,8},{8,7},{9,10},{10,... | collective-permute-start | bytes 208904 | tf_op jit(solution)/shard_map/ppermute | solution.py:604
  7.3 1.5 %collective-permute-start.2 = (f32[136,128]{1,0:T(8,128)S(1)}, f32[136,128]{1,0:T(8,128)S(1)}, u32[]{:S(2)}, u32[]{:S(2)}) collective-permute-start(f32[136,128]{1,0:T(8,128)S(1)} %get-tuple-element.62), channel_id=1, source_target_pairs={{0,1},{1,0},{2,3},{3,2},{4,5},{5,4},{6,7},{7,6},{8,9},{9,8},{10,11... | collective-permute-start | bytes 208904 | tf_op jit(solution)/shard_map/ppermute | solution.py:605
  8.8 1.4 %shard_map.145.hot = bf16[8192,256]{1,0:T(8,128)(2,1)S(1)} custom-call(s32[128,64]{1,0:T(8,128)S(1)} %bitcast.23), custom_call_target="tpu_custom_call" | custom-call | flops 1000000000 | bytes 1048576 | tf_op jit(solution)/shard_map/pallas_call | solution.py:568
  10.2 0.0 collective-permute-done.3.far_col
  10.3 0.3 collective-permute-done.2.near_col
  10.5 1.8 %shard_map.144 = (f32[6,72,384]{2,1,0:T(8,128)S(1)}, f32[64,384]{1,0:T(8,128)S(1)}, s32[64,128]{1,0:T(8,128)S(1)}, s32[64,128]{1,0:T(8,128)S(1)}, s32[128,128]{1...) custom-call(f32[5,72,256]{2,1,0:T(8,128)S(1)} %get-tuple-element.60., ...), custom_call_target="tpu_custom_call" | custom-call | flops 1000000000 | bytes 1048576 | tf_op jit(solution)/shard_map/pallas_call | solution.py:568
  12.3 25.0 %all_to_all.15 = f32[128,1,768]{2,1,0:T(1,128)S(1)} all-to-all(f32[128,1,768]{2,1,0:T(1,128)S(1)} %bitcast.21), channel_id=1, replica_groups=mesh['row'=8,'col'=16] {'row','col'}, dimensions={0} | all-to-all | bytes 786432 | tf_op jit(solution)/shard_map/all_to_all | solution.py:664
  37.3 1.4 %shard_map.146 = (f32[64,384]{1,0:T(8,128)S(1)}, f32[12,128]{1,0:T(8,128)S(1)}, f32[12,128]{1,0:T(8,128)S(1)}, f32[64,128]{1,0:T(8,128)S(1)}, f32[128,128]{1,0:T(8,128)S(1)}) custom-call(f32[768,128]{1,0:T(8,128)S(1)} %bitcast.16, f32[64,384]{1,0:T(8,128)S(1)} %get-tuple-element.69.surface, f32[64,384]{1,0:T(8,128)S(1)} %get-tuple-element.70.inverse, ...), custom_call_target="tpu_custom_call" | custom-call | flops 1000000000 | bytes 1048576 | tf_op jit(solution)/shard_map/pallas_call | solution.py:568
  38.7 0.8 %collective-permute-start.5 = (f32[12,128]{1,0:T(8,128)S(1)}, f32[12,128]{1,0:T(8,128)S(1)}, u32[]{:S(2)}, u32[]{:S(2)}) collective-permute-start(f32[12,128]{1,0:T(8,128)S(1)} %shard_map.147), channel_id=1, source_target_pairs={{0,1},{1,0},{2,3},{3,2},{4,5},{5,4},{6,7},{7,6},{8,9},{9,8},{10,11... | collective-permute-start | bytes 18440 | tf_op jit(solution)/shard_map/ppermute | solution.py:604
  39.5 0.4 collective-permute-start.4
  39.9 1.8 %shard_map.148 = (f32[64,128]{1,0:T(8,128)S(1)}, f32[64,128]{1,0:T(8,128)S(1)}) custom-call(f32[768,128]{1,0:T(8,128)S(1)} %bitcast.17, f32[64,128]{1,0:T(8,128)S(1)} %get-tuple-element.64.nodes, s32[64,128]{1,0:T(8,128)S(1)} %get-tuple-element.82.node_high, s32[64,128]{1,0:T(8,128)S(1)} %get-tuple-element.83.node_low, ...), custom_call_target="tpu_custom_call" | custom-call | flops 1000000000 | bytes 1048576 | tf_op jit(solution)/shard_map/pallas_call | solution.py:568
  41.7 0.1 collective-permute-done.5.far
  41.8 0.0 collective-permute-done.4.near
  41.8 1.5 %shard_map.149 = (f32[64,384]{1,0:T(8,128)S(1)}, f32[64,128]{1,0:T(8,128)S(1)}, f32[128,128]{1,0:T(8,128)S(1)}, f32[512,128]{1,0:T(8,128)S(1)}) custom-call(f32[64,384]{1,0:T(8,128)S(1)} %get-tuple-element.77.surface, f32[12,128]{1,0:T(8,128)S(1)} %collective-permute-done.4.near, f32[12,128]{1,0:T(8,128)S(1)} %collective-permute-done.5.far, ...), custom_call_target="tpu_custom_call" | custom-call | flops 1000000000 | bytes 1048576 | tf_op jit(solution)/shard_map/pallas_call | solution.py:568
  43.4 15.5 %all_to_all.16 = f32[128,1,512]{2,1,0:T(1,128)S(1)} all-to-all(f32[128,1,512]{2,1,0:T(1,128)S(1)} %bitcast.25), channel_id=1, replica_groups=mesh['row'=8,'col'=16] {'row','col'}, dimensions={0} | all-to-all | bytes 524288 | tf_op jit(solution)/shard_map/all_to_all | solution.py:664
  58.8 1.4 %shard_map.150 = (f32[64,384]{1,0:T(8,128)S(1)}, f32[48,128]{1,0:T(8,128)S(1)}, f32[12,128]{1,0:T(8,128)S(1)}) custom-call(f32[512,128]{1,0:T(8,128)S(1)} %bitcast.13, f32[64,384]{1,0:T(8,128)S(1)} %get-tuple-element.90.surface, f32[64,384]{1,0:T(8,128)S(1)} %get-tuple-element.70.inverse, f32[64,128]{1,0:T(8,128)S(1)} %get-tuple-element.91.heads, ...), custom_call_target="tpu_custom_call" | custom-call | flops 1000000000 | bytes 1048576 | tf_op jit(solution)/shard_map/pallas_call | solution.py:568
  60.2 0.8 collective-permute-start.6
  61.0 0.3 collective-permute-start.7
  61.3 0.7 shard_map.151.rest_1_
  62.0 0.0 collective-permute-done.6.rest_0_.near
  62.0 1.1 %shard_map.152 = (f32[64,128]{1,0:T(8,128)S(1)}, f32[64,128]{1,0:T(8,128)S(1)}) custom-call(f32[512,128]{1,0:T(8,128)S(1)} %bitcast.15, f32[64,128]{1,0:T(8,128)S(1)} %get-tuple-element.88.nodes, s32[64,128]{1,0:T(8,128)S(1)} %get-tuple-element.82.node_high, s32[64,128]{1,0:T(8,128)S(1)} %get-tuple-element.83.node_low, ...), custom_call_target="tpu_custom_call" | custom-call | flops 1000000000 | bytes 1048576 | tf_op jit(solution)/shard_map/pallas_call | solution.py:568
  63.1 1.2 %collective-permute-done.7.far = f32[12,128]{1,0:T(8,128)S(1)} collective-permute-done((f32[12,128]{1,0:T(8,128)S(1)}, f32[12,128]{1,0:T(8,128)S(1)}, u32[]{:S(2)}, u32[]{:S(2)}) %collective-permute-start.7) | collective-permute-done | bytes 6176 | tf_op jit(solution)/shard_map/ppermute | solution.py:604
  64.3 1.3 %shard_map.153 = (f32[64,384]{1,0:T(8,128)S(1)}, f32[64,128]{1,0:T(8,128)S(1)}, f32[128,128]{1,0:T(8,128)S(1)}, f32[384,128]{1,0:T(8,128)S(1)}) custom-call(f32[64,384]{1,0:T(8,128)S(1)} %get-tuple-element.95.surface, f32[48,128]{1,0:T(8,128)S(1)} %collective-permute-done.6.rest_0_.near, f32[12,128]{1,0:T(8,128)S(1)} %collective-permute-done.7.far, ...), custom_call_target="tpu_custom_call" | custom-call | flops 1000000000 | bytes 1048576 | tf_op jit(solution)/shard_map/pallas_call | solution.py:568
  65.6 14.1 %all_to_all.17 = f32[128,1,384]{2,1,0:T(1,128)S(1)} all-to-all(f32[128,1,384]{2,1,0:T(1,128)S(1)} %bitcast.26), channel_id=1, replica_groups=mesh['row'=8,'col'=16] {'row','col'}, dimensions={0} | all-to-all | bytes 393216 | tf_op jit(solution)/shard_map/all_to_all | solution.py:664
  79.7 0.5 collective-permute-start.8
  80.2 1.9 %shard_map.154 = (f32[64,256]{1,0:T(8,128)}, f32[64,128]{1,0:T(8,128)S(1)}) custom-call(f32[384,128]{1,0:T(8,128)S(1)} %bitcast.19, f32[64,384]{1,0:T(8,128)S(1)} %get-tuple-element.101.surface, f32[64,384]{1,0:T(8,128)S(1)} %get-tuple-element.70.inverse, f32[64,128]{1,0:T(8,128)S(1)} %get-tuple-element.102.heads, f32[128,128]{1,0:T(8,128)S(1)} %get-tuple-element.103.zone, ...), custom_call_target="tpu_custom_call" | custom-call | flops 1000000000 | bytes 1048576 | tf_op jit(solution)/shard_map/pallas_call | solution.py:568
  82.1 0.0 collective-permute-done.8.rest_0_
  82.1 1.0 %shard_map.156 = f32[32,256]{1,0:T(8,128)} custom-call(f32[384,128]{1,0:T(8,128)S(1)} %bitcast.20, f32[64,128]{1,0:T(8,128)S(1)} %get-tuple-element.99.nodes, s32[64,128]{1,0:T(8,128)S(1)} %get-tuple-element.82.node_high, s32[64,128]{1,0:T(8,128)S(1)} %get-tuple-element.83.node_low, f32[64,128]{1,0:T(8,128)S(1)} %get-tuple-element.65.coef, ...), custom_call_target="tpu_custom_call" | custom-call | flops 1000000000 | bytes 1048576 | tf_op jit(solution)/shard_map/pallas_call | solution.py:568
  (3 shorter events, 0.0 us)
Async XLA Ops:
  0.6 4.6 %copy-start.1 = (f32[32,256]{1,0:T(8,128)S(1)}, f32[32,256]{1,0:T(8,128)}, u32[]{:S(2)}) copy-start(f32[32,256]{1,0:T(8,128)} %pipes.3) | copy-start | bytes 98308
  0.6 4.4 %copy-start.5 = (s32[128,1,64]{0,2,1:T(8,128)S(1)}, s32[128,1,64]{0,2,1:T(8,128)}, u32[]{:S(2)}) copy-start(s32[128,1,64]{0,2,1:T(8,128)} %param.24) | copy-start | bytes 98308
  0.7 4.4 %copy-start.6 = (f32[128,1,64]{0,2,1:T(8,128)S(1)}, f32[128,1,64]{0,2,1:T(8,128)}, u32[]{:S(2)}) copy-start(f32[128,1,64]{0,2,1:T(8,128)} %param.25) | copy-start | bytes 98308
  0.7 4.6 %copy-start = (f32[4,32,32]{2,1,0:T(8,128)S(1)}, f32[4,32,32]{2,1,0:T(8,128)}, u32[]{:S(2)}) copy-start(f32[4,32,32]{2,1,0:T(8,128)} %param.22) | copy-start | bytes 49156
  0.7 4.6 %copy-start.4 = (s32[256]{0:T(256)S(1)}, s32[256]{0:T(256)}, u32[]{:S(2)}) copy-start(s32[256]{0:T(256)} %param.21) | copy-start | bytes 3076
  0.7 4.6 %copy-start.3 = (s32[256]{0:T(256)S(1)}, s32[256]{0:T(256)}, u32[]{:S(2)}) copy-start(s32[256]{0:T(256)} %param.20) | copy-start | bytes 3076
  0.7 4.6 %copy-start.2 = (s32[256]{0:T(256)S(1)}, s32[256]{0:T(256)}, u32[]{:S(2)}) copy-start(s32[256]{0:T(256)} %param.19) | copy-start | bytes 3076
  1.8 4.1 %copy-start.7 = (s32[1,128,64]{1,2,0:T(8,128)S(1)}, s32[1,128,64]{1,2,0:T(8,128)}, u32[]{:S(2)}) copy-start(s32[1,128,64]{1,2,0:T(8,128)} %param.23) | copy-start | bytes 98308
  1.8 4.2 %collective-permute-start.1 = (f32[40,128]{1,0:T(8,128)S(1)}, f32[40,128]{1,0:T(8,128)S(1)}, u32[]{:S(2)}, u32[]{:S(2)}) collective-permute-start(f32[40,128]{1,0:T(8,128)S(1)} %get-tuple-element.55), channel_id=1, source_target_pairs={{0,1},{1,0},{2,3},{3,2},{4,5},{5,4},{6,7},{7,6},{8,9},{9,8},{10,11... | collective-permute-start | bytes 61448 | tf_op jit(solution)/shard_map/ppermute | solution.py:604
  4.5 1.6 %collective-permute-start = (f32[48,128]{1,0:T(8,128)S(1)}, f32[48,128]{1,0:T(8,128)S(1)}, u32[]{:S(2)}, u32[]{:S(2)}) collective-permute-start(f32[48,128]{1,0:T(8,128)S(1)} %shard_map.141), channel_id=1, source_target_pairs={{0,16},{1,17},{2,18},{3,19},{4,20},{5,21},{6,22},{7,23},{8,24},{9,... | collective-permute-start | bytes 73736 | tf_op jit(solution)/shard_map/ppermute | solution.py:605
  6.2 4.0 %collective-permute-start.3 = (f32[136,128]{1,0:T(8,128)S(1)}, f32[136,128]{1,0:T(8,128)S(1)}, u32[]{:S(2)}, u32[]{:S(2)}) collective-permute-start(f32[136,128]{1,0:T(8,128)S(1)} %get-tuple-element.62), channel_id=1, source_target_pairs={{0,16},{1,2},{2,1},{3,4},{4,3},{5,6},{6,5},{7,8},{8,7},{9,10},{10,... | collective-permute-start | bytes 208904 | tf_op jit(solution)/shard_map/ppermute | solution.py:604
  7.3 3.2 %collective-permute-start.2 = (f32[136,128]{1,0:T(8,128)S(1)}, f32[136,128]{1,0:T(8,128)S(1)}, u32[]{:S(2)}, u32[]{:S(2)}) collective-permute-start(f32[136,128]{1,0:T(8,128)S(1)} %get-tuple-element.62), channel_id=1, source_target_pairs={{0,1},{1,0},{2,3},{3,2},{4,5},{5,4},{6,7},{7,6},{8,9},{9,8},{10,11... | collective-permute-start | bytes 208904 | tf_op jit(solution)/shard_map/ppermute | solution.py:605
  38.7 3.2 %collective-permute-start.5 = (f32[12,128]{1,0:T(8,128)S(1)}, f32[12,128]{1,0:T(8,128)S(1)}, u32[]{:S(2)}, u32[]{:S(2)}) collective-permute-start(f32[12,128]{1,0:T(8,128)S(1)} %shard_map.147), channel_id=1, source_target_pairs={{0,1},{1,0},{2,3},{3,2},{4,5},{5,4},{6,7},{7,6},{8,9},{9,8},{10,11... | collective-permute-start | bytes 18440 | tf_op jit(solution)/shard_map/ppermute | solution.py:604
  39.5 2.3 %collective-permute-start.4 = (f32[12,128]{1,0:T(8,128)S(1)}, f32[12,128]{1,0:T(8,128)S(1)}, u32[]{:S(2)}, u32[]{:S(2)}) collective-permute-start(f32[12,128]{1,0:T(8,128)S(1)} %get-tuple-element.78), channel_id=1, source_target_pairs={{0,16},{1,17},{2,18},{3,19},{4,20},{5,21},{6,22},{7,23},{8,24},{9,... | collective-permute-start | bytes 18440 | tf_op jit(solution)/shard_map/ppermute | solution.py:605
  60.2 1.8 %collective-permute-start.6 = (f32[48,128]{1,0:T(8,128)S(1)}, f32[48,128]{1,0:T(8,128)S(1)}, u32[]{:S(2)}, u32[]{:S(2)}) collective-permute-start(f32[48,128]{1,0:T(8,128)S(1)} %get-tuple-element.96), channel_id=1, source_target_pairs={{0,16},{1,17},{2,18},{3,19},{4,20},{5,21},{6,22},{7,23},{8,24},{9,... | collective-permute-start | bytes 73736 | tf_op jit(solution)/shard_map/ppermute | solution.py:605
  61.0 3.3 %collective-permute-start.7 = (f32[12,128]{1,0:T(8,128)S(1)}, f32[12,128]{1,0:T(8,128)S(1)}, u32[]{:S(2)}, u32[]{:S(2)}) collective-permute-start(f32[12,128]{1,0:T(8,128)S(1)} %get-tuple-element.97), channel_id=1, source_target_pairs={{0,1},{1,0},{2,3},{3,2},{4,5},{5,4},{6,7},{7,6},{8,9},{9,8},{10,11... | collective-permute-start | bytes 18440 | tf_op jit(solution)/shard_map/ppermute | solution.py:604
  79.7 2.4 %collective-permute-start.8 = (f32[32,128]{1,0:T(8,128)S(1)}, f32[32,128]{1,0:T(8,128)S(1)}, u32[]{:S(2)}, u32[]{:S(2)}) collective-permute-start(f32[32,128]{1,0:T(8,128)S(1)} %shard_map.155), channel_id=1, source_target_pairs={{0,16},{1,17},{2,18},{3,19},{4,20},{5,21},{6,22},{7,23},{8,24},{9,... | collective-permute-start | bytes 49160 | tf_op jit(solution)/shard_map/ppermute | solution.py:599

commit v13 on v10

--- a/solution.py
+++ b/solution.py
@@ -333,10 +333,11 @@
     surface_out[...] = state[:64]
     cell_table[0:64, :] = state[:64, 0:128]
     cell_table[64:128, :] = state[:64, 128:256]
+    tiles = 4 if zone_place is None else 5
     heads = jnp.concatenate(
         [
-            gathered_by_product(cell_table[...], cell_high, cell_low, 4),
-            gathered(cell_table, 128, cell_high[32:64, :], cell_low[32:64, :]),
+            gathered_by_product(cell_table[...], cell_high, cell_low, tiles),
+            gathered(cell_table, 128, cell_high[8 * tiles :, :], cell_low[8 * tiles :, :]),
         ],
         axis=0,
     )

time: 83.4 us -> 83.2 us (level)
  no operation moved by 1% of the time
where the time goes in v13:
time: 83.2 us; the launch traced here: 83 us
  blocking collectives  55 us (66%)
  Pallas kernels  17.2 us (21%)
  starting transfers between devices  8.54 us (10%)
  waiting for transfers between devices  1.17 us (1%)
  between operations  0.88 us (1%)
    all_to_all x3, blocking collectives, body(): lax.all_to_all(sent.reshape(128, 1, -1), ('row', 'col'), split_axis=0, co...  55 us
    pallas_call x17, Pallas kernels, call(): pl.pallas_call(kernel, out_shape=outputs, in_specs=[pl.BlockSpec(memory_s...  17.2 us
    ppermute x4, starting transfers between devices, swapped(): far = lax.ppermute(far, ('row', 'col'), routes[1])  5.12 us
    ppermute x4, starting transfers between devices, swapped(): return (lax.ppermute(near, ('row', 'col'), routes[0]), far)  2.94 us
  transfers between devices with their start and end apart: 9, of which 3 were waited for; matrix products, arithmetic and copies ran while one was open for 0% of the time, Pallas kernels for 9%

profile of v13, /device:TPU:1, one launch (start us, length us, event | category | flops | bytes accessed | tf_op | source)
XLA Modules:
  0.0 83.0 jit_solution(12447862603879012447)
XLA Ops:
  0.6 0.0 copy-start.1
  0.6 0.0 copy-start.5
  0.7 0.0 copy-start.6
  0.7 0.0 copy-start
  0.7 0.0 copy-start.4
  0.7 0.0 copy-start.3
  0.7 0.0 copy-start.2
  0.7 1.1 %shard_map.140 = (f32[5,64,256]{2,1,0:T(8,128)S(1)}, f32[48,128]{1,0:T(8,128)S(1)}, f32[40,128]{1,0:T(8,128)S(1)}) custom-call(f32[64,256]{1,0:T(8,128)} %surface.1, f32[64,256]{1,0:T(8,128)} %cond_x.1, f32[64,256]{1,0:T(8,128)} %cond_y.1, f32[64,256]{1,0:T(8,128)} %porosity.1, f32[64,256]{1,0:T(8,128)} %rainfall.1, f32[32,256]{1,0:T(8,128)} %pipes.3), custom_call_target="tpu_custom_call" | custom-call | flops 1000000000 | bytes 1048576 | tf_op jit(solution)/shard_map/pallas_call | solution.py:554
  1.8 0.0 copy-start.7
  1.8 2.7 %collective-permute-start.1 = (f32[40,128]{1,0:T(8,128)S(1)}, f32[40,128]{1,0:T(8,128)S(1)}, u32[]{:S(2)}, u32[]{:S(2)}) collective-permute-start(f32[40,128]{1,0:T(8,128)S(1)} %get-tuple-element.53), channel_id=1, source_target_pairs={{0,1},{1,0},{2,3},{3,2},{4,5},{5,4},{6,7},{7,6},{8,9},{9,8},{10,11... | collective-permute-start | bytes 61448 | tf_op jit(solution)/shard_map/ppermute | solution.py:590
  4.5 0.5 collective-permute-start
  5.0 0.0 copy-done.5
  5.0 0.1 copy.18
  5.1 0.0 copy-done.6
  5.1 0.1 copy.19
  5.2 0.0 copy-done.1
  5.2 0.0 copy-done
  5.2 0.0 copy-done.4
  5.2 0.0 copy-done.3
  5.2 0.0 copy-done.2
  5.3 0.7 shard_map.142
  6.0 0.0 copy-done.7
  6.0 0.1 copy.20
  6.1 0.0 collective-permute-done.1.far
  6.1 0.0 collective-permute-done.near
  6.1 0.1 shard_map.143
  6.2 1.1 %collective-permute-start.3 = (f32[136,128]{1,0:T(8,128)S(1)}, f32[136,128]{1,0:T(8,128)S(1)}, u32[]{:S(2)}, u32[]{:S(2)}) collective-permute-start(f32[136,128]{1,0:T(8,128)S(1)} %get-tuple-element.60), channel_id=1, source_target_pairs={{0,16},{1,2},{2,1},{3,4},{4,3},{5,6},{6,5},{7,8},{8,7},{9,10},{10,... | collective-permute-start | bytes 208904 | tf_op jit(solution)/shard_map/ppermute | solution.py:590
  7.3 1.5 %collective-permute-start.2 = (f32[136,128]{1,0:T(8,128)S(1)}, f32[136,128]{1,0:T(8,128)S(1)}, u32[]{:S(2)}, u32[]{:S(2)}) collective-permute-start(f32[136,128]{1,0:T(8,128)S(1)} %get-tuple-element.60), channel_id=1, source_target_pairs={{0,1},{1,0},{2,3},{3,2},{4,5},{5,4},{6,7},{7,6},{8,9},{9,8},{10,11... | collective-permute-start | bytes 208904 | tf_op jit(solution)/shard_map/ppermute | solution.py:591
  8.8 1.4 %shard_map.145.hot = bf16[8192,256]{1,0:T(8,128)(2,1)S(1)} custom-call(s32[128,64]{1,0:T(8,128)S(1)} %bitcast.23), custom_call_target="tpu_custom_call" | custom-call | flops 1000000000 | bytes 1048576 | tf_op jit(solution)/shard_map/pallas_call | solution.py:554
  10.2 0.0 collective-permute-done.3.far_col
  10.3 0.3 collective-permute-done.2.near_col
  10.5 1.7 %shard_map.144 = (f32[6,72,384]{2,1,0:T(8,128)S(1)}, f32[64,384]{1,0:T(8,128)S(1)}, s32[64,128]{1,0:T(8,128)S(1)}, s32[64,128]{1,0:T(8,128)S(1)}, s32[128,128]{1...) custom-call(f32[5,72,256]{2,1,0:T(8,128)S(1)} %get-tuple-element.58., ...), custom_call_target="tpu_custom_call" | custom-call | flops 1000000000 | bytes 1048576 | tf_op jit(solution)/shard_map/pallas_call | solution.py:554
  12.2 25.0 %all_to_all.15 = f32[128,1,768]{2,1,0:T(1,128)S(1)} all-to-all(f32[128,1,768]{2,1,0:T(1,128)S(1)} %bitcast.21), channel_id=1, replica_groups=mesh['row'=8,'col'=16] {'row','col'}, dimensions={0} | all-to-all | bytes 786432 | tf_op jit(solution)/shard_map/all_to_all | solution.py:650
  37.2 1.4 %shard_map.146 = (f32[64,384]{1,0:T(8,128)S(1)}, f32[12,128]{1,0:T(8,128)S(1)}, f32[12,128]{1,0:T(8,128)S(1)}, f32[64,128]{1,0:T(8,128)S(1)}, f32[128,128]{1,0:T(8,128)S(1)}) custom-call(f32[768,128]{1,0:T(8,128)S(1)} %bitcast.16, f32[64,384]{1,0:T(8,128)S(1)} %get-tuple-element.67.surface, f32[64,384]{1,0:T(8,128)S(1)} %get-tuple-element.68.inverse, ...), custom_call_target="tpu_custom_call" | custom-call | flops 1000000000 | bytes 1048576 | tf_op jit(solution)/shard_map/pallas_call | solution.py:554
  38.5 0.8 %collective-permute-start.5 = (f32[12,128]{1,0:T(8,128)S(1)}, f32[12,128]{1,0:T(8,128)S(1)}, u32[]{:S(2)}, u32[]{:S(2)}) collective-permute-start(f32[12,128]{1,0:T(8,128)S(1)} %shard_map.147), channel_id=1, source_target_pairs={{0,1},{1,0},{2,3},{3,2},{4,5},{5,4},{6,7},{7,6},{8,9},{9,8},{10,11... | collective-permute-start | bytes 18440 | tf_op jit(solution)/shard_map/ppermute | solution.py:590
  39.4 0.4 collective-permute-start.4
  39.8 1.8 %shard_map.148 = (f32[64,128]{1,0:T(8,128)S(1)}, f32[64,128]{1,0:T(8,128)S(1)}) custom-call(f32[768,128]{1,0:T(8,128)S(1)} %bitcast.17, f32[64,128]{1,0:T(8,128)S(1)} %get-tuple-element.62.nodes, s32[64,128]{1,0:T(8,128)S(1)} %get-tuple-element.80.node_high, s32[64,128]{1,0:T(8,128)S(1)} %get-tuple-element.81.node_low, ...), custom_call_target="tpu_custom_call" | custom-call | flops 1000000000 | bytes 1048576 | tf_op jit(solution)/shard_map/pallas_call | solution.py:554
  41.6 0.1 collective-permute-done.5.far
  41.7 0.0 collective-permute-done.4.near
  41.7 1.5 %shard_map.149 = (f32[64,384]{1,0:T(8,128)S(1)}, f32[64,128]{1,0:T(8,128)S(1)}, f32[128,128]{1,0:T(8,128)S(1)}, f32[512,128]{1,0:T(8,128)S(1)}) custom-call(f32[64,384]{1,0:T(8,128)S(1)} %get-tuple-element.75.surface, f32[12,128]{1,0:T(8,128)S(1)} %collective-permute-done.4.near, f32[12,128]{1,0:T(8,128)S(1)} %collective-permute-done.5.far, ...), custom_call_target="tpu_custom_call" | custom-call | flops 1000000000 | bytes 1048576 | tf_op jit(solution)/shard_map/pallas_call | solution.py:554
  43.2 15.5 %all_to_all.16 = f32[128,1,512]{2,1,0:T(1,128)S(1)} all-to-all(f32[128,1,512]{2,1,0:T(1,128)S(1)} %bitcast.25), channel_id=1, replica_groups=mesh['row'=8,'col'=16] {'row','col'}, dimensions={0} | all-to-all | bytes 524288 | tf_op jit(solution)/shard_map/all_to_all | solution.py:650
  58.6 1.4 %shard_map.150 = (f32[64,384]{1,0:T(8,128)S(1)}, f32[48,128]{1,0:T(8,128)S(1)}, f32[12,128]{1,0:T(8,128)S(1)}) custom-call(f32[512,128]{1,0:T(8,128)S(1)} %bitcast.13, f32[64,384]{1,0:T(8,128)S(1)} %get-tuple-element.88.surface, f32[64,384]{1,0:T(8,128)S(1)} %get-tuple-element.68.inverse, f32[64,128]{1,0:T(8,128)S(1)} %get-tuple-element.89.heads, ...), custom_call_target="tpu_custom_call" | custom-call | flops 1000000000 | bytes 1048576 | tf_op jit(solution)/shard_map/pallas_call | solution.py:554
  60.0 0.6 collective-permute-start.6
  60.6 0.5 collective-permute-start.7
  61.1 0.7 shard_map.151.rest_1_
  61.8 0.0 collective-permute-done.6.rest_0_.near
  61.8 1.1 %shard_map.152 = (f32[64,128]{1,0:T(8,128)S(1)}, f32[64,128]{1,0:T(8,128)S(1)}) custom-call(f32[512,128]{1,0:T(8,128)S(1)} %bitcast.15, f32[64,128]{1,0:T(8,128)S(1)} %get-tuple-element.86.nodes, s32[64,128]{1,0:T(8,128)S(1)} %get-tuple-element.80.node_high, s32[64,128]{1,0:T(8,128)S(1)} %get-tuple-element.81.node_low, ...), custom_call_target="tpu_custom_call" | custom-call | flops 1000000000 | bytes 1048576 | tf_op jit(solution)/shard_map/pallas_call | solution.py:554
  62.9 0.8 collective-permute-done.7.far
  63.7 1.3 %shard_map.153 = (f32[64,384]{1,0:T(8,128)S(1)}, f32[64,128]{1,0:T(8,128)S(1)}, f32[128,128]{1,0:T(8,128)S(1)}, f32[384,128]{1,0:T(8,128)S(1)}) custom-call(f32[64,384]{1,0:T(8,128)S(1)} %get-tuple-element.93.surface, f32[48,128]{1,0:T(8,128)S(1)} %collective-permute-done.6.rest_0_.near, f32[12,128]{1,0:T(8,128)S(1)} %collective-permute-done.7.far, ...), custom_call_target="tpu_custom_call" | custom-call | flops 1000000000 | bytes 1048576 | tf_op jit(solution)/shard_map/pallas_call | solution.py:554
  64.9 14.5 %all_to_all.17 = f32[128,1,384]{2,1,0:T(1,128)S(1)} all-to-all(f32[128,1,384]{2,1,0:T(1,128)S(1)} %bitcast.26), channel_id=1, replica_groups=mesh['row'=8,'col'=16] {'row','col'}, dimensions={0} | all-to-all | bytes 393216 | tf_op jit(solution)/shard_map/all_to_all | solution.py:650
  79.5 0.5 collective-permute-start.8
  80.0 1.4 %shard_map.154 = f32[64,256]{1,0:T(8,128)} custom-call(f32[384,128]{1,0:T(8,128)S(1)} %bitcast.19, f32[64,384]{1,0:T(8,128)S(1)} %get-tuple-element.99.surface, f32[64,384]{1,0:T(8,128)S(1)} %get-tuple-element.68.inverse, f32[64,128]{1,0:T(8,128)S(1)} %get-tuple-element.100.heads, f32[128,128]{1,0:T(8,128)S(1)} %get-tuple-element.101.zone, ...), custom_call_target="tpu_custom_call" | custom-call | flops 1000000000 | bytes 1048576 | tf_op jit(solution)/shard_map/pallas_call | solution.py:554
  81.4 0.0 collective-permute-done.8.rest_0_
  81.4 1.6 %shard_map.156 = f32[32,256]{1,0:T(8,128)} custom-call(f32[384,128]{1,0:T(8,128)S(1)} %bitcast.20, f32[64,128]{1,0:T(8,128)S(1)} %get-tuple-element.97.nodes, s32[64,128]{1,0:T(8,128)S(1)} %get-tuple-element.80.node_high, s32[64,128]{1,0:T(8,128)S(1)} %get-tuple-element.81.node_low, f32[64,128]{1,0:T(8,128)S(1)} %get-tuple-element.63.coef, ...), custom_call_target="tpu_custom_call" | custom-call | flops 1000000000 | bytes 1048576 | tf_op jit(solution)/shard_map/pallas_call | solution.py:554
  (3 shorter events, 0.0 us)
Async XLA Ops:
  0.6 4.6 %copy-start.1 = (f32[32,256]{1,0:T(8,128)S(1)}, f32[32,256]{1,0:T(8,128)}, u32[]{:S(2)}) copy-start(f32[32,256]{1,0:T(8,128)} %pipes.3) | copy-start | bytes 98308
  0.6 4.4 %copy-start.5 = (s32[128,1,64]{0,2,1:T(8,128)S(1)}, s32[128,1,64]{0,2,1:T(8,128)}, u32[]{:S(2)}) copy-start(s32[128,1,64]{0,2,1:T(8,128)} %param.24) | copy-start | bytes 98308
  0.7 4.4 %copy-start.6 = (f32[128,1,64]{0,2,1:T(8,128)S(1)}, f32[128,1,64]{0,2,1:T(8,128)}, u32[]{:S(2)}) copy-start(f32[128,1,64]{0,2,1:T(8,128)} %param.25) | copy-start | bytes 98308
  0.7 4.6 %copy-start = (f32[4,32,32]{2,1,0:T(8,128)S(1)}, f32[4,32,32]{2,1,0:T(8,128)}, u32[]{:S(2)}) copy-start(f32[4,32,32]{2,1,0:T(8,128)} %param.22) | copy-start | bytes 49156
  0.7 4.6 %copy-start.4 = (s32[256]{0:T(256)S(1)}, s32[256]{0:T(256)}, u32[]{:S(2)}) copy-start(s32[256]{0:T(256)} %param.21) | copy-start | bytes 3076
  0.7 4.6 %copy-start.3 = (s32[256]{0:T(256)S(1)}, s32[256]{0:T(256)}, u32[]{:S(2)}) copy-start(s32[256]{0:T(256)} %param.20) | copy-start | bytes 3076
  0.7 4.6 %copy-start.2 = (s32[256]{0:T(256)S(1)}, s32[256]{0:T(256)}, u32[]{:S(2)}) copy-start(s32[256]{0:T(256)} %param.19) | copy-start | bytes 3076
  1.8 4.1 %copy-start.7 = (s32[1,128,64]{1,2,0:T(8,128)S(1)}, s32[1,128,64]{1,2,0:T(8,128)}, u32[]{:S(2)}) copy-start(s32[1,128,64]{1,2,0:T(8,128)} %param.23) | copy-start | bytes 98308
  1.8 4.2 %collective-permute-start.1 = (f32[40,128]{1,0:T(8,128)S(1)}, f32[40,128]{1,0:T(8,128)S(1)}, u32[]{:S(2)}, u32[]{:S(2)}) collective-permute-start(f32[40,128]{1,0:T(8,128)S(1)} %get-tuple-element.53), channel_id=1, source_target_pairs={{0,1},{1,0},{2,3},{3,2},{4,5},{5,4},{6,7},{7,6},{8,9},{9,8},{10,11... | collective-permute-start | bytes 61448 | tf_op jit(solution)/shard_map/ppermute | solution.py:590
  4.5 1.6 %collective-permute-start = (f32[48,128]{1,0:T(8,128)S(1)}, f32[48,128]{1,0:T(8,128)S(1)}, u32[]{:S(2)}, u32[]{:S(2)}) collective-permute-start(f32[48,128]{1,0:T(8,128)S(1)} %shard_map.141), channel_id=1, source_target_pairs={{0,16},{1,17},{2,18},{3,19},{4,20},{5,21},{6,22},{7,23},{8,24},{9,... | collective-permute-start | bytes 73736 | tf_op jit(solution)/shard_map/ppermute | solution.py:591
  6.2 4.0 %collective-permute-start.3 = (f32[136,128]{1,0:T(8,128)S(1)}, f32[136,128]{1,0:T(8,128)S(1)}, u32[]{:S(2)}, u32[]{:S(2)}) collective-permute-start(f32[136,128]{1,0:T(8,128)S(1)} %get-tuple-element.60), channel_id=1, source_target_pairs={{0,16},{1,2},{2,1},{3,4},{4,3},{5,6},{6,5},{7,8},{8,7},{9,10},{10,... | collective-permute-start | bytes 208904 | tf_op jit(solution)/shard_map/ppermute | solution.py:590
  7.3 3.2 %collective-permute-start.2 = (f32[136,128]{1,0:T(8,128)S(1)}, f32[136,128]{1,0:T(8,128)S(1)}, u32[]{:S(2)}, u32[]{:S(2)}) collective-permute-start(f32[136,128]{1,0:T(8,128)S(1)} %get-tuple-element.60), channel_id=1, source_target_pairs={{0,1},{1,0},{2,3},{3,2},{4,5},{5,4},{6,7},{7,6},{8,9},{9,8},{10,11... | collective-permute-start | bytes 208904 | tf_op jit(solution)/shard_map/ppermute | solution.py:591
  38.5 3.2 %collective-permute-start.5 = (f32[12,128]{1,0:T(8,128)S(1)}, f32[12,128]{1,0:T(8,128)S(1)}, u32[]{:S(2)}, u32[]{:S(2)}) collective-permute-start(f32[12,128]{1,0:T(8,128)S(1)} %shard_map.147), channel_id=1, source_target_pairs={{0,1},{1,0},{2,3},{3,2},{4,5},{5,4},{6,7},{7,6},{8,9},{9,8},{10,11... | collective-permute-start | bytes 18440 | tf_op jit(solution)/shard_map/ppermute | solution.py:590
  39.4 2.3 %collective-permute-start.4 = (f32[12,128]{1,0:T(8,128)S(1)}, f32[12,128]{1,0:T(8,128)S(1)}, u32[]{:S(2)}, u32[]{:S(2)}) collective-permute-start(f32[12,128]{1,0:T(8,128)S(1)} %get-tuple-element.76), channel_id=1, source_target_pairs={{0,16},{1,17},{2,18},{3,19},{4,20},{5,21},{6,22},{7,23},{8,24},{9,... | collective-permute-start | bytes 18440 | tf_op jit(solution)/shard_map/ppermute | solution.py:591
  60.0 1.8 %collective-permute-start.6 = (f32[48,128]{1,0:T(8,128)S(1)}, f32[48,128]{1,0:T(8,128)S(1)}, u32[]{:S(2)}, u32[]{:S(2)}) collective-permute-start(f32[48,128]{1,0:T(8,128)S(1)} %get-tuple-element.94), channel_id=1, source_target_pairs={{0,16},{1,17},{2,18},{3,19},{4,20},{5,21},{6,22},{7,23},{8,24},{9,... | collective-permute-start | bytes 73736 | tf_op jit(solution)/shard_map/ppermute | solution.py:591
  60.6 3.1 %collective-permute-start.7 = (f32[12,128]{1,0:T(8,128)S(1)}, f32[12,128]{1,0:T(8,128)S(1)}, u32[]{:S(2)}, u32[]{:S(2)}) collective-permute-start(f32[12,128]{1,0:T(8,128)S(1)} %get-tuple-element.95), channel_id=1, source_target_pairs={{0,1},{1,0},{2,3},{3,2},{4,5},{5,4},{6,7},{7,6},{8,9},{9,8},{10,11... | collective-permute-start | bytes 18440 | tf_op jit(solution)/shard_map/ppermute | solution.py:590
  79.5 1.9 %collective-permute-start.8 = (f32[32,128]{1,0:T(8,128)S(1)}, f32[32,128]{1,0:T(8,128)S(1)}, u32[]{:S(2)}, u32[]{:S(2)}) collective-permute-start(f32[32,128]{1,0:T(8,128)S(1)} %shard_map.155), channel_id=1, source_target_pairs={{0,16},{1,17},{2,18},{3,19},{4,20},{5,21},{6,22},{7,23},{8,24},{9,... | collective-permute-start | bytes 49160 | tf_op jit(solution)/shard_map/ppermute | solution.py:585
